TPU v7x, 128 devices: a whole 4x4x4 slice. The times are simulated.
128 devices in a mesh: plane: 8 (over x, core), elem: 16 (over z, y).
Axes of the slice: x: 4, y: 4, z: 4, core: 2. Of those that a mesh axis runs over, the one named last changes fastest.
Arguments:
- scalar_modes: float32 [256, 6, 6, 2048], P('plane', None, None, 'elem'), may hold values from -6 to 6
- velocity: float32 [2, 256, 6, 6, 2048], P(None, None, None, None, ('elem', 'plane')), may hold values from -0.5 to 0.5
- viscosity: float32 [2048], P('elem'), may hold values from 0.05 to 0.5
- mortar_links: int32 [8, 2048], P(None, 'elem'), may hold values from 0 to 2047, as said below
- mortar_sides: int32 [2, 8, 2048], P(None, None, 'elem'), may hold values from 0 to 3, as said below
- layout: int32 [2048], P('elem'), may hold values from 0 to 1, as said below
Outputs:
- advanced: float32 [256, 6, 6, 2048], P('plane', None, None, 'elem')
Inputs may be any that keep to these rules, and one draw needn't show every extreme that they name: `mortar_links`: slots 0 and 1 lie on the west face, 2 and 3 on the east, 4 and 5 on the south, 6 and 7 on the north; an unused slot names the element itself. The relation is symmetric (the neighbour's slot on the opposite face names the element back, with the two rows of mortar_sides swapped). A west neighbour lies on the same index of elem or on the index before, an east neighbour on the same or the one after, cyclically; south and north neighbours on the same. At most 16 elements of one index of elem have a west neighbour on another index (likewise east), and some index has exactly that many. `mortar_sides`: 0 the whole face, 1 its lower half, 2 its upper half, 3 an unused slot (both rows 3). The second slot of a face is used only where the first has own code 1 and the second own code 2. `layout`: 0: the element is 1 wide and 2 tall; 1: 2 wide and 1 tall. All elements of one index of elem share it.
All inputs are finite; a program needn't handle non-finite values.
Results may differ from a plain program's by a relative error of at most 0.0003.
Values sent between devices are 32-bit elements; how exact they have to be, the bound alone decides.
No kernel may reach another device: no remote copies, remote signals or barrier semaphores. Data moves between devices by JAX's collectives and lax.ppermute only.
A program may use at most 128 MiB of HBM per device.

v0:
```python
import math

import jax
import jax.numpy as jnp
import numpy as np
from jax import lax
from jax.sharding import PartitionSpec as P

ITERS = 4


highest = lax.Precision.HIGHEST
inv_step = 2.0
penalty = 10.0
spanwise = 0.0625


def from_behind(array, axis, by):
    devices = lax.axis_size(axis)
    return lax.ppermute(array, axis, [(i, (i + by) % devices) for i in range(devices)])


def lagrange_at(points, targets):
    matrix_out = np.ones((6, 6))
    for row_a in range(6):
        for col_b in range(6):
            for other_k in range(6):
                if other_k != col_b:
                    matrix_out[row_a, col_b] *= (targets[row_a] - points[other_k]) / (
                        points[col_b] - points[other_k]
                    )
    return matrix_out


def node_tables():
    root_seven = math.sqrt(7.0)
    outer_point = math.sqrt(1.0 / 3.0 + 2.0 * root_seven / 21.0)
    inner_point = math.sqrt(1.0 / 3.0 - 2.0 * root_seven / 21.0)
    points = np.array([-1.0, -outer_point, -inner_point, inner_point, outer_point, 1.0])
    weights = np.array(
        [
            1.0 / 15.0,
            (14.0 - root_seven) / 30.0,
            (14.0 + root_seven) / 30.0,
            (14.0 + root_seven) / 30.0,
            (14.0 - root_seven) / 30.0,
            1.0 / 15.0,
        ]
    )
    barycentric = np.array(
        [
            1.0
            / np.prod([points[col_j] - points[other_k] for other_k in range(6) if other_k != col_j])
            for col_j in range(6)
        ]
    )
    derivative = np.zeros((6, 6))
    for row_i in range(6):
        for col_j in range(6):
            if row_i != col_j:
                derivative[row_i, col_j] = (
                    barycentric[col_j] / barycentric[row_i] / (points[row_i] - points[col_j])
                )
        derivative[row_i, row_i] = -np.sum(derivative[row_i])
    lower_half = lagrange_at(points, (points - 1.0) / 2.0)
    upper_half = lagrange_at(points, (points + 1.0) / 2.0)
    stiffness = derivative.T @ (weights[:, None] * derivative)
    return (
        jnp.asarray(weights, jnp.float32),
        jnp.asarray(derivative, jnp.float32),
        jnp.asarray(lower_half, jnp.float32),
        jnp.asarray(upper_half, jnp.float32),
        jnp.asarray(stiffness, jnp.float32),
    )


def plane_tables(plane_count):
    planes = np.arange(plane_count)[:, None]
    coeffs = np.arange(plane_count)[None, :]
    harmonic = (coeffs + 1) // 2
    phase_angle = 2.0 * np.pi * (harmonic * planes % plane_count) / plane_count
    synthesis = np.where(
        coeffs == 0, 1.0, np.where(coeffs % 2 == 1, np.cos(phase_angle), np.sin(phase_angle))
    )
    normalizer = np.where(
        (coeffs == 0) | (coeffs == plane_count - 1), float(plane_count), plane_count / 2.0
    )
    analysis = (synthesis / normalizer).T
    return (jnp.asarray(synthesis, jnp.float32), jnp.asarray(analysis, jnp.float32))


def transform(matrix, volume):
    flat = jnp.dot(matrix, volume.reshape(volume.shape[0], -1), precision=highest)
    return flat.reshape(volume.shape)


def along_first(matrix, volume):
    return jnp.einsum("ia,zaje->zije", matrix, volume, precision=highest)


def along_second(matrix, volume):
    return jnp.einsum("jb,zibe->zije", matrix, volume, precision=highest)


def on_face(matrix, trace_in):
    return jnp.einsum("ab,zbe->zae", matrix, trace_in, precision=highest)


def cut_face(trace_in, code_hot, lower_half, upper_half):
    return (
        trace_in * code_hot[0]
        + on_face(lower_half, trace_in) * code_hot[1]
        + on_face(upper_half, trace_in) * code_hot[2]
    )


def spread_face(jump_in, code_hot, lower_half, upper_half):
    return (
        jump_in * code_hot[0]
        + on_face(lower_half.T, jump_in) * code_hot[1]
        + on_face(upper_half.T, jump_in) * code_hot[2]
    )


def face_traces(volume):
    return [volume[:, 0, :, :], volume[:, 5, :, :], volume[:, :, 0, :], volume[:, :, 5, :]]


def code_table(codes):
    return jnp.stack([(codes == level_id).astype(jnp.float32) for level_id in range(3)], axis=1)


def add_faces(result, extras):
    result = result.at[:, 0, :, :].add(extras[0])
    result = result.at[:, 5, :, :].add(extras[1])
    result = result.at[:, :, 0, :].add(extras[2])
    return result.at[:, :, 5, :].add(extras[3])


def mortar_sum(faces, neighbours, own_hot, far_hot, weights, lower_half, upper_half):
    extras = []
    for face_id in range(4):
        total_face = jnp.zeros_like(faces[face_id])
        for half_id in range(2):
            slot_id = 2 * face_id + half_id
            jump_in = cut_face(faces[face_id], own_hot[slot_id], lower_half, upper_half) - cut_face(
                neighbours[slot_id], far_hot[slot_id], lower_half, upper_half
            )
            total_face = total_face + spread_face(
                weights[None, :, None] * jump_in, own_hot[slot_id], lower_half, upper_half
            )
        extras.append(penalty * total_face)
    return extras


def local_part(volume, shift_mode, viscosity, ratio_x, ratio_y, weights, stiffness):
    grad_x = along_first(stiffness, volume) * weights[None, None, :, None]
    grad_y = along_second(stiffness, volume) * weights[None, :, None, None]
    mass_w = 0.5 * weights[:, None] * weights[None, :]
    return (
        viscosity * (ratio_x * grad_x + ratio_y * grad_y)
        + shift_mode * mass_w[None, :, :, None] * volume
    )


def mode_sum(left_in, right_in):
    return jnp.sum(left_in * right_in, axis=(1, 2, 3))


def per_mode(values):
    return values[:, None, None, None]


def shards(scalar_modes, velocity, viscosity, mortar_links, mortar_sides, layout):
    weights, derivative, lower_half, upper_half, stiffness = node_tables()
    mode_count = scalar_modes.shape[0]
    per_dev = scalar_modes.shape[3]
    total_planes = velocity.shape[1]
    synthesis, analysis = plane_tables(total_planes)
    plane_id = lax.axis_index("plane")
    elem_id = lax.axis_index("elem")
    width_x = jnp.where(layout == 0, 1.0, 2.0).astype(jnp.float32)
    width_y = 3.0 - width_x
    ratio_x = width_y / width_x
    ratio_y = width_x / width_y
    own_hot = code_table(mortar_sides[0])
    far_hot = code_table(mortar_sides[1])
    grad_x = along_first(derivative, scalar_modes) * (2.0 / width_x)
    grad_y = along_second(derivative, scalar_modes) * (2.0 / width_y)
    moved_x, moved_y = (
        lax.all_to_all(grad_x, "plane", split_axis=3, concat_axis=0, tiled=True),
        lax.all_to_all(grad_y, "plane", split_axis=3, concat_axis=0, tiled=True),
    )
    phys_x = transform(synthesis, moved_x)
    phys_y = transform(synthesis, moved_y)
    product = -(velocity[0] * phys_x + velocity[1] * phys_y)
    advection = lax.all_to_all(
        transform(analysis, product), "plane", split_axis=0, concat_axis=3, tiled=True
    )
    mass_w = 0.5 * weights[:, None] * weights[None, :]
    rhs_all = mass_w[None, :, :, None] * (inv_step * scalar_modes + advection)
    neighbour_dev = mortar_links // per_dev
    neighbour_loc = mortar_links % per_dev
    remote = neighbour_dev != elem_id
    west_index = jnp.where(remote[0:2], per_dev + neighbour_loc[0:2], neighbour_loc[0:2])
    east_index = jnp.where(remote[2:4], per_dev + neighbour_loc[2:4], neighbour_loc[2:4])

    def operate(volume, shift_mode):
        faces = face_traces(volume)
        from_west = from_behind(faces[1], "elem", 1)
        from_east = from_behind(faces[0], "elem", -1)
        west_pool = jnp.concatenate([faces[1], from_west], axis=2)
        east_pool = jnp.concatenate([faces[0], from_east], axis=2)
        neighbours = [
            jnp.take(west_pool, west_index[0], axis=2),
            jnp.take(west_pool, west_index[1], axis=2),
            jnp.take(east_pool, east_index[0], axis=2),
            jnp.take(east_pool, east_index[1], axis=2),
            jnp.take(faces[3], neighbour_loc[4], axis=2),
            jnp.take(faces[3], neighbour_loc[5], axis=2),
            jnp.take(faces[2], neighbour_loc[6], axis=2),
            jnp.take(faces[2], neighbour_loc[7], axis=2),
        ]
        result = local_part(volume, shift_mode, viscosity, ratio_x, ratio_y, weights, stiffness)
        return add_faces(
            result, mortar_sum(faces, neighbours, own_hot, far_hot, weights, lower_half, upper_half)
        )

    coeff_id = plane_id * mode_count + jnp.arange(mode_count, dtype=jnp.int32)
    harmonic = ((coeff_id + 1) // 2).astype(jnp.float32)
    shift_mode = inv_step + viscosity[None, None, None, :] * per_mode((spanwise * harmonic) ** 2)
    solution = scalar_modes
    residual = rhs_all - operate(scalar_modes, shift_mode)

    def norm_total(vector_in):
        return lax.psum(mode_sum(vector_in, vector_in), "elem")

    direction = residual
    norm_now = norm_total(residual)
    for turn_id in range(ITERS):
        image_dir = operate(direction, shift_mode)
        step_size = norm_now / lax.psum(mode_sum(direction, image_dir), "elem")
        solution = solution + per_mode(step_size) * direction
        if turn_id + 1 < ITERS:
            residual = residual - per_mode(step_size) * image_dir
            norm_next = norm_total(residual)
            direction = residual + per_mode(norm_next / norm_now) * direction
            norm_now = norm_next
    return solution


def solution(mesh):
    placed = (
        P("plane", None, None, "elem"),
        P(None, None, None, None, ("elem", "plane")),
        P("elem"),
        P(None, "elem"),
        P(None, None, "elem"),
        P("elem"),
    )
    return jax.shard_map(
        shards,
        mesh=mesh,
        in_specs=placed,
        out_specs=P("plane", None, None, "elem"),
        check_vma=False,
    )
```

profile of v0, /device:TPU:0, one launch (start us, length us, event | category | flops | bytes accessed | tf_op | source)
XLA Modules:
  0.0 849.9 jit_solution(13594954370959136757)
XLA Ops:
  5.8 3.5 reshape.1642
  9.3 4.5 all-to-all-start.1
  15.5 5.5 collective-permute-start.1
  56.3 3.1 copy.3219
  59.4 3.4 reshape.1644
  84.0 4.8 all-to-all-start
  93.5 2.8 reshape.1643
  96.4 3.3 copy.3225
  101.1 3.2 reduce.41
  104.3 2.8 reshape.1645
  107.1 3.3 copy.3221
  115.7 5.2 copy.3226
  120.8 5.4 reshape.1646
  126.2 4.8 all-to-all-start.2
  134.0 8.1 all-to-all-done.2
  144.2 5.4 reshape.1647
  149.7 4.7 copy.3228
  249.8 40.7 %all-reduce = (f32[32]{0:T(128)S(1)}, f32[32]{0:T(128)S(1)}) all-reduce(f32[32]{0:T(128)S(1)} %copy-done.350, f32[32]{0:T(128)S(1)} %multiply_reduce_fusion.6), channel_id=1, replica_groups=mesh['plane'=8,'elem'=16] {'elem'}, use_global_device_ids=true, to_apply=%region_1.4 | all-reduce | flops 64 | bytes 512 | tf_op jit(solution)/shard_map/psum | solution.py:236
  290.8 35.5 %psum.58 = f32[32]{0:T(128)S(1)} all-reduce(f32[32]{0:T(128)S(1)} %get-tuple-element.251), channel_id=1, replica_groups=mesh['plane'=8,'elem'=16] {'elem'}, use_global_device_ids=true, to_apply=%region_5.8 | all-reduce | flops 32 | bytes 256 | tf_op jit(solution)/shard_map/psum | solution.py:236
  431.6 40.8 %psum.59 = f32[32]{0:T(128)S(1)} all-reduce(f32[32]{0:T(128)S(1)} %multiply_reduce_fusion.4), channel_id=1, replica_groups=mesh['plane'=8,'elem'=16] {'elem'}, use_global_device_ids=true, to_apply=%region_7.10 | all-reduce | flops 32 | bytes 256 | tf_op jit(solution)/shard_map/psum | solution.py:242
  473.2 35.6 %psum.60 = f32[32]{0:T(128)S(1)} all-reduce(f32[32]{0:T(128)} %get-tuple-element.249), channel_id=1, replica_groups=mesh['plane'=8,'elem'=16] {'elem'}, use_global_device_ids=true, to_apply=%region_9.12 | all-reduce | flops 32 | bytes 256 | tf_op jit(solution)/shard_map/psum | solution.py:236
  618.7 41.4 %psum.61 = f32[32]{0:T(128)} all-reduce(f32[32]{0:T(128)} %multiply_reduce_fusion.2), channel_id=1, replica_groups=mesh['plane'=8,'elem'=16] {'elem'}, use_global_device_ids=true, to_apply=%region_11.14 | all-reduce | flops 32 | bytes 256 | tf_op jit(solution)/shard_map/psum | solution.py:242
  662.2 35.6 %psum.62 = f32[32]{0:T(128)S(1)} all-reduce(f32[32]{0:T(128)} %multiply_reduce_fusion.1), channel_id=1, replica_groups=mesh['plane'=8,'elem'=16] {'elem'}, use_global_device_ids=true, to_apply=%region_13.16 | all-reduce | flops 32 | bytes 256 | tf_op jit(solution)/shard_map/psum | solution.py:236
  806.4 40.8 %psum.63 = f32[32]{0:T(128)S(1)} all-reduce(f32[32]{0:T(128)S(1)} %multiply_reduce_fusion), channel_id=1, replica_groups=mesh['plane'=8,'elem'=16] {'elem'}, use_global_device_ids=true, to_apply=%region_15.18 | all-reduce | flops 32 | bytes 256 | tf_op jit(solution)/shard_map/psum | solution.py:242
  (1223 shorter events, 499.1 us)
Async XLA Ops:
  9.3 74.7 %all-to-all-start.1 = ((f32[8,1,18432]{2,1,0:T(1,128)}), f32[8,1,18432]{2,1,0:T(1,128)S(1)}, u32[]{:S(2)}, u32[]{:S(2)}) async-start(f32[8,1,18432]{2,1,0:T(1,128)} %reshape.1642), calls=%async_computation.1 | async-start | bytes 1179648 | tf_op jit(solution)/shard_map/all_to_all | solution.py:192
  13.8 50.5 %collective-permute-start = (f32[32,6,128]{2,0,1:T(8,128)S(1)}, f32[32,6,128]{2,0,1:T(8,128)}, u32[]{:S(2)}, u32[]{:S(2)}) collective-permute-start(f32[32,6,128]{2,0,1:T(8,128)S(1)} %get-tuple-element.302), channel_id=1, source_target_pairs={{0,1},{1,2},{2,3},{3,4},{4,5},{5,6},{6,7},{7,8},{8,9},{9,10},{10,1... | collective-permute-start | bytes 294920 | tf_op jit(solution)/shard_map/ppermute | solution.py:20
  15.5 60.9 %collective-permute-start.1 = (f32[32,6,128]{2,0,1:T(8,128)S(1)}, f32[32,6,128]{2,0,1:T(8,128)}, u32[]{:S(2)}, u32[]{:S(2)}) collective-permute-start(f32[32,6,128]{2,0,1:T(8,128)S(1)} %get-tuple-element.301), channel_id=1, source_target_pairs={{0,15},{1,0},{2,1},{3,2},{4,3},{5,4},{6,5},{7,6},{8,7},{9,8},{10,9... | collective-permute-start | bytes 294920 | tf_op jit(solution)/shard_map/ppermute | solution.py:20
  27.5 18.7 %copy-start.264 = (pred[128]{0:T(512)(128)(4,1)}, pred[128]{0:T(512)(128)(4,1)S(1)}, u32[]{:S(2)}) copy-start(pred[128]{0:T(512)(128)(4,1)S(1)} %get-tuple-element.359) | copy-start | bytes 388
  27.5 24.3 %copy-start.262 = (pred[128]{0:T(512)(128)(4,1)}, pred[128]{0:T(512)(128)(4,1)S(1)}, u32[]{:S(2)}) copy-start(pred[128]{0:T(512)(128)(4,1)S(1)} %get-tuple-element.255) | copy-start | bytes 388
  32.5 19.4 %copy-start.173 = (f32[128]{0:T(128)}, f32[128]{0:T(128)S(1)}, u32[]{:S(2)}) copy-start(f32[128]{0:T(128)S(1)} %get-tuple-element.394) | copy-start | bytes 1540
  32.5 19.4 %copy-start.288 = (f32[128]{0:T(128)}, f32[128]{0:T(128)S(1)}, u32[]{:S(2)}) copy-start(f32[128]{0:T(128)S(1)} %get-tuple-element.319) | copy-start | bytes 1540
  33.1 18.7 %copy-start.192 = (f32[128]{0:T(128)}, f32[128]{0:T(128)S(1)}, u32[]{:S(2)}) copy-start(f32[128]{0:T(128)S(1)} %get-tuple-element.343) | copy-start | bytes 1540
  84.0 17.1 %all-to-all-start = ((f32[8,1,18432]{2,1,0:T(1,128)}), f32[8,1,18432]{2,1,0:T(1,128)}, u32[]{:S(2)}, u32[]{:S(2)}) async-start(f32[8,1,18432]{2,1,0:T(1,128)} %reshape.1644), calls=%async_computation | async-start | bytes 1179648 | tf_op jit(solution)/shard_map/all_to_all | solution.py:191
  126.2 15.9 %all-to-all-start.2 = ((f32[8,1,18432]{2,1,0:T(1,128)}), f32[8,1,18432]{2,1,0:T(1,128)S(1)}, u32[]{:S(2)}, u32[]{:S(2)}) async-start(f32[8,1,18432]{2,1,0:T(1,128)} %reshape.1646), calls=%async_computation.2 | async-start | bytes 1179648 | tf_op jit(solution)/shard_map/all_to_all | solution.py:197
  165.5 51.0 %copy-start.70 = (f32[32,128,6]{1,2,0:T(8,128)}, f32[32,128,6]{1,2,0:T(8,128)S(1)}, u32[]{:S(2)}) copy-start(f32[32,128,6]{1,2,0:T(8,128)S(1)} %fusion.365) | copy-start | bytes 294916
  165.6 62.1 %collective-permute-start.3 = (f32[32,6,128]{2,0,1:T(8,128)S(1)}, f32[32,6,128]{2,0,1:T(8,128)}, u32[]{:S(2)}, u32[]{:S(2)}) collective-permute-start(f32[32,6,128]{2,0,1:T(8,128)S(1)} %get-tuple-element.295), channel_id=1, source_target_pairs={{0,15},{1,0},{2,1},{3,2},{4,3},{5,4},{6,5},{7,6},{8,7},{9,8},{10,9... | collective-permute-start | bytes 294920 | tf_op jit(solution)/shard_map/ppermute | solution.py:20
  167.5 39.0 %collective-permute-start.2 = (f32[32,6,128]{2,0,1:T(8,128)S(1)}, f32[32,6,128]{2,0,1:T(8,128)}, u32[]{:S(2)}, u32[]{:S(2)}) collective-permute-start(f32[32,6,128]{2,0,1:T(8,128)S(1)} %get-tuple-element.296), channel_id=1, source_target_pairs={{0,1},{1,2},{2,3},{3,4},{4,5},{5,6},{6,7},{7,8},{8,9},{9,10},{10,1... | collective-permute-start | bytes 294920 | tf_op jit(solution)/shard_map/ppermute | solution.py:20
  290.5 37.7 %copy-start.344 = (f32[32]{0:T(128)}, f32[32]{0:T(128)S(1)}, u32[]{:S(2)}) copy-start(f32[32]{0:T(128)S(1)} %div.66) | copy-start | bytes 388
  334.3 73.6 %collective-permute-start.5 = (f32[32,6,128]{2,0,1:T(8,128)}, f32[32,6,128]{2,0,1:T(8,128)}, u32[]{:S(2)}, u32[]{:S(2)}) collective-permute-start(f32[32,6,128]{2,0,1:T(8,128)} %get-tuple-element.289), channel_id=1, source_target_pairs={{0,15},{1,0},{2,1},{3,2},{4,3},{5,4},{6,5},{7,6},{8,7},{9,8},{10,9... | collective-permute-start | bytes 294920 | tf_op jit(solution)/shard_map/ppermute | solution.py:20
  336.3 49.2 %collective-permute-start.4 = (f32[32,6,128]{2,0,1:T(8,128)}, f32[32,6,128]{2,0,1:T(8,128)}, u32[]{:S(2)}, u32[]{:S(2)}) collective-permute-start(f32[32,6,128]{2,0,1:T(8,128)} %get-tuple-element.290), channel_id=1, source_target_pairs={{0,1},{1,2},{2,3},{3,4},{4,5},{5,6},{6,7},{7,8},{8,9},{9,10},{10,1... | collective-permute-start | bytes 294920 | tf_op jit(solution)/shard_map/ppermute | solution.py:20
  431.0 41.4 %copy-start.353 = (f32[32]{0:T(128)S(1)}, f32[32]{0:T(128)}, u32[]{:S(2)}) copy-start(f32[32]{0:T(128)} %copy-done.352) | copy-start | bytes 388
  473.2 187.5 %copy-start.3 = (f32[32,6,6,128]{3,0,1,2:T(8,128)}, f32[32,6,6,128]{3,0,1,2:T(8,128)S(1)}, u32[]{:S(2)}) copy-start(f32[32,6,6,128]{3,0,1,2:T(8,128)S(1)} %get-tuple-element.250) | copy-start | bytes 1769476
  517.8 73.7 %collective-permute-start.7 = (f32[32,6,128]{2,0,1:T(8,128)}, f32[32,6,128]{2,0,1:T(8,128)}, u32[]{:S(2)}, u32[]{:S(2)}) collective-permute-start(f32[32,6,128]{2,0,1:T(8,128)} %get-tuple-element.283), channel_id=1, source_target_pairs={{0,15},{1,0},{2,1},{3,2},{4,3},{5,4},{6,5},{7,6},{8,7},{9,8},{10,9... | collective-permute-start | bytes 294920 | tf_op jit(solution)/shard_map/ppermute | solution.py:20
  519.8 49.3 %collective-permute-start.6 = (f32[32,6,128]{2,0,1:T(8,128)}, f32[32,6,128]{2,0,1:T(8,128)}, u32[]{:S(2)}, u32[]{:S(2)}) collective-permute-start(f32[32,6,128]{2,0,1:T(8,128)} %get-tuple-element.284), channel_id=1, source_target_pairs={{0,1},{1,2},{2,3},{3,4},{4,5},{5,6},{6,7},{7,8},{8,9},{9,10},{10,1... | collective-permute-start | bytes 294920 | tf_op jit(solution)/shard_map/ppermute | solution.py:20
  704.7 20.6 %copy-start.190 = (f32[128]{0:T(128)S(1)}, f32[128]{0:T(128)}, u32[]{:S(2)}) copy-start(f32[128]{0:T(128)} %copy-done.185) | copy-start | bytes 1540
  708.4 74.0 %collective-permute-start.9 = (f32[32,6,128]{2,0,1:T(8,128)}, f32[32,6,128]{2,0,1:T(8,128)}, u32[]{:S(2)}, u32[]{:S(2)}) collective-permute-start(f32[32,6,128]{2,0,1:T(8,128)} %get-tuple-element.277), channel_id=1, source_target_pairs={{0,15},{1,0},{2,1},{3,2},{4,3},{5,4},{6,5},{7,6},{8,7},{9,8},{10,9... | collective-permute-start | bytes 294920 | tf_op jit(solution)/shard_map/ppermute | solution.py:20
  710.4 49.5 %collective-permute-start.8 = (f32[32,6,128]{2,0,1:T(8,128)}, f32[32,6,128]{2,0,1:T(8,128)}, u32[]{:S(2)}, u32[]{:S(2)}) collective-permute-start(f32[32,6,128]{2,0,1:T(8,128)} %get-tuple-element.278), channel_id=1, source_target_pairs={{0,1},{1,2},{2,3},{3,4},{4,5},{5,6},{6,7},{7,8},{8,9},{9,10},{10,1... | collective-permute-start | bytes 294920 | tf_op jit(solution)/shard_map/ppermute | solution.py:20
  805.7 42.1 %copy-start.342 = (f32[32]{0:T(128)S(1)}, f32[32]{0:T(128)}, u32[]{:S(2)}) copy-start(f32[32]{0:T(128)} %copy-done.341) | copy-start | bytes 388
  (344 other events, 1704.1 us)
where the time goes:
time: 861 us; the launch traced here: 850 us
  blocking collectives  270 us (31%)
  local copies, waits for them, and re-layouts  260 us (30%)
  matrix products  159 us (18%)
  other arithmetic  115 us (13%)
  starting transfers between devices  29.8 us (3%)
    psum x4, blocking collectives, norm_total(): return lax.psum(mode_sum(vector_in, vector_in), 'elem')  147 us
    dot_general x200, matrix products, on_face(): return jnp.einsum('ab,zbe->zae', matrix, trace_in, precision=highest)  139 us
    psum x3, blocking collectives, shards(): step_size = norm_now / lax.psum(mode_sum(direction, image_dir), 'elem')  123 us
    mul x40, other arithmetic, mortar_sum(): weights[None, :, None] * jump_in  36.9 us
    unnamed x716, local copies, waits for them, and re-layouts  28.6 us
    gather x10, local copies, waits for them, and re-layouts, operate(): jnp.take(faces[3], neighbour_loc[4], axis=2)  20.5 us
    gather x10, local copies, waits for them, and re-layouts, operate(): jnp.take(faces[2], neighbour_loc[6], axis=2)  20.5 us
    gather x10, local copies, waits for them, and re-layouts, operate(): jnp.take(faces[2], neighbour_loc[7], axis=2)  20.5 us
  transfers between devices with their start and end apart: 13, of which 1 were waited for; matrix products, arithmetic and copies ran while one was open for 41% of the time, Pallas kernels for 0%

commit v1 on v0

v1 whole, which is shorter than its diff:
```python
import math

import jax
import jax.numpy as jnp
import ml_dtypes
import numpy as np
from jax import lax
from jax.experimental import pallas as pl
from jax.experimental.pallas import tpu as pltpu
from jax.sharding import PartitionSpec as P

F32 = jnp.float32
BF16 = jnp.bfloat16
PENALTY = 10.0
SPANWISE = 0.0625
VMEM = pltpu.VMEM
SMEM = pltpu.SMEM
LIST_W, LIST_E, RANK, REMOTE, LOCAL = 0, 1, 2, 6, 10


def lagrange_at(points, targets):
    out = np.ones((6, 6))
    for row in range(6):
        for col in range(6):
            for other in range(6):
                if other != col:
                    out[row, col] *= (targets[row] - points[other]) / (points[col] - points[other])
    return out


def node_tables():
    root = math.sqrt(7.0)
    outer = math.sqrt(1.0 / 3.0 + 2.0 * root / 21.0)
    inner = math.sqrt(1.0 / 3.0 - 2.0 * root / 21.0)
    points = np.array([-1.0, -outer, -inner, inner, outer, 1.0])
    half = [1.0 / 15.0, (14.0 - root) / 30.0, (14.0 + root) / 30.0]
    weights = np.array(half + half[::-1])
    bary = np.array(
        [1.0 / np.prod([points[c] - points[k] for k in range(6) if k != c]) for c in range(6)]
    )
    deriv = np.zeros((6, 6))
    for i in range(6):
        for j in range(6):
            if i != j:
                deriv[i, j] = bary[j] / bary[i] / (points[i] - points[j])
        deriv[i, i] = -np.sum(deriv[i])
    lower = lagrange_at(points, (points - 1.0) / 2.0)
    upper = lagrange_at(points, (points + 1.0) / 2.0)
    stiff = deriv.T @ (weights[:, None] * deriv)
    return weights, deriv, lower, upper, stiff


W, D, QLO, QHI, K1 = node_tables()
HALVES = [np.eye(6), QLO, QHI]


def plane_tables(count):
    planes = np.arange(count)[:, None]
    coeffs = np.arange(count)[None, :]
    harmonic = (coeffs + 1) // 2
    phase = 2.0 * np.pi * (harmonic * planes % count) / count
    synth = np.where(coeffs == 0, 1.0, np.where(coeffs % 2 == 1, np.cos(phase), np.sin(phase)))
    norm = np.where((coeffs == 0) | (coeffs == count - 1), float(count), count / 2.0)
    return synth, (synth / norm).T


def split_table(table):
    table = np.asarray(table, np.float32)
    high = table.astype(ml_dtypes.bfloat16)
    low = (table - high.astype(np.float32)).astype(ml_dtypes.bfloat16)
    return np.stack([high, low])


def fold(matrix):
    plus = (matrix[:3, :3] + matrix[:3, :2:-1]) / 2.0
    minus = (matrix[:3, :3] - matrix[:3, :2:-1]) / 2.0
    return plus, minus


STIFF_FOLD = fold(K1 / W[:, None])
DERIV_FOLD = fold(D)


def folded(values, tables, sign):
    plus, minus = tables
    even = [values[a] + values[5 - a] for a in range(3)]
    odd = [values[a] - values[5 - a] for a in range(3)]
    out = [None] * 6
    for i in range(3):
        e = sum(float(plus[i, a]) * even[a] for a in range(3))
        o = sum(float(minus[i, a]) * odd[a] for a in range(3))
        out[i] = e + o
        out[5 - i] = e - o if sign > 0 else o - e
    return out


def split(value):
    high = value.astype(BF16)
    return high, (value - high.astype(F32)).astype(BF16)


def lane_ids(shape):
    return lax.broadcasted_iota(jnp.int32, shape, len(shape) - 1)


def call(kernel, outs, scratch, operands, spaces, flops=4_000_000):
    total = sum(int(np.prod(o.shape)) * 4 for o in outs)
    total += sum(int(np.prod(o.shape)) * 4 for o in operands)
    return pl.pallas_call(
        kernel,
        out_shape=outs,
        in_specs=[pl.BlockSpec(memory_space=s) for s in spaces],
        out_specs=[pl.BlockSpec(memory_space=VMEM) for _ in outs],
        scratch_shapes=scratch,
        compiler_params=pltpu.CompilerParams(vmem_limit_bytes=40 * 2**20),
        cost_estimate=pl.CostEstimate(flops=flops, bytes_accessed=total, transcendentals=0),
    )(*operands)


def shape(*dims, dtype=F32):
    return jax.ShapeDtypeStruct(dims, dtype)


def prep_kernel(meta, links, sides, visc, layout, idx, tab, own_c, far_c):
    me = meta[1]
    dev = lax.shift_right_logical(links[...], 7)
    loc = jnp.bitwise_and(links[...], 127)
    remote = (dev != me).astype(jnp.int32)
    idx[LOCAL : LOCAL + 8, :] = loc
    idx[REMOTE : REMOTE + 4, :] = remote[0:4]
    idx[18:24, :] = jnp.zeros((6, 128), jnp.int32)
    row = lax.broadcasted_iota(jnp.int32, (128, 128), 0)
    col = lane_ids((128, 128))
    for side in range(2):
        rem = [remote[2 * side + t : 2 * side + t + 1] for t in range(2)]
        far = [loc[2 * side + t : 2 * side + t + 1] for t in range(2)]
        any_rem = jnp.maximum(rem[0], rem[1])
        before = jnp.sum(jnp.where(col < row, any_rem, 0).astype(F32), axis=1, keepdims=True)
        mine = jnp.sum(jnp.where(col == row, any_rem, 0).astype(F32), axis=1, keepdims=True)
        slot = jnp.bitwise_and(col, 15).astype(F32)
        chosen = jnp.where((before == slot) & (mine > 0.0), row.astype(F32), 0.0)
        listed = jnp.sum(chosen, axis=0, keepdims=True).astype(jnp.int32)
        idx[side : side + 1, :] = listed
        named = jnp.where(
            ((far[0] == row) & (rem[0] > 0)) | ((far[1] == row) & (rem[1] > 0)), 1.0, 0.0
        )
        named = jnp.max(named, axis=1, keepdims=True)
        for t in range(2):
            rank = jnp.sum(jnp.where(row < far[t], named, 0.0), axis=0, keepdims=True)
            rank = jnp.where(rem[t] > 0, rank.astype(jnp.int32), 0)
            idx[RANK + 2 * side + t : RANK + 2 * side + t + 1, :] = rank
    nu = visc[...]
    wide = layout[...] == 0
    own, other = sides[0], sides[1]
    tab[0:1, :] = nu * jnp.where(wide, 2.0, 0.5)
    tab[1:2, :] = nu * jnp.where(wide, 0.5, 2.0)
    tab[2:3, :] = nu
    tab[3:4, :] = (own[4:5] == 0).astype(F32)
    tab[4:5, :] = (own[6:7] == 0).astype(F32)
    tab[5:8, :] = jnp.zeros((3, 128), F32)
    own_hot = [(own == o).astype(F32) for o in range(3)]
    pair_hot = [[own_hot[o] * (other == c).astype(F32) for c in range(3)] for o in range(3)]
    own_m = [PENALTY * HALVES[o].T @ np.diag(W) @ HALVES[o] for o in range(3)]
    far_m = [
        [-PENALTY * HALVES[o].T @ np.diag(W) @ HALVES[c] for c in range(3)] for o in range(3)
    ]
    for a in range(6):
        for b in range(6):
            mine = sum(float(own_m[o][a, b]) * own_hot[o] for o in range(3))
            own_c[6 * a + b] = mine + pltpu.roll(mine, 7, 0)
            far_c[6 * a + b] = sum(
                float(far_m[o][c][a, b]) * pair_hot[o][c] for o in range(3) for c in range(3)
            )


def take(value, index):
    return jnp.take_along_axis(value, index, axis=1)


def compact(faces, group, idx, send_w, send_e):
    part = lax.shift_right_logical(lane_ids((8, 128)), 4)
    for face, row, ref in ((faces[0], LIST_W, send_w), (faces[1], LIST_E, send_e)):
        index = jnp.broadcast_to(idx[row : row + 1, :], (8, 128))
        for c in range(3):
            low, high = take(face[2 * c], index), take(face[2 * c + 1], index)
            old = ref[8 * c : 8 * c + 8, :]
            new = jnp.where(part == group, low, jnp.where(part == group + 4, high, old))
            ref[8 * c : 8 * c + 8, :] = new


def operator(group, meta, idx, tab, own_c, far_c, v_ref, from_w, from_e, out):
    rows = pl.ds(pl.multiple_of(group * 8, 8), 8)
    v = [[v_ref[6 * i + j, rows, :] for j in range(6)] for i in range(6)]
    q = meta[0] * 32 + group * 8 + lax.broadcasted_iota(jnp.int32, (8, 128), 0)
    harmonic = lax.shift_right_logical(q + 1, 1).astype(F32) * SPANWISE
    cx, cy, nu = tab[0:1, :], tab[1:2, :], tab[2:3, :]
    shift = 1.0 + 0.5 * nu * (harmonic * harmonic)
    res = [[shift * v[i][j] for j in range(6)] for i in range(6)]
    for j in range(6):
        g = folded([v[i][j] for i in range(6)], STIFF_FOLD, 1)
        for i in range(6):
            res[i][j] = res[i][j] + cx * g[i]
    for i in range(6):
        g = folded(v[i], STIFF_FOLD, 1)
        for j in range(6):
            out[6 * i + j, rows, :] = float(W[i] * W[j]) * (res[i][j] + cy * g[j])

    def nodes(face):
        return [(0, b) if face == 0 else (5, b) if face == 1 else (b, 0) if face == 2 else (b, 5)
                for b in range(6)]

    def row_of(ref, r):
        return jnp.broadcast_to(ref[r : r + 1, :], (8, 128))

    def general(face):
        own = [v[i][j] for i, j in nodes(face)]
        far = [v[i][j] for i, j in nodes(face ^ 1)]
        near = []
        for s in (2 * face, 2 * face + 1):
            local = row_of(idx, LOCAL + s)
            got = [take(far[b], local) for b in range(6)]
            if face < 2:
                pool = from_w if face == 0 else from_e
                rank = row_of(idx, RANK + s) + 16 * group
                rem = row_of(idx, REMOTE + s) > 0
                for b in range(6):
                    c = b // 2
                    sent = take(pool[8 * c : 8 * c + 8, :], rank + 64 * (b % 2))
                    got[b] = jnp.where(rem, sent, got[b])
            near.append(got)
        for a in range(6):
            i, j = nodes(face)[a]
            extra = out[6 * i + j, rows, :]
            for b in range(6):
                extra = extra + own_c[6 * a + b, 2 * face : 2 * face + 1, :] * own[b]
                for t in range(2):
                    s = 2 * face + t
                    extra = extra + far_c[6 * a + b, s : s + 1, :] * near[t][b]
            out[6 * i + j, rows, :] = extra

    general(0)
    general(1)

    @pl.when(meta[2] == 0)
    def _():
        for face in (2, 3):
            active = tab[face + 1 : face + 2, :]
            local = row_of(idx, LOCAL + 2 * face)
            for a in range(6):
                i, j = nodes(face)[a]
                fi, fj = nodes(face ^ 1)[a]
                jump = active * (v[i][j] - take(v[fi][fj], local))
                out[6 * i + j, rows, :] += float(PENALTY * W[a]) * jump

    @pl.when(meta[2] != 0)
    def _():
        general(2)
        general(3)

    return rows, v


def faces_of(ref, rows):
    return [ref[b, rows, :] for b in range(6)], [ref[30 + b, rows, :] for b in range(6)]


def store_sums(acc, pad, count):
    width = count * 128
    lhs = (
        lax.broadcasted_iota(jnp.int32, (8, width), 0)
        == lax.shift_right_logical(lane_ids((8, width)), 7)
    ).astype(F32)
    sums = lax.dot_general(
        lhs, acc[...], (((1,), (1,)), ((), ())),
        precision=lax.Precision.HIGHEST, preferred_element_type=F32,
    )
    pad[...] = jnp.ones((8, 128), F32)
    pad[:, 0:32] = sums


def start_kernel(meta, idx, tab, own_c, far_c, v, from_w, from_e, out):
    def body(group, carry):
        rows, _ = operator(group, meta, idx, tab, own_c, far_c, v, from_w, from_e, out)
        for i in range(6):
            for j in range(6):
                n = 6 * i + j
                out[n, rows, :] = float(W[i] * W[j]) * v[n, rows, :] - out[n, rows, :]
        return carry

    lax.fori_loop(0, 4, body, 0)


def apply_kernel(meta, idx, tab, own_c, far_c, v, from_w, from_e, out, send_w, send_e):
    def body(group, carry):
        rows, _ = operator(group, meta, idx, tab, own_c, far_c, v, from_w, from_e, out)
        compact(faces_of(out, rows), group, idx, send_w, send_e)
        return carry

    lax.fori_loop(0, 4, body, 0)


def apply_last_kernel(meta, idx, tab, own_c, far_c, v, from_w, from_e, out):
    def body(group, carry):
        operator(group, meta, idx, tab, own_c, far_c, v, from_w, from_e, out)
        return carry

    lax.fori_loop(0, 4, body, 0)


def apply_sum_kernel(
    meta, idx, tab, own_c, far_c, v, from_w, from_e, v0, out, send_w, send_e, red, acc, pad
):
    def body(group, carry):
        rows, _ = operator(group, meta, idx, tab, own_c, far_c, v, from_w, from_e, out)
        compact(faces_of(out, rows), group, idx, send_w, send_e)
        sums = [jnp.zeros((8, 128), F32)] * 5
        for n in range(36):
            a, b, c = v0[n, rows, :], v[n, rows, :], out[n, rows, :]
            for k, term in enumerate((a * a, a * b, b * b, b * c, c * c)):
                sums[k] = sums[k] + term
        for k in range(5):
            acc[rows, 128 * k : 128 * k + 128] = sums[k]
        return carry

    lax.fori_loop(0, 4, body, 0)
    store_sums(acc, pad, 5)
    for k in range(16):
        red[k] = pad[...]


def energy_kernel(
    meta, idx, tab, own_c, far_c, v, from_w, from_e, part, red, out, acc, pad
):
    def body(group, carry):
        rows, _ = operator(group, meta, idx, tab, own_c, far_c, v, from_w, from_e, out)
        total = jnp.zeros((8, 128), F32)
        for n in range(36):
            total = total + v[n, rows, :] * out[n, rows, :]
        acc[rows, :] = total
        return carry

    lax.fori_loop(0, 4, body, 0)
    store_sums(acc, pad, 1)
    row = lax.broadcasted_iota(jnp.int32, (8, 128), 0)
    last = jnp.broadcast_to(pad[0:1, :], (8, 128))
    mixed = jnp.where(row == 7, last, part[...])
    for k in range(16):
        red[k] = mixed


def send_kernel(idx, v, send_w, send_e):
    def body(group, carry):
        rows = pl.ds(pl.multiple_of(group * 8, 8), 8)
        compact(faces_of(v, rows), group, idx, send_w, send_e)
        return carry

    lax.fori_loop(0, 4, body, 0)


def residual_kernel(idx, back, base, out, send_w, send_e):
    for g in range(9):
        turned = back[:, 16 * g : 16 * g + 16, :].reshape(128, 128).T
        for m in range(4):
            n = 4 * g + m
            out[n] = base[n] + turned[32 * m : 32 * m + 32]

    def body(group, carry):
        rows = pl.ds(pl.multiple_of(group * 8, 8), 8)
        compact(faces_of(out, rows), group, idx, send_w, send_e)
        return carry

    lax.fori_loop(0, 4, body, 0)


def spread(rows, coef):
    rows = rows + [jnp.zeros((1, 128), F32)] * (8 - len(rows))
    turned = jnp.concatenate(rows, axis=0).T
    for k in range(coef.shape[0]):
        coef[k] = jnp.broadcast_to(turned[0:32, k : k + 1], (32, 128))


def total_rows(red):
    total = red[0]
    for k in range(1, 16):
        total = total + red[k]
    return [total[k : k + 1] for k in range(8)]


def half_kernel(
    idx, red, v0, v1, v2, v3, x0, r2, p2, y, x2, send_w, send_e, part, coef, acc, pad
):
    m00, m01, m11, m12, m22 = total_rows(red)[:5]
    a0 = m00 / m01
    g1 = m00 - 2.0 * a0 * m01 + a0 * a0 * m11
    b0 = 1.0 + g1 / m00
    a1 = g1 / (b0 * b0 * m01 - 2.0 * b0 * a0 * m11 + a0 * a0 * m12)
    c1 = -(a0 + a1 * b0)
    c2 = a0 * a1
    g2 = m00 + 2.0 * c1 * m01 + (c1 * c1 + 2.0 * c2) * m11 + 2.0 * c1 * c2 * m12 + c2 * c2 * m22
    b1 = g2 / g1
    spread([c1, c2, 1.0 + b1 * b0, c1 - b1 * a0], coef)

    def body(group, carry):
        rows = pl.ds(pl.multiple_of(group * 8, 8), 8)
        k1, k2, d0, d1 = [coef[k, rows, :] for k in range(4)]
        sums = [jnp.zeros((8, 128), F32)] * 7
        for n in range(36):
            w0, w1, w2, w3 = v0[n, rows, :], v1[n, rows, :], v2[n, rows, :], v3[n, rows, :]
            rr = w0 + k1 * w1 + k2 * w2
            ar = w1 + k1 * w2 + k2 * w3
            pp = d0 * w0 + d1 * w1 + k2 * w2
            yy = d0 * w1 + d1 * w2 + k2 * w3
            r2[n, rows, :] = rr
            p2[n, rows, :] = pp
            y[n, rows, :] = yy
            x2[n, rows, :] = x0[n, rows, :] - k1 * w0 - k2 * w1
            for k, term in enumerate((rr * rr, rr * pp, rr * ar, rr * yy, yy * ar, pp * yy, yy * yy)):
                sums[k] = sums[k] + term
        for k in range(7):
            acc[rows, 128 * k : 128 * k + 128] = sums[k]
        compact(faces_of(y, rows), group, idx, send_w, send_e)
        return carry

    lax.fori_loop(0, 4, body, 0)
    store_sums(acc, pad, 7)
    part[...] = pad[...]


def finish_kernel(red, r2, p2, y, x2, out, coef):
    rr, rp, rar, ry, yar, py, yy, yz = total_rows(red)
    a2 = rp / py
    g3 = rr - 2.0 * a2 * ry + a2 * a2 * yy
    b2 = g3 / rr
    d3 = rar + 2.0 * b2 * ry - 2.0 * a2 * yar + b2 * b2 * py - 2.0 * a2 * b2 * yy + a2 * a2 * yz
    a3 = g3 / d3
    spread([a3, a2 + a3 * b2, -a2 * a3], coef)
    for n in range(36):
        out[n] = x2[n] + coef[0] * r2[n] + coef[1] * p2[n] + coef[2] * y[n]


def pack_kernel(u, out):
    for g in range(9):
        turned = u[4 * g : 4 * g + 4].reshape(128, 128).T
        out[:, 16 * g : 16 * g + 16, :] = turned.reshape(8, 16, 128)


def block_turn(blocks):
    part = lax.shift_right_logical(lane_ids(blocks[0].shape), 5)
    rolled = [blocks[0]] + [pltpu.roll(blocks[s], 32 * s, 1) for s in range(1, 4)]
    out = []
    for m in range(4):
        mixed = rolled[-m % 4]
        for t in range(1, 4):
            mixed = jnp.where(part == t, rolled[(t - m) % 4], mixed)
        out.append(pltpu.roll(mixed, 128 - 32 * m, 1) if m else mixed)
    return out


def product3(high, low, table):
    def dot(a, b):
        return jnp.dot(a, b, preferred_element_type=F32)

    return dot(high, table[0]) + dot(high, table[1]) + dot(low, table[0])


def advect_kernel(meta, came, speed, synth, analy, out, high, low, phys):
    for g in range(9):
        for h in range(2):
            pieces = block_turn([came[4 * h + s, 16 * g : 16 * g + 16, :] for s in range(4)])
            for m in range(4):
                n = 16 * (4 * g + m)
                hi, lo = split(pieces[m])
                high[n : n + 16, 128 * h : 128 * h + 128] = hi
                low[n : n + 16, 128 * h : 128 * h + 128] = lo
    for i in range(6):
        part = slice(96 * i, 96 * i + 96)
        phys[part, :] = product3(high[part, :], low[part, :], synth)
    wide = meta[3] == 0
    sx = jnp.where(wide, 2.0, 1.0)
    sy = jnp.where(wide, 1.0, 2.0)
    for h in range(2):
        cols = slice(128 * h, 128 * h + 128)
        u = [[phys[16 * (6 * i + j) : 16 * (6 * i + j) + 16, cols] for j in range(6)] for i in range(6)]
        acc = [[None] * 6 for _ in range(6)]
        for j in range(6):
            g = folded([u[i][j] for i in range(6)], DERIV_FOLD, -1)
            for i in range(6):
                acc[i][j] = sx * (speed[0, 6 * i + j, :, cols] * g[i])
        for i in range(6):
            g = folded(u[i], DERIV_FOLD, -1)
            for j in range(6):
                n = 16 * (6 * i + j)
                total = acc[i][j] + sy * (speed[1, 6 * i + j, :, cols] * g[j])
                hi, lo = split(float(-0.5 * W[i] * W[j]) * total)
                high[n : n + 16, cols] = hi
                low[n : n + 16, cols] = lo
    for i in range(6):
        part = slice(96 * i, 96 * i + 96)
        phys[part, :] = product3(high[part, :], low[part, :], analy)
    for g in range(9):
        for h in range(2):
            cols = slice(128 * h, 128 * h + 128)
            pieces = block_turn(
                [phys[16 * (4 * g + m) : 16 * (4 * g + m) + 16, cols] for m in range(4)]
            )
            for s in range(4):
                out[4 * h + s, 16 * g : 16 * g + 16, :] = pieces[s]


def shift_by(array, by):
    count = lax.axis_size("elem")
    return lax.ppermute(array, "elem", [(i, (i + by) % count) for i in range(count)])


def shards(scalar_modes, velocity, viscosity, mortar_links, mortar_sides, layout):
    u = jnp.transpose(scalar_modes, (1, 2, 0, 3)).reshape(36, 32, 128)
    speed = jnp.transpose(velocity, (0, 2, 3, 4, 1)).reshape(2, 36, 16, 256)
    synth, analy = plane_tables(256)
    synth = jnp.asarray(split_table(synth.T))
    analy = jnp.asarray(split_table(analy.T))
    cross = mortar_sides[:, 4:8]
    mixed = jnp.any((cross == 1) | (cross == 2)) | jnp.any(cross[:, 1::2] != 3)
    meta = jnp.stack(
        [lax.axis_index("plane"), lax.axis_index("elem"), mixed.astype(jnp.int32), layout[0]]
    ).astype(jnp.int32)

    vol, edge = shape(36, 32, 128), shape(24, 128)
    blocks = shape(8, 144, 128)
    packed = call(pack_kernel, [blocks], [], [u], [VMEM])[0]
    came = lax.all_to_all(packed, "plane", 0, 0, tiled=True)

    tables = call(
        prep_kernel,
        [shape(24, 128, dtype=jnp.int32), shape(8, 128), shape(36, 8, 128), shape(36, 8, 128)],
        [],
        [meta, mortar_links, mortar_sides, viscosity[None], layout[None]],
        [SMEM] + [VMEM] * 4,
    )
    idx = tables[0]
    head = [meta, *tables]

    def trade(send_w, send_e):
        return shift_by(send_e, 1), shift_by(send_w, -1)

    def run(kernel, outs, scratch, operands):
        args = head + operands
        return call(kernel, outs, scratch, args, [SMEM] + [VMEM] * (len(args) - 1))

    sums = [VMEM((32, 640), F32), VMEM((8, 128), F32)]
    edges = call(send_kernel, [edge, edge], [], [idx, u], [VMEM] * 2)
    base = run(start_kernel, [vol], [], [u, *trade(*edges)])[0]

    back = call(
        advect_kernel,
        [blocks],
        [VMEM((576, 256), BF16), VMEM((576, 256), BF16), VMEM((576, 256), F32)],
        [meta, came, speed, synth, analy],
        [SMEM] + [VMEM] * 4,
    )[0]
    back = lax.all_to_all(back, "plane", 0, 0, tiled=True)

    v0, *edges = call(
        residual_kernel, [vol, edge, edge], [], [idx, back, base], [VMEM] * 3
    )
    v1, *edges = run(apply_kernel, [vol, edge, edge], [], [v0, *trade(*edges)])
    v2, send_w, send_e, red = run(
        apply_sum_kernel,
        [vol, edge, edge, shape(16, 8, 128)],
        sums,
        [v1, *trade(*edges), v0],
    )
    red = lax.all_to_all(red, "elem", 0, 0, tiled=True)
    v3 = run(apply_last_kernel, [vol], [], [v2, *trade(send_w, send_e)])[0]
    r2, p2, y, x2, send_w, send_e, part = call(
        half_kernel,
        [vol, vol, vol, vol, edge, edge, shape(8, 128)],
        [VMEM((4, 32, 128), F32), VMEM((32, 896), F32), VMEM((8, 128), F32)],
        [idx, red, v0, v1, v2, v3, u],
        [VMEM] * 7,
    )
    red = run(
        energy_kernel,
        [shape(16, 8, 128)],
        [VMEM((36, 32, 128), F32), VMEM((32, 128), F32), VMEM((8, 128), F32)],
        [y, *trade(send_w, send_e), part],
    )[0]
    red = lax.all_to_all(red, "elem", 0, 0, tiled=True)
    out = call(
        finish_kernel, [vol], [VMEM((3, 32, 128), F32)], [red, r2, p2, y, x2], [VMEM] * 5
    )[0]
    return jnp.transpose(out.reshape(6, 6, 32, 128), (2, 0, 1, 3))


def solution(mesh):
    placed = (
        P("plane", None, None, "elem"),
        P(None, None, None, None, ("elem", "plane")),
        P("elem"),
        P(None, "elem"),
        P(None, None, "elem"),
        P("elem"),
    )
    return jax.shard_map(
        shards,
        mesh=mesh,
        in_specs=placed,
        out_specs=P("plane", None, None, "elem"),
        check_vma=False,
    )
```

time: 861 us -> 98.4 us (0.11); the launches traced: 850 us -> 97.9 us
  local copies, waits for them, and re-layouts: 260 us -> 1.13 us
  blocking collectives: 270 us -> 14.2 us
  matrix products: 159 us -> 0 us
  other arithmetic: 115 us -> 1.53 us
  Pallas kernels: 0 us -> 18.9 us
  starting transfers between devices: 29.8 us -> 44.2 us
    psum x7 -> x0, blocking collectives: 270 us -> none  [the longest x4 147 us: norm_total(): return lax.psum(mode_sum(vector_in, vector_in), 'elem')]
    gather x80 -> x0, local copies, waits for them, and re-layouts: 161 us -> none  [the longest x10 20.5 us: operate(): jnp.take(faces[3], neighbour_loc[4], axis=2)]
    dot_general x215 -> x0, matrix products: 159 us -> none  [the longest x200 139 us: on_face(): return jnp.einsum('ab,zbe->zae', matrix, trace_in, precision=highest)]
    mul x42 -> x0, other arithmetic: 38.9 us -> none  [the longest x40 36.9 us: mortar_sum(): weights[None, :, None] * jump_in]
    select_n x41 -> x0, other arithmetic: 28.4 us -> none  [the longest x5 3.91 us: operate(): jnp.take(east_pool, east_index[0], axis=2)]
    unnamed x716 -> x18, local copies, waits for them, and re-layouts: 28.6 us -> 1.1 us
    concatenate x10 -> x0, local copies, waits for them, and re-layouts: 20.6 us -> none  [the longest x5 10.3 us: operate(): east_pool = jnp.concatenate([faces[0], from_east], axis=2)]
    pallas_call x0 -> x12, Pallas kernels: none -> 18.9 us  [call(): pl.pallas_call(kernel, out_shape=outs, in_specs=[pl.BlockSpec(memory_spac...]
  transfers between devices with their start and end apart: 13 -> 13, of which waited for: 1 -> 6; matrix products, arithmetic and copies ran while one was open for 41% -> 2% of each run, Pallas kernels for 0% -> 5%
where the time goes in v1:
time: 98.4 us; the launch traced here: 97.9 us
  starting transfers between devices  44.2 us (45%)
  Pallas kernels  18.9 us (19%)
  waiting for transfers between devices  16.4 us (17%)
  blocking collectives  14.2 us (14%)
  other arithmetic  1.53 us (2%)
  between operations  1.53 us (2%)
  local copies, waits for them, and re-layouts  1.13 us (1%)
    ppermute x10, starting transfers between devices, shift_by(): lax.ppermute(array, 'elem', [(i, (i + by) % count) for i in range(count)])  29.3 us
    pallas_call x12, Pallas kernels, call(): pl.pallas_call(kernel, out_shape=outs, in_specs=[pl.BlockSpec(memory_spac...  18.9 us
    all_to_all x1, blocking collectives, shards(): red = lax.all_to_all(red, 'elem', 0, 0, tiled=True)  14.2 us
    ppermute x10, waiting for transfers between devices, shift_by(): lax.ppermute(array, 'elem', [(i, (i + by) % count) for i in range(count)])  8.33 us
    all_to_all x1, waiting for transfers between devices, shards(): came = lax.all_to_all(packed, 'plane', 0, 0, tiled=True)  8.1 us
    all_to_all x1, starting transfers between devices, shards(): red = lax.all_to_all(red, 'elem', 0, 0, tiled=True)  6.8 us
    all_to_all x1, starting transfers between devices, shards(): came = lax.all_to_all(packed, 'plane', 0, 0, tiled=True)  4.38 us
    all_to_all x1, starting transfers between devices, shards(): back = lax.all_to_all(back, 'plane', 0, 0, tiled=True)  3.67 us
  transfers between devices with their start and end apart: 13, of which 6 were waited for; matrix products, arithmetic and copies ran while one was open for 2% of the time, Pallas kernels for 5%

profile of v1, /device:TPU:0, one launch (start us, length us, event | category | flops | bytes accessed | tf_op | source)
XLA Modules:
  0.0 97.9 jit_solution(16731399812098158177)
XLA Ops:
  2.1 4.4 %all-to-all-start = ((f32[8,144,128]{2,1,0:T(8,128)}), f32[8,144,128]{2,1,0:T(8,128)S(1)}, u32[]{:S(2)}, u32[]{:S(2)}) async-start(f32[8,144,128]{2,1,0:T(8,128)} %shard_map.83), calls=%async_computation | async-start | bytes 1179648 | tf_op jit(solution)/shard_map/all_to_all | solution.py:530
  9.5 8.1 %all-to-all-done.came = f32[8,144,128]{2,1,0:T(8,128)S(1)} async-done(((f32[8,144,128]{2,1,0:T(8,128)}), f32[8,144,128]{2,1,0:T(8,128)S(1)}, u32[]{:S(2)}, u32[]{:S(2)}) %all-to-all-start) | async-done | bytes 589856 | tf_op jit(solution)/shard_map/all_to_all | solution.py:530
  17.6 3.1 %shard_map.84 = f32[8,144,128]{2,1,0:T(8,128)} custom-call(s32[4]{0:T(128)S(1)} %pad_add_fusion.meta, f32[8,144,128]{2,1,0:T(8,128)S(1)} %all-to-all-done.came, f32[2,36,16,256]{3,2,1,0:T(8,128)S(1)} %bitcast.19, bf16[2,256,256]{2,1,0:T(8,128)(2,1)S(1)} %copy-done.4, bf16[2,256,256]{2,1,0:T(8,128)(2,1)S(1)} %copy-done.3), custom_call_target="tpu_custom_call" | custom-call | flops 4000000 | bytes 3407888 | tf_op jit(solution)/shard_map/pallas_call | solution.py:109
  20.7 3.7 %all-to-all-start.1 = ((f32[8,144,128]{2,1,0:T(8,128)}), f32[8,144,128]{2,1,0:T(8,128)S(1)}, u32[]{:S(2)}, u32[]{:S(2)}) async-start(f32[8,144,128]{2,1,0:T(8,128)} %shard_map.84), calls=%async_computation.1 | async-start | bytes 1179648 | tf_op jit(solution)/shard_map/all_to_all | solution.py:560
  25.6 1.7 %collective-permute-start = (f32[24,128]{1,0:T(8,128)S(1)}, f32[24,128]{1,0:T(8,128)S(1)}, u32[]{:S(2)}, u32[]{:S(2)}) collective-permute-start(f32[24,128]{1,0:T(8,128)S(1)} %get-tuple-element.32), channel_id=1, source_target_pairs={{0,1},{1,2},{2,3},{3,4},{4,5},{5,6},{6,7},{7,8},{8,9},{9,10},{10,1... | collective-permute-start | bytes 36872 | tf_op jit(solution)/shard_map/ppermute | solution.py:512
  27.2 5.0 %collective-permute-start.1 = (f32[24,128]{1,0:T(8,128)S(1)}, f32[24,128]{1,0:T(8,128)S(1)}, u32[]{:S(2)}, u32[]{:S(2)}) collective-permute-start(f32[24,128]{1,0:T(8,128)S(1)} %get-tuple-element.33), channel_id=1, source_target_pairs={{0,15},{1,0},{2,1},{3,2},{4,3},{5,4},{6,5},{7,6},{8,7},{9,8},{10,9... | collective-permute-start | bytes 36872 | tf_op jit(solution)/shard_map/ppermute | solution.py:512
  32.2 1.6 %collective-permute-done.from_w = f32[24,128]{1,0:T(8,128)S(1)} collective-permute-done((f32[24,128]{1,0:T(8,128)S(1)}, f32[24,128]{1,0:T(8,128)S(1)}, u32[]{:S(2)}, u32[]{:S(2)}) %collective-permute-start) | collective-permute-done | bytes 12320 | tf_op jit(solution)/shard_map/ppermute | solution.py:512
  33.8 1.8 %shard_map.86.base = f32[36,32,128]{2,1,0:T(8,128)S(1)} custom-call(s32[4]{0:T(128)S(1)} %pad_add_fusion.meta, s32[24,128]{1,0:T(8,128)S(1)} %get-tuple-element.28.idx, f32[8,128]{1,0:T(8,128)S(1)} %get-tuple-element.29.tab, f32[36,8,128]{2,1,0:T(8,128)S(1)} %get-tuple-element.30.own_c, f32[36,8,128]{2,1,0:T(8,128)S(1)} %get-tuple-element.31.far_c, ...), custom_call_target="tpu_custom_call" | custom-call | flops 4000000 | bytes 1515536 | tf_op jit(solution)/shard_map/pallas_call | solution.py:109
  37.6 5.0 %collective-permute-start.3 = (f32[24,128]{1,0:T(8,128)S(1)}, f32[24,128]{1,0:T(8,128)S(1)}, u32[]{:S(2)}, u32[]{:S(2)}) collective-permute-start(f32[24,128]{1,0:T(8,128)S(1)} %get-tuple-element.36), channel_id=1, source_target_pairs={{0,15},{1,0},{2,1},{3,2},{4,3},{5,4},{6,5},{7,6},{8,7},{9,8},{10,9... | collective-permute-start | bytes 36872 | tf_op jit(solution)/shard_map/ppermute | solution.py:512
  42.6 1.6 %collective-permute-done.2.from_w = f32[24,128]{1,0:T(8,128)S(1)} collective-permute-done((f32[24,128]{1,0:T(8,128)S(1)}, f32[24,128]{1,0:T(8,128)S(1)}, u32[]{:S(2)}, u32[]{:S(2)}) %collective-permute-start.2) | collective-permute-done | bytes 12320 | tf_op jit(solution)/shard_map/ppermute | solution.py:512
  44.2 2.0 %shard_map.88 = (f32[36,32,128]{2,1,0:T(8,128)S(1)}, f32[24,128]{1,0:T(8,128)S(1)}, f32[24,128]{1,0:T(8,128)S(1)}) custom-call(s32[4]{0:T(128)S(1)} %pad_add_fusion.meta, s32[24,128]{1,0:T(8,128)S(1)} %get-tuple-element.28.idx, f32[8,128]{1,0:T(8,128)S(1)} %get-tuple-element.29.tab, f32[36,8,128]{2,1,0:T(8,128)S(1)} %get-tuple-element.30.own_c, ...), custom_call_target="tpu_custom_call" | custom-call | flops 4000000 | bytes 1540112 | tf_op jit(solution)/shard_map/pallas_call | solution.py:109
  46.3 5.5 %collective-permute-start.5 = (f32[24,128]{1,0:T(8,128)S(1)}, f32[24,128]{1,0:T(8,128)S(1)}, u32[]{:S(2)}, u32[]{:S(2)}) collective-permute-start(f32[24,128]{1,0:T(8,128)S(1)} %get-tuple-element.39), channel_id=1, source_target_pairs={{0,15},{1,0},{2,1},{3,2},{4,3},{5,4},{6,5},{7,6},{8,7},{9,8},{10,9... | collective-permute-start | bytes 36872 | tf_op jit(solution)/shard_map/ppermute | solution.py:512
  51.8 1.6 %collective-permute-done.4.from_w = f32[24,128]{1,0:T(8,128)S(1)} collective-permute-done((f32[24,128]{1,0:T(8,128)S(1)}, f32[24,128]{1,0:T(8,128)S(1)}, u32[]{:S(2)}, u32[]{:S(2)}) %collective-permute-start.4) | collective-permute-done | bytes 12320 | tf_op jit(solution)/shard_map/ppermute | solution.py:512
  53.4 2.9 %shard_map.89 = (f32[36,32,128]{2,1,0:T(8,128)S(1)}, f32[24,128]{1,0:T(8,128)S(1)}, f32[24,128]{1,0:T(8,128)S(1)}, f32[16,8,128]{2,1,0:T(8,128)}) custom-call(s32[4]{0:T(128)S(1)} %pad_add_fusion.meta, s32[24,128]{1,0:T(8,128)S(1)} %get-tuple-element.28.idx, f32[8,128]{1,0:T(8,128)S(1)} %get-tuple-element.29.tab, f32[36,8,128]{2,1,0:T(8,128)S(1)} %get-tuple-element.30.own_c, ...), custom_call_target="tpu_custom_call" | custom-call | flops 4000000 | bytes 2195472 | tf_op jit(solution)/shard_map/pallas_call | solution.py:109
  56.2 6.8 %all-to-all-start.2 = ((f32[16,8,128]{2,1,0:T(8,128)}), f32[16,8,128]{2,1,0:T(8,128)S(1)}, u32[]{:S(2)}, u32[]{:S(2)}) async-start(f32[16,8,128]{2,1,0:T(8,128)} %get-tuple-element.40), calls=%async_computation.2 | async-start | bytes 131072 | tf_op jit(solution)/shard_map/all_to_all | solution.py:572
  63.0 1.9 %collective-permute-start.6 = (f32[24,128]{1,0:T(8,128)S(1)}, f32[24,128]{1,0:T(8,128)S(1)}, u32[]{:S(2)}, u32[]{:S(2)}) collective-permute-start(f32[24,128]{1,0:T(8,128)S(1)} %get-tuple-element.42), channel_id=1, source_target_pairs={{0,1},{1,2},{2,3},{3,4},{4,5},{5,6},{6,7},{7,8},{8,9},{9,10},{10,1... | collective-permute-start | bytes 36872 | tf_op jit(solution)/shard_map/ppermute | solution.py:512
  65.0 3.5 %collective-permute-start.7 = (f32[24,128]{1,0:T(8,128)S(1)}, f32[24,128]{1,0:T(8,128)S(1)}, u32[]{:S(2)}, u32[]{:S(2)}) collective-permute-start(f32[24,128]{1,0:T(8,128)S(1)} %get-tuple-element.43), channel_id=1, source_target_pairs={{0,15},{1,0},{2,1},{3,2},{4,3},{5,4},{6,5},{7,6},{8,7},{9,8},{10,9... | collective-permute-start | bytes 36872 | tf_op jit(solution)/shard_map/ppermute | solution.py:512
  68.4 1.9 %collective-permute-done.6.from_w = f32[24,128]{1,0:T(8,128)S(1)} collective-permute-done((f32[24,128]{1,0:T(8,128)S(1)}, f32[24,128]{1,0:T(8,128)S(1)}, u32[]{:S(2)}, u32[]{:S(2)}) %collective-permute-start.6) | collective-permute-done | bytes 12320 | tf_op jit(solution)/shard_map/ppermute | solution.py:512
  70.3 1.7 %shard_map.90.v3 = f32[36,32,128]{2,1,0:T(8,128)S(1)} custom-call(s32[4]{0:T(128)S(1)} %pad_add_fusion.meta, s32[24,128]{1,0:T(8,128)S(1)} %get-tuple-element.28.idx, f32[8,128]{1,0:T(8,128)S(1)} %get-tuple-element.29.tab, f32[36,8,128]{2,1,0:T(8,128)S(1)} %get-tuple-element.30.own_c, f32[36,8,128]{2,1,0:T(8,128)S(1)} %get-tuple-element.31.far_c, ...), custom_call_target="tpu_custom_call" | custom-call | flops 4000000 | bytes 1515536 | tf_op jit(solution)/shard_map/pallas_call | solution.py:109
  72.0 1.4 %shard_map.91 = (f32[36,32,128]{2,1,0:T(8,128)S(1)}, f32[36,32,128]{2,1,0:T(8,128)S(1)}, f32[36,32,128]{2,1,0:T(8,128)S(1)}, f32[36,32,128]{2,1,0:T(8,128)S(1)},...) custom-call(s32[24,128]{1,0:T(8,128)S(1)} %get-tuple-element.28.idx, ...), custom_call_target="tpu_custom_call" | custom-call | flops 4000000 | bytes 5414912 | tf_op jit(solution)/shard_map/pallas_call | solution.py:109
  73.5 5.4 %collective-permute-start.9 = (f32[24,128]{1,0:T(8,128)S(1)}, f32[24,128]{1,0:T(8,128)S(1)}, u32[]{:S(2)}, u32[]{:S(2)}) collective-permute-start(f32[24,128]{1,0:T(8,128)S(1)} %get-tuple-element.46), channel_id=1, source_target_pairs={{0,15},{1,0},{2,1},{3,2},{4,3},{5,4},{6,5},{7,6},{8,7},{9,8},{10,9... | collective-permute-start | bytes 36872 | tf_op jit(solution)/shard_map/ppermute | solution.py:512
  78.9 1.7 %collective-permute-done.8.from_w = f32[24,128]{1,0:T(8,128)S(1)} collective-permute-done((f32[24,128]{1,0:T(8,128)S(1)}, f32[24,128]{1,0:T(8,128)S(1)}, u32[]{:S(2)}, u32[]{:S(2)}) %collective-permute-start.8) | collective-permute-done | bytes 12320 | tf_op jit(solution)/shard_map/ppermute | solution.py:512
  80.5 2.0 %shard_map.92 = f32[16,8,128]{2,1,0:T(8,128)S(1)} custom-call(s32[4]{0:T(128)S(1)} %pad_add_fusion.meta, s32[24,128]{1,0:T(8,128)S(1)} %get-tuple-element.28.idx, f32[8,128]{1,0:T(8,128)S(1)} %get-tuple-element.29.tab, f32[36,8,128]{2,1,0:T(8,128)S(1)} %get-tuple-element.30.own_c, f32[36,8,128]{2,1,0:T(8,128)S(1)} %get-tuple-element.31.far_c, ...), custom_call_target="tpu_custom_call" | custom-call | flops 4000000 | bytes 995344 | tf_op jit(solution)/shard_map/pallas_call | solution.py:109
  82.5 14.2 %all_to_all.20.red = f32[16,8,128]{2,1,0:T(8,128)S(1)} all-to-all(f32[16,8,128]{2,1,0:T(8,128)S(1)} %shard_map.92), channel_id=1, replica_groups=mesh['plane'=8,'elem'=16] {'elem'}, dimensions={0} | all-to-all | bytes 131072 | tf_op jit(solution)/shard_map/all_to_all | solution.py:587
  (38 shorter events, 8.2 us)
Async XLA Ops:
  0.0 1.1 %copy-start = (f32[32,6,6,128]{3,0,2,1:T(8,128)S(1)}, f32[32,6,6,128]{3,0,2,1:T(8,128)}, u32[]{:S(2)}) copy-start(f32[32,6,6,128]{3,0,2,1:T(8,128)} %param.8) | copy-start | bytes 1769476
  1.1 5.5 %copy-start.5 = (s32[2,8,128]{2,1,0:T(8,128)S(1)}, s32[2,8,128]{2,1,0:T(8,128)}, u32[]{:S(2)}) copy-start(s32[2,8,128]{2,1,0:T(8,128)} %sides.1) | copy-start | bytes 24580
  1.1 8.3 %copy-start.6 = (s32[128]{0:T(128)S(1)}, s32[128]{0:T(128)}, u32[]{:S(2)}) copy-start(s32[128]{0:T(128)} %param.13) | copy-start | bytes 1540
  1.1 16.5 %copy-start.2 = (f32[2,256,6,6,16]{1,4,3,2,0:T(8,128)S(1)}, f32[2,256,6,6,16]{1,4,3,2,0:T(8,128)}, u32[]{:S(2)}) copy-start(f32[2,256,6,6,16]{1,4,3,2,0:T(8,128)} %param.9) | copy-start | bytes 3538948
  1.1 16.5 %copy-start.3 = (bf16[2,256,256]{2,1,0:T(8,128)(2,1)S(1)}, bf16[2,256,256]{2,1,0:T(8,128)(2,1)}, u32[]{:S(2)}) copy-start(bf16[2,256,256]{2,1,0:T(8,128)(2,1)} %constant.22.clone.analy) | copy-start | bytes 786436
  1.1 16.5 %copy-start.4 = (bf16[2,256,256]{2,1,0:T(8,128)(2,1)S(1)}, bf16[2,256,256]{2,1,0:T(8,128)(2,1)}, u32[]{:S(2)}) copy-start(bf16[2,256,256]{2,1,0:T(8,128)(2,1)} %constant.21.clone.synth) | copy-start | bytes 786436
  2.1 15.4 %all-to-all-start = ((f32[8,144,128]{2,1,0:T(8,128)}), f32[8,144,128]{2,1,0:T(8,128)S(1)}, u32[]{:S(2)}, u32[]{:S(2)}) async-start(f32[8,144,128]{2,1,0:T(8,128)} %shard_map.83), calls=%async_computation | async-start | bytes 1179648 | tf_op jit(solution)/shard_map/all_to_all | solution.py:530
  20.7 3.7 %copy-start.7 = (s32[8,128]{1,0:T(8,128)S(1)}, s32[8,128]{1,0:T(8,128)}, u32[]{:S(2)}) copy-start(s32[8,128]{1,0:T(8,128)} %links.1) | copy-start | bytes 12292
  20.7 3.7 %copy-start.8 = (f32[128]{0:T(128)S(1)}, f32[128]{0:T(128)}, u32[]{:S(2)}) copy-start(f32[128]{0:T(128)} %param.10) | copy-start | bytes 1540
  20.7 4.5 %copy-start.1 = (f32[32,6,6,128]{3,0,2,1:T(8,128)S(1)}, f32[32,6,6,128]{3,0,2,1:T(8,128)}, u32[]{:S(2)}) copy-start(f32[32,6,6,128]{3,0,2,1:T(8,128)} %param.8) | copy-start | bytes 1769476
  20.7 15.0 %all-to-all-start.1 = ((f32[8,144,128]{2,1,0:T(8,128)}), f32[8,144,128]{2,1,0:T(8,128)S(1)}, u32[]{:S(2)}, u32[]{:S(2)}) async-start(f32[8,144,128]{2,1,0:T(8,128)} %shard_map.84), calls=%async_computation.1 | async-start | bytes 1179648 | tf_op jit(solution)/shard_map/all_to_all | solution.py:560
  25.6 8.2 %collective-permute-start = (f32[24,128]{1,0:T(8,128)S(1)}, f32[24,128]{1,0:T(8,128)S(1)}, u32[]{:S(2)}, u32[]{:S(2)}) collective-permute-start(f32[24,128]{1,0:T(8,128)S(1)} %get-tuple-element.32), channel_id=1, source_target_pairs={{0,1},{1,2},{2,3},{3,4},{4,5},{5,6},{6,7},{7,8},{8,9},{9,10},{10,1... | collective-permute-start | bytes 36872 | tf_op jit(solution)/shard_map/ppermute | solution.py:512
  27.2 6.6 %collective-permute-start.1 = (f32[24,128]{1,0:T(8,128)S(1)}, f32[24,128]{1,0:T(8,128)S(1)}, u32[]{:S(2)}, u32[]{:S(2)}) collective-permute-start(f32[24,128]{1,0:T(8,128)S(1)} %get-tuple-element.33), channel_id=1, source_target_pairs={{0,15},{1,0},{2,1},{3,2},{4,3},{5,4},{6,5},{7,6},{8,7},{9,8},{10,9... | collective-permute-start | bytes 36872 | tf_op jit(solution)/shard_map/ppermute | solution.py:512
  36.3 7.9 %collective-permute-start.2 = (f32[24,128]{1,0:T(8,128)S(1)}, f32[24,128]{1,0:T(8,128)S(1)}, u32[]{:S(2)}, u32[]{:S(2)}) collective-permute-start(f32[24,128]{1,0:T(8,128)S(1)} %get-tuple-element.35), channel_id=1, source_target_pairs={{0,1},{1,2},{2,3},{3,4},{4,5},{5,6},{6,7},{7,8},{8,9},{9,10},{10,1... | collective-permute-start | bytes 36872 | tf_op jit(solution)/shard_map/ppermute | solution.py:512
  37.6 6.6 %collective-permute-start.3 = (f32[24,128]{1,0:T(8,128)S(1)}, f32[24,128]{1,0:T(8,128)S(1)}, u32[]{:S(2)}, u32[]{:S(2)}) collective-permute-start(f32[24,128]{1,0:T(8,128)S(1)} %get-tuple-element.36), channel_id=1, source_target_pairs={{0,15},{1,0},{2,1},{3,2},{4,3},{5,4},{6,5},{7,6},{8,7},{9,8},{10,9... | collective-permute-start | bytes 36872 | tf_op jit(solution)/shard_map/ppermute | solution.py:512
  46.2 7.2 %collective-permute-start.4 = (f32[24,128]{1,0:T(8,128)S(1)}, f32[24,128]{1,0:T(8,128)S(1)}, u32[]{:S(2)}, u32[]{:S(2)}) collective-permute-start(f32[24,128]{1,0:T(8,128)S(1)} %get-tuple-element.38), channel_id=1, source_target_pairs={{0,1},{1,2},{2,3},{3,4},{4,5},{5,6},{6,7},{7,8},{8,9},{9,10},{10,1... | collective-permute-start | bytes 36872 | tf_op jit(solution)/shard_map/ppermute | solution.py:512
  46.3 7.1 %collective-permute-start.5 = (f32[24,128]{1,0:T(8,128)S(1)}, f32[24,128]{1,0:T(8,128)S(1)}, u32[]{:S(2)}, u32[]{:S(2)}) collective-permute-start(f32[24,128]{1,0:T(8,128)S(1)} %get-tuple-element.39), channel_id=1, source_target_pairs={{0,15},{1,0},{2,1},{3,2},{4,3},{5,4},{6,5},{7,6},{8,7},{9,8},{10,9... | collective-permute-start | bytes 36872 | tf_op jit(solution)/shard_map/ppermute | solution.py:512
  56.2 15.8 %all-to-all-start.2 = ((f32[16,8,128]{2,1,0:T(8,128)}), f32[16,8,128]{2,1,0:T(8,128)S(1)}, u32[]{:S(2)}, u32[]{:S(2)}) async-start(f32[16,8,128]{2,1,0:T(8,128)} %get-tuple-element.40), calls=%async_computation.2 | async-start | bytes 131072 | tf_op jit(solution)/shard_map/all_to_all | solution.py:572
  63.0 7.3 %collective-permute-start.6 = (f32[24,128]{1,0:T(8,128)S(1)}, f32[24,128]{1,0:T(8,128)S(1)}, u32[]{:S(2)}, u32[]{:S(2)}) collective-permute-start(f32[24,128]{1,0:T(8,128)S(1)} %get-tuple-element.42), channel_id=1, source_target_pairs={{0,1},{1,2},{2,3},{3,4},{4,5},{5,6},{6,7},{7,8},{8,9},{9,10},{10,1... | collective-permute-start | bytes 36872 | tf_op jit(solution)/shard_map/ppermute | solution.py:512
  65.0 5.4 %collective-permute-start.7 = (f32[24,128]{1,0:T(8,128)S(1)}, f32[24,128]{1,0:T(8,128)S(1)}, u32[]{:S(2)}, u32[]{:S(2)}) collective-permute-start(f32[24,128]{1,0:T(8,128)S(1)} %get-tuple-element.43), channel_id=1, source_target_pairs={{0,15},{1,0},{2,1},{3,2},{4,3},{5,4},{6,5},{7,6},{8,7},{9,8},{10,9... | collective-permute-start | bytes 36872 | tf_op jit(solution)/shard_map/ppermute | solution.py:512
  73.5 7.0 %collective-permute-start.8 = (f32[24,128]{1,0:T(8,128)S(1)}, f32[24,128]{1,0:T(8,128)S(1)}, u32[]{:S(2)}, u32[]{:S(2)}) collective-permute-start(f32[24,128]{1,0:T(8,128)S(1)} %get-tuple-element.45), channel_id=1, source_target_pairs={{0,1},{1,2},{2,3},{3,4},{4,5},{5,6},{6,7},{7,8},{8,9},{9,10},{10,1... | collective-permute-start | bytes 36872 | tf_op jit(solution)/shard_map/ppermute | solution.py:512
  73.5 7.0 %collective-permute-start.9 = (f32[24,128]{1,0:T(8,128)S(1)}, f32[24,128]{1,0:T(8,128)S(1)}, u32[]{:S(2)}, u32[]{:S(2)}) collective-permute-start(f32[24,128]{1,0:T(8,128)S(1)} %get-tuple-element.46), channel_id=1, source_target_pairs={{0,15},{1,0},{2,1},{3,2},{4,3},{5,4},{6,5},{7,6},{8,7},{9,8},{10,9... | collective-permute-start | bytes 36872 | tf_op jit(solution)/shard_map/ppermute | solution.py:512

commit v2 on v1

v2 whole, which is shorter than its diff:
```python
import math

import jax
import jax.numpy as jnp
import ml_dtypes
import numpy as np
from jax import lax
from jax.experimental import pallas as pl
from jax.experimental.pallas import tpu as pltpu
from jax.sharding import PartitionSpec as P

F32 = jnp.float32
BF16 = jnp.bfloat16
PENALTY = 10.0
SPANWISE = 0.0625
VMEM = pltpu.VMEM
SMEM = pltpu.SMEM
SELF, ANY, LOCAL = 2, 4, 10


def lagrange_at(points, targets):
    out = np.ones((6, 6))
    for row in range(6):
        for col in range(6):
            for other in range(6):
                if other != col:
                    out[row, col] *= (targets[row] - points[other]) / (points[col] - points[other])
    return out


def node_tables():
    root = math.sqrt(7.0)
    outer = math.sqrt(1.0 / 3.0 + 2.0 * root / 21.0)
    inner = math.sqrt(1.0 / 3.0 - 2.0 * root / 21.0)
    points = np.array([-1.0, -outer, -inner, inner, outer, 1.0])
    half = [1.0 / 15.0, (14.0 - root) / 30.0, (14.0 + root) / 30.0]
    weights = np.array(half + half[::-1])
    bary = np.array(
        [1.0 / np.prod([points[c] - points[k] for k in range(6) if k != c]) for c in range(6)]
    )
    deriv = np.zeros((6, 6))
    for i in range(6):
        for j in range(6):
            if i != j:
                deriv[i, j] = bary[j] / bary[i] / (points[i] - points[j])
        deriv[i, i] = -np.sum(deriv[i])
    lower = lagrange_at(points, (points - 1.0) / 2.0)
    upper = lagrange_at(points, (points + 1.0) / 2.0)
    stiff = deriv.T @ (weights[:, None] * deriv)
    return weights, deriv, lower, upper, stiff


W, D, QLO, QHI, K1 = node_tables()
HALVES = [np.eye(6), QLO, QHI]


def plane_tables(count):
    planes = np.arange(count)[:, None]
    coeffs = np.arange(count)[None, :]
    harmonic = (coeffs + 1) // 2
    phase = 2.0 * np.pi * (harmonic * planes % count) / count
    synth = np.where(coeffs == 0, 1.0, np.where(coeffs % 2 == 1, np.cos(phase), np.sin(phase)))
    norm = np.where((coeffs == 0) | (coeffs == count - 1), float(count), count / 2.0)
    return synth, (synth / norm).T


def split_table(table):
    table = np.asarray(table, np.float32)
    high = table.astype(ml_dtypes.bfloat16)
    low = (table - high.astype(np.float32)).astype(ml_dtypes.bfloat16)
    return np.stack([high, low])


def fold(matrix):
    plus = (matrix[:3, :3] + matrix[:3, :2:-1]) / 2.0
    minus = (matrix[:3, :3] - matrix[:3, :2:-1]) / 2.0
    return plus, minus


STIFF_FOLD = fold(K1 / W[:, None])
DERIV_FOLD = fold(D)


def folded(values, tables, sign):
    plus, minus = tables
    even = [values[a] + values[5 - a] for a in range(3)]
    odd = [values[a] - values[5 - a] for a in range(3)]
    out = [None] * 6
    for i in range(3):
        e = sum(float(plus[i, a]) * even[a] for a in range(3))
        o = sum(float(minus[i, a]) * odd[a] for a in range(3))
        out[i] = e + o
        out[5 - i] = e - o if sign > 0 else o - e
    return out


def split(value):
    high = value.astype(BF16)
    return high, (value - high.astype(F32)).astype(BF16)


def lane_ids(shape):
    return lax.broadcasted_iota(jnp.int32, shape, len(shape) - 1)


def call(kernel, outs, scratch, operands, spaces, flops=4_000_000):
    total = sum(int(np.prod(o.shape)) * 4 for o in outs)
    total += sum(int(np.prod(o.shape)) * 4 for o in operands)
    return pl.pallas_call(
        kernel,
        out_shape=outs,
        in_specs=[pl.BlockSpec(memory_space=s) for s in spaces],
        out_specs=[pl.BlockSpec(memory_space=VMEM) for _ in outs],
        scratch_shapes=scratch,
        compiler_params=pltpu.CompilerParams(vmem_limit_bytes=40 * 2**20),
        cost_estimate=pl.CostEstimate(flops=flops, bytes_accessed=total, transcendentals=0),
    )(*operands)


def shape(*dims, dtype=F32):
    return jax.ShapeDtypeStruct(dims, dtype)


def take(value, index):
    return jnp.take_along_axis(value, index, axis=1)


def take_row(value, index):
    wide = jnp.broadcast_to(value, (8, 128)), jnp.broadcast_to(index, (8, 128))
    return take(*wide)[0:1]


def prep_kernel(meta, links, sides, visc, layout, idx, edge_idx, tab, own_c, far_c, edge_own, edge_far):
    me = meta[1]
    dev = lax.shift_right_logical(links[...], 7)
    loc = jnp.bitwise_and(links[...], 127)
    remote = (dev != me).astype(jnp.int32)
    idx[LOCAL : LOCAL + 8, :] = loc
    row = lax.broadcasted_iota(jnp.int32, (128, 128), 0)
    col = lane_ids((128, 128))
    lane = lane_ids((1, 128))
    slot = jnp.bitwise_and(lane, 15)
    own, other = sides[0], sides[1]
    listed, present, ranks = [], [], []
    for side in range(2):
        rem = [remote[2 * side + t : 2 * side + t + 1] for t in range(2)]
        far = [loc[2 * side + t : 2 * side + t + 1] for t in range(2)]
        any_rem = jnp.maximum(rem[0], rem[1])
        before = jnp.sum(jnp.where(col < row, any_rem, 0).astype(F32), axis=1, keepdims=True)
        mine = jnp.sum(jnp.where(col == row, any_rem, 0).astype(F32), axis=1, keepdims=True)
        chosen = jnp.where((before == slot.astype(F32)) & (mine > 0.0), 1.0, 0.0)
        listed.append(jnp.sum(chosen * row.astype(F32), axis=0, keepdims=True).astype(jnp.int32))
        present.append(jnp.sum(chosen, axis=0, keepdims=True).astype(jnp.int32))
        idx[side : side + 1, :] = listed[side]
        mine_at = jnp.sum(jnp.where(row == col, before, 0.0), axis=0, keepdims=True)
        mine_at = jnp.where(any_rem > 0, mine_at.astype(jnp.int32), 0)
        idx[SELF + side : SELF + side + 1, :] = mine_at
        idx[ANY + side : ANY + side + 1, :] = any_rem
        named = jnp.where(
            ((far[0] == row) & (rem[0] > 0)) | ((far[1] == row) & (rem[1] > 0)), 1.0, 0.0
        )
        named = jnp.max(named, axis=1, keepdims=True)
        for t in range(2):
            rank = jnp.sum(jnp.where(row < far[t], named, 0.0), axis=0, keepdims=True)
            ranks.append(jnp.where(rem[t] > 0, rank.astype(jnp.int32), 0))
    idx[6:10, :] = jnp.zeros((4, 128), jnp.int32)
    idx[18:24, :] = jnp.zeros((6, 128), jnp.int32)

    west = lane < 64
    base = jnp.bitwise_and(lane, 112)
    element = jnp.where(west, listed[0], listed[1])
    here = jnp.where(west, present[0], present[1]) > 0

    def pick(rows_w, rows_e):
        return jnp.where(west, take_row(rows_w, element), take_row(rows_e, element))

    rank, live, mine, theirs = [], [], [], []
    for t in range(2):
        rank.append(pick(ranks[t], ranks[2 + t]))
        live.append((pick(remote[t : t + 1], remote[2 + t : 3 + t]) > 0) & here)
        mine.append(jnp.where(live[t], pick(own[t : t + 1], own[2 + t : 3 + t]), 3))
        theirs.append(jnp.where(live[t], pick(other[t : t + 1], other[2 + t : 3 + t]), 3))
    first = jnp.full((1, 128), 99, jnp.int32)
    last = jnp.full((1, 128), -1, jnp.int32)
    for t in range(2):
        target = jnp.where(live[t], rank[t], 99)
        for r in range(16):
            hit = take_row(target, base + r) == slot
            first = jnp.where(hit, jnp.minimum(first, 16 * t + r), first)
            last = jnp.where(hit, jnp.maximum(last, 16 * t + r), last)
    exists = [last >= 0, last > first]
    key = [jnp.where(exists[0], first, 0), jnp.where(exists[1], last, 0)]
    back = [base + jnp.bitwise_and(k, 15) for k in key]

    def from_key(k, pair):
        value = jnp.where(key[k] >= 16, take_row(pair[1], back[k]), take_row(pair[0], back[k]))
        return jnp.where(exists[k], value, 3)

    near_own = [from_key(k, theirs) for k in range(2)]
    near_far = [from_key(k, mine) for k in range(2)]
    edge_idx[...] = jnp.zeros((8, 128), jnp.int32)
    for k in range(2):
        edge_idx[k : k + 1, :] = base + rank[k]
        edge_idx[2 + k : 3 + k, :] = back[k]
    none = jnp.full((4, 128), 3, jnp.int32)
    edge_mine = jnp.concatenate([mine[0], mine[1], near_own[0], near_own[1], none], axis=0)
    edge_theirs = jnp.concatenate([theirs[0], theirs[1], near_far[0], near_far[1], none], axis=0)

    nu = visc[...]
    wide = layout[...] == 0
    tab[0:1, :] = nu * jnp.where(wide, 2.0, 0.5)
    tab[1:2, :] = nu * jnp.where(wide, 0.5, 2.0)
    tab[2:3, :] = nu
    inside = jnp.where(remote > 0, 3, own)
    for face in range(4):
        plain = (inside[2 * face : 2 * face + 1] == 0) & (other[2 * face : 2 * face + 1] == 0)
        tab[3 + face : 4 + face, :] = plain.astype(F32)
    tab[7:8, :] = jnp.zeros((1, 128), F32)
    mine_m = [PENALTY * HALVES[o].T @ np.diag(W) @ HALVES[o] for o in range(3)]
    far_m = [
        [-PENALTY * HALVES[o].T @ np.diag(W) @ HALVES[c] for c in range(3)] for o in range(3)
    ]
    for code, facing, own_ref, far_ref in (
        (inside, other, own_c, far_c),
        (edge_mine, edge_theirs, edge_own, edge_far),
    ):
        hot = [(code == o).astype(F32) for o in range(3)]
        pair = [[hot[o] * (facing == c).astype(F32) for c in range(3)] for o in range(3)]
        for a in range(6):
            for b in range(6):
                n = 6 * a + b
                total = sum(float(mine_m[o][a, b]) * hot[o] for o in range(3))
                own_ref[n] = total + pltpu.roll(total, 7, 0)
                far_ref[n] = sum(
                    float(far_m[o][c][a, b]) * pair[o][c] for o in range(3) for c in range(3)
                )


def group_rows(group):
    return pl.ds(pl.multiple_of(group * 8, 8), 8)


def row_of(ref, r):
    return jnp.broadcast_to(ref[r : r + 1, :], (8, 128))


def face_nodes(face):
    return [
        6 * i + j
        for i, j in [
            (0, b) if face == 0 else (5, b) if face == 1 else (b, 0) if face == 2 else (b, 5)
            for b in range(6)
        ]
    ]


def inner(group, env, v_ref, out):
    meta, idx, tab, own_c, far_c = env
    rows = group_rows(group)
    v = [v_ref[n, rows, :] for n in range(36)]
    q = meta[0] * 32 + group * 8 + lax.broadcasted_iota(jnp.int32, (8, 128), 0)
    harmonic = lax.shift_right_logical(q + 1, 1).astype(F32) * SPANWISE
    cx, cy, nu = tab[0:1, :], tab[1:2, :], tab[2:3, :]
    shift = 1.0 + 0.5 * nu * (harmonic * harmonic)
    res = [shift * v[n] for n in range(36)]
    for j in range(6):
        g = folded([v[6 * i + j] for i in range(6)], STIFF_FOLD, 1)
        for i in range(6):
            res[6 * i + j] = res[6 * i + j] + cx * g[i]
    for i in range(6):
        g = folded(v[6 * i : 6 * i + 6], STIFF_FOLD, 1)
        for j in range(6):
            out[6 * i + j, rows, :] = float(W[i] * W[j]) * (res[6 * i + j] + cy * g[j])

    @pl.when(meta[2] == 0)
    def _():
        for face in range(4):
            active = tab[3 + face : 4 + face, :]
            local = row_of(idx, LOCAL + 2 * face)
            for a in range(6):
                n, m = face_nodes(face)[a], face_nodes(face ^ 1)[a]
                jump = active * (v_ref[n, rows, :] - take(v_ref[m, rows, :], local))
                out[n, rows, :] += float(PENALTY * W[a]) * jump

    @pl.when(meta[2] != 0)
    def _():
        for face in range(4):
            mine = [v_ref[n, rows, :] for n in face_nodes(face)]
            theirs = [
                [take(v_ref[n, rows, :], row_of(idx, LOCAL + 2 * face + t)) for n in face_nodes(face ^ 1)]
                for t in range(2)
            ]
            for a in range(6):
                n = face_nodes(face)[a]
                extra = out[n, rows, :]
                for b in range(6):
                    extra = extra + own_c[6 * a + b, 2 * face : 2 * face + 1, :] * mine[b]
                    for t in range(2):
                        s = 2 * face + t
                        extra = extra + far_c[6 * a + b, s : s + 1, :] * theirs[t][b]
                out[n, rows, :] = extra


def compact(group, idx, v_ref, h_ref, send_w, send_e):
    rows = group_rows(group)
    part = lax.shift_right_logical(lane_ids((8, 128)), 4)
    for face, ref in ((0, send_w), (1, send_e)):
        index = row_of(idx, face)
        for b in range(6):
            n = face_nodes(face)[b]
            low, high = take(v_ref[n, rows, :], index), take(h_ref[n, rows, :], index)
            old = ref[8 * b : 8 * b + 8, :]
            new = jnp.where(part == group, low, jnp.where(part == group + 4, high, old))
            ref[8 * b : 8 * b + 8, :] = new


def outer(group, idx, edge, first):
    found = {}
    for face in range(2):
        lanes = row_of(idx, SELF + face) + (64 * face + 16 * group)
        on = row_of(idx, ANY + face) > 0
        for b in range(6):
            value = take(edge[first + 8 * b : first + 8 * b + 8, :], lanes)
            found[face_nodes(face)[b]] = jnp.where(on, value, 0.0)
    return found


def edge_blocks(ref):
    return [ref[8 * b : 8 * b + 8, :] for b in range(6)]


def merge(to_w, to_e):
    west = lane_ids((8, 128)) < 64
    plain, inner_h = [], []
    for w, e in zip(edge_blocks(to_w), edge_blocks(to_e)):
        plain.append(jnp.where(west, w, pltpu.roll(e, 64, 1)))
        inner_h.append(jnp.where(west, pltpu.roll(w, 64, 1), e))
    return plain, inner_h


def edge_term(edge_idx, edge_own, edge_far, mine, theirs, row):
    near = [[take(t, row_of(edge_idx, row + k)) for t in theirs] for k in range(2)]
    out = []
    for a in range(6):
        total = None
        for b in range(6):
            n = 6 * a + b
            term = edge_own[n, row : row + 1, :] * mine[b]
            for k in range(2):
                term = term + edge_far[n, row + k : row + k + 1, :] * near[k][b]
            total = term if total is None else total + term
        out.append(total)
    return out


def store_sums(acc, pad, first, count):
    width = count * 128
    lhs = (
        lax.broadcasted_iota(jnp.int32, (8, width), 0)
        == lax.shift_right_logical(lane_ids((8, width)), 7) + first
    ).astype(F32)
    sums = lax.dot_general(
        lhs, acc[...], (((1,), (1,)), ((), ())),
        precision=lax.Precision.HIGHEST, preferred_element_type=F32,
    )
    pad[...] = jnp.ones((8, 128), F32)
    pad[:, 0:32] = sums


HALF = 10.0


def guess_kernel(meta, idx, tab, own_c, far_c, u, out, send_w, send_e):
    env = (meta, idx, tab, own_c, far_c)

    def body(group, carry):
        inner(group, env, u, out)
        compact(group, idx, u, out, send_w, send_e)
        return carry

    lax.fori_loop(0, 4, body, 0)


def base_kernel(idx, edge_idx, edge_own, edge_far, u, hu, to_w, to_e, from_w, from_e, out, edge):
    mine, _ = merge(to_w, to_e)
    theirs, _ = merge(from_w, from_e)
    for b, value in enumerate(edge_term(edge_idx, edge_own, edge_far, mine, theirs, 0)):
        edge[8 * b : 8 * b + 8, :] = value

    def body(group, carry):
        rows = group_rows(group)
        extra = outer(group, idx, edge, 0)
        for n in range(36):
            image = hu[n, rows, :]
            if n in extra:
                image = image + extra[n]
            out[n, rows, :] = float(W[n // 6] * W[n % 6]) * u[n, rows, :] - image
        return carry

    lax.fori_loop(0, 4, body, 0)


def residual_kernel(meta, idx, tab, own_c, far_c, back, base, out, h_out, send_w, send_e):
    env = (meta, idx, tab, own_c, far_c)
    for g in range(9):
        turned = back[:, 16 * g : 16 * g + 16, :].reshape(128, 128).T
        for m in range(4):
            n = 4 * g + m
            out[n] = base[n] + turned[32 * m : 32 * m + 32]

    def body(group, carry):
        inner(group, env, out, h_out)
        compact(group, idx, out, h_out, send_w, send_e)
        return carry

    lax.fori_loop(0, 4, body, 0)


def edge_steps(tables, to_w, to_e, from_w, from_e, before, edge, keep):
    edge_idx, edge_own, edge_far = tables
    mine, mine_h = merge(to_w, to_e)
    theirs, theirs_h = merge(from_w, from_e)
    scale = (1.0 if before is None else 2.0) / HALF
    first = edge_term(edge_idx, edge_own, edge_far, mine, theirs, 0)
    facing = edge_term(edge_idx, edge_own, edge_far, theirs, mine, 2)
    mine_next, theirs_next = [], []
    for b in range(6):
        if before is None:
            mine_next.append(scale * (mine_h[b] + first[b]) - mine[b])
            theirs_next.append(scale * (theirs_h[b] + facing[b]) - theirs[b])
        else:
            old = before[8 * b : 8 * b + 8, :], before[48 + 8 * b : 56 + 8 * b, :]
            mine_next.append(scale * (mine_h[b] + first[b]) - 2.0 * mine[b] - old[0])
            theirs_next.append(scale * (theirs_h[b] + facing[b]) - 2.0 * theirs[b] - old[1])
    second = edge_term(edge_idx, edge_own, edge_far, mine_next, theirs_next, 0)
    for b in range(6):
        edge[8 * b : 8 * b + 8, :] = first[b]
        edge[48 + 8 * b : 56 + 8 * b, :] = second[b]
        if keep is not None:
            keep[8 * b : 8 * b + 8, :] = mine_next[b]
            keep[48 + 8 * b : 56 + 8 * b, :] = theirs_next[b]


def two_steps_kernel(
    meta, idx, tab, own_c, far_c, edge_idx, edge_own, edge_far,
    t0, h0, to_w, to_e, from_w, from_e,
    t1, t2, h2, send_w, send_e, keep, part, edge, h1, acc, pad,
):
    env = (meta, idx, tab, own_c, far_c)
    tables = (edge_idx, edge_own, edge_far)
    edge_steps(tables, to_w, to_e, from_w, from_e, None, edge, keep)

    def body(group, carry):
        rows = group_rows(group)
        extra = outer(group, idx, edge, 0)
        sums = [jnp.zeros((8, 128), F32)] * 5
        for n in range(36):
            image = h0[n, rows, :]
            if n in extra:
                image = image + extra[n]
            a = t0[n, rows, :]
            b = (1.0 / HALF) * image - a
            t1[n, rows, :] = b
            for k, term in enumerate((a * a, a * b, b * b)):
                sums[k] = sums[k] + term
        inner(group, env, t1, h1)
        extra = outer(group, idx, edge, 48)
        for n in range(36):
            image = h1[n, rows, :]
            if n in extra:
                image = image + extra[n]
            b = t1[n, rows, :]
            c = (2.0 / HALF) * image - 2.0 * b - t0[n, rows, :]
            t2[n, rows, :] = c
            sums[3] = sums[3] + b * c
            sums[4] = sums[4] + c * c
        for k in range(5):
            acc[rows, 128 * k : 128 * k + 128] = sums[k]
        inner(group, env, t2, h2)
        compact(group, idx, t2, h2, send_w, send_e)
        return carry

    lax.fori_loop(0, 4, body, 0)
    store_sums(acc, pad, 0, 5)
    part[...] = pad[...]


def last_steps_kernel(
    meta, idx, tab, own_c, far_c, edge_idx, edge_own, edge_far,
    t1, t2, h2, to_w, to_e, from_w, from_e, keep, part,
    t3, red, edge, h3, acc, pad,
):
    env = (meta, idx, tab, own_c, far_c)
    tables = (edge_idx, edge_own, edge_far)
    edge_steps(tables, to_w, to_e, from_w, from_e, keep, edge, None)

    def body(group, carry):
        rows = group_rows(group)
        extra = outer(group, idx, edge, 0)
        sums = [jnp.zeros((8, 128), F32)] * 3
        for n in range(36):
            image = h2[n, rows, :]
            if n in extra:
                image = image + extra[n]
            c = t2[n, rows, :]
            d = (2.0 / HALF) * image - 2.0 * c - t1[n, rows, :]
            t3[n, rows, :] = d
            sums[0] = sums[0] + c * d
            sums[1] = sums[1] + d * d
        inner(group, env, t3, h3)
        extra = outer(group, idx, edge, 48)
        for n in range(36):
            image = h3[n, rows, :]
            if n in extra:
                image = image + extra[n]
            d = t3[n, rows, :]
            sums[2] = sums[2] + d * ((2.0 / HALF) * image - 2.0 * d - t2[n, rows, :])
        for k in range(3):
            acc[rows, 128 * k : 128 * k + 128] = sums[k]
        return carry

    lax.fori_loop(0, 4, body, 0)
    store_sums(acc, pad, 5, 3)
    row = lax.broadcasted_iota(jnp.int32, (8, 128), 0)
    mixed = jnp.where(row < 5, part[...], pad[...])
    for k in range(16):
        red[k] = mixed


def finish_kernel(red, x0, t0, t1, t2, t3, out, coef):
    total = red[0]
    for k in range(1, 16):
        total = total + red[k]
    even = [total[2 * k : 2 * k + 1] for k in range(4)]
    odd = [total[2 * k + 1 : 2 * k + 2] for k in range(4)]
    moment = []
    for k in range(4):
        moment.append(even[0] if k == 0 else 2.0 * even[k] - even[0])
        moment.append(odd[0] if k == 0 else 2.0 * odd[k] - odd[0])

    def inner_product(i, j):
        return 0.5 * (moment[i + j] + moment[abs(i - j)])

    def energy(i, j):
        shifted = 0.5 * (inner_product(i, j + 1) + inner_product(i, abs(j - 1)))
        return HALF * (shifted + inner_product(i, j))

    low = [[None] * 4 for _ in range(4)]
    diag, inverse, half = [], [], []
    for j in range(4):
        d = energy(j, j)
        value = moment[j]
        for k in range(j):
            d = d - low[j][k] * low[j][k] * diag[k]
            value = value - low[j][k] * half[k]
        diag.append(d)
        half.append(value)
        inverse.append(1.0 / d)
        for i in range(j + 1, 4):
            e = energy(i, j)
            for k in range(j):
                e = e - low[i][k] * low[j][k] * diag[k]
            low[i][j] = e * inverse[j]
    weight = [half[k] * inverse[k] for k in range(4)]
    for i in (2, 1, 0):
        for k in range(i + 1, 4):
            weight[i] = weight[i] - low[k][i] * weight[k]
    turned = jnp.concatenate(weight + [jnp.zeros((4, 128), F32)], axis=0).T
    for k in range(4):
        coef[k] = jnp.broadcast_to(turned[0:32, k : k + 1], (32, 128))
    for n in range(36):
        out[n] = x0[n] + coef[0] * t0[n] + coef[1] * t1[n] + coef[2] * t2[n] + coef[3] * t3[n]


def pack_kernel(u, out):
    for g in range(9):
        turned = u[4 * g : 4 * g + 4].reshape(128, 128).T
        out[:, 16 * g : 16 * g + 16, :] = turned.reshape(8, 16, 128)


def block_turn(blocks):
    part = lax.shift_right_logical(lane_ids(blocks[0].shape), 5)
    rolled = [blocks[0]] + [pltpu.roll(blocks[s], 32 * s, 1) for s in range(1, 4)]
    out = []
    for m in range(4):
        mixed = rolled[-m % 4]
        for t in range(1, 4):
            mixed = jnp.where(part == t, rolled[(t - m) % 4], mixed)
        out.append(pltpu.roll(mixed, 128 - 32 * m, 1) if m else mixed)
    return out


def product3(high, low, table):
    def dot(a, b):
        return jnp.dot(a, b, preferred_element_type=F32)

    return dot(high, table[0]) + dot(high, table[1]) + dot(low, table[0])


def advect_kernel(meta, came, speed, synth, analy, out, high, low, phys):
    for g in range(9):
        for h in range(2):
            pieces = block_turn([came[4 * h + s, 16 * g : 16 * g + 16, :] for s in range(4)])
            for m in range(4):
                n = 16 * (4 * g + m)
                hi, lo = split(pieces[m])
                high[n : n + 16, 128 * h : 128 * h + 128] = hi
                low[n : n + 16, 128 * h : 128 * h + 128] = lo
    for i in range(6):
        part = slice(96 * i, 96 * i + 96)
        phys[part, :] = product3(high[part, :], low[part, :], synth)
    wide = meta[3] == 0
    sx = jnp.where(wide, 2.0, 1.0)
    sy = jnp.where(wide, 1.0, 2.0)
    for h in range(2):
        cols = slice(128 * h, 128 * h + 128)
        u = [[phys[16 * (6 * i + j) : 16 * (6 * i + j) + 16, cols] for j in range(6)] for i in range(6)]
        acc = [[None] * 6 for _ in range(6)]
        for j in range(6):
            g = folded([u[i][j] for i in range(6)], DERIV_FOLD, -1)
            for i in range(6):
                acc[i][j] = sx * (speed[0, 6 * i + j, :, cols] * g[i])
        for i in range(6):
            g = folded(u[i], DERIV_FOLD, -1)
            for j in range(6):
                n = 16 * (6 * i + j)
                total = acc[i][j] + sy * (speed[1, 6 * i + j, :, cols] * g[j])
                hi, lo = split(float(-0.5 * W[i] * W[j]) * total)
                high[n : n + 16, cols] = hi
                low[n : n + 16, cols] = lo
    for i in range(6):
        part = slice(96 * i, 96 * i + 96)
        phys[part, :] = product3(high[part, :], low[part, :], analy)
    for g in range(9):
        for h in range(2):
            cols = slice(128 * h, 128 * h + 128)
            pieces = block_turn(
                [phys[16 * (4 * g + m) : 16 * (4 * g + m) + 16, cols] for m in range(4)]
            )
            for s in range(4):
                out[4 * h + s, 16 * g : 16 * g + 16, :] = pieces[s]


def shift_by(array, by):
    count = lax.axis_size("elem")
    return lax.ppermute(array, "elem", [(i, (i + by) % count) for i in range(count)])


def shards(scalar_modes, velocity, viscosity, mortar_links, mortar_sides, layout):
    u = jnp.transpose(scalar_modes, (1, 2, 0, 3)).reshape(36, 32, 128)
    speed = jnp.transpose(velocity, (0, 2, 3, 4, 1)).reshape(2, 36, 16, 256)
    synth, analy = plane_tables(256)
    synth = jnp.asarray(split_table(synth.T))
    analy = jnp.asarray(split_table(analy.T))
    plane_id, elem_id = lax.axis_index("plane"), lax.axis_index("elem")
    own, other = mortar_sides[0], mortar_sides[1]
    second = jnp.arange(8)[:, None] % 2 == 1
    plain = (own == 3) | ((own == 0) & (other == 0) & ~second) | (mortar_links // 128 != elem_id)
    mixed = jnp.any(~plain)
    meta = jnp.stack([plane_id, elem_id, mixed.astype(jnp.int32), layout[0]]).astype(jnp.int32)

    vol, edge = shape(36, 32, 128), shape(48, 128)
    both = shape(96, 128)
    blocks = shape(8, 144, 128)
    packed = call(pack_kernel, [blocks], [], [u], [VMEM])[0]
    came = lax.all_to_all(packed, "plane", 0, 0, tiled=True)

    table = shape(36, 8, 128)
    idx, edge_idx, tab, own_c, far_c, edge_own, edge_far = call(
        prep_kernel,
        [shape(24, 128, dtype=jnp.int32), shape(8, 128, dtype=jnp.int32), shape(8, 128)] + [table] * 4,
        [],
        [meta, mortar_links, mortar_sides, viscosity[None], layout[None]],
        [SMEM] + [VMEM] * 4,
    )
    head = [meta, idx, tab, own_c, far_c]
    edges = [edge_idx, edge_own, edge_far]

    def run(kernel, outs, scratch, args):
        return call(kernel, outs, scratch, args, [SMEM if a is meta else VMEM for a in args])

    def trade(send_w, send_e):
        return shift_by(send_e, 1), shift_by(send_w, -1)

    hu, *sent = run(guess_kernel, [vol, edge, edge], [], head + [u])
    got = trade(*sent)
    came, *got = lax.optimization_barrier((came, *got))
    back = run(
        advect_kernel,
        [blocks],
        [VMEM((576, 256), BF16), VMEM((576, 256), BF16), VMEM((576, 256), F32)],
        [meta, came, speed, synth, analy],
    )[0]
    back = lax.all_to_all(back, "plane", 0, 0, tiled=True)
    base = run(
        base_kernel, [vol], [VMEM((48, 128), F32)], [idx, *edges, u, hu, *sent, *got]
    )[0]

    def work(count):
        return [
            VMEM((96, 128), F32),
            VMEM((36, 32, 128), F32),
            VMEM((32, 128 * count), F32),
            VMEM((8, 128), F32),
        ]

    t0, h0, *sent = run(residual_kernel, [vol, vol, edge, edge], [], head + [back, base])
    got = trade(*sent)
    t1, t2, h2, to_w, to_e, keep, part = run(
        two_steps_kernel,
        [vol, vol, vol, edge, edge, both, shape(8, 128)],
        work(5),
        head + edges + [t0, h0, *sent, *got],
    )
    got = trade(to_w, to_e)
    t3, red = run(
        last_steps_kernel,
        [vol, shape(16, 8, 128)],
        work(3),
        head + edges + [t1, t2, h2, to_w, to_e, *got, keep, part],
    )
    red = lax.all_to_all(red, "elem", 0, 0, tiled=True)
    out = run(finish_kernel, [vol], [VMEM((4, 32, 128), F32)], [red, u, t0, t1, t2, t3])[0]
    return jnp.transpose(out.reshape(6, 6, 32, 128), (2, 0, 1, 3))


def solution(mesh):
    placed = (
        P("plane", None, None, "elem"),
        P(None, None, None, None, ("elem", "plane")),
        P("elem"),
        P(None, "elem"),
        P(None, None, "elem"),
        P("elem"),
    )
    return jax.shard_map(
        shards,
        mesh=mesh,
        in_specs=placed,
        out_specs=P("plane", None, None, "elem"),
        check_vma=False,
    )
```

time: 98.4 us -> 83.4 us (0.85)
  starting transfers between devices: 44.2 us -> 23.6 us
  local copies, waits for them, and re-layouts: 1.13 us -> 7.75 us
  waiting for transfers between devices: 16.4 us -> 22.2 us
  blocking collectives: 14.2 us -> 10.2 us
  Pallas kernels: 18.9 us -> 17.5 us
    ppermute x10 -> x6, starting transfers between devices: 29.3 us -> 14.3 us  [shift_by(): lax.ppermute(array, 'elem', [(i, (i + by) % count) for i in range(count)])]
    all_to_all x1, waiting for transfers between devices: 0.01 us -> 9.37 us  [shards(): back = lax.all_to_all(back, 'plane', 0, 0, tiled=True)]
    all_to_all x1, waiting for transfers between devices: 8.1 us -> 0.01 us  [shards(): came = lax.all_to_all(packed, 'plane', 0, 0, tiled=True)]
    all_to_all x1 -> x0, starting transfers between devices: 6.8 us -> none  [shards(): red = lax.all_to_all(red, 'elem', 0, 0, tiled=True)]
    unnamed x18 -> x48, local copies, waits for them, and re-layouts: 1.1 us -> 7.75 us
    ppermute x10 -> x6, waiting for transfers between devices: 8.33 us -> 12.9 us  [shift_by(): lax.ppermute(array, 'elem', [(i, (i + by) % count) for i in range(count)])]
    all_to_all x1, blocking collectives: 14.2 us -> 10.2 us  [shards(): red = lax.all_to_all(red, 'elem', 0, 0, tiled=True)]
    pallas_call x12 -> x9, Pallas kernels: 18.9 us -> 17.5 us  [call(): pl.pallas_call(kernel, out_shape=outs, in_specs=[pl.BlockSpec(memory_spac...]
  transfers between devices with their start and end apart: 13 -> 8, of which waited for: 6 -> 6; matrix products, arithmetic and copies ran while one was open for 2% -> 1% of each run, Pallas kernels for 5% -> 4%
where the time goes in v2:
time: 83.4 us; the launch traced here: 82.9 us
  starting transfers between devices  23.6 us (28%)
  waiting for transfers between devices  22.2 us (27%)
  Pallas kernels  17.5 us (21%)
  blocking collectives  10.2 us (12%)
  local copies, waits for them, and re-layouts  7.75 us (9%)
    pallas_call x9, Pallas kernels, call(): pl.pallas_call(kernel, out_shape=outs, in_specs=[pl.BlockSpec(memory_spac...  17.5 us
    ppermute x6, starting transfers between devices, shift_by(): lax.ppermute(array, 'elem', [(i, (i + by) % count) for i in range(count)])  14.3 us
    ppermute x6, waiting for transfers between devices, shift_by(): lax.ppermute(array, 'elem', [(i, (i + by) % count) for i in range(count)])  12.9 us
    all_to_all x1, blocking collectives, shards(): red = lax.all_to_all(red, 'elem', 0, 0, tiled=True)  10.2 us
    all_to_all x1, waiting for transfers between devices, shards(): back = lax.all_to_all(back, 'plane', 0, 0, tiled=True)  9.37 us
    unnamed x48, local copies, waits for them, and re-layouts  7.75 us
    all_to_all x1, starting transfers between devices, shards(): back = lax.all_to_all(back, 'plane', 0, 0, tiled=True)  4.87 us
    all_to_all x1, starting transfers between devices, shards(): came = lax.all_to_all(packed, 'plane', 0, 0, tiled=True)  4.51 us
  transfers between devices with their start and end apart: 8, of which 6 were waited for; matrix products, arithmetic and copies ran while one was open for 1% of the time, Pallas kernels for 4%

profile of v2, /device:TPU:0, one launch (start us, length us, event | category | flops | bytes accessed | tf_op | source)
XLA Modules:
  0.0 82.9 jit_solution(10895133822685536924)
XLA Ops:
  0.0 1.1 %copy-done = f32[32,6,6,128]{3,0,2,1:T(8,128)S(1)} copy-done((f32[32,6,6,128]{3,0,2,1:T(8,128)S(1)}, f32[32,6,6,128]{3,0,2,1:T(8,128)}, u32[]{:S(2)}) %copy-start) | copy-done | bytes 589848
  1.1 1.1 %shard_map.83 = f32[8,144,128]{2,1,0:T(8,128)} custom-call(f32[36,32,128]{2,1,0:T(8,128)S(1)} %bitcast.29), custom_call_target="tpu_custom_call" | custom-call | flops 4000000 | bytes 1179648 | tf_op jit(solution)/shard_map/pallas_call | solution.py:109
  2.1 4.5 %all-to-all-start = ((f32[8,144,128]{2,1,0:T(8,128)}), f32[8,144,128]{2,1,0:T(8,128)S(1)}, u32[]{:S(2)}, u32[]{:S(2)}) async-start(f32[8,144,128]{2,1,0:T(8,128)} %shard_map.83), calls=%async_computation | async-start | bytes 1179648 | tf_op jit(solution)/shard_map/all_to_all | solution.py:666
  8.2 1.2 %shard_map.82 = (s32[24,128]{1,0:T(8,128)S(1)}, s32[8,128]{1,0:T(8,128)S(1)}, f32[8,128]{1,0:T(8,128)S(1)}, f32[36,8,128]{2,1,0:T(8,128)S(1)}, f32[36,8,128]{2,1...) custom-call(s32[4]{0:T(128)S(1)} %pad_add_fusion.meta, s32[8,128]{1,0:T(8,128)S(1)} %copy-done.21, ...), custom_call_target="tpu_custom_call" | custom-call | flops 4000000 | bytes 623632 | tf_op jit(solution)/shard_map/pallas_call | solution.py:109
  9.9 1.8 %shard_map.84 = (f32[36,32,128]{2,1,0:T(8,128)S(1)}, f32[48,128]{1,0:T(8,128)S(1)}, f32[48,128]{1,0:T(8,128)S(1)}) custom-call(s32[4]{0:T(128)S(1)} %pad_add_fusion.meta, s32[24,128]{1,0:T(8,128)S(1)} %get-tuple-element.31.idx, f32[8,128]{1,0:T(8,128)S(1)} %get-tuple-element.32.tab, f32[36,8,128]{2,1,0:T(8,128)S(1)} %get-tuple-element.33.own_c, ...), custom_call_target="tpu_custom_call" | custom-call | flops 4000000 | bytes 1540112 | tf_op jit(solution)/shard_map/pallas_call | solution.py:109
  11.8 1.6 %collective-permute-start = (f32[48,128]{1,0:T(8,128)S(1)}, f32[48,128]{1,0:T(8,128)S(1)}, u32[]{:S(2)}, u32[]{:S(2)}) collective-permute-start(f32[48,128]{1,0:T(8,128)S(1)} %get-tuple-element.38.to_e), channel_id=1, source_target_pairs={{0,1},{1,2},{2,3},{3,4},{4,5},{5,6},{6,7},{7,8},{8,9},{9,10},{10,1... | collective-permute-start | bytes 73736 | tf_op jit(solution)/shard_map/ppermute | solution.py:646
  14.0 5.0 %collective-permute-start.1 = (f32[48,128]{1,0:T(8,128)S(1)}, f32[48,128]{1,0:T(8,128)S(1)}, u32[]{:S(2)}, u32[]{:S(2)}) collective-permute-start(f32[48,128]{1,0:T(8,128)S(1)} %get-tuple-element.39.to_w), channel_id=1, source_target_pairs={{0,15},{1,0},{2,1},{3,2},{4,3},{5,4},{6,5},{7,6},{8,7},{9,8},{10,9... | collective-permute-start | bytes 73736 | tf_op jit(solution)/shard_map/ppermute | solution.py:646
  21.4 0.9 %copy-done.5 = bf16[2,256,256]{2,1,0:T(8,128)(2,1)S(1)} copy-done((bf16[2,256,256]{2,1,0:T(8,128)(2,1)S(1)}, bf16[2,256,256]{2,1,0:T(8,128)(2,1)}, u32[]{:S(2)}) %copy-start.5) | copy-done | bytes 262168
  22.4 0.9 %copy-done.6 = bf16[2,256,256]{2,1,0:T(8,128)(2,1)S(1)} copy-done((bf16[2,256,256]{2,1,0:T(8,128)(2,1)S(1)}, bf16[2,256,256]{2,1,0:T(8,128)(2,1)}, u32[]{:S(2)}) %copy-start.6) | copy-done | bytes 262168
  24.0 3.1 %shard_map.85 = f32[8,144,128]{2,1,0:T(8,128)} custom-call(s32[4]{0:T(128)S(1)} %copy-done.18, f32[8,144,128]{2,1,0:T(8,128)S(1)} %all-to-all-done.came, f32[2,36,16,256]{3,2,1,0:T(8,128)S(1)} %bitcast.33, bf16[2,256,256]{2,1,0:T(8,128)(2,1)S(1)} %copy-done.6, bf16[2,256,256]{2,1,0:T(8,128)(2,1)S(1)} %copy-done.5), custom_call_target="tpu_custom_call" | custom-call | flops 4000000 | bytes 3407888 | tf_op jit(solution)/shard_map/pallas_call | solution.py:109
  27.2 4.9 %all-to-all-start.1 = ((f32[8,144,128]{2,1,0:T(8,128)}), f32[8,144,128]{2,1,0:T(8,128)S(1)}, u32[]{:S(2)}, u32[]{:S(2)}) async-start(f32[8,144,128]{2,1,0:T(8,128)} %shard_map.85), calls=%async_computation.1 | async-start | bytes 1179648 | tf_op jit(solution)/shard_map/all_to_all | solution.py:694
  32.1 1.1 %copy-done.4 = f32[36,32,128]{2,1,0:T(8,128)S(1)} copy-done((f32[36,32,128]{2,1,0:T(8,128)S(1)}, f32[36,32,128]{2,1,0:T(8,128)}, u32[]{:S(2)}) %copy-start.4) | copy-done | bytes 589848
  33.7 9.4 %all-to-all-done.1.back = f32[8,144,128]{2,1,0:T(8,128)S(1)} async-done(((f32[8,144,128]{2,1,0:T(8,128)}), f32[8,144,128]{2,1,0:T(8,128)S(1)}, u32[]{:S(2)}, u32[]{:S(2)}) %all-to-all-start.1) | async-done | bytes 589856 | tf_op jit(solution)/shard_map/all_to_all | solution.py:694
  43.1 2.1 %shard_map.87 = (f32[36,32,128]{2,1,0:T(8,128)S(1)}, f32[36,32,128]{2,1,0:T(8,128)S(1)}, f32[48,128]{1,0:T(8,128)S(1)}, f32[48,128]{1,0:T(8,128)S(1)}) custom-call(s32[4]{0:T(128)S(1)} %copy-done.19, s32[24,128]{1,0:T(8,128)S(1)} %get-tuple-element.31.idx, f32[8,128]{1,0:T(8,128)S(1)} %get-tuple-element.32.tab, f32[36,8,128]{2,1,0:T(8,128)S(1)} %get-tuple-element.33.own_c, ...), custom_call_target="tpu_custom_call" | custom-call | flops 4000000 | bytes 2719760 | tf_op jit(solution)/shard_map/pallas_call | solution.py:109
  45.1 5.5 %collective-permute-start.3 = (f32[48,128]{1,0:T(8,128)S(1)}, f32[48,128]{1,0:T(8,128)S(1)}, u32[]{:S(2)}, u32[]{:S(2)}) collective-permute-start(f32[48,128]{1,0:T(8,128)S(1)} %get-tuple-element.46.to_w), channel_id=1, source_target_pairs={{0,15},{1,0},{2,1},{3,2},{4,3},{5,4},{6,5},{7,6},{8,7},{9,8},{10,9... | collective-permute-start | bytes 73736 | tf_op jit(solution)/shard_map/ppermute | solution.py:646
  50.7 1.5 %collective-permute-done.3.from_e = f32[48,128]{1,0:T(8,128)S(1)} collective-permute-done((f32[48,128]{1,0:T(8,128)S(1)}, f32[48,128]{1,0:T(8,128)S(1)}, u32[]{:S(2)}, u32[]{:S(2)}) %collective-permute-start.3) | collective-permute-done | bytes 24608 | tf_op jit(solution)/shard_map/ppermute | solution.py:646
  52.2 5.6 %collective-permute-done.2.from_w = f32[48,128]{1,0:T(8,128)S(1)} collective-permute-done((f32[48,128]{1,0:T(8,128)S(1)}, f32[48,128]{1,0:T(8,128)S(1)}, u32[]{:S(2)}, u32[]{:S(2)}) %collective-permute-start.2) | collective-permute-done | bytes 24608 | tf_op jit(solution)/shard_map/ppermute | solution.py:646
  57.8 3.7 %shard_map.88 = (f32[36,32,128]{2,1,0:T(8,128)S(1)}, f32[36,32,128]{2,1,0:T(8,128)S(1)}, f32[36,32,128]{2,1,0:T(8,128)S(1)}, f32[48,128]{1,0:T(8,128)S(1)}, f32[...) custom-call(s32[4]{0:T(128)S(1)} %copy-done.19, s32[24,128]{1,0:T(8,128)S(1)} %get-tuple-element.31.idx, ...), custom_call_target="tpu_custom_call" | custom-call | flops 4000000 | bytes 3760144 | tf_op jit(solution)/shard_map/pallas_call | solution.py:109
  61.5 2.0 %collective-permute-start.4 = (f32[48,128]{1,0:T(8,128)S(1)}, f32[48,128]{1,0:T(8,128)S(1)}, u32[]{:S(2)}, u32[]{:S(2)}) collective-permute-start(f32[48,128]{1,0:T(8,128)S(1)} %get-tuple-element.52.to_e), channel_id=1, source_target_pairs={{0,1},{1,2},{2,3},{3,4},{4,5},{5,6},{6,7},{7,8},{8,9},{9,10},{10,1... | collective-permute-start | bytes 73736 | tf_op jit(solution)/shard_map/ppermute | solution.py:646
  63.6 1.8 %collective-permute-done.5.from_e = f32[48,128]{1,0:T(8,128)S(1)} collective-permute-done((f32[48,128]{1,0:T(8,128)S(1)}, f32[48,128]{1,0:T(8,128)S(1)}, u32[]{:S(2)}, u32[]{:S(2)}) %collective-permute-start.5) | collective-permute-done | bytes 24608 | tf_op jit(solution)/shard_map/ppermute | solution.py:646
  65.4 3.4 %collective-permute-done.4.from_w = f32[48,128]{1,0:T(8,128)S(1)} collective-permute-done((f32[48,128]{1,0:T(8,128)S(1)}, f32[48,128]{1,0:T(8,128)S(1)}, u32[]{:S(2)}, u32[]{:S(2)}) %collective-permute-start.4) | collective-permute-done | bytes 24608 | tf_op jit(solution)/shard_map/ppermute | solution.py:646
  68.7 2.6 %shard_map.89 = (f32[36,32,128]{2,1,0:T(8,128)S(1)}, f32[16,8,128]{2,1,0:T(8,128)S(1)}) custom-call(s32[4]{0:T(128)S(1)} %copy-done.19, s32[24,128]{1,0:T(8,128)S(1)} %get-tuple-element.31.idx, f32[8,128]{1,0:T(8,128)S(1)} %get-tuple-element.32.tab, f32[36,8,128]{2,1,0:T(8,128)S(1)} %get-tuple-element.33.own_c, f32[36,8,128]{2,1,0:T(8,128)S(1)} %get-tuple-element.34.far_c, ...), custom_call_target="tpu_custom_call" | custom-call | flops 4000000 | bytes 3186704 | tf_op jit(solution)/shard_map/pallas_call | solution.py:109
  71.4 10.2 %all_to_all.15.red = f32[16,8,128]{2,1,0:T(8,128)S(1)} all-to-all(f32[16,8,128]{2,1,0:T(8,128)S(1)} %get-tuple-element.55), channel_id=1, replica_groups=mesh['plane'=8,'elem'=16] {'elem'}, dimensions={0} | all-to-all | bytes 131072 | tf_op jit(solution)/shard_map/all_to_all | solution.py:722
  81.6 1.4 %shard_map.90 = f32[36,32,128]{2,1,0:T(8,128)} custom-call(f32[16,8,128]{2,1,0:T(8,128)S(1)} %all_to_all.15.red, f32[36,32,128]{2,1,0:T(8,128)S(1)} %bitcast.32, f32[36,32,128]{2,1,0:T(8,128)S(1)} %get-tuple-element.44.t0, f32[36,32,128]{2,1,0:T(8,128)S(1)} %get-tuple-element.48.t1, f32[36,32,128]{2,1,0:T(8,128)S(1)} %get-tuple-element.49.t2, ...), custom_call_target="tpu_custom_call" | custom-call | flops 4000000 | bytes 3604480 | tf_op jit(solution)/shard_map/pallas_call | solution.py:109
  (53 shorter events, 5.7 us)
Async XLA Ops:
  0.0 1.1 %copy-start = (f32[32,6,6,128]{3,0,2,1:T(8,128)S(1)}, f32[32,6,6,128]{3,0,2,1:T(8,128)}, u32[]{:S(2)}) copy-start(f32[32,6,6,128]{3,0,2,1:T(8,128)} %param.8) | copy-start | bytes 1769476
  1.1 5.6 %copy-start.20 = (s32[2,8,128]{2,1,0:T(8,128)S(1)}, s32[2,8,128]{2,1,0:T(8,128)}, u32[]{:S(2)}) copy-start(s32[2,8,128]{2,1,0:T(8,128)} %sides.1) | copy-start | bytes 24580
  1.1 5.6 %copy-start.21 = (s32[8,128]{1,0:T(8,128)S(1)}, s32[8,128]{1,0:T(8,128)}, u32[]{:S(2)}) copy-start(s32[8,128]{1,0:T(8,128)} %links.1) | copy-start | bytes 12292
  1.1 7.0 %copy-start.22 = (s32[128]{0:T(128)S(1)}, s32[128]{0:T(128)}, u32[]{:S(2)}) copy-start(s32[128]{0:T(128)} %param.13) | copy-start | bytes 1540
  1.1 7.1 %copy-start.23 = (f32[128]{0:T(128)S(1)}, f32[128]{0:T(128)}, u32[]{:S(2)}) copy-start(f32[128]{0:T(128)} %param.10) | copy-start | bytes 1540
  1.1 8.8 %copy-start.1 = (f32[32,6,6,128]{3,0,2,1:T(8,128)S(1)}, f32[32,6,6,128]{3,0,2,1:T(8,128)}, u32[]{:S(2)}) copy-start(f32[32,6,6,128]{3,0,2,1:T(8,128)} %param.8) | copy-start | bytes 1769476
  2.1 19.3 %copy-start.2 = (f32[2,256,6,6,16]{1,4,3,2,0:T(8,128)S(1)}, f32[2,256,6,6,16]{1,4,3,2,0:T(8,128)}, u32[]{:S(2)}) copy-start(f32[2,256,6,6,16]{1,4,3,2,0:T(8,128)} %param.9) | copy-start | bytes 3538948
  2.1 19.3 %all-to-all-start = ((f32[8,144,128]{2,1,0:T(8,128)}), f32[8,144,128]{2,1,0:T(8,128)S(1)}, u32[]{:S(2)}, u32[]{:S(2)}) async-start(f32[8,144,128]{2,1,0:T(8,128)} %shard_map.83), calls=%async_computation | async-start | bytes 1179648 | tf_op jit(solution)/shard_map/all_to_all | solution.py:666
  8.1 3.6 %copy-start.17 = (s32[4]{0:T(128)}, s32[4]{0:T(128)S(1)}, u32[]{:S(2)}) copy-start(s32[4]{0:T(128)S(1)} %pad_add_fusion.meta) | copy-start | bytes 52
  11.8 15.4 %copy-start.3 = (f32[36,32,128]{2,1,0:T(8,128)}, f32[36,32,128]{2,1,0:T(8,128)S(1)}, u32[]{:S(2)}) copy-start(f32[36,32,128]{2,1,0:T(8,128)S(1)} %get-tuple-element.41.hu) | copy-start | bytes 1769476
  11.8 8.4 %collective-permute-start = (f32[48,128]{1,0:T(8,128)S(1)}, f32[48,128]{1,0:T(8,128)S(1)}, u32[]{:S(2)}, u32[]{:S(2)}) collective-permute-start(f32[48,128]{1,0:T(8,128)S(1)} %get-tuple-element.38.to_e), channel_id=1, source_target_pairs={{0,1},{1,2},{2,3},{3,4},{4,5},{5,6},{6,7},{7,8},{8,9},{9,10},{10,1... | collective-permute-start | bytes 73736 | tf_op jit(solution)/shard_map/ppermute | solution.py:646
  14.0 6.8 %collective-permute-start.1 = (f32[48,128]{1,0:T(8,128)S(1)}, f32[48,128]{1,0:T(8,128)S(1)}, u32[]{:S(2)}, u32[]{:S(2)}) collective-permute-start(f32[48,128]{1,0:T(8,128)S(1)} %get-tuple-element.39.to_w), channel_id=1, source_target_pairs={{0,15},{1,0},{2,1},{3,2},{4,3},{5,4},{6,5},{7,6},{8,7},{9,8},{10,9... | collective-permute-start | bytes 73736 | tf_op jit(solution)/shard_map/ppermute | solution.py:646
  27.1 4.9 %copy-start.8 = (s32[8,128]{1,0:T(8,128)S(1)}, s32[8,128]{1,0:T(8,128)}, u32[]{:S(2)}) copy-start(s32[8,128]{1,0:T(8,128)} %copy-done.7) | copy-start | bytes 12292
  27.1 4.9 %copy-start.10 = (f32[48,128]{1,0:T(8,128)S(1)}, f32[48,128]{1,0:T(8,128)}, u32[]{:S(2)}) copy-start(f32[48,128]{1,0:T(8,128)} %copy-done.9) | copy-start | bytes 73732
  27.1 4.9 %copy-start.12 = (f32[48,128]{1,0:T(8,128)S(1)}, f32[48,128]{1,0:T(8,128)}, u32[]{:S(2)}) copy-start(f32[48,128]{1,0:T(8,128)} %copy-done.11) | copy-start | bytes 73732
  27.1 4.9 %copy-start.14 = (f32[48,128]{1,0:T(8,128)S(1)}, f32[48,128]{1,0:T(8,128)}, u32[]{:S(2)}) copy-start(f32[48,128]{1,0:T(8,128)} %copy-done.13) | copy-start | bytes 73732
  27.1 4.9 %copy-start.16 = (f32[48,128]{1,0:T(8,128)S(1)}, f32[48,128]{1,0:T(8,128)}, u32[]{:S(2)}) copy-start(f32[48,128]{1,0:T(8,128)} %copy-done.15) | copy-start | bytes 73732
  27.2 15.9 %all-to-all-start.1 = ((f32[8,144,128]{2,1,0:T(8,128)}), f32[8,144,128]{2,1,0:T(8,128)S(1)}, u32[]{:S(2)}, u32[]{:S(2)}) async-start(f32[8,144,128]{2,1,0:T(8,128)} %shard_map.85), calls=%async_computation.1 | async-start | bytes 1179648 | tf_op jit(solution)/shard_map/all_to_all | solution.py:694
  32.0 11.1 %copy-start.19 = (s32[4]{0:T(128)S(1)}, s32[4]{0:T(128)}, u32[]{:S(2)}) copy-start(s32[4]{0:T(128)} %copy-done.17) | copy-start | bytes 52
  32.1 1.1 %copy-start.4 = (f32[36,32,128]{2,1,0:T(8,128)S(1)}, f32[36,32,128]{2,1,0:T(8,128)}, u32[]{:S(2)}) copy-start(f32[36,32,128]{2,1,0:T(8,128)} %copy-done.3) | copy-start | bytes 1769476
  45.1 7.0 %collective-permute-start.3 = (f32[48,128]{1,0:T(8,128)S(1)}, f32[48,128]{1,0:T(8,128)S(1)}, u32[]{:S(2)}, u32[]{:S(2)}) collective-permute-start(f32[48,128]{1,0:T(8,128)S(1)} %get-tuple-element.46.to_w), channel_id=1, source_target_pairs={{0,15},{1,0},{2,1},{3,2},{4,3},{5,4},{6,5},{7,6},{8,7},{9,8},{10,9... | collective-permute-start | bytes 73736 | tf_op jit(solution)/shard_map/ppermute | solution.py:646
  50.7 7.1 %collective-permute-start.2 = (f32[48,128]{1,0:T(8,128)S(1)}, f32[48,128]{1,0:T(8,128)S(1)}, u32[]{:S(2)}, u32[]{:S(2)}) collective-permute-start(f32[48,128]{1,0:T(8,128)S(1)} %get-tuple-element.47.to_e), channel_id=1, source_target_pairs={{0,1},{1,2},{2,3},{3,4},{4,5},{5,6},{6,7},{7,8},{8,9},{9,10},{10,1... | collective-permute-start | bytes 73736 | tf_op jit(solution)/shard_map/ppermute | solution.py:646
  61.5 3.8 %collective-permute-start.5 = (f32[48,128]{1,0:T(8,128)S(1)}, f32[48,128]{1,0:T(8,128)S(1)}, u32[]{:S(2)}, u32[]{:S(2)}) collective-permute-start(f32[48,128]{1,0:T(8,128)S(1)} %get-tuple-element.51.to_w), channel_id=1, source_target_pairs={{0,15},{1,0},{2,1},{3,2},{4,3},{5,4},{6,5},{7,6},{8,7},{9,8},{10,9... | collective-permute-start | bytes 73736 | tf_op jit(solution)/shard_map/ppermute | solution.py:646
  61.5 7.2 %collective-permute-start.4 = (f32[48,128]{1,0:T(8,128)S(1)}, f32[48,128]{1,0:T(8,128)S(1)}, u32[]{:S(2)}, u32[]{:S(2)}) collective-permute-start(f32[48,128]{1,0:T(8,128)S(1)} %get-tuple-element.52.to_e), channel_id=1, source_target_pairs={{0,1},{1,2},{2,3},{3,4},{4,5},{5,6},{6,7},{7,8},{8,9},{9,10},{10,1... | collective-permute-start | bytes 73736 | tf_op jit(solution)/shard_map/ppermute | solution.py:646
  (8 other events, 5.6 us)

commit v3 on v2

--- a/solution.py
+++ b/solution.py
@@ -103,17 +103,17 @@
     return lax.broadcasted_iota(jnp.int32, shape, len(shape) - 1)
 
 
-def call(kernel, outs, scratch, operands, spaces, flops=4_000_000):
+def call(kernel, outs, scratch, operands, spaces, out_space=VMEM, grant=3):
     total = sum(int(np.prod(o.shape)) * 4 for o in outs)
     total += sum(int(np.prod(o.shape)) * 4 for o in operands)
     return pl.pallas_call(
         kernel,
         out_shape=outs,
         in_specs=[pl.BlockSpec(memory_space=s) for s in spaces],
-        out_specs=[pl.BlockSpec(memory_space=VMEM) for _ in outs],
+        out_specs=[pl.BlockSpec(memory_space=out_space) for _ in outs],
         scratch_shapes=scratch,
-        compiler_params=pltpu.CompilerParams(vmem_limit_bytes=40 * 2**20),
-        cost_estimate=pl.CostEstimate(flops=flops, bytes_accessed=total, transcendentals=0),
+        compiler_params=pltpu.CompilerParams(vmem_limit_bytes=grant * 2**20),
+        cost_estimate=pl.CostEstimate(flops=4_000_000, bytes_accessed=total, transcendentals=0),
     )(*operands)
 
 
@@ -254,51 +254,88 @@
     ]
 
 
-def inner(group, env, v_ref, out):
-    meta, idx, tab, own_c, far_c = env
+def either(meta, loop):
+    for plain in (True, False):
+
+        @pl.when((meta[2] == 0) == plain)
+        def _(plain=plain):
+            lax.fori_loop(0, 4, lambda group, carry: loop(group, plain) or carry, 0)
+
+
+def weighted(factors, values):
+    total = float(factors[0]) * values[0]
+    for f, v in zip(factors[1:], values[1:]):
+        total = total + float(f) * v
+    return total
+
+
+def plain_terms(env, v):
+    _, idx, tab, _, _ = env
+
+    def of_face(face):
+        active = row_of(tab, 3 + face)
+        local = row_of(idx, LOCAL + 2 * face)
+
+        def term(a):
+            n, m = face_nodes(face)[a], face_nodes(face ^ 1)[a]
+            return (float(PENALTY * W[a]) * active) * (v(n) - take(v(m), local))
+
+        return term
+
+    return [of_face(face) for face in range(4)]
+
+
+def general_terms(env, v):
+    _, idx, _, own_c, far_c = env
+    found = []
+    for face in range(4):
+        mine = [v(n) for n in face_nodes(face)]
+        theirs = [
+            [take(v(n), row_of(idx, LOCAL + 2 * face + t)) for n in face_nodes(face ^ 1)]
+            for t in range(2)
+        ]
+        values = []
+        for a in range(6):
+            extra = jnp.zeros((8, 128), F32)
+            for b in range(6):
+                extra = extra + own_c[6 * a + b, 2 * face : 2 * face + 1, :] * mine[b]
+                for t in range(2):
+                    s = 2 * face + t
+                    extra = extra + far_c[6 * a + b, s : s + 1, :] * theirs[t][b]
+            values.append(extra)
+        found.append(values.__getitem__)
+    return found
+
+
+def inner(group, env, v_ref, plain, emit):
+    meta, _, tab, _, _ = env
     rows = group_rows(group)
-    v = [v_ref[n, rows, :] for n in range(36)]
+
+    def v(n):
+        return v_ref[n, rows, :]
+
+    terms = (plain_terms if plain else general_terms)(env, v)
     q = meta[0] * 32 + group * 8 + lax.broadcasted_iota(jnp.int32, (8, 128), 0)
     harmonic = lax.shift_right_logical(q + 1, 1).astype(F32) * SPANWISE
-    cx, cy, nu = tab[0:1, :], tab[1:2, :], tab[2:3, :]
-    shift = 1.0 + 0.5 * nu * (harmonic * harmonic)
-    res = [shift * v[n] for n in range(36)]
-    for j in range(6):
-        g = folded([v[6 * i + j] for i in range(6)], STIFF_FOLD, 1)
-        for i in range(6):
-            res[6 * i + j] = res[6 * i + j] + cx * g[i]
-    for i in range(6):
-        g = folded(v[6 * i : 6 * i + 6], STIFF_FOLD, 1)
-        for j in range(6):
-            out[6 * i + j, rows, :] = float(W[i] * W[j]) * (res[6 * i + j] + cy * g[j])
-
-    @pl.when(meta[2] == 0)
-    def _():
-        for face in range(4):
-            active = tab[3 + face : 4 + face, :]
-            local = row_of(idx, LOCAL + 2 * face)
-            for a in range(6):
-                n, m = face_nodes(face)[a], face_nodes(face ^ 1)[a]
-                jump = active * (v_ref[n, rows, :] - take(v_ref[m, rows, :], local))
-                out[n, rows, :] += float(PENALTY * W[a]) * jump
-
-    @pl.when(meta[2] != 0)
-    def _():
-        for face in range(4):
-            mine = [v_ref[n, rows, :] for n in face_nodes(face)]
-            theirs = [
-                [take(v_ref[n, rows, :], row_of(idx, LOCAL + 2 * face + t)) for n in face_nodes(face ^ 1)]
-                for t in range(2)
-            ]
-            for a in range(6):
-                n = face_nodes(face)[a]
-                extra = out[n, rows, :]
-                for b in range(6):
-                    extra = extra + own_c[6 * a + b, 2 * face : 2 * face + 1, :] * mine[b]
-                    for t in range(2):
-                        s = 2 * face + t
-                        extra = extra + far_c[6 * a + b, s : s + 1, :] * theirs[t][b]
-                out[n, rows, :] = extra
+    cx, cy = row_of(tab, 0), row_of(tab, 1)
+    shift = 1.0 + 0.5 * tab[2:3, :] * (harmonic * harmonic)
+    plus, minus = STIFF_FOLD
+    even = [[v(6 * a + j) + v(30 - 6 * a + j) for a in range(3)] for j in range(6)]
+    odd = [[v(6 * a + j) - v(30 - 6 * a + j) for a in range(3)] for j in range(6)]
+    for i in range(3):
+        e = [weighted(plus[i], even[j]) for j in range(6)]
+        o = [weighted(minus[i], odd[j]) for j in range(6)]
+        for line in (i, 5 - i):
+            mine = [v(6 * line + j) for j in range(6)]
+            g = folded(mine, STIFF_FOLD, 1)
+            for j in range(6):
+                n = 6 * line + j
+                gx = e[j] + o[j] if line == i else e[j] - o[j]
+                value = float(W[line] * W[j]) * (shift * mine[j] + cx * gx + cy * g[j])
+                for face, (at, b) in enumerate(((line == 0, j), (line == 5, j), (j == 0, line), (j == 5, line))):
+                    if at:
+                        value = value + terms[face](b)
+                emit(n, value)
 
 
 def compact(group, idx, v_ref, h_ref, send_w, send_e):
@@ -342,14 +379,13 @@
     near = [[take(t, row_of(edge_idx, row + k)) for t in theirs] for k in range(2)]
     out = []
     for a in range(6):
-        total = None
+        chains = [None] * 3
         for b in range(6):
             n = 6 * a + b
-            term = edge_own[n, row : row + 1, :] * mine[b]
-            for k in range(2):
-                term = term + edge_far[n, row + k : row + k + 1, :] * near[k][b]
-            total = term if total is None else total + term
-        out.append(total)
+            terms = [edge_own[n, row : row + 1, :] * mine[b]]
+            terms += [edge_far[n, row + k : row + k + 1, :] * near[k][b] for k in range(2)]
+            chains = terms if chains[0] is None else [c + t for c, t in zip(chains, terms)]
+        out.append(chains[0] + (chains[1] + chains[2]))
     return out
 
 
@@ -370,15 +406,21 @@
 HALF = 10.0
 
 
+def store(ref, rows):
+    def emit(n, value):
+        ref[n, rows, :] = value
+
+    return emit
+
+
 def guess_kernel(meta, idx, tab, own_c, far_c, u, out, send_w, send_e):
     env = (meta, idx, tab, own_c, far_c)
 
-    def body(group, carry):
-        inner(group, env, u, out)
+    def loop(group, plain):
+        inner(group, env, u, plain, store(out, group_rows(group)))
         compact(group, idx, u, out, send_w, send_e)
-        return carry
-
-    lax.fori_loop(0, 4, body, 0)
+
+    either(meta, loop)
 
 
 def base_kernel(idx, edge_idx, edge_own, edge_far, u, hu, to_w, to_e, from_w, from_e, out, edge):
@@ -408,12 +450,11 @@
             n = 4 * g + m
             out[n] = base[n] + turned[32 * m : 32 * m + 32]
 
-    def body(group, carry):
-        inner(group, env, out, h_out)
+    def loop(group, plain):
+        inner(group, env, out, plain, store(h_out, group_rows(group)))
         compact(group, idx, out, h_out, send_w, send_e)
-        return carry
-
-    lax.fori_loop(0, 4, body, 0)
+
+    either(meta, loop)
 
 
 def edge_steps(tables, to_w, to_e, from_w, from_e, before, edge, keep):
@@ -444,13 +485,13 @@
 def two_steps_kernel(
     meta, idx, tab, own_c, far_c, edge_idx, edge_own, edge_far,
     t0, h0, to_w, to_e, from_w, from_e,
-    t1, t2, h2, send_w, send_e, keep, part, edge, h1, acc, pad,
+    t1, t2, h2, send_w, send_e, keep, part, edge, acc, pad,
 ):
     env = (meta, idx, tab, own_c, far_c)
     tables = (edge_idx, edge_own, edge_far)
     edge_steps(tables, to_w, to_e, from_w, from_e, None, edge, keep)
 
-    def body(group, carry):
+    def loop(group, plain):
         rows = group_rows(group)
         extra = outer(group, idx, edge, 0)
         sums = [jnp.zeros((8, 128), F32)] * 5
@@ -463,24 +504,24 @@
             t1[n, rows, :] = b
             for k, term in enumerate((a * a, a * b, b * b)):
                 sums[k] = sums[k] + term
-        inner(group, env, t1, h1)
-        extra = outer(group, idx, edge, 48)
-        for n in range(36):
-            image = h1[n, rows, :]
-            if n in extra:
-                image = image + extra[n]
+        extra_next = outer(group, idx, edge, 48)
+
+        def emit(n, image):
+            if n in extra_next:
+                image = image + extra_next[n]
             b = t1[n, rows, :]
             c = (2.0 / HALF) * image - 2.0 * b - t0[n, rows, :]
             t2[n, rows, :] = c
             sums[3] = sums[3] + b * c
             sums[4] = sums[4] + c * c
+
+        inner(group, env, t1, plain, emit)
         for k in range(5):
             acc[rows, 128 * k : 128 * k + 128] = sums[k]
-        inner(group, env, t2, h2)
+        inner(group, env, t2, plain, store(h2, rows))
         compact(group, idx, t2, h2, send_w, send_e)
-        return carry
-
-    lax.fori_loop(0, 4, body, 0)
+
+    either(meta, loop)
     store_sums(acc, pad, 0, 5)
     part[...] = pad[...]
 
@@ -488,13 +529,13 @@
 def last_steps_kernel(
     meta, idx, tab, own_c, far_c, edge_idx, edge_own, edge_far,
     t1, t2, h2, to_w, to_e, from_w, from_e, keep, part,
-    t3, red, edge, h3, acc, pad,
+    t3, red, edge, acc, pad,
 ):
     env = (meta, idx, tab, own_c, far_c)
     tables = (edge_idx, edge_own, edge_far)
     edge_steps(tables, to_w, to_e, from_w, from_e, keep, edge, None)
 
-    def body(group, carry):
+    def loop(group, plain):
         rows = group_rows(group)
         extra = outer(group, idx, edge, 0)
         sums = [jnp.zeros((8, 128), F32)] * 3
@@ -507,19 +548,19 @@
             t3[n, rows, :] = d
             sums[0] = sums[0] + c * d
             sums[1] = sums[1] + d * d
-        inner(group, env, t3, h3)
-        extra = outer(group, idx, edge, 48)
-        for n in range(36):
-            image = h3[n, rows, :]
-            if n in extra:
-                image = image + extra[n]
+        extra_next = outer(group, idx, edge, 48)
+
+        def emit(n, image):
+            if n in extra_next:
+                image = image + extra_next[n]
             d = t3[n, rows, :]
             sums[2] = sums[2] + d * ((2.0 / HALF) * image - 2.0 * d - t2[n, rows, :])
+
+        inner(group, env, t3, plain, emit)
         for k in range(3):
             acc[rows, 128 * k : 128 * k + 128] = sums[k]
-        return carry
-
-    lax.fori_loop(0, 4, body, 0)
+
+    either(meta, loop)
     store_sums(acc, pad, 5, 3)
     row = lax.broadcasted_iota(jnp.int32, (8, 128), 0)
     mixed = jnp.where(row < 5, part[...], pad[...])
@@ -527,7 +568,7 @@
         red[k] = mixed
 
 
-def finish_kernel(red, x0, t0, t1, t2, t3, out, coef):
+def finish_kernel(red, x0, t0, t1, t2, t3, out, coef, held, sems):
     total = red[0]
     for k in range(1, 16):
         total = total + red[k]
@@ -568,13 +609,26 @@
     turned = jnp.concatenate(weight + [jnp.zeros((4, 128), F32)], axis=0).T
     for k in range(4):
         coef[k] = jnp.broadcast_to(turned[0:32, k : k + 1], (32, 128))
-    for n in range(36):
-        out[n] = x0[n] + coef[0] * t0[n] + coef[1] * t1[n] + coef[2] * t2[n] + coef[3] * t3[n]
-
-
-def pack_kernel(u, out):
+    copies = []
+    for c in range(6):
+        for n in range(6 * c, 6 * c + 6):
+            held[n] = x0[n] + coef[0] * t0[n] + coef[1] * t1[n] + coef[2] * t2[n] + coef[3] * t3[n]
+        part = pl.ds(6 * c, 6)
+        copies.append(pltpu.make_async_copy(held.at[part], out.at[part], sems.at[c]))
+        copies[c].start()
+    for copy in copies:
+        copy.wait()
+
+
+def pack_kernel(u, out, held, sems):
+    copies = []
     for g in range(9):
-        turned = u[4 * g : 4 * g + 4].reshape(128, 128).T
+        part = pl.ds(4 * g, 4)
+        copies.append(pltpu.make_async_copy(u.at[part], held.at[part], sems.at[g]))
+        copies[g].start()
+    for g in range(9):
+        copies[g].wait()
+        turned = held[4 * g : 4 * g + 4].reshape(128, 128).T
         out[:, 16 * g : 16 * g + 16, :] = turned.reshape(8, 16, 128)
 
 
@@ -662,7 +716,13 @@
     vol, edge = shape(36, 32, 128), shape(48, 128)
     both = shape(96, 128)
     blocks = shape(8, 144, 128)
-    packed = call(pack_kernel, [blocks], [], [u], [VMEM])[0]
+    packed = call(
+        pack_kernel,
+        [blocks],
+        [VMEM((36, 32, 128), F32), pltpu.SemaphoreType.DMA((9,))],
+        [u],
+        [pl.ANY],
+    )[0]
     came = lax.all_to_all(packed, "plane", 0, 0, tiled=True)
 
     table = shape(36, 8, 128)
@@ -676,8 +736,9 @@
     head = [meta, idx, tab, own_c, far_c]
     edges = [edge_idx, edge_own, edge_far]
 
-    def run(kernel, outs, scratch, args):
-        return call(kernel, outs, scratch, args, [SMEM if a is meta else VMEM for a in args])
+    def run(kernel, outs, scratch, args, grant=3):
+        spaces = [SMEM if a is meta else VMEM for a in args]
+        return call(kernel, outs, scratch, args, spaces, grant=grant)
 
     def trade(send_w, send_e):
         return shift_by(send_e, 1), shift_by(send_w, -1)
@@ -690,6 +751,7 @@
         [blocks],
         [VMEM((576, 256), BF16), VMEM((576, 256), BF16), VMEM((576, 256), F32)],
         [meta, came, speed, synth, analy],
+        grant=8,
     )[0]
     back = lax.all_to_all(back, "plane", 0, 0, tiled=True)
     base = run(
@@ -699,7 +761,6 @@
     def work(count):
         return [
             VMEM((96, 128), F32),
-            VMEM((36, 32, 128), F32),
             VMEM((32, 128 * count), F32),
             VMEM((8, 128), F32),
         ]
@@ -720,7 +781,14 @@
         head + edges + [t1, t2, h2, to_w, to_e, *got, keep, part],
     )
     red = lax.all_to_all(red, "elem", 0, 0, tiled=True)
-    out = run(finish_kernel, [vol], [VMEM((4, 32, 128), F32)], [red, u, t0, t1, t2, t3])[0]
+    out = call(
+        finish_kernel,
+        [vol],
+        [VMEM((4, 32, 128), F32), VMEM((36, 32, 128), F32), pltpu.SemaphoreType.DMA((6,))],
+        [red, u, t0, t1, t2, t3],
+        [VMEM] * 6,
+        pl.ANY,
+    )[0]
     return jnp.transpose(out.reshape(6, 6, 32, 128), (2, 0, 1, 3))
 
 

time: 83.4 us -> 82.1 us (0.984)
  Pallas kernels: 17.5 us -> 16.1 us
    pallas_call x9, Pallas kernels: 17.5 us -> 16.1 us  [call(): pl.pallas_call(kernel, out_shape=outs, in_specs=[pl.BlockSpec(memory_spac...]
where the time goes in v3:
time: 82.1 us; the launch traced here: 81.6 us
  starting transfers between devices  23.6 us (29%)
  waiting for transfers between devices  22.2 us (27%)
  Pallas kernels  16.1 us (20%)
  blocking collectives  10.2 us (12%)
  local copies, waits for them, and re-layouts  7.75 us (9%)
  other arithmetic  0.83 us (1%)
    pallas_call x9, Pallas kernels, call(): pl.pallas_call(kernel, out_shape=outs, in_specs=[pl.BlockSpec(memory_spac...  16.1 us
    ppermute x6, starting transfers between devices, shift_by(): lax.ppermute(array, 'elem', [(i, (i + by) % count) for i in range(count)])  14.2 us
    ppermute x6, waiting for transfers between devices, shift_by(): lax.ppermute(array, 'elem', [(i, (i + by) % count) for i in range(count)])  12.9 us
    all_to_all x1, blocking collectives, shards(): red = lax.all_to_all(red, 'elem', 0, 0, tiled=True)  10.2 us
    all_to_all x1, waiting for transfers between devices, shards(): back = lax.all_to_all(back, 'plane', 0, 0, tiled=True)  9.36 us
    unnamed x48, local copies, waits for them, and re-layouts  7.75 us
    all_to_all x1, starting transfers between devices, shards(): back = lax.all_to_all(back, 'plane', 0, 0, tiled=True)  4.87 us
    all_to_all x1, starting transfers between devices, shards(): came = lax.all_to_all(packed, 'plane', 0, 0, tiled=True)  4.53 us
  transfers between devices with their start and end apart: 8, of which 6 were waited for; matrix products, arithmetic and copies ran while one was open for 1% of the time, Pallas kernels for 4%

profile of v3, /device:TPU:0, one launch (start us, length us, event | category | flops | bytes accessed | tf_op | source)
XLA Modules:
  0.0 81.6 jit_solution(2934591934075388570)
XLA Ops:
  0.0 1.1 %copy-done = f32[32,6,6,128]{3,0,2,1:T(8,128)S(1)} copy-done((f32[32,6,6,128]{3,0,2,1:T(8,128)S(1)}, f32[32,6,6,128]{3,0,2,1:T(8,128)}, u32[]{:S(2)}) %copy-start) | copy-done | bytes 589848
  1.1 2.6 %shard_map.83 = f32[8,144,128]{2,1,0:T(8,128)} custom-call(f32[36,32,128]{2,1,0:T(8,128)S(1)} %bitcast.29), custom_call_target="tpu_custom_call" | custom-call | flops 4000000 | bytes 1179648 | tf_op jit(solution)/shard_map/pallas_call | solution.py:109
  3.7 4.5 %all-to-all-start = ((f32[8,144,128]{2,1,0:T(8,128)}), f32[8,144,128]{2,1,0:T(8,128)S(1)}, u32[]{:S(2)}, u32[]{:S(2)}) async-start(f32[8,144,128]{2,1,0:T(8,128)} %shard_map.83), calls=%async_computation | async-start | bytes 1179648 | tf_op jit(solution)/shard_map/all_to_all | solution.py:726
  9.7 1.2 %shard_map.82 = (s32[24,128]{1,0:T(8,128)S(1)}, s32[8,128]{1,0:T(8,128)S(1)}, f32[8,128]{1,0:T(8,128)S(1)}, f32[36,8,128]{2,1,0:T(8,128)S(1)}, f32[36,8,128]{2,1...) custom-call(s32[4]{0:T(128)S(1)} %pad_add_fusion.meta, s32[8,128]{1,0:T(8,128)S(1)} %copy-done.21, ...), custom_call_target="tpu_custom_call" | custom-call | flops 4000000 | bytes 623632 | tf_op jit(solution)/shard_map/pallas_call | solution.py:109
  11.5 1.3 %shard_map.84 = (f32[36,32,128]{2,1,0:T(8,128)S(1)}, f32[48,128]{1,0:T(8,128)S(1)}, f32[48,128]{1,0:T(8,128)S(1)}) custom-call(s32[4]{0:T(128)S(1)} %pad_add_fusion.meta, s32[24,128]{1,0:T(8,128)S(1)} %get-tuple-element.31.idx, f32[8,128]{1,0:T(8,128)S(1)} %get-tuple-element.32.tab, f32[36,8,128]{2,1,0:T(8,128)S(1)} %get-tuple-element.33.own_c, ...), custom_call_target="tpu_custom_call" | custom-call | flops 4000000 | bytes 1540112 | tf_op jit(solution)/shard_map/pallas_call | solution.py:109
  12.8 1.6 %collective-permute-start = (f32[48,128]{1,0:T(8,128)S(1)}, f32[48,128]{1,0:T(8,128)S(1)}, u32[]{:S(2)}, u32[]{:S(2)}) collective-permute-start(f32[48,128]{1,0:T(8,128)S(1)} %get-tuple-element.38.to_e), channel_id=1, source_target_pairs={{0,1},{1,2},{2,3},{3,4},{4,5},{5,6},{6,7},{7,8},{8,9},{9,10},{10,1... | collective-permute-start | bytes 73736 | tf_op jit(solution)/shard_map/ppermute | solution.py:700
  15.0 5.0 %collective-permute-start.1 = (f32[48,128]{1,0:T(8,128)S(1)}, f32[48,128]{1,0:T(8,128)S(1)}, u32[]{:S(2)}, u32[]{:S(2)}) collective-permute-start(f32[48,128]{1,0:T(8,128)S(1)} %get-tuple-element.39.to_w), channel_id=1, source_target_pairs={{0,15},{1,0},{2,1},{3,2},{4,3},{5,4},{6,5},{7,6},{8,7},{9,8},{10,9... | collective-permute-start | bytes 73736 | tf_op jit(solution)/shard_map/ppermute | solution.py:700
  22.5 0.9 %copy-done.5 = bf16[2,256,256]{2,1,0:T(8,128)(2,1)S(1)} copy-done((bf16[2,256,256]{2,1,0:T(8,128)(2,1)S(1)}, bf16[2,256,256]{2,1,0:T(8,128)(2,1)}, u32[]{:S(2)}) %copy-start.5) | copy-done | bytes 262168
  23.4 0.9 %copy-done.6 = bf16[2,256,256]{2,1,0:T(8,128)(2,1)S(1)} copy-done((bf16[2,256,256]{2,1,0:T(8,128)(2,1)S(1)}, bf16[2,256,256]{2,1,0:T(8,128)(2,1)}, u32[]{:S(2)}) %copy-start.6) | copy-done | bytes 262168
  25.0 3.1 %shard_map.85 = f32[8,144,128]{2,1,0:T(8,128)} custom-call(s32[4]{0:T(128)S(1)} %copy-done.18, f32[8,144,128]{2,1,0:T(8,128)S(1)} %all-to-all-done.came, f32[2,36,16,256]{3,2,1,0:T(8,128)S(1)} %bitcast.33, bf16[2,256,256]{2,1,0:T(8,128)(2,1)S(1)} %copy-done.6, bf16[2,256,256]{2,1,0:T(8,128)(2,1)S(1)} %copy-done.5), custom_call_target="tpu_custom_call" | custom-call | flops 4000000 | bytes 3407888 | tf_op jit(solution)/shard_map/pallas_call | solution.py:109
  28.2 4.9 %all-to-all-start.1 = ((f32[8,144,128]{2,1,0:T(8,128)}), f32[8,144,128]{2,1,0:T(8,128)S(1)}, u32[]{:S(2)}, u32[]{:S(2)}) async-start(f32[8,144,128]{2,1,0:T(8,128)} %shard_map.85), calls=%async_computation.1 | async-start | bytes 1179648 | tf_op jit(solution)/shard_map/all_to_all | solution.py:756
  33.1 1.1 %copy-done.4 = f32[36,32,128]{2,1,0:T(8,128)S(1)} copy-done((f32[36,32,128]{2,1,0:T(8,128)S(1)}, f32[36,32,128]{2,1,0:T(8,128)}, u32[]{:S(2)}) %copy-start.4) | copy-done | bytes 589848
  34.7 9.4 %all-to-all-done.1.back = f32[8,144,128]{2,1,0:T(8,128)S(1)} async-done(((f32[8,144,128]{2,1,0:T(8,128)}), f32[8,144,128]{2,1,0:T(8,128)S(1)}, u32[]{:S(2)}, u32[]{:S(2)}) %all-to-all-start.1) | async-done | bytes 589856 | tf_op jit(solution)/shard_map/all_to_all | solution.py:756
  44.1 1.5 %shard_map.87 = (f32[36,32,128]{2,1,0:T(8,128)S(1)}, f32[36,32,128]{2,1,0:T(8,128)S(1)}, f32[48,128]{1,0:T(8,128)S(1)}, f32[48,128]{1,0:T(8,128)S(1)}) custom-call(s32[4]{0:T(128)S(1)} %copy-done.19, s32[24,128]{1,0:T(8,128)S(1)} %get-tuple-element.31.idx, f32[8,128]{1,0:T(8,128)S(1)} %get-tuple-element.32.tab, f32[36,8,128]{2,1,0:T(8,128)S(1)} %get-tuple-element.33.own_c, ...), custom_call_target="tpu_custom_call" | custom-call | flops 4000000 | bytes 2719760 | tf_op jit(solution)/shard_map/pallas_call | solution.py:109
  45.6 5.5 %collective-permute-start.3 = (f32[48,128]{1,0:T(8,128)S(1)}, f32[48,128]{1,0:T(8,128)S(1)}, u32[]{:S(2)}, u32[]{:S(2)}) collective-permute-start(f32[48,128]{1,0:T(8,128)S(1)} %get-tuple-element.46.to_w), channel_id=1, source_target_pairs={{0,15},{1,0},{2,1},{3,2},{4,3},{5,4},{6,5},{7,6},{8,7},{9,8},{10,9... | collective-permute-start | bytes 73736 | tf_op jit(solution)/shard_map/ppermute | solution.py:700
  51.2 1.5 %collective-permute-done.3.from_e = f32[48,128]{1,0:T(8,128)S(1)} collective-permute-done((f32[48,128]{1,0:T(8,128)S(1)}, f32[48,128]{1,0:T(8,128)S(1)}, u32[]{:S(2)}, u32[]{:S(2)}) %collective-permute-start.3) | collective-permute-done | bytes 24608 | tf_op jit(solution)/shard_map/ppermute | solution.py:700
  52.7 5.6 %collective-permute-done.2.from_w = f32[48,128]{1,0:T(8,128)S(1)} collective-permute-done((f32[48,128]{1,0:T(8,128)S(1)}, f32[48,128]{1,0:T(8,128)S(1)}, u32[]{:S(2)}, u32[]{:S(2)}) %collective-permute-start.2) | collective-permute-done | bytes 24608 | tf_op jit(solution)/shard_map/ppermute | solution.py:700
  58.3 2.6 %shard_map.88 = (f32[36,32,128]{2,1,0:T(8,128)S(1)}, f32[36,32,128]{2,1,0:T(8,128)S(1)}, f32[36,32,128]{2,1,0:T(8,128)S(1)}, f32[48,128]{1,0:T(8,128)S(1)}, f32[...) custom-call(s32[4]{0:T(128)S(1)} %copy-done.19, s32[24,128]{1,0:T(8,128)S(1)} %get-tuple-element.31.idx, ...), custom_call_target="tpu_custom_call" | custom-call | flops 4000000 | bytes 3760144 | tf_op jit(solution)/shard_map/pallas_call | solution.py:109
  60.9 2.0 %collective-permute-start.4 = (f32[48,128]{1,0:T(8,128)S(1)}, f32[48,128]{1,0:T(8,128)S(1)}, u32[]{:S(2)}, u32[]{:S(2)}) collective-permute-start(f32[48,128]{1,0:T(8,128)S(1)} %get-tuple-element.52.to_e), channel_id=1, source_target_pairs={{0,1},{1,2},{2,3},{3,4},{4,5},{5,6},{6,7},{7,8},{8,9},{9,10},{10,1... | collective-permute-start | bytes 73736 | tf_op jit(solution)/shard_map/ppermute | solution.py:700
  62.9 1.8 %collective-permute-done.5.from_e = f32[48,128]{1,0:T(8,128)S(1)} collective-permute-done((f32[48,128]{1,0:T(8,128)S(1)}, f32[48,128]{1,0:T(8,128)S(1)}, u32[]{:S(2)}, u32[]{:S(2)}) %collective-permute-start.5) | collective-permute-done | bytes 24608 | tf_op jit(solution)/shard_map/ppermute | solution.py:700
  64.7 3.4 %collective-permute-done.4.from_w = f32[48,128]{1,0:T(8,128)S(1)} collective-permute-done((f32[48,128]{1,0:T(8,128)S(1)}, f32[48,128]{1,0:T(8,128)S(1)}, u32[]{:S(2)}, u32[]{:S(2)}) %collective-permute-start.4) | collective-permute-done | bytes 24608 | tf_op jit(solution)/shard_map/ppermute | solution.py:700
  68.1 2.0 %shard_map.89 = (f32[36,32,128]{2,1,0:T(8,128)S(1)}, f32[16,8,128]{2,1,0:T(8,128)S(1)}) custom-call(s32[4]{0:T(128)S(1)} %copy-done.19, s32[24,128]{1,0:T(8,128)S(1)} %get-tuple-element.31.idx, f32[8,128]{1,0:T(8,128)S(1)} %get-tuple-element.32.tab, f32[36,8,128]{2,1,0:T(8,128)S(1)} %get-tuple-element.33.own_c, f32[36,8,128]{2,1,0:T(8,128)S(1)} %get-tuple-element.34.far_c, ...), custom_call_target="tpu_custom_call" | custom-call | flops 4000000 | bytes 3186704 | tf_op jit(solution)/shard_map/pallas_call | solution.py:109
  70.1 10.2 %all_to_all.15.red = f32[16,8,128]{2,1,0:T(8,128)S(1)} all-to-all(f32[16,8,128]{2,1,0:T(8,128)S(1)} %get-tuple-element.55), channel_id=1, replica_groups=mesh['plane'=8,'elem'=16] {'elem'}, dimensions={0} | all-to-all | bytes 131072 | tf_op jit(solution)/shard_map/all_to_all | solution.py:783
  80.3 1.3 %shard_map.90 = f32[36,32,128]{2,1,0:T(8,128)} custom-call(f32[16,8,128]{2,1,0:T(8,128)S(1)} %all_to_all.15.red, f32[36,32,128]{2,1,0:T(8,128)S(1)} %bitcast.32, f32[36,32,128]{2,1,0:T(8,128)S(1)} %get-tuple-element.44.t0, f32[36,32,128]{2,1,0:T(8,128)S(1)} %get-tuple-element.48.t1, f32[36,32,128]{2,1,0:T(8,128)S(1)} %get-tuple-element.49.t2, ...), custom_call_target="tpu_custom_call" | custom-call | flops 4000000 | bytes 3604480 | tf_op jit(solution)/shard_map/pallas_call | solution.py:109
  (53 shorter events, 5.7 us)
Async XLA Ops:
  0.0 1.1 %copy-start = (f32[32,6,6,128]{3,0,2,1:T(8,128)S(1)}, f32[32,6,6,128]{3,0,2,1:T(8,128)}, u32[]{:S(2)}) copy-start(f32[32,6,6,128]{3,0,2,1:T(8,128)} %param.8) | copy-start | bytes 1769476
  1.1 7.1 %copy-start.20 = (s32[2,8,128]{2,1,0:T(8,128)S(1)}, s32[2,8,128]{2,1,0:T(8,128)}, u32[]{:S(2)}) copy-start(s32[2,8,128]{2,1,0:T(8,128)} %sides.1) | copy-start | bytes 24580
  1.1 7.2 %copy-start.21 = (s32[8,128]{1,0:T(8,128)S(1)}, s32[8,128]{1,0:T(8,128)}, u32[]{:S(2)}) copy-start(s32[8,128]{1,0:T(8,128)} %links.1) | copy-start | bytes 12292
  1.1 8.5 %copy-start.22 = (s32[128]{0:T(128)S(1)}, s32[128]{0:T(128)}, u32[]{:S(2)}) copy-start(s32[128]{0:T(128)} %param.13) | copy-start | bytes 1540
  1.1 8.6 %copy-start.23 = (f32[128]{0:T(128)S(1)}, f32[128]{0:T(128)}, u32[]{:S(2)}) copy-start(f32[128]{0:T(128)} %param.10) | copy-start | bytes 1540
  1.1 10.4 %copy-start.1 = (f32[32,6,6,128]{3,0,2,1:T(8,128)S(1)}, f32[32,6,6,128]{3,0,2,1:T(8,128)}, u32[]{:S(2)}) copy-start(f32[32,6,6,128]{3,0,2,1:T(8,128)} %param.8) | copy-start | bytes 1769476
  3.7 18.8 %copy-start.2 = (f32[2,256,6,6,16]{1,4,3,2,0:T(8,128)S(1)}, f32[2,256,6,6,16]{1,4,3,2,0:T(8,128)}, u32[]{:S(2)}) copy-start(f32[2,256,6,6,16]{1,4,3,2,0:T(8,128)} %param.9) | copy-start | bytes 3538948
  3.7 18.8 %all-to-all-start = ((f32[8,144,128]{2,1,0:T(8,128)}), f32[8,144,128]{2,1,0:T(8,128)S(1)}, u32[]{:S(2)}, u32[]{:S(2)}) async-start(f32[8,144,128]{2,1,0:T(8,128)} %shard_map.83), calls=%async_computation | async-start | bytes 1179648 | tf_op jit(solution)/shard_map/all_to_all | solution.py:726
  9.7 11.5 %copy-start.17 = (s32[4]{0:T(128)}, s32[4]{0:T(128)S(1)}, u32[]{:S(2)}) copy-start(s32[4]{0:T(128)S(1)} %pad_add_fusion.meta) | copy-start | bytes 52
  12.8 15.4 %copy-start.3 = (f32[36,32,128]{2,1,0:T(8,128)}, f32[36,32,128]{2,1,0:T(8,128)S(1)}, u32[]{:S(2)}) copy-start(f32[36,32,128]{2,1,0:T(8,128)S(1)} %get-tuple-element.41.hu) | copy-start | bytes 1769476
  12.8 8.4 %collective-permute-start = (f32[48,128]{1,0:T(8,128)S(1)}, f32[48,128]{1,0:T(8,128)S(1)}, u32[]{:S(2)}, u32[]{:S(2)}) collective-permute-start(f32[48,128]{1,0:T(8,128)S(1)} %get-tuple-element.38.to_e), channel_id=1, source_target_pairs={{0,1},{1,2},{2,3},{3,4},{4,5},{5,6},{6,7},{7,8},{8,9},{9,10},{10,1... | collective-permute-start | bytes 73736 | tf_op jit(solution)/shard_map/ppermute | solution.py:700
  15.0 6.8 %collective-permute-start.1 = (f32[48,128]{1,0:T(8,128)S(1)}, f32[48,128]{1,0:T(8,128)S(1)}, u32[]{:S(2)}, u32[]{:S(2)}) collective-permute-start(f32[48,128]{1,0:T(8,128)S(1)} %get-tuple-element.39.to_w), channel_id=1, source_target_pairs={{0,15},{1,0},{2,1},{3,2},{4,3},{5,4},{6,5},{7,6},{8,7},{9,8},{10,9... | collective-permute-start | bytes 73736 | tf_op jit(solution)/shard_map/ppermute | solution.py:700
  28.1 4.9 %copy-start.8 = (s32[8,128]{1,0:T(8,128)S(1)}, s32[8,128]{1,0:T(8,128)}, u32[]{:S(2)}) copy-start(s32[8,128]{1,0:T(8,128)} %copy-done.7) | copy-start | bytes 12292
  28.1 4.9 %copy-start.10 = (f32[48,128]{1,0:T(8,128)S(1)}, f32[48,128]{1,0:T(8,128)}, u32[]{:S(2)}) copy-start(f32[48,128]{1,0:T(8,128)} %copy-done.9) | copy-start | bytes 73732
  28.1 4.9 %copy-start.12 = (f32[48,128]{1,0:T(8,128)S(1)}, f32[48,128]{1,0:T(8,128)}, u32[]{:S(2)}) copy-start(f32[48,128]{1,0:T(8,128)} %copy-done.11) | copy-start | bytes 73732
  28.1 4.9 %copy-start.14 = (f32[48,128]{1,0:T(8,128)S(1)}, f32[48,128]{1,0:T(8,128)}, u32[]{:S(2)}) copy-start(f32[48,128]{1,0:T(8,128)} %copy-done.13) | copy-start | bytes 73732
  28.2 4.9 %copy-start.16 = (f32[48,128]{1,0:T(8,128)S(1)}, f32[48,128]{1,0:T(8,128)}, u32[]{:S(2)}) copy-start(f32[48,128]{1,0:T(8,128)} %copy-done.15) | copy-start | bytes 73732
  28.2 15.9 %all-to-all-start.1 = ((f32[8,144,128]{2,1,0:T(8,128)}), f32[8,144,128]{2,1,0:T(8,128)S(1)}, u32[]{:S(2)}, u32[]{:S(2)}) async-start(f32[8,144,128]{2,1,0:T(8,128)} %shard_map.85), calls=%async_computation.1 | async-start | bytes 1179648 | tf_op jit(solution)/shard_map/all_to_all | solution.py:756
  33.0 11.1 %copy-start.19 = (s32[4]{0:T(128)S(1)}, s32[4]{0:T(128)}, u32[]{:S(2)}) copy-start(s32[4]{0:T(128)} %copy-done.17) | copy-start | bytes 52
  33.1 1.1 %copy-start.4 = (f32[36,32,128]{2,1,0:T(8,128)S(1)}, f32[36,32,128]{2,1,0:T(8,128)}, u32[]{:S(2)}) copy-start(f32[36,32,128]{2,1,0:T(8,128)} %copy-done.3) | copy-start | bytes 1769476
  45.6 7.0 %collective-permute-start.3 = (f32[48,128]{1,0:T(8,128)S(1)}, f32[48,128]{1,0:T(8,128)S(1)}, u32[]{:S(2)}, u32[]{:S(2)}) collective-permute-start(f32[48,128]{1,0:T(8,128)S(1)} %get-tuple-element.46.to_w), channel_id=1, source_target_pairs={{0,15},{1,0},{2,1},{3,2},{4,3},{5,4},{6,5},{7,6},{8,7},{9,8},{10,9... | collective-permute-start | bytes 73736 | tf_op jit(solution)/shard_map/ppermute | solution.py:700
  51.1 7.1 %collective-permute-start.2 = (f32[48,128]{1,0:T(8,128)S(1)}, f32[48,128]{1,0:T(8,128)S(1)}, u32[]{:S(2)}, u32[]{:S(2)}) collective-permute-start(f32[48,128]{1,0:T(8,128)S(1)} %get-tuple-element.47.to_e), channel_id=1, source_target_pairs={{0,1},{1,2},{2,3},{3,4},{4,5},{5,6},{6,7},{7,8},{8,9},{9,10},{10,1... | collective-permute-start | bytes 73736 | tf_op jit(solution)/shard_map/ppermute | solution.py:700
  60.9 3.8 %collective-permute-start.5 = (f32[48,128]{1,0:T(8,128)S(1)}, f32[48,128]{1,0:T(8,128)S(1)}, u32[]{:S(2)}, u32[]{:S(2)}) collective-permute-start(f32[48,128]{1,0:T(8,128)S(1)} %get-tuple-element.51.to_w), channel_id=1, source_target_pairs={{0,15},{1,0},{2,1},{3,2},{4,3},{5,4},{6,5},{7,6},{8,7},{9,8},{10,9... | collective-permute-start | bytes 73736 | tf_op jit(solution)/shard_map/ppermute | solution.py:700
  60.9 7.2 %collective-permute-start.4 = (f32[48,128]{1,0:T(8,128)S(1)}, f32[48,128]{1,0:T(8,128)S(1)}, u32[]{:S(2)}, u32[]{:S(2)}) collective-permute-start(f32[48,128]{1,0:T(8,128)S(1)} %get-tuple-element.52.to_e), channel_id=1, source_target_pairs={{0,1},{1,2},{2,3},{3,4},{4,5},{5,6},{6,7},{7,8},{8,9},{9,10},{10,1... | collective-permute-start | bytes 73736 | tf_op jit(solution)/shard_map/ppermute | solution.py:700
  (8 other events, 5.6 us)

commit v4 on v3

--- a/solution.py
+++ b/solution.py
@@ -15,6 +15,7 @@
 SPANWISE = 0.0625
 VMEM = pltpu.VMEM
 SMEM = pltpu.SMEM
+HBM = pltpu.HBM
 SELF, ANY, LOCAL = 2, 4, 10
 
 
@@ -103,18 +104,22 @@
     return lax.broadcasted_iota(jnp.int32, shape, len(shape) - 1)
 
 
-def call(kernel, outs, scratch, operands, spaces, out_space=VMEM, grant=3):
+def call(kernel, outs, scratch, operands, spaces, out_spaces=None, grant=3):
     total = sum(int(np.prod(o.shape)) * 4 for o in outs)
     total += sum(int(np.prod(o.shape)) * 4 for o in operands)
     return pl.pallas_call(
         kernel,
         out_shape=outs,
         in_specs=[pl.BlockSpec(memory_space=s) for s in spaces],
-        out_specs=[pl.BlockSpec(memory_space=out_space) for _ in outs],
+        out_specs=[pl.BlockSpec(memory_space=s) for s in out_spaces or [VMEM] * len(outs)],
         scratch_shapes=scratch,
         compiler_params=pltpu.CompilerParams(vmem_limit_bytes=grant * 2**20),
         cost_estimate=pl.CostEstimate(flops=4_000_000, bytes_accessed=total, transcendentals=0),
-    )(*operands)
+    )(*[far(a) if s == HBM else a for a, s in zip(operands, spaces)])
+
+
+def far(array):
+    return pltpu.with_memory_space_constraint(array, HBM)
 
 
 def shape(*dims, dtype=F32):
@@ -130,17 +135,27 @@
     return take(*wide)[0:1]
 
 
-def prep_kernel(meta, links, sides, visc, layout, idx, edge_idx, tab, own_c, far_c, edge_own, edge_far):
-    me = meta[1]
+def prep_kernel(
+    place, links, sides, visc, layout, meta, idx, edge_idx, tab, own_c, far_c, edge_own, edge_far
+):
+    me = place[1]
     dev = lax.shift_right_logical(links[...], 7)
     loc = jnp.bitwise_and(links[...], 127)
     remote = (dev != me).astype(jnp.int32)
     idx[LOCAL : LOCAL + 8, :] = loc
+    own, other = sides[0], sides[1]
+    inside = jnp.where(remote > 0, 3, own)
+    whole = (inside == 0) & (other == 0)
+    second = jnp.bitwise_and(lax.broadcasted_iota(jnp.int32, (8, 128), 0), 1) == 1
+    odd_one = jnp.where(inside == 3, 0.0, jnp.where(whole & ~second, 0.0, 1.0))
+    meta[0] = place[0]
+    meta[1] = place[1]
+    meta[2] = jnp.max(odd_one).astype(jnp.int32)
+    meta[3] = jnp.max(layout[...].astype(F32)).astype(jnp.int32)
     row = lax.broadcasted_iota(jnp.int32, (128, 128), 0)
     col = lane_ids((128, 128))
     lane = lane_ids((1, 128))
     slot = jnp.bitwise_and(lane, 15)
-    own, other = sides[0], sides[1]
     listed, present, ranks = [], [], []
     for side in range(2):
         rem = [remote[2 * side + t : 2 * side + t + 1] for t in range(2)]
@@ -211,10 +226,8 @@
     tab[0:1, :] = nu * jnp.where(wide, 2.0, 0.5)
     tab[1:2, :] = nu * jnp.where(wide, 0.5, 2.0)
     tab[2:3, :] = nu
-    inside = jnp.where(remote > 0, 3, own)
     for face in range(4):
-        plain = (inside[2 * face : 2 * face + 1] == 0) & (other[2 * face : 2 * face + 1] == 0)
-        tab[3 + face : 4 + face, :] = plain.astype(F32)
+        tab[3 + face : 4 + face, :] = whole[2 * face : 2 * face + 1].astype(F32)
     tab[7:8, :] = jnp.zeros((1, 128), F32)
     mine_m = [PENALTY * HALVES[o].T @ np.diag(W) @ HALVES[o] for o in range(3)]
     far_m = [
@@ -620,7 +633,7 @@
         copy.wait()
 
 
-def pack_kernel(u, out, held, sems):
+def pack_kernel(u, out, held, ready, sems):
     copies = []
     for g in range(9):
         part = pl.ds(4 * g, 4)
@@ -629,7 +642,12 @@
     for g in range(9):
         copies[g].wait()
         turned = held[4 * g : 4 * g + 4].reshape(128, 128).T
-        out[:, 16 * g : 16 * g + 16, :] = turned.reshape(8, 16, 128)
+        ready[:, 16 * g : 16 * g + 16, :] = turned.reshape(8, 16, 128)
+        part = pl.ds(16 * g, 16)
+        copies[g] = pltpu.make_async_copy(ready.at[:, part], out.at[:, part], sems.at[9 + g])
+        copies[g].start()
+    for copy in copies:
+        copy.wait()
 
 
 def block_turn(blocks):
@@ -651,7 +669,18 @@
     return dot(high, table[0]) + dot(high, table[1]) + dot(low, table[0])
 
 
-def advect_kernel(meta, came, speed, synth, analy, out, high, low, phys):
+def advect_kernel(
+    meta, came, speed_far, synth_far, analy_far, out,
+    high, low, phys, speed, synth, analy, ready, sems,
+):
+    loads = [
+        pltpu.make_async_copy(far, near, sems.at[k])
+        for k, (far, near) in enumerate(
+            ((synth_far, synth), (speed_far, speed), (analy_far, analy))
+        )
+    ]
+    for load in loads:
+        load.start()
     for g in range(9):
         for h in range(2):
             pieces = block_turn([came[4 * h + s, 16 * g : 16 * g + 16, :] for s in range(4)])
@@ -660,9 +689,11 @@
                 hi, lo = split(pieces[m])
                 high[n : n + 16, 128 * h : 128 * h + 128] = hi
                 low[n : n + 16, 128 * h : 128 * h + 128] = lo
-    for i in range(6):
-        part = slice(96 * i, 96 * i + 96)
+    loads[0].wait()
+    for i in range(2):
+        part = slice(288 * i, 288 * i + 288)
         phys[part, :] = product3(high[part, :], low[part, :], synth)
+    loads[1].wait()
     wide = meta[3] == 0
     sx = jnp.where(wide, 2.0, 1.0)
     sy = jnp.where(wide, 1.0, 2.0)
@@ -682,9 +713,11 @@
                 hi, lo = split(float(-0.5 * W[i] * W[j]) * total)
                 high[n : n + 16, cols] = hi
                 low[n : n + 16, cols] = lo
-    for i in range(6):
-        part = slice(96 * i, 96 * i + 96)
+    loads[2].wait()
+    for i in range(2):
+        part = slice(288 * i, 288 * i + 288)
         phys[part, :] = product3(high[part, :], low[part, :], analy)
+    stores = []
     for g in range(9):
         for h in range(2):
             cols = slice(128 * h, 128 * h + 128)
@@ -692,7 +725,12 @@
                 [phys[16 * (4 * g + m) : 16 * (4 * g + m) + 16, cols] for m in range(4)]
             )
             for s in range(4):
-                out[4 * h + s, 16 * g : 16 * g + 16, :] = pieces[s]
+                ready[4 * h + s, 16 * g : 16 * g + 16, :] = pieces[s]
+        part = pl.ds(16 * g, 16)
+        stores.append(pltpu.make_async_copy(ready.at[:, part], out.at[:, part], sems.at[3 + g]))
+        stores[g].start()
+    for store_ in stores:
+        store_.wait()
 
 
 def shift_by(array, by):
@@ -706,12 +744,7 @@
     synth, analy = plane_tables(256)
     synth = jnp.asarray(split_table(synth.T))
     analy = jnp.asarray(split_table(analy.T))
-    plane_id, elem_id = lax.axis_index("plane"), lax.axis_index("elem")
-    own, other = mortar_sides[0], mortar_sides[1]
-    second = jnp.arange(8)[:, None] % 2 == 1
-    plain = (own == 3) | ((own == 0) & (other == 0) & ~second) | (mortar_links // 128 != elem_id)
-    mixed = jnp.any(~plain)
-    meta = jnp.stack([plane_id, elem_id, mixed.astype(jnp.int32), layout[0]]).astype(jnp.int32)
+    place = jnp.stack([lax.axis_index("plane"), lax.axis_index("elem")]).astype(jnp.int32)
 
     vol, edge = shape(36, 32, 128), shape(48, 128)
     both = shape(96, 128)
@@ -719,26 +752,33 @@
     packed = call(
         pack_kernel,
         [blocks],
-        [VMEM((36, 32, 128), F32), pltpu.SemaphoreType.DMA((9,))],
+        [VMEM((36, 32, 128), F32), VMEM((8, 144, 128), F32), pltpu.SemaphoreType.DMA((18,))],
         [u],
-        [pl.ANY],
+        [HBM],
+        [HBM],
     )[0]
     came = lax.all_to_all(packed, "plane", 0, 0, tiled=True)
 
     table = shape(36, 8, 128)
-    idx, edge_idx, tab, own_c, far_c, edge_own, edge_far = call(
+    meta, idx, edge_idx, tab, own_c, far_c, edge_own, edge_far = call(
         prep_kernel,
-        [shape(24, 128, dtype=jnp.int32), shape(8, 128, dtype=jnp.int32), shape(8, 128)] + [table] * 4,
+        [
+            shape(4, dtype=jnp.int32),
+            shape(24, 128, dtype=jnp.int32),
+            shape(8, 128, dtype=jnp.int32),
+            shape(8, 128),
+        ]
+        + [table] * 4,
         [],
-        [meta, mortar_links, mortar_sides, viscosity[None], layout[None]],
+        [place, mortar_links, mortar_sides, viscosity[None], layout[None]],
         [SMEM] + [VMEM] * 4,
+        [SMEM] + [VMEM] * 7,
     )
     head = [meta, idx, tab, own_c, far_c]
     edges = [edge_idx, edge_own, edge_far]
 
-    def run(kernel, outs, scratch, args, grant=3):
-        spaces = [SMEM if a is meta else VMEM for a in args]
-        return call(kernel, outs, scratch, args, spaces, grant=grant)
+    def run(kernel, outs, scratch, args):
+        return call(kernel, outs, scratch, args, [SMEM if a is meta else VMEM for a in args])
 
     def trade(send_w, send_e):
         return shift_by(send_e, 1), shift_by(send_w, -1)
@@ -746,12 +786,23 @@
     hu, *sent = run(guess_kernel, [vol, edge, edge], [], head + [u])
     got = trade(*sent)
     came, *got = lax.optimization_barrier((came, *got))
-    back = run(
+    back = call(
         advect_kernel,
         [blocks],
-        [VMEM((576, 256), BF16), VMEM((576, 256), BF16), VMEM((576, 256), F32)],
+        [
+            VMEM((576, 256), BF16),
+            VMEM((576, 256), BF16),
+            VMEM((576, 256), F32),
+            VMEM((2, 36, 16, 256), F32),
+            VMEM((2, 256, 256), BF16),
+            VMEM((2, 256, 256), BF16),
+            VMEM((8, 144, 128), F32),
+            pltpu.SemaphoreType.DMA((12,)),
+        ],
         [meta, came, speed, synth, analy],
-        grant=8,
+        [SMEM, VMEM, HBM, HBM, HBM],
+        [HBM],
+        grant=12,
     )[0]
     back = lax.all_to_all(back, "plane", 0, 0, tiled=True)
     base = run(
@@ -787,7 +838,7 @@
         [VMEM((4, 32, 128), F32), VMEM((36, 32, 128), F32), pltpu.SemaphoreType.DMA((6,))],
         [red, u, t0, t1, t2, t3],
         [VMEM] * 6,
-        pl.ANY,
+        [HBM],
     )[0]
     return jnp.transpose(out.reshape(6, 6, 32, 128), (2, 0, 1, 3))
 

time: 82.1 us -> 76.8 us (0.935)
  local copies, waits for them, and re-layouts: 7.75 us -> 0.02 us
  waiting for transfers between devices: 22.2 us -> 24.6 us
  Pallas kernels: 16.1 us -> 18.1 us
    unnamed x48 -> x10, local copies, waits for them, and re-layouts: 7.75 us -> 0.02 us
    pallas_call x9, Pallas kernels: 16.1 us -> 18.1 us  [call(): pl.pallas_call(kernel, out_shape=outs, in_specs=[pl.BlockSpec(memory_spac...]
    ppermute x6, waiting for transfers between devices: 12.9 us -> 14.1 us  [shift_by(): lax.ppermute(array, 'elem', [(i, (i + by) % count) for i in range(count)])]
    all_to_all x1, waiting for transfers between devices: 9.36 us -> 10.5 us  [shards(): back = lax.all_to_all(back, 'plane', 0, 0, tiled=True)]
  transfers between devices with their start and end apart: 8 -> 8, of which waited for: 6 -> 6; matrix products, arithmetic and copies ran while one was open for 1% -> 0% of each run, Pallas kernels for 4% -> 5%
where the time goes in v4:
time: 76.8 us; the launch traced here: 76.4 us
  waiting for transfers between devices  24.6 us (32%)
  starting transfers between devices  23.3 us (30%)
  Pallas kernels  18.1 us (24%)
  blocking collectives  10.2 us (13%)
    pallas_call x9, Pallas kernels, call(): pl.pallas_call(kernel, out_shape=outs, in_specs=[pl.BlockSpec(memory_spac...  18.1 us
    ppermute x6, starting transfers between devices, shift_by(): lax.ppermute(array, 'elem', [(i, (i + by) % count) for i in range(count)])  14.2 us
    ppermute x6, waiting for transfers between devices, shift_by(): lax.ppermute(array, 'elem', [(i, (i + by) % count) for i in range(count)])  14.1 us
    all_to_all x1, waiting for transfers between devices, shards(): back = lax.all_to_all(back, 'plane', 0, 0, tiled=True)  10.5 us
    all_to_all x1, blocking collectives, shards(): red = lax.all_to_all(red, 'elem', 0, 0, tiled=True)  10.2 us
    all_to_all x1, starting transfers between devices, shards(): back = lax.all_to_all(back, 'plane', 0, 0, tiled=True)  4.74 us
    all_to_all x1, starting transfers between devices, shards(): came = lax.all_to_all(packed, 'plane', 0, 0, tiled=True)  4.41 us
  transfers between devices with their start and end apart: 8, of which 6 were waited for; matrix products, arithmetic and copies ran while one was open for 0% of the time, Pallas kernels for 5%

profile of v4, /device:TPU:0, one launch (start us, length us, event | category | flops | bytes accessed | tf_op | source)
XLA Modules:
  0.0 76.4 jit_solution(10294390275068010404)
XLA Ops:
  0.0 2.6 %shard_map.83 = f32[8,144,128]{2,1,0:T(8,128)} custom-call(f32[36,32,128]{2,1,0:T(8,128)} %bitcast.13), custom_call_target="tpu_custom_call" | custom-call | flops 4000000 | bytes 1179648 | tf_op jit(solution)/shard_map/pallas_call | solution.py:110
  2.6 4.4 %all-to-all-start = ((f32[8,144,128]{2,1,0:T(8,128)}), f32[8,144,128]{2,1,0:T(8,128)S(1)}, u32[]{:S(2)}, u32[]{:S(2)}) async-start(f32[8,144,128]{2,1,0:T(8,128)} %shard_map.83), calls=%async_computation | async-start | bytes 1179648 | tf_op jit(solution)/shard_map/all_to_all | solution.py:760
  7.0 0.1 pad_add_fusion.place
  7.1 1.7 %shard_map.82 = (s32[4]{0:T(128)S(1)}, s32[24,128]{1,0:T(8,128)S(1)}, s32[8,128]{1,0:T(8,128)S(1)}, f32[8,128]{1,0:T(8,128)S(1)}, f32[36,8,128]{2,1,0:T(8,128)S(...) custom-call(s32[2]{0:T(128)S(1)} %pad_add_fusion.place, ...), custom_call_target="tpu_custom_call" | custom-call | flops 4000000 | bytes 623640 | tf_op jit(solution)/shard_map/pallas_call | solution.py:110
  8.9 1.3 %shard_map.84 = (f32[36,32,128]{2,1,0:T(8,128)S(1)}, f32[48,128]{1,0:T(8,128)S(1)}, f32[48,128]{1,0:T(8,128)S(1)}) custom-call(s32[4]{0:T(128)S(1)} %get-tuple-element.32.meta, s32[24,128]{1,0:T(8,128)S(1)} %get-tuple-element.33.idx, f32[8,128]{1,0:T(8,128)S(1)} %get-tuple-element.34.tab, f32[36,8,128]{2,1,0:T(8,128)S(1)} %get-tuple-element.35.own_c, ...), custom_call_target="tpu_custom_call" | custom-call | flops 4000000 | bytes 1540112 | tf_op jit(solution)/shard_map/pallas_call | solution.py:110
  10.2 1.6 %collective-permute-start = (f32[48,128]{1,0:T(8,128)S(1)}, f32[48,128]{1,0:T(8,128)S(1)}, u32[]{:S(2)}, u32[]{:S(2)}) collective-permute-start(f32[48,128]{1,0:T(8,128)S(1)} %get-tuple-element.40.to_e), channel_id=1, source_target_pairs={{0,1},{1,2},{2,3},{3,4},{4,5},{5,6},{6,7},{7,8},{8,9},{9,10},{10,1... | collective-permute-start | bytes 73736 | tf_op jit(solution)/shard_map/ppermute | solution.py:738
  11.8 5.0 %collective-permute-start.1 = (f32[48,128]{1,0:T(8,128)S(1)}, f32[48,128]{1,0:T(8,128)S(1)}, u32[]{:S(2)}, u32[]{:S(2)}) collective-permute-start(f32[48,128]{1,0:T(8,128)S(1)} %get-tuple-element.41.to_w), channel_id=1, source_target_pairs={{0,15},{1,0},{2,1},{3,2},{4,3},{5,4},{6,5},{7,6},{8,7},{9,8},{10,9... | collective-permute-start | bytes 73736 | tf_op jit(solution)/shard_map/ppermute | solution.py:738
  16.8 1.8 %collective-permute-done.from_w = f32[48,128]{1,0:T(8,128)S(1)} collective-permute-done((f32[48,128]{1,0:T(8,128)S(1)}, f32[48,128]{1,0:T(8,128)S(1)}, u32[]{:S(2)}, u32[]{:S(2)}) %collective-permute-start) | collective-permute-done | bytes 24608 | tf_op jit(solution)/shard_map/ppermute | solution.py:738
  18.6 4.5 %shard_map.85 = f32[8,144,128]{2,1,0:T(8,128)} custom-call(s32[4]{0:T(128)S(1)} %get-tuple-element.32.meta, f32[8,144,128]{2,1,0:T(8,128)S(1)} %all-to-all-done.came, f32[2,36,16,256]{3,2,1,0:T(8,128)} %bitcast.19, bf16[2,256,256]{2,1,0:T(8,128)(2,1)} %constant.13.clone.synth_far, bf16[2,256,256]{2,1,0:T(8,128)(2,1)} %constant.14.clone.analy_far), custom_call_target="tpu_custom_call" | custom-call | flops 4000000 | bytes 3407888 | tf_op jit(solution)/shard_map/pallas_call | solution.py:110
  23.1 4.7 %all-to-all-start.1 = ((f32[8,144,128]{2,1,0:T(8,128)}), f32[8,144,128]{2,1,0:T(8,128)S(1)}, u32[]{:S(2)}, u32[]{:S(2)}) async-start(f32[8,144,128]{2,1,0:T(8,128)} %shard_map.85), calls=%async_computation.1 | async-start | bytes 1179648 | tf_op jit(solution)/shard_map/all_to_all | solution.py:807
  27.9 0.6 shard_map.86.base
  28.4 10.5 %all-to-all-done.1.back = f32[8,144,128]{2,1,0:T(8,128)S(1)} async-done(((f32[8,144,128]{2,1,0:T(8,128)}), f32[8,144,128]{2,1,0:T(8,128)S(1)}, u32[]{:S(2)}, u32[]{:S(2)}) %all-to-all-start.1) | async-done | bytes 589856 | tf_op jit(solution)/shard_map/all_to_all | solution.py:807
  38.9 1.5 %shard_map.87 = (f32[36,32,128]{2,1,0:T(8,128)S(1)}, f32[36,32,128]{2,1,0:T(8,128)S(1)}, f32[48,128]{1,0:T(8,128)S(1)}, f32[48,128]{1,0:T(8,128)S(1)}) custom-call(s32[4]{0:T(128)S(1)} %get-tuple-element.32.meta, s32[24,128]{1,0:T(8,128)S(1)} %get-tuple-element.33.idx, f32[8,128]{1,0:T(8,128)S(1)} %get-tuple-element.34.tab, ...), custom_call_target="tpu_custom_call" | custom-call | flops 4000000 | bytes 2719760 | tf_op jit(solution)/shard_map/pallas_call | solution.py:110
  40.5 5.5 %collective-permute-start.3 = (f32[48,128]{1,0:T(8,128)S(1)}, f32[48,128]{1,0:T(8,128)S(1)}, u32[]{:S(2)}, u32[]{:S(2)}) collective-permute-start(f32[48,128]{1,0:T(8,128)S(1)} %get-tuple-element.48.to_w), channel_id=1, source_target_pairs={{0,15},{1,0},{2,1},{3,2},{4,3},{5,4},{6,5},{7,6},{8,7},{9,8},{10,9... | collective-permute-start | bytes 73736 | tf_op jit(solution)/shard_map/ppermute | solution.py:738
  46.0 1.5 %collective-permute-done.3.from_e = f32[48,128]{1,0:T(8,128)S(1)} collective-permute-done((f32[48,128]{1,0:T(8,128)S(1)}, f32[48,128]{1,0:T(8,128)S(1)}, u32[]{:S(2)}, u32[]{:S(2)}) %collective-permute-start.3) | collective-permute-done | bytes 24608 | tf_op jit(solution)/shard_map/ppermute | solution.py:738
  47.5 5.6 %collective-permute-done.2.from_w = f32[48,128]{1,0:T(8,128)S(1)} collective-permute-done((f32[48,128]{1,0:T(8,128)S(1)}, f32[48,128]{1,0:T(8,128)S(1)}, u32[]{:S(2)}, u32[]{:S(2)}) %collective-permute-start.2) | collective-permute-done | bytes 24608 | tf_op jit(solution)/shard_map/ppermute | solution.py:738
  53.1 2.6 %shard_map.88 = (f32[36,32,128]{2,1,0:T(8,128)S(1)}, f32[36,32,128]{2,1,0:T(8,128)S(1)}, f32[36,32,128]{2,1,0:T(8,128)S(1)}, f32[48,128]{1,0:T(8,128)S(1)}, f32[...) custom-call(s32[4]{0:T(128)S(1)} %get-tuple-element.32.meta, s32[24,128]{1,0:T(8,128)S(1)} %get-tuple-element.33.idx, ...), custom_call_target="tpu_custom_call" | custom-call | flops 4000000 | bytes 3760144 | tf_op jit(solution)/shard_map/pallas_call | solution.py:110
  55.7 0.0 collective-permute-start.5
  55.7 2.0 %collective-permute-start.4 = (f32[48,128]{1,0:T(8,128)S(1)}, f32[48,128]{1,0:T(8,128)S(1)}, u32[]{:S(2)}, u32[]{:S(2)}) collective-permute-start(f32[48,128]{1,0:T(8,128)S(1)} %get-tuple-element.54.to_e), channel_id=1, source_target_pairs={{0,1},{1,2},{2,3},{3,4},{4,5},{5,6},{6,7},{7,8},{8,9},{9,10},{10,1... | collective-permute-start | bytes 73736 | tf_op jit(solution)/shard_map/ppermute | solution.py:738
  57.7 1.8 %collective-permute-done.5.from_e = f32[48,128]{1,0:T(8,128)S(1)} collective-permute-done((f32[48,128]{1,0:T(8,128)S(1)}, f32[48,128]{1,0:T(8,128)S(1)}, u32[]{:S(2)}, u32[]{:S(2)}) %collective-permute-start.5) | collective-permute-done | bytes 24608 | tf_op jit(solution)/shard_map/ppermute | solution.py:738
  59.5 3.4 %collective-permute-done.4.from_w = f32[48,128]{1,0:T(8,128)S(1)} collective-permute-done((f32[48,128]{1,0:T(8,128)S(1)}, f32[48,128]{1,0:T(8,128)S(1)}, u32[]{:S(2)}, u32[]{:S(2)}) %collective-permute-start.4) | collective-permute-done | bytes 24608 | tf_op jit(solution)/shard_map/ppermute | solution.py:738
  62.9 2.0 %shard_map.89 = (f32[36,32,128]{2,1,0:T(8,128)S(1)}, f32[16,8,128]{2,1,0:T(8,128)S(1)}) custom-call(s32[4]{0:T(128)S(1)} %get-tuple-element.32.meta, s32[24,128]{1,0:T(8,128)S(1)} %get-tuple-element.33.idx, f32[8,128]{1,0:T(8,128)S(1)} %get-tuple-element.34.tab, f32[36,8,128]{2,1,0:T(8,128)S(1)} %get-tuple-element.35.own_c, ...), custom_call_target="tpu_custom_call" | custom-call | flops 4000000 | bytes 3186704 | tf_op jit(solution)/shard_map/pallas_call | solution.py:110
  64.9 10.2 %all_to_all.15.red = f32[16,8,128]{2,1,0:T(8,128)S(1)} all-to-all(f32[16,8,128]{2,1,0:T(8,128)S(1)} %get-tuple-element.57), channel_id=1, replica_groups=mesh['plane'=8,'elem'=16] {'elem'}, dimensions={0} | all-to-all | bytes 131072 | tf_op jit(solution)/shard_map/all_to_all | solution.py:834
  75.1 1.3 %shard_map.90 = f32[36,32,128]{2,1,0:T(8,128)} custom-call(f32[16,8,128]{2,1,0:T(8,128)S(1)} %all_to_all.15.red, f32[36,32,128]{2,1,0:T(8,128)S(1)} %bitcast.16, f32[36,32,128]{2,1,0:T(8,128)S(1)} %get-tuple-element.46.t0, f32[36,32,128]{2,1,0:T(8,128)S(1)} %get-tuple-element.50.t1, f32[36,32,128]{2,1,0:T(8,128)S(1)} %get-tuple-element.51.t2, ...), custom_call_target="tpu_custom_call" | custom-call | flops 4000000 | bytes 3604480 | tf_op jit(solution)/shard_map/pallas_call | solution.py:110
  (13 shorter events, 0.0 us)
Async XLA Ops:
  0.0 7.1 %copy-start.1 = (s32[2,8,128]{2,1,0:T(8,128)S(1)}, s32[2,8,128]{2,1,0:T(8,128)}, u32[]{:S(2)}) copy-start(s32[2,8,128]{2,1,0:T(8,128)} %sides.1) | copy-start | bytes 24580
  0.0 7.1 %copy-start.2 = (s32[8,128]{1,0:T(8,128)S(1)}, s32[8,128]{1,0:T(8,128)}, u32[]{:S(2)}) copy-start(s32[8,128]{1,0:T(8,128)} %links.1) | copy-start | bytes 12292
  0.0 7.1 %copy-start.3 = (f32[128]{0:T(128)S(1)}, f32[128]{0:T(128)}, u32[]{:S(2)}) copy-start(f32[128]{0:T(128)} %param.10) | copy-start | bytes 1540
  0.0 7.1 %copy-start.4 = (s32[128]{0:T(128)S(1)}, s32[128]{0:T(128)}, u32[]{:S(2)}) copy-start(s32[128]{0:T(128)} %param.13) | copy-start | bytes 1540
  0.0 8.9 %copy-start = (f32[32,6,6,128]{3,0,2,1:T(8,128)S(1)}, f32[32,6,6,128]{3,0,2,1:T(8,128)}, u32[]{:S(2)}) copy-start(f32[32,6,6,128]{3,0,2,1:T(8,128)} %param.8) | copy-start | bytes 1769476
  2.6 16.0 %all-to-all-start = ((f32[8,144,128]{2,1,0:T(8,128)}), f32[8,144,128]{2,1,0:T(8,128)S(1)}, u32[]{:S(2)}, u32[]{:S(2)}) async-start(f32[8,144,128]{2,1,0:T(8,128)} %shard_map.83), calls=%async_computation | async-start | bytes 1179648 | tf_op jit(solution)/shard_map/all_to_all | solution.py:760
  10.2 8.4 %collective-permute-start = (f32[48,128]{1,0:T(8,128)S(1)}, f32[48,128]{1,0:T(8,128)S(1)}, u32[]{:S(2)}, u32[]{:S(2)}) collective-permute-start(f32[48,128]{1,0:T(8,128)S(1)} %get-tuple-element.40.to_e), channel_id=1, source_target_pairs={{0,1},{1,2},{2,3},{3,4},{4,5},{5,6},{6,7},{7,8},{8,9},{9,10},{10,1... | collective-permute-start | bytes 73736 | tf_op jit(solution)/shard_map/ppermute | solution.py:738
  11.8 6.8 %collective-permute-start.1 = (f32[48,128]{1,0:T(8,128)S(1)}, f32[48,128]{1,0:T(8,128)S(1)}, u32[]{:S(2)}, u32[]{:S(2)}) collective-permute-start(f32[48,128]{1,0:T(8,128)S(1)} %get-tuple-element.41.to_w), channel_id=1, source_target_pairs={{0,15},{1,0},{2,1},{3,2},{4,3},{5,4},{6,5},{7,6},{8,7},{9,8},{10,9... | collective-permute-start | bytes 73736 | tf_op jit(solution)/shard_map/ppermute | solution.py:738
  23.1 15.8 %all-to-all-start.1 = ((f32[8,144,128]{2,1,0:T(8,128)}), f32[8,144,128]{2,1,0:T(8,128)S(1)}, u32[]{:S(2)}, u32[]{:S(2)}) async-start(f32[8,144,128]{2,1,0:T(8,128)} %shard_map.85), calls=%async_computation.1 | async-start | bytes 1179648 | tf_op jit(solution)/shard_map/all_to_all | solution.py:807
  40.5 7.0 %collective-permute-start.3 = (f32[48,128]{1,0:T(8,128)S(1)}, f32[48,128]{1,0:T(8,128)S(1)}, u32[]{:S(2)}, u32[]{:S(2)}) collective-permute-start(f32[48,128]{1,0:T(8,128)S(1)} %get-tuple-element.48.to_w), channel_id=1, source_target_pairs={{0,15},{1,0},{2,1},{3,2},{4,3},{5,4},{6,5},{7,6},{8,7},{9,8},{10,9... | collective-permute-start | bytes 73736 | tf_op jit(solution)/shard_map/ppermute | solution.py:738
  46.0 7.1 %collective-permute-start.2 = (f32[48,128]{1,0:T(8,128)S(1)}, f32[48,128]{1,0:T(8,128)S(1)}, u32[]{:S(2)}, u32[]{:S(2)}) collective-permute-start(f32[48,128]{1,0:T(8,128)S(1)} %get-tuple-element.49.to_e), channel_id=1, source_target_pairs={{0,1},{1,2},{2,3},{3,4},{4,5},{5,6},{6,7},{7,8},{8,9},{9,10},{10,1... | collective-permute-start | bytes 73736 | tf_op jit(solution)/shard_map/ppermute | solution.py:738
  55.7 3.8 %collective-permute-start.5 = (f32[48,128]{1,0:T(8,128)S(1)}, f32[48,128]{1,0:T(8,128)S(1)}, u32[]{:S(2)}, u32[]{:S(2)}) collective-permute-start(f32[48,128]{1,0:T(8,128)S(1)} %get-tuple-element.53.to_w), channel_id=1, source_target_pairs={{0,15},{1,0},{2,1},{3,2},{4,3},{5,4},{6,5},{7,6},{8,7},{9,8},{10,9... | collective-permute-start | bytes 73736 | tf_op jit(solution)/shard_map/ppermute | solution.py:738
  55.7 7.2 %collective-permute-start.4 = (f32[48,128]{1,0:T(8,128)S(1)}, f32[48,128]{1,0:T(8,128)S(1)}, u32[]{:S(2)}, u32[]{:S(2)}) collective-permute-start(f32[48,128]{1,0:T(8,128)S(1)} %get-tuple-element.54.to_e), channel_id=1, source_target_pairs={{0,1},{1,2},{2,3},{3,4},{4,5},{5,6},{6,7},{7,8},{8,9},{9,10},{10,1... | collective-permute-start | bytes 73736 | tf_op jit(solution)/shard_map/ppermute | solution.py:738

commit v5 on v4

--- a/solution.py
+++ b/solution.py
@@ -61,8 +61,7 @@
     harmonic = (coeffs + 1) // 2
     phase = 2.0 * np.pi * (harmonic * planes % count) / count
     synth = np.where(coeffs == 0, 1.0, np.where(coeffs % 2 == 1, np.cos(phase), np.sin(phase)))
-    norm = np.where((coeffs == 0) | (coeffs == count - 1), float(count), count / 2.0)
-    return synth, (synth / norm).T
+    return synth
 
 
 def split_table(table):
@@ -426,36 +425,34 @@
     return emit
 
 
-def guess_kernel(meta, idx, tab, own_c, far_c, u, out, send_w, send_e):
+def guess_kernel(meta, idx, tab, own_c, far_c, u_far, out, send_w, send_e, u, sem):
     env = (meta, idx, tab, own_c, far_c)
+    copy = pltpu.make_async_copy(u_far, u, sem)
+    copy.start()
+    copy.wait()
 
     def loop(group, plain):
-        inner(group, env, u, plain, store(out, group_rows(group)))
-        compact(group, idx, u, out, send_w, send_e)
+        rows = group_rows(group)
+
+        def emit(n, value):
+            out[n, rows, :] = float(W[n // 6] * W[n % 6]) * u[n, rows, :] - value
+
+        inner(group, env, u, plain, emit)
+        compact(group, idx, u, u, send_w, send_e)
 
     either(meta, loop)
 
 
-def base_kernel(idx, edge_idx, edge_own, edge_far, u, hu, to_w, to_e, from_w, from_e, out, edge):
+def guess_edge_kernel(edge_idx, edge_own, edge_far, to_w, to_e, from_w, from_e, edge):
     mine, _ = merge(to_w, to_e)
     theirs, _ = merge(from_w, from_e)
     for b, value in enumerate(edge_term(edge_idx, edge_own, edge_far, mine, theirs, 0)):
         edge[8 * b : 8 * b + 8, :] = value
 
-    def body(group, carry):
-        rows = group_rows(group)
-        extra = outer(group, idx, edge, 0)
-        for n in range(36):
-            image = hu[n, rows, :]
-            if n in extra:
-                image = image + extra[n]
-            out[n, rows, :] = float(W[n // 6] * W[n % 6]) * u[n, rows, :] - image
-        return carry
-
-    lax.fori_loop(0, 4, body, 0)
-
-
-def residual_kernel(meta, idx, tab, own_c, far_c, back, base, out, h_out, send_w, send_e):
+
+def residual_kernel(
+    meta, idx, tab, own_c, far_c, back, base, edge, out, h_out, send_w, send_e
+):
     env = (meta, idx, tab, own_c, far_c)
     for g in range(9):
         turned = back[:, 16 * g : 16 * g + 16, :].reshape(128, 128).T
@@ -464,7 +461,10 @@
             out[n] = base[n] + turned[32 * m : 32 * m + 32]
 
     def loop(group, plain):
-        inner(group, env, out, plain, store(h_out, group_rows(group)))
+        rows = group_rows(group)
+        for n, extra in outer(group, idx, edge, 0).items():
+            out[n, rows, :] -= extra
+        inner(group, env, out, plain, store(h_out, rows))
         compact(group, idx, out, h_out, send_w, send_e)
 
     either(meta, loop)
@@ -623,10 +623,10 @@
     for k in range(4):
         coef[k] = jnp.broadcast_to(turned[0:32, k : k + 1], (32, 128))
     copies = []
-    for c in range(6):
-        for n in range(6 * c, 6 * c + 6):
+    for c in range(3):
+        for n in range(12 * c, 12 * c + 12):
             held[n] = x0[n] + coef[0] * t0[n] + coef[1] * t1[n] + coef[2] * t2[n] + coef[3] * t3[n]
-        part = pl.ds(6 * c, 6)
+        part = pl.ds(12 * c, 12)
         copies.append(pltpu.make_async_copy(held.at[part], out.at[part], sems.at[c]))
         copies[c].start()
     for copy in copies:
@@ -634,19 +634,20 @@
 
 
 def pack_kernel(u, out, held, ready, sems):
-    copies = []
-    for g in range(9):
-        part = pl.ds(4 * g, 4)
-        copies.append(pltpu.make_async_copy(u.at[part], held.at[part], sems.at[g]))
-        copies[g].start()
-    for g in range(9):
-        copies[g].wait()
-        turned = held[4 * g : 4 * g + 4].reshape(128, 128).T
-        ready[:, 16 * g : 16 * g + 16, :] = turned.reshape(8, 16, 128)
-        part = pl.ds(16 * g, 16)
-        copies[g] = pltpu.make_async_copy(ready.at[:, part], out.at[:, part], sems.at[9 + g])
-        copies[g].start()
-    for copy in copies:
+    loads, stores = [], []
+    for c in range(3):
+        part = pl.ds(12 * c, 12)
+        loads.append(pltpu.make_async_copy(u.at[part], held.at[part], sems.at[c]))
+        loads[c].start()
+    for c in range(3):
+        loads[c].wait()
+        for g in range(3 * c, 3 * c + 3):
+            turned = held[4 * g : 4 * g + 4].reshape(128, 128).T
+            ready[:, 16 * g : 16 * g + 16, :] = turned.reshape(8, 16, 128)
+        part = pl.ds(48 * c, 48)
+        stores.append(pltpu.make_async_copy(ready.at[:, part], out.at[:, part], sems.at[3 + c]))
+        stores[c].start()
+    for copy in stores:
         copy.wait()
 
 
@@ -662,25 +663,14 @@
     return out
 
 
-def product3(high, low, table):
+def product3(high, low, table, dim):
     def dot(a, b):
-        return jnp.dot(a, b, preferred_element_type=F32)
+        return lax.dot_general(a, b, (((1,), (dim,)), ((), ())), preferred_element_type=F32)
 
     return dot(high, table[0]) + dot(high, table[1]) + dot(low, table[0])
 
 
-def advect_kernel(
-    meta, came, speed_far, synth_far, analy_far, out,
-    high, low, phys, speed, synth, analy, ready, sems,
-):
-    loads = [
-        pltpu.make_async_copy(far, near, sems.at[k])
-        for k, (far, near) in enumerate(
-            ((synth_far, synth), (speed_far, speed), (analy_far, analy))
-        )
-    ]
-    for load in loads:
-        load.start()
+def advect_kernel(meta, came, speed, synth, out, high, low, phys, ready, sem):
     for g in range(9):
         for h in range(2):
             pieces = block_turn([came[4 * h + s, 16 * g : 16 * g + 16, :] for s in range(4)])
@@ -689,11 +679,9 @@
                 hi, lo = split(pieces[m])
                 high[n : n + 16, 128 * h : 128 * h + 128] = hi
                 low[n : n + 16, 128 * h : 128 * h + 128] = lo
-    loads[0].wait()
     for i in range(2):
         part = slice(288 * i, 288 * i + 288)
-        phys[part, :] = product3(high[part, :], low[part, :], synth)
-    loads[1].wait()
+        phys[part, :] = product3(high[part, :], low[part, :], synth, 1)
     wide = meta[3] == 0
     sx = jnp.where(wide, 2.0, 1.0)
     sy = jnp.where(wide, 1.0, 2.0)
@@ -713,24 +701,22 @@
                 hi, lo = split(float(-0.5 * W[i] * W[j]) * total)
                 high[n : n + 16, cols] = hi
                 low[n : n + 16, cols] = lo
-    loads[2].wait()
     for i in range(2):
         part = slice(288 * i, 288 * i + 288)
-        phys[part, :] = product3(high[part, :], low[part, :], analy)
-    stores = []
-    for g in range(9):
-        for h in range(2):
-            cols = slice(128 * h, 128 * h + 128)
+        phys[part, :] = product3(high[part, :], low[part, :], synth, 0)
+    for h in range(2):
+        q = lane_ids((16, 128)) + 128 * h
+        norm = jnp.where((q == 0) | (q == 255), 1.0 / 256, 1.0 / 128)
+        cols = slice(128 * h, 128 * h + 128)
+        for g in range(9):
             pieces = block_turn(
-                [phys[16 * (4 * g + m) : 16 * (4 * g + m) + 16, cols] for m in range(4)]
+                [norm * phys[16 * (4 * g + m) : 16 * (4 * g + m) + 16, cols] for m in range(4)]
             )
             for s in range(4):
                 ready[4 * h + s, 16 * g : 16 * g + 16, :] = pieces[s]
-        part = pl.ds(16 * g, 16)
-        stores.append(pltpu.make_async_copy(ready.at[:, part], out.at[:, part], sems.at[3 + g]))
-        stores[g].start()
-    for store_ in stores:
-        store_.wait()
+    copy = pltpu.make_async_copy(ready, out, sem)
+    copy.start()
+    copy.wait()
 
 
 def shift_by(array, by):
@@ -741,9 +727,7 @@
 def shards(scalar_modes, velocity, viscosity, mortar_links, mortar_sides, layout):
     u = jnp.transpose(scalar_modes, (1, 2, 0, 3)).reshape(36, 32, 128)
     speed = jnp.transpose(velocity, (0, 2, 3, 4, 1)).reshape(2, 36, 16, 256)
-    synth, analy = plane_tables(256)
-    synth = jnp.asarray(split_table(synth.T))
-    analy = jnp.asarray(split_table(analy.T))
+    synth = jnp.asarray(split_table(plane_tables(256)))
     place = jnp.stack([lax.axis_index("plane"), lax.axis_index("elem")]).astype(jnp.int32)
 
     vol, edge = shape(36, 32, 128), shape(48, 128)
@@ -752,7 +736,7 @@
     packed = call(
         pack_kernel,
         [blocks],
-        [VMEM((36, 32, 128), F32), VMEM((8, 144, 128), F32), pltpu.SemaphoreType.DMA((18,))],
+        [VMEM((36, 32, 128), F32), VMEM((8, 144, 128), F32), pltpu.SemaphoreType.DMA((6,))],
         [u],
         [HBM],
         [HBM],
@@ -783,9 +767,14 @@
     def trade(send_w, send_e):
         return shift_by(send_e, 1), shift_by(send_w, -1)
 
-    hu, *sent = run(guess_kernel, [vol, edge, edge], [], head + [u])
-    got = trade(*sent)
-    came, *got = lax.optimization_barrier((came, *got))
+    base, *sent = call(
+        guess_kernel,
+        [vol, edge, edge],
+        [VMEM((36, 32, 128), F32), pltpu.SemaphoreType.DMA],
+        head + [u],
+        [SMEM] + [VMEM] * 4 + [HBM],
+    )
+    came, *sent = lax.optimization_barrier((came, *sent))
     back = call(
         advect_kernel,
         [blocks],
@@ -793,21 +782,17 @@
             VMEM((576, 256), BF16),
             VMEM((576, 256), BF16),
             VMEM((576, 256), F32),
-            VMEM((2, 36, 16, 256), F32),
-            VMEM((2, 256, 256), BF16),
-            VMEM((2, 256, 256), BF16),
             VMEM((8, 144, 128), F32),
-            pltpu.SemaphoreType.DMA((12,)),
+            pltpu.SemaphoreType.DMA,
         ],
-        [meta, came, speed, synth, analy],
-        [SMEM, VMEM, HBM, HBM, HBM],
+        [meta, came, speed, synth],
+        [SMEM, VMEM, VMEM, VMEM],
         [HBM],
-        grant=12,
+        grant=8,
     )[0]
+    back, *sent = lax.optimization_barrier((back, *sent))
     back = lax.all_to_all(back, "plane", 0, 0, tiled=True)
-    base = run(
-        base_kernel, [vol], [VMEM((48, 128), F32)], [idx, *edges, u, hu, *sent, *got]
-    )[0]
+    guess_edge = run(guess_edge_kernel, [shape(48, 128)], [], [*edges, *sent, *trade(*sent)])[0]
 
     def work(count):
         return [
@@ -816,7 +801,7 @@
             VMEM((8, 128), F32),
         ]
 
-    t0, h0, *sent = run(residual_kernel, [vol, vol, edge, edge], [], head + [back, base])
+    t0, h0, *sent = run(residual_kernel, [vol, vol, edge, edge], [], head + [back, base, guess_edge])
     got = trade(*sent)
     t1, t2, h2, to_w, to_e, keep, part = run(
         two_steps_kernel,
@@ -835,7 +820,7 @@
     out = call(
         finish_kernel,
         [vol],
-        [VMEM((4, 32, 128), F32), VMEM((36, 32, 128), F32), pltpu.SemaphoreType.DMA((6,))],
+        [VMEM((4, 32, 128), F32), VMEM((36, 32, 128), F32), pltpu.SemaphoreType.DMA((3,))],
         [red, u, t0, t1, t2, t3],
         [VMEM] * 6,
         [HBM],

time: 76.8 us -> 74.6 us (0.971)
  starting transfers between devices: 23.3 us -> 20.3 us
  waiting for transfers between devices: 24.6 us -> 26.5 us
  Pallas kernels: 18.1 us -> 17 us
    all_to_all x1, waiting for transfers between devices: 10.5 us -> 0.01 us  [shards(): back = lax.all_to_all(back, 'plane', 0, 0, tiled=True)]
    all_to_all x1, waiting for transfers between devices: 0.01 us -> 7.02 us  [shards(): came = lax.all_to_all(packed, 'plane', 0, 0, tiled=True)]
    ppermute x6, waiting for transfers between devices: 14.1 us -> 19.4 us  [shift_by(): lax.ppermute(array, 'elem', [(i, (i + by) % count) for i in range(count)])]
    ppermute x6, starting transfers between devices: 14.2 us -> 12.2 us  [shift_by(): lax.ppermute(array, 'elem', [(i, (i + by) % count) for i in range(count)])]
    all_to_all x1, starting transfers between devices: 4.74 us -> 3.55 us  [shards(): back = lax.all_to_all(back, 'plane', 0, 0, tiled=True)]
    pallas_call x9, Pallas kernels: 18.1 us -> 17 us  [call(): pl.pallas_call(kernel, out_shape=outs, in_specs=[pl.BlockSpec(memory_spac...]
  transfers between devices with their start and end apart: 8 -> 8, of which waited for: 6 -> 7; matrix products, arithmetic and copies ran while one was open for 0% -> 0% of each run, Pallas kernels for 5% -> 6%
where the time goes in v5:
time: 74.6 us; the launch traced here: 74.2 us
  waiting for transfers between devices  26.5 us (36%)
  starting transfers between devices  20.3 us (27%)
  Pallas kernels  17 us (23%)
  blocking collectives  10.2 us (14%)
    ppermute x6, waiting for transfers between devices, shift_by(): lax.ppermute(array, 'elem', [(i, (i + by) % count) for i in range(count)])  19.4 us
    pallas_call x9, Pallas kernels, call(): pl.pallas_call(kernel, out_shape=outs, in_specs=[pl.BlockSpec(memory_spac...  17 us
    ppermute x6, starting transfers between devices, shift_by(): lax.ppermute(array, 'elem', [(i, (i + by) % count) for i in range(count)])  12.2 us
    all_to_all x1, blocking collectives, shards(): red = lax.all_to_all(red, 'elem', 0, 0, tiled=True)  10.2 us
    all_to_all x1, waiting for transfers between devices, shards(): came = lax.all_to_all(packed, 'plane', 0, 0, tiled=True)  7.02 us
    all_to_all x1, starting transfers between devices, shards(): came = lax.all_to_all(packed, 'plane', 0, 0, tiled=True)  4.53 us
    all_to_all x1, starting transfers between devices, shards(): back = lax.all_to_all(back, 'plane', 0, 0, tiled=True)  3.55 us
  transfers between devices with their start and end apart: 8, of which 7 were waited for; matrix products, arithmetic and copies ran while one was open for 0% of the time, Pallas kernels for 6%

profile of v5, /device:TPU:0, one launch (start us, length us, event | category | flops | bytes accessed | tf_op | source)
XLA Modules:
  0.0 74.2 jit_solution(2605094098807993251)
XLA Ops:
  0.0 2.1 %shard_map.74 = f32[8,144,128]{2,1,0:T(8,128)} custom-call(f32[36,32,128]{2,1,0:T(8,128)} %bitcast.13), custom_call_target="tpu_custom_call" | custom-call | flops 4000000 | bytes 1179648 | tf_op jit(solution)/shard_map/pallas_call | solution.py:109
  2.2 4.5 %all-to-all-start = ((f32[8,144,128]{2,1,0:T(8,128)}), f32[8,144,128]{2,1,0:T(8,128)S(1)}, u32[]{:S(2)}, u32[]{:S(2)}) async-start(f32[8,144,128]{2,1,0:T(8,128)} %shard_map.74), calls=%async_computation | async-start | bytes 1179648 | tf_op jit(solution)/shard_map/all_to_all | solution.py:744
  6.7 0.1 pad_add_fusion.place
  6.8 1.7 %shard_map.73 = (s32[4]{0:T(128)S(1)}, s32[24,128]{1,0:T(8,128)S(1)}, s32[8,128]{1,0:T(8,128)S(1)}, f32[8,128]{1,0:T(8,128)S(1)}, f32[36,8,128]{2,1,0:T(8,128)S(...) custom-call(s32[2]{0:T(128)S(1)} %pad_add_fusion.place, ...), custom_call_target="tpu_custom_call" | custom-call | flops 4000000 | bytes 623640 | tf_op jit(solution)/shard_map/pallas_call | solution.py:109
  8.5 2.2 %shard_map.75 = (f32[36,32,128]{2,1,0:T(8,128)S(1)}, f32[48,128]{1,0:T(8,128)S(1)}, f32[48,128]{1,0:T(8,128)S(1)}) custom-call(s32[4]{0:T(128)S(1)} %get-tuple-element.35.meta, s32[24,128]{1,0:T(8,128)S(1)} %get-tuple-element.36.idx, f32[8,128]{1,0:T(8,128)S(1)} %get-tuple-element.37.tab, f32[36,8,128]{2,1,0:T(8,128)S(1)} %get-tuple-element.38.own_c, ...), custom_call_target="tpu_custom_call" | custom-call | flops 4000000 | bytes 1540112 | tf_op jit(solution)/shard_map/pallas_call | solution.py:109
  10.7 7.0 %all-to-all-done.came = f32[8,144,128]{2,1,0:T(8,128)S(1)} async-done(((f32[8,144,128]{2,1,0:T(8,128)}), f32[8,144,128]{2,1,0:T(8,128)S(1)}, u32[]{:S(2)}, u32[]{:S(2)}) %all-to-all-start) | async-done | bytes 589856 | tf_op jit(solution)/shard_map/all_to_all | solution.py:744
  17.7 3.0 %shard_map.76 = f32[8,144,128]{2,1,0:T(8,128)} custom-call(s32[4]{0:T(128)S(1)} %get-tuple-element.35.meta, f32[8,144,128]{2,1,0:T(8,128)S(1)} %all-to-all-done.came, f32[2,36,16,256]{3,2,1,0:T(8,128)S(1)} %bitcast.16, bf16[2,256,256]{2,1,0:T(8,128)(2,1)S(1)} %copy-done.2), custom_call_target="tpu_custom_call" | custom-call | flops 4000000 | bytes 2883600 | tf_op jit(solution)/shard_map/pallas_call | solution.py:109
  20.8 3.6 %all-to-all-start.1 = ((f32[8,144,128]{2,1,0:T(8,128)}), f32[8,144,128]{2,1,0:T(8,128)S(1)}, u32[]{:S(2)}, u32[]{:S(2)}) async-start(f32[8,144,128]{2,1,0:T(8,128)} %shard_map.76), calls=%async_computation.1 | async-start | bytes 1179648 | tf_op jit(solution)/shard_map/all_to_all | solution.py:794
  24.3 6.6 %collective-permute-start.1 = (f32[48,128]{1,0:T(8,128)S(1)}, f32[48,128]{1,0:T(8,128)S(1)}, u32[]{:S(2)}, u32[]{:S(2)}) collective-permute-start(f32[48,128]{1,0:T(8,128)S(1)} %get-tuple-element.50.to_w), channel_id=1, source_target_pairs={{0,15},{1,0},{2,1},{3,2},{4,3},{5,4},{6,5},{7,6},{8,7},{9,8},{10,9... | collective-permute-start | bytes 73736 | tf_op jit(solution)/shard_map/ppermute | solution.py:724
  30.9 1.5 %collective-permute-done.1.from_e = f32[48,128]{1,0:T(8,128)S(1)} collective-permute-done((f32[48,128]{1,0:T(8,128)S(1)}, f32[48,128]{1,0:T(8,128)S(1)}, u32[]{:S(2)}, u32[]{:S(2)}) %collective-permute-start.1) | collective-permute-done | bytes 24608 | tf_op jit(solution)/shard_map/ppermute | solution.py:724
  32.4 5.6 %collective-permute-done.from_w = f32[48,128]{1,0:T(8,128)S(1)} collective-permute-done((f32[48,128]{1,0:T(8,128)S(1)}, f32[48,128]{1,0:T(8,128)S(1)}, u32[]{:S(2)}, u32[]{:S(2)}) %collective-permute-start) | collective-permute-done | bytes 24608 | tf_op jit(solution)/shard_map/ppermute | solution.py:724
  38.0 0.2 shard_map.77.edge
  38.2 1.8 %shard_map.78 = (f32[36,32,128]{2,1,0:T(8,128)S(1)}, f32[36,32,128]{2,1,0:T(8,128)S(1)}, f32[48,128]{1,0:T(8,128)S(1)}, f32[48,128]{1,0:T(8,128)S(1)}) custom-call(s32[4]{0:T(128)S(1)} %get-tuple-element.35.meta, s32[24,128]{1,0:T(8,128)S(1)} %get-tuple-element.36.idx, f32[8,128]{1,0:T(8,128)S(1)} %get-tuple-element.37.tab, ...), custom_call_target="tpu_custom_call" | custom-call | flops 4000000 | bytes 2744336 | tf_op jit(solution)/shard_map/pallas_call | solution.py:109
  40.0 3.6 %collective-permute-start.3 = (f32[48,128]{1,0:T(8,128)S(1)}, f32[48,128]{1,0:T(8,128)S(1)}, u32[]{:S(2)}, u32[]{:S(2)}) collective-permute-start(f32[48,128]{1,0:T(8,128)S(1)} %get-tuple-element.54.to_w), channel_id=1, source_target_pairs={{0,15},{1,0},{2,1},{3,2},{4,3},{5,4},{6,5},{7,6},{8,7},{9,8},{10,9... | collective-permute-start | bytes 73736 | tf_op jit(solution)/shard_map/ppermute | solution.py:724
  43.7 1.5 %collective-permute-done.3.from_e = f32[48,128]{1,0:T(8,128)S(1)} collective-permute-done((f32[48,128]{1,0:T(8,128)S(1)}, f32[48,128]{1,0:T(8,128)S(1)}, u32[]{:S(2)}, u32[]{:S(2)}) %collective-permute-start.3) | collective-permute-done | bytes 24608 | tf_op jit(solution)/shard_map/ppermute | solution.py:724
  45.2 5.6 %collective-permute-done.2.from_w = f32[48,128]{1,0:T(8,128)S(1)} collective-permute-done((f32[48,128]{1,0:T(8,128)S(1)}, f32[48,128]{1,0:T(8,128)S(1)}, u32[]{:S(2)}, u32[]{:S(2)}) %collective-permute-start.2) | collective-permute-done | bytes 24608 | tf_op jit(solution)/shard_map/ppermute | solution.py:724
  50.8 2.6 %shard_map.79 = (f32[36,32,128]{2,1,0:T(8,128)S(1)}, f32[36,32,128]{2,1,0:T(8,128)S(1)}, f32[36,32,128]{2,1,0:T(8,128)S(1)}, f32[48,128]{1,0:T(8,128)S(1)}, f32[...) custom-call(s32[4]{0:T(128)S(1)} %get-tuple-element.35.meta, s32[24,128]{1,0:T(8,128)S(1)} %get-tuple-element.36.idx, ...), custom_call_target="tpu_custom_call" | custom-call | flops 4000000 | bytes 3760144 | tf_op jit(solution)/shard_map/pallas_call | solution.py:109
  53.4 0.0 collective-permute-start.5
  53.4 2.0 %collective-permute-start.4 = (f32[48,128]{1,0:T(8,128)S(1)}, f32[48,128]{1,0:T(8,128)S(1)}, u32[]{:S(2)}, u32[]{:S(2)}) collective-permute-start(f32[48,128]{1,0:T(8,128)S(1)} %get-tuple-element.60.to_e), channel_id=1, source_target_pairs={{0,1},{1,2},{2,3},{3,4},{4,5},{5,6},{6,7},{7,8},{8,9},{9,10},{10,1... | collective-permute-start | bytes 73736 | tf_op jit(solution)/shard_map/ppermute | solution.py:724
  55.5 1.8 %collective-permute-done.5.from_e = f32[48,128]{1,0:T(8,128)S(1)} collective-permute-done((f32[48,128]{1,0:T(8,128)S(1)}, f32[48,128]{1,0:T(8,128)S(1)}, u32[]{:S(2)}, u32[]{:S(2)}) %collective-permute-start.5) | collective-permute-done | bytes 24608 | tf_op jit(solution)/shard_map/ppermute | solution.py:724
  57.3 3.4 %collective-permute-done.4.from_w = f32[48,128]{1,0:T(8,128)S(1)} collective-permute-done((f32[48,128]{1,0:T(8,128)S(1)}, f32[48,128]{1,0:T(8,128)S(1)}, u32[]{:S(2)}, u32[]{:S(2)}) %collective-permute-start.4) | collective-permute-done | bytes 24608 | tf_op jit(solution)/shard_map/ppermute | solution.py:724
  60.6 2.0 %shard_map.80 = (f32[36,32,128]{2,1,0:T(8,128)S(1)}, f32[16,8,128]{2,1,0:T(8,128)S(1)}) custom-call(s32[4]{0:T(128)S(1)} %get-tuple-element.35.meta, s32[24,128]{1,0:T(8,128)S(1)} %get-tuple-element.36.idx, f32[8,128]{1,0:T(8,128)S(1)} %get-tuple-element.37.tab, f32[36,8,128]{2,1,0:T(8,128)S(1)} %get-tuple-element.38.own_c, ...), custom_call_target="tpu_custom_call" | custom-call | flops 4000000 | bytes 3186704 | tf_op jit(solution)/shard_map/pallas_call | solution.py:109
  62.6 10.2 %all_to_all.15.red = f32[16,8,128]{2,1,0:T(8,128)S(1)} all-to-all(f32[16,8,128]{2,1,0:T(8,128)S(1)} %get-tuple-element.63), channel_id=1, replica_groups=mesh['plane'=8,'elem'=16] {'elem'}, dimensions={0} | all-to-all | bytes 131072 | tf_op jit(solution)/shard_map/all_to_all | solution.py:819
  72.9 1.4 %shard_map.81 = f32[36,32,128]{2,1,0:T(8,128)} custom-call(f32[16,8,128]{2,1,0:T(8,128)S(1)} %all_to_all.15.red, f32[36,32,128]{2,1,0:T(8,128)S(1)} %bitcast.15, f32[36,32,128]{2,1,0:T(8,128)S(1)} %get-tuple-element.52.t0, f32[36,32,128]{2,1,0:T(8,128)S(1)} %get-tuple-element.56.t1, f32[36,32,128]{2,1,0:T(8,128)S(1)} %get-tuple-element.57.t2, ...), custom_call_target="tpu_custom_call" | custom-call | flops 4000000 | bytes 3604480 | tf_op jit(solution)/shard_map/pallas_call | solution.py:109
  (17 shorter events, 0.0 us)
Async XLA Ops:
  0.0 6.8 %copy-start.3 = (s32[2,8,128]{2,1,0:T(8,128)S(1)}, s32[2,8,128]{2,1,0:T(8,128)}, u32[]{:S(2)}) copy-start(s32[2,8,128]{2,1,0:T(8,128)} %sides.1) | copy-start | bytes 24580
  0.0 6.8 %copy-start.4 = (s32[8,128]{1,0:T(8,128)S(1)}, s32[8,128]{1,0:T(8,128)}, u32[]{:S(2)}) copy-start(s32[8,128]{1,0:T(8,128)} %links.1) | copy-start | bytes 12292
  0.0 6.8 %copy-start.5 = (f32[128]{0:T(128)S(1)}, f32[128]{0:T(128)}, u32[]{:S(2)}) copy-start(f32[128]{0:T(128)} %param.9) | copy-start | bytes 1540
  0.0 6.8 %copy-start.6 = (s32[128]{0:T(128)S(1)}, s32[128]{0:T(128)}, u32[]{:S(2)}) copy-start(s32[128]{0:T(128)} %param.12) | copy-start | bytes 1540
  2.1 15.6 %copy-start.1 = (f32[2,256,6,6,16]{1,4,3,2,0:T(8,128)S(1)}, f32[2,256,6,6,16]{1,4,3,2,0:T(8,128)}, u32[]{:S(2)}) copy-start(f32[2,256,6,6,16]{1,4,3,2,0:T(8,128)} %param.8) | copy-start | bytes 3538948
  2.1 15.6 %copy-start.2 = (bf16[2,256,256]{2,1,0:T(8,128)(2,1)S(1)}, bf16[2,256,256]{2,1,0:T(8,128)(2,1)}, u32[]{:S(2)}) copy-start(bf16[2,256,256]{2,1,0:T(8,128)(2,1)} %constant.11.clone.synth) | copy-start | bytes 786436
  2.2 15.6 %all-to-all-start = ((f32[8,144,128]{2,1,0:T(8,128)}), f32[8,144,128]{2,1,0:T(8,128)S(1)}, u32[]{:S(2)}, u32[]{:S(2)}) async-start(f32[8,144,128]{2,1,0:T(8,128)} %shard_map.74), calls=%async_computation | async-start | bytes 1179648 | tf_op jit(solution)/shard_map/all_to_all | solution.py:744
  20.8 17.4 %all-to-all-start.1 = ((f32[8,144,128]{2,1,0:T(8,128)}), f32[8,144,128]{2,1,0:T(8,128)S(1)}, u32[]{:S(2)}, u32[]{:S(2)}) async-start(f32[8,144,128]{2,1,0:T(8,128)} %shard_map.76), calls=%async_computation.1 | async-start | bytes 1179648 | tf_op jit(solution)/shard_map/all_to_all | solution.py:794
  24.3 8.1 %collective-permute-start.1 = (f32[48,128]{1,0:T(8,128)S(1)}, f32[48,128]{1,0:T(8,128)S(1)}, u32[]{:S(2)}, u32[]{:S(2)}) collective-permute-start(f32[48,128]{1,0:T(8,128)S(1)} %get-tuple-element.50.to_w), channel_id=1, source_target_pairs={{0,15},{1,0},{2,1},{3,2},{4,3},{5,4},{6,5},{7,6},{8,7},{9,8},{10,9... | collective-permute-start | bytes 73736 | tf_op jit(solution)/shard_map/ppermute | solution.py:724
  30.9 7.1 %collective-permute-start = (f32[48,128]{1,0:T(8,128)S(1)}, f32[48,128]{1,0:T(8,128)S(1)}, u32[]{:S(2)}, u32[]{:S(2)}) collective-permute-start(f32[48,128]{1,0:T(8,128)S(1)} %get-tuple-element.51.to_e), channel_id=1, source_target_pairs={{0,1},{1,2},{2,3},{3,4},{4,5},{5,6},{6,7},{7,8},{8,9},{9,10},{10,1... | collective-permute-start | bytes 73736 | tf_op jit(solution)/shard_map/ppermute | solution.py:724
  40.0 5.2 %collective-permute-start.3 = (f32[48,128]{1,0:T(8,128)S(1)}, f32[48,128]{1,0:T(8,128)S(1)}, u32[]{:S(2)}, u32[]{:S(2)}) collective-permute-start(f32[48,128]{1,0:T(8,128)S(1)} %get-tuple-element.54.to_w), channel_id=1, source_target_pairs={{0,15},{1,0},{2,1},{3,2},{4,3},{5,4},{6,5},{7,6},{8,7},{9,8},{10,9... | collective-permute-start | bytes 73736 | tf_op jit(solution)/shard_map/ppermute | solution.py:724
  43.7 7.1 %collective-permute-start.2 = (f32[48,128]{1,0:T(8,128)S(1)}, f32[48,128]{1,0:T(8,128)S(1)}, u32[]{:S(2)}, u32[]{:S(2)}) collective-permute-start(f32[48,128]{1,0:T(8,128)S(1)} %get-tuple-element.55.to_e), channel_id=1, source_target_pairs={{0,1},{1,2},{2,3},{3,4},{4,5},{5,6},{6,7},{7,8},{8,9},{9,10},{10,1... | collective-permute-start | bytes 73736 | tf_op jit(solution)/shard_map/ppermute | solution.py:724
  53.4 3.8 %collective-permute-start.5 = (f32[48,128]{1,0:T(8,128)S(1)}, f32[48,128]{1,0:T(8,128)S(1)}, u32[]{:S(2)}, u32[]{:S(2)}) collective-permute-start(f32[48,128]{1,0:T(8,128)S(1)} %get-tuple-element.59.to_w), channel_id=1, source_target_pairs={{0,15},{1,0},{2,1},{3,2},{4,3},{5,4},{6,5},{7,6},{8,7},{9,8},{10,9... | collective-permute-start | bytes 73736 | tf_op jit(solution)/shard_map/ppermute | solution.py:724
  53.4 7.2 %collective-permute-start.4 = (f32[48,128]{1,0:T(8,128)S(1)}, f32[48,128]{1,0:T(8,128)S(1)}, u32[]{:S(2)}, u32[]{:S(2)}) collective-permute-start(f32[48,128]{1,0:T(8,128)S(1)} %get-tuple-element.60.to_e), channel_id=1, source_target_pairs={{0,1},{1,2},{2,3},{3,4},{4,5},{5,6},{6,7},{7,8},{8,9},{9,10},{10,1... | collective-permute-start | bytes 73736 | tf_op jit(solution)/shard_map/ppermute | solution.py:724
  60.6 12.2 %copy-start = (f32[32,6,6,128]{3,0,2,1:T(8,128)S(1)}, f32[32,6,6,128]{3,0,2,1:T(8,128)}, u32[]{:S(2)}) copy-start(f32[32,6,6,128]{3,0,2,1:T(8,128)} %param.7) | copy-start | bytes 1769476

commit v6 on v5

--- a/solution.py
+++ b/solution.py
@@ -271,7 +271,9 @@
 
         @pl.when((meta[2] == 0) == plain)
         def _(plain=plain):
-            lax.fori_loop(0, 4, lambda group, carry: loop(group, plain) or carry, 0)
+            lax.fori_loop(
+                0, 4, lambda group, carry: loop(group, plain) or carry, 0, unroll=2 if plain else 1
+            )
 
 
 def weighted(factors, values):
@@ -350,17 +352,18 @@
                 emit(n, value)
 
 
-def compact(group, idx, v_ref, h_ref, send_w, send_e):
-    rows = group_rows(group)
+def compact(idx, v_ref, h_ref, send_w, send_e):
     part = lax.shift_right_logical(lane_ids((8, 128)), 4)
     for face, ref in ((0, send_w), (1, send_e)):
         index = row_of(idx, face)
         for b in range(6):
             n = face_nodes(face)[b]
-            low, high = take(v_ref[n, rows, :], index), take(h_ref[n, rows, :], index)
-            old = ref[8 * b : 8 * b + 8, :]
-            new = jnp.where(part == group, low, jnp.where(part == group + 4, high, old))
-            ref[8 * b : 8 * b + 8, :] = new
+            value = take(v_ref[n, 0:8, :], index)
+            for k in range(1, 8):
+                source = v_ref if k < 4 else h_ref
+                other = take(source[n, 8 * (k % 4) : 8 * (k % 4) + 8, :], index)
+                value = jnp.where(part == k, other, value)
+            ref[8 * b : 8 * b + 8, :] = value
 
 
 def outer(group, idx, edge, first):
@@ -438,9 +441,9 @@
             out[n, rows, :] = float(W[n // 6] * W[n % 6]) * u[n, rows, :] - value
 
         inner(group, env, u, plain, emit)
-        compact(group, idx, u, u, send_w, send_e)
 
     either(meta, loop)
+    compact(idx, u, u, send_w, send_e)
 
 
 def guess_edge_kernel(edge_idx, edge_own, edge_far, to_w, to_e, from_w, from_e, edge):
@@ -454,20 +457,24 @@
     meta, idx, tab, own_c, far_c, back, base, edge, out, h_out, send_w, send_e
 ):
     env = (meta, idx, tab, own_c, far_c)
-    for g in range(9):
-        turned = back[:, 16 * g : 16 * g + 16, :].reshape(128, 128).T
+
+    def turn(g, carry):
+        part = pl.ds(pl.multiple_of(16 * g, 16), 16)
+        turned = back[:, part, :].reshape(128, 128).T
         for m in range(4):
-            n = 4 * g + m
-            out[n] = base[n] + turned[32 * m : 32 * m + 32]
+            out[4 * g + m] = base[4 * g + m] + turned[32 * m : 32 * m + 32]
+        return carry
+
+    lax.fori_loop(0, 9, turn, 0, unroll=3)
 
     def loop(group, plain):
         rows = group_rows(group)
         for n, extra in outer(group, idx, edge, 0).items():
             out[n, rows, :] -= extra
         inner(group, env, out, plain, store(h_out, rows))
-        compact(group, idx, out, h_out, send_w, send_e)
 
     either(meta, loop)
+    compact(idx, out, h_out, send_w, send_e)
 
 
 def edge_steps(tables, to_w, to_e, from_w, from_e, before, edge, keep):
@@ -498,7 +505,7 @@
 def two_steps_kernel(
     meta, idx, tab, own_c, far_c, edge_idx, edge_own, edge_far,
     t0, h0, to_w, to_e, from_w, from_e,
-    t1, t2, h2, send_w, send_e, keep, part, edge, acc, pad,
+    t1, t2, h2, send_w, send_e, keep, edge,
 ):
     env = (meta, idx, tab, own_c, far_c)
     tables = (edge_idx, edge_own, edge_far)
@@ -507,34 +514,38 @@
     def loop(group, plain):
         rows = group_rows(group)
         extra = outer(group, idx, edge, 0)
-        sums = [jnp.zeros((8, 128), F32)] * 5
         for n in range(36):
             image = h0[n, rows, :]
             if n in extra:
                 image = image + extra[n]
-            a = t0[n, rows, :]
-            b = (1.0 / HALF) * image - a
-            t1[n, rows, :] = b
-            for k, term in enumerate((a * a, a * b, b * b)):
-                sums[k] = sums[k] + term
+            t1[n, rows, :] = (1.0 / HALF) * image - t0[n, rows, :]
         extra_next = outer(group, idx, edge, 48)
 
         def emit(n, image):
             if n in extra_next:
                 image = image + extra_next[n]
-            b = t1[n, rows, :]
-            c = (2.0 / HALF) * image - 2.0 * b - t0[n, rows, :]
-            t2[n, rows, :] = c
-            sums[3] = sums[3] + b * c
-            sums[4] = sums[4] + c * c
+            t2[n, rows, :] = (2.0 / HALF) * image - 2.0 * t1[n, rows, :] - t0[n, rows, :]
 
         inner(group, env, t1, plain, emit)
+        inner(group, env, t2, plain, store(h2, rows))
+
+    either(meta, loop)
+    compact(idx, t2, h2, send_w, send_e)
+
+
+def sums_kernel(t0, t1, t2, part, acc, pad):
+    def body(group, carry):
+        rows = group_rows(group)
+        sums = [jnp.zeros((8, 128), F32)] * 5
+        for n in range(36):
+            a, b, c = t0[n, rows, :], t1[n, rows, :], t2[n, rows, :]
+            for k, term in enumerate((a * a, a * b, b * b, b * c, c * c)):
+                sums[k] = sums[k] + term
         for k in range(5):
             acc[rows, 128 * k : 128 * k + 128] = sums[k]
-        inner(group, env, t2, plain, store(h2, rows))
-        compact(group, idx, t2, h2, send_w, send_e)
-
-    either(meta, loop)
+        return carry
+
+    lax.fori_loop(0, 4, body, 0)
     store_sums(acc, pad, 0, 5)
     part[...] = pad[...]
 
@@ -624,8 +635,12 @@
         coef[k] = jnp.broadcast_to(turned[0:32, k : k + 1], (32, 128))
     copies = []
     for c in range(3):
-        for n in range(12 * c, 12 * c + 12):
-            held[n] = x0[n] + coef[0] * t0[n] + coef[1] * t1[n] + coef[2] * t2[n] + coef[3] * t3[n]
+        def add(n, carry):
+            terms = coef[0] * t0[n] + coef[1] * t1[n] + coef[2] * t2[n] + coef[3] * t3[n]
+            held[n] = x0[n] + terms
+            return carry
+
+        lax.fori_loop(12 * c, 12 * c + 12, add, 0, unroll=3)
         part = pl.ds(12 * c, 12)
         copies.append(pltpu.make_async_copy(held.at[part], out.at[part], sems.at[c]))
         copies[c].start()
@@ -641,9 +656,14 @@
         loads[c].start()
     for c in range(3):
         loads[c].wait()
-        for g in range(3 * c, 3 * c + 3):
-            turned = held[4 * g : 4 * g + 4].reshape(128, 128).T
-            ready[:, 16 * g : 16 * g + 16, :] = turned.reshape(8, 16, 128)
+
+        def turn(g, carry):
+            turned = held[pl.ds(4 * g, 4)].reshape(128, 128).T
+            part = pl.ds(pl.multiple_of(16 * g, 16), 16)
+            ready[:, part, :] = turned.reshape(8, 16, 128)
+            return carry
+
+        lax.fori_loop(3 * c, 3 * c + 3, turn, 0)
         part = pl.ds(48 * c, 48)
         stores.append(pltpu.make_async_copy(ready.at[:, part], out.at[:, part], sems.at[3 + c]))
         stores[c].start()
@@ -670,53 +690,72 @@
     return dot(high, table[0]) + dot(high, table[1]) + dot(low, table[0])
 
 
-def advect_kernel(meta, came, speed, synth, out, high, low, phys, ready, sem):
-    for g in range(9):
+def advect_kernel(meta, came, speed, synth, out, high, low, phys, grad, ready, sems):
+    def rows_of(n):
+        return pl.ds(pl.multiple_of(16 * n, 16), 16)
+
+    def spread(g, carry):
         for h in range(2):
-            pieces = block_turn([came[4 * h + s, 16 * g : 16 * g + 16, :] for s in range(4)])
+            cols = slice(128 * h, 128 * h + 128)
+            pieces = block_turn([came[4 * h + s, rows_of(g), :] for s in range(4)])
             for m in range(4):
-                n = 16 * (4 * g + m)
                 hi, lo = split(pieces[m])
-                high[n : n + 16, 128 * h : 128 * h + 128] = hi
-                low[n : n + 16, 128 * h : 128 * h + 128] = lo
+                high[rows_of(4 * g + m), cols] = hi
+                low[rows_of(4 * g + m), cols] = lo
+        return carry
+
+    lax.fori_loop(0, 9, spread, 0)
     for i in range(2):
         part = slice(288 * i, 288 * i + 288)
         phys[part, :] = product3(high[part, :], low[part, :], synth, 1)
     wide = meta[3] == 0
     sx = jnp.where(wide, 2.0, 1.0)
     sy = jnp.where(wide, 1.0, 2.0)
-    for h in range(2):
-        cols = slice(128 * h, 128 * h + 128)
-        u = [[phys[16 * (6 * i + j) : 16 * (6 * i + j) + 16, cols] for j in range(6)] for i in range(6)]
-        acc = [[None] * 6 for _ in range(6)]
-        for j in range(6):
-            g = folded([u[i][j] for i in range(6)], DERIV_FOLD, -1)
+
+    def advance(h, carry):
+        cols = pl.ds(pl.multiple_of(128 * h, 128), 128)
+
+        def line_x(j, carry):
+            g = folded([phys[rows_of(6 * i + j), cols] for i in range(6)], DERIV_FOLD, -1)
             for i in range(6):
-                acc[i][j] = sx * (speed[0, 6 * i + j, :, cols] * g[i])
+                n = 6 * i + j
+                grad[rows_of(n), cols] = sx * (speed[0, n, :, cols] * g[i])
+            return carry
+
+        lax.fori_loop(0, 6, line_x, 0, unroll=2)
         for i in range(6):
-            g = folded(u[i], DERIV_FOLD, -1)
+            g = folded([phys[rows_of(6 * i + j), cols] for j in range(6)], DERIV_FOLD, -1)
             for j in range(6):
-                n = 16 * (6 * i + j)
-                total = acc[i][j] + sy * (speed[1, 6 * i + j, :, cols] * g[j])
+                n = 6 * i + j
+                total = grad[rows_of(n), cols] + sy * (speed[1, n, :, cols] * g[j])
                 hi, lo = split(float(-0.5 * W[i] * W[j]) * total)
-                high[n : n + 16, cols] = hi
-                low[n : n + 16, cols] = lo
+                high[rows_of(n), cols] = hi
+                low[rows_of(n), cols] = lo
+        return carry
+
+    lax.fori_loop(0, 2, advance, 0)
     for i in range(2):
         part = slice(288 * i, 288 * i + 288)
         phys[part, :] = product3(high[part, :], low[part, :], synth, 0)
-    for h in range(2):
-        q = lane_ids((16, 128)) + 128 * h
-        norm = jnp.where((q == 0) | (q == 255), 1.0 / 256, 1.0 / 128)
-        cols = slice(128 * h, 128 * h + 128)
-        for g in range(9):
-            pieces = block_turn(
-                [norm * phys[16 * (4 * g + m) : 16 * (4 * g + m) + 16, cols] for m in range(4)]
-            )
+
+    def gather(g, carry):
+        for h in range(2):
+            q = lane_ids((16, 128)) + 128 * h
+            norm = jnp.where((q == 0) | (q == 255), 1.0 / 256, 1.0 / 128)
+            cols = slice(128 * h, 128 * h + 128)
+            pieces = block_turn([norm * phys[rows_of(4 * g + m), cols] for m in range(4)])
             for s in range(4):
-                ready[4 * h + s, 16 * g : 16 * g + 16, :] = pieces[s]
-    copy = pltpu.make_async_copy(ready, out, sem)
-    copy.start()
-    copy.wait()
+                ready[4 * h + s, rows_of(g), :] = pieces[s]
+        return carry
+
+    copies = []
+    for c in range(3):
+        lax.fori_loop(3 * c, 3 * c + 3, gather, 0)
+        part = pl.ds(48 * c, 48)
+        copies.append(pltpu.make_async_copy(ready.at[:, part], out.at[:, part], sems.at[c]))
+        copies[c].start()
+    for copy in copies:
+        copy.wait()
 
 
 def shift_by(array, by):
@@ -782,8 +821,9 @@
             VMEM((576, 256), BF16),
             VMEM((576, 256), BF16),
             VMEM((576, 256), F32),
+            VMEM((576, 256), F32),
             VMEM((8, 144, 128), F32),
-            pltpu.SemaphoreType.DMA,
+            pltpu.SemaphoreType.DMA((3,)),
         ],
         [meta, came, speed, synth],
         [SMEM, VMEM, VMEM, VMEM],
@@ -803,13 +843,14 @@
 
     t0, h0, *sent = run(residual_kernel, [vol, vol, edge, edge], [], head + [back, base, guess_edge])
     got = trade(*sent)
-    t1, t2, h2, to_w, to_e, keep, part = run(
+    t1, t2, h2, to_w, to_e, keep = run(
         two_steps_kernel,
-        [vol, vol, vol, edge, edge, both, shape(8, 128)],
-        work(5),
+        [vol, vol, vol, edge, edge, both],
+        [VMEM((96, 128), F32)],
         head + edges + [t0, h0, *sent, *got],
     )
     got = trade(to_w, to_e)
+    part = run(sums_kernel, [shape(8, 128)], work(5)[1:], [t0, t1, t2])[0]
     t3, red = run(
         last_steps_kernel,
         [vol, shape(16, 8, 128)],

time: 74.6 us -> 76.8 us (1.029)
  Pallas kernels: 17 us -> 19.8 us
    pallas_call x9 -> x10, Pallas kernels: 17 us -> 19.8 us  [call(): pl.pallas_call(kernel, out_shape=outs, in_specs=[pl.BlockSpec(memory_spac...]
where the time goes in v6:
time: 76.8 us; the launch traced here: 76.5 us
  waiting for transfers between devices  25.9 us (34%)
  starting transfers between devices  20.4 us (27%)
  Pallas kernels  19.8 us (26%)
  blocking collectives  10.2 us (13%)
    pallas_call x10, Pallas kernels, call(): pl.pallas_call(kernel, out_shape=outs, in_specs=[pl.BlockSpec(memory_spac...  19.8 us
    ppermute x6, waiting for transfers between devices, shift_by(): lax.ppermute(array, 'elem', [(i, (i + by) % count) for i in range(count)])  19 us
    ppermute x6, starting transfers between devices, shift_by(): lax.ppermute(array, 'elem', [(i, (i + by) % count) for i in range(count)])  12.3 us
    all_to_all x1, blocking collectives, shards(): red = lax.all_to_all(red, 'elem', 0, 0, tiled=True)  10.2 us
    all_to_all x1, waiting for transfers between devices, shards(): came = lax.all_to_all(packed, 'plane', 0, 0, tiled=True)  6.95 us
    all_to_all x1, starting transfers between devices, shards(): came = lax.all_to_all(packed, 'plane', 0, 0, tiled=True)  4.53 us
    all_to_all x1, starting transfers between devices, shards(): back = lax.all_to_all(back, 'plane', 0, 0, tiled=True)  3.55 us
  transfers between devices with their start and end apart: 8, of which 7 were waited for; matrix products, arithmetic and copies ran while one was open for 0% of the time, Pallas kernels for 6%

profile of v6, /device:TPU:0, one launch (start us, length us, event | category | flops | bytes accessed | tf_op | source)
XLA Modules:
  0.0 76.5 jit_solution(11471217489164861446)
XLA Ops:
  0.0 2.6 %shard_map.74 = f32[8,144,128]{2,1,0:T(8,128)} custom-call(f32[36,32,128]{2,1,0:T(8,128)} %bitcast.13), custom_call_target="tpu_custom_call" | custom-call | flops 4000000 | bytes 1179648 | tf_op jit(solution)/shard_map/pallas_call | solution.py:109
  2.7 4.5 %all-to-all-start = ((f32[8,144,128]{2,1,0:T(8,128)}), f32[8,144,128]{2,1,0:T(8,128)S(1)}, u32[]{:S(2)}, u32[]{:S(2)}) async-start(f32[8,144,128]{2,1,0:T(8,128)} %shard_map.74), calls=%async_computation | async-start | bytes 1179648 | tf_op jit(solution)/shard_map/all_to_all | solution.py:783
  7.2 0.1 pad_add_fusion.place
  7.3 1.7 %shard_map.73 = (s32[4]{0:T(128)S(1)}, s32[24,128]{1,0:T(8,128)S(1)}, s32[8,128]{1,0:T(8,128)S(1)}, f32[8,128]{1,0:T(8,128)S(1)}, f32[36,8,128]{2,1,0:T(8,128)S(...) custom-call(s32[2]{0:T(128)S(1)} %pad_add_fusion.place, ...), custom_call_target="tpu_custom_call" | custom-call | flops 4000000 | bytes 623640 | tf_op jit(solution)/shard_map/pallas_call | solution.py:109
  9.0 2.3 %shard_map.75 = (f32[36,32,128]{2,1,0:T(8,128)S(1)}, f32[48,128]{1,0:T(8,128)S(1)}, f32[48,128]{1,0:T(8,128)S(1)}) custom-call(s32[4]{0:T(128)S(1)} %get-tuple-element.34.meta, s32[24,128]{1,0:T(8,128)S(1)} %get-tuple-element.35.idx, f32[8,128]{1,0:T(8,128)S(1)} %get-tuple-element.36.tab, f32[36,8,128]{2,1,0:T(8,128)S(1)} %get-tuple-element.37.own_c, ...), custom_call_target="tpu_custom_call" | custom-call | flops 4000000 | bytes 1540112 | tf_op jit(solution)/shard_map/pallas_call | solution.py:109
  11.3 6.9 %all-to-all-done.came = f32[8,144,128]{2,1,0:T(8,128)S(1)} async-done(((f32[8,144,128]{2,1,0:T(8,128)}), f32[8,144,128]{2,1,0:T(8,128)S(1)}, u32[]{:S(2)}, u32[]{:S(2)}) %all-to-all-start) | async-done | bytes 589856 | tf_op jit(solution)/shard_map/all_to_all | solution.py:783
  18.2 5.4 %shard_map.76 = f32[8,144,128]{2,1,0:T(8,128)} custom-call(s32[4]{0:T(128)S(1)} %get-tuple-element.34.meta, f32[8,144,128]{2,1,0:T(8,128)S(1)} %all-to-all-done.came, f32[2,36,16,256]{3,2,1,0:T(8,128)S(1)} %bitcast.16, bf16[2,256,256]{2,1,0:T(8,128)(2,1)S(1)} %copy-done.2), custom_call_target="tpu_custom_call" | custom-call | flops 4000000 | bytes 2883600 | tf_op jit(solution)/shard_map/pallas_call | solution.py:109
  23.6 3.6 %all-to-all-start.1 = ((f32[8,144,128]{2,1,0:T(8,128)}), f32[8,144,128]{2,1,0:T(8,128)S(1)}, u32[]{:S(2)}, u32[]{:S(2)}) async-start(f32[8,144,128]{2,1,0:T(8,128)} %shard_map.76), calls=%async_computation.1 | async-start | bytes 1179648 | tf_op jit(solution)/shard_map/all_to_all | solution.py:834
  27.2 6.6 %collective-permute-start.1 = (f32[48,128]{1,0:T(8,128)S(1)}, f32[48,128]{1,0:T(8,128)S(1)}, u32[]{:S(2)}, u32[]{:S(2)}) collective-permute-start(f32[48,128]{1,0:T(8,128)S(1)} %get-tuple-element.49.to_w), channel_id=1, source_target_pairs={{0,15},{1,0},{2,1},{3,2},{4,3},{5,4},{6,5},{7,6},{8,7},{9,8},{10,9... | collective-permute-start | bytes 73736 | tf_op jit(solution)/shard_map/ppermute | solution.py:763
  33.8 1.5 %collective-permute-done.1.from_e = f32[48,128]{1,0:T(8,128)S(1)} collective-permute-done((f32[48,128]{1,0:T(8,128)S(1)}, f32[48,128]{1,0:T(8,128)S(1)}, u32[]{:S(2)}, u32[]{:S(2)}) %collective-permute-start.1) | collective-permute-done | bytes 24608 | tf_op jit(solution)/shard_map/ppermute | solution.py:763
  35.3 5.6 %collective-permute-done.from_w = f32[48,128]{1,0:T(8,128)S(1)} collective-permute-done((f32[48,128]{1,0:T(8,128)S(1)}, f32[48,128]{1,0:T(8,128)S(1)}, u32[]{:S(2)}, u32[]{:S(2)}) %collective-permute-start) | collective-permute-done | bytes 24608 | tf_op jit(solution)/shard_map/ppermute | solution.py:763
  40.9 0.2 shard_map.77.edge
  41.1 1.7 %shard_map.78 = (f32[36,32,128]{2,1,0:T(8,128)S(1)}, f32[36,32,128]{2,1,0:T(8,128)S(1)}, f32[48,128]{1,0:T(8,128)S(1)}, f32[48,128]{1,0:T(8,128)S(1)}) custom-call(s32[4]{0:T(128)S(1)} %get-tuple-element.34.meta, s32[24,128]{1,0:T(8,128)S(1)} %get-tuple-element.35.idx, f32[8,128]{1,0:T(8,128)S(1)} %get-tuple-element.36.tab, ...), custom_call_target="tpu_custom_call" | custom-call | flops 4000000 | bytes 2744336 | tf_op jit(solution)/shard_map/pallas_call | solution.py:109
  42.8 3.6 %collective-permute-start.3 = (f32[48,128]{1,0:T(8,128)S(1)}, f32[48,128]{1,0:T(8,128)S(1)}, u32[]{:S(2)}, u32[]{:S(2)}) collective-permute-start(f32[48,128]{1,0:T(8,128)S(1)} %get-tuple-element.53.to_w), channel_id=1, source_target_pairs={{0,15},{1,0},{2,1},{3,2},{4,3},{5,4},{6,5},{7,6},{8,7},{9,8},{10,9... | collective-permute-start | bytes 73736 | tf_op jit(solution)/shard_map/ppermute | solution.py:763
  46.4 1.5 %collective-permute-done.3.from_e = f32[48,128]{1,0:T(8,128)S(1)} collective-permute-done((f32[48,128]{1,0:T(8,128)S(1)}, f32[48,128]{1,0:T(8,128)S(1)}, u32[]{:S(2)}, u32[]{:S(2)}) %collective-permute-start.3) | collective-permute-done | bytes 24608 | tf_op jit(solution)/shard_map/ppermute | solution.py:763
  48.0 5.6 %collective-permute-done.2.from_w = f32[48,128]{1,0:T(8,128)S(1)} collective-permute-done((f32[48,128]{1,0:T(8,128)S(1)}, f32[48,128]{1,0:T(8,128)S(1)}, u32[]{:S(2)}, u32[]{:S(2)}) %collective-permute-start.2) | collective-permute-done | bytes 24608 | tf_op jit(solution)/shard_map/ppermute | solution.py:763
  53.6 2.2 %shard_map.79 = (f32[36,32,128]{2,1,0:T(8,128)S(1)}, f32[36,32,128]{2,1,0:T(8,128)S(1)}, f32[36,32,128]{2,1,0:T(8,128)S(1)}, f32[48,128]{1,0:T(8,128)S(1)}, f32[...) custom-call(s32[4]{0:T(128)S(1)} %get-tuple-element.34.meta, s32[24,128]{1,0:T(8,128)S(1)} %get-tuple-element.35.idx, ...), custom_call_target="tpu_custom_call" | custom-call | flops 4000000 | bytes 3756048 | tf_op jit(solution)/shard_map/pallas_call | solution.py:109
  55.9 2.0 %collective-permute-start.4 = (f32[48,128]{1,0:T(8,128)S(1)}, f32[48,128]{1,0:T(8,128)S(1)}, u32[]{:S(2)}, u32[]{:S(2)}) collective-permute-start(f32[48,128]{1,0:T(8,128)S(1)} %get-tuple-element.59.to_e), channel_id=1, source_target_pairs={{0,1},{1,2},{2,3},{3,4},{4,5},{5,6},{6,7},{7,8},{8,9},{9,10},{10,1... | collective-permute-start | bytes 73736 | tf_op jit(solution)/shard_map/ppermute | solution.py:763
  57.9 0.5 shard_map.80.part
  58.4 1.3 %collective-permute-done.5.from_e = f32[48,128]{1,0:T(8,128)S(1)} collective-permute-done((f32[48,128]{1,0:T(8,128)S(1)}, f32[48,128]{1,0:T(8,128)S(1)}, u32[]{:S(2)}, u32[]{:S(2)}) %collective-permute-start.5) | collective-permute-done | bytes 24608 | tf_op jit(solution)/shard_map/ppermute | solution.py:763
  59.7 3.4 %collective-permute-done.4.from_w = f32[48,128]{1,0:T(8,128)S(1)} collective-permute-done((f32[48,128]{1,0:T(8,128)S(1)}, f32[48,128]{1,0:T(8,128)S(1)}, u32[]{:S(2)}, u32[]{:S(2)}) %collective-permute-start.4) | collective-permute-done | bytes 24608 | tf_op jit(solution)/shard_map/ppermute | solution.py:763
  63.1 1.9 %shard_map.81 = (f32[36,32,128]{2,1,0:T(8,128)S(1)}, f32[16,8,128]{2,1,0:T(8,128)S(1)}) custom-call(s32[4]{0:T(128)S(1)} %get-tuple-element.34.meta, s32[24,128]{1,0:T(8,128)S(1)} %get-tuple-element.35.idx, f32[8,128]{1,0:T(8,128)S(1)} %get-tuple-element.36.tab, f32[36,8,128]{2,1,0:T(8,128)S(1)} %get-tuple-element.37.own_c, ...), custom_call_target="tpu_custom_call" | custom-call | flops 4000000 | bytes 3186704 | tf_op jit(solution)/shard_map/pallas_call | solution.py:109
  65.0 10.2 %all_to_all.15.red = f32[16,8,128]{2,1,0:T(8,128)S(1)} all-to-all(f32[16,8,128]{2,1,0:T(8,128)S(1)} %get-tuple-element.61), channel_id=1, replica_groups=mesh['plane'=8,'elem'=16] {'elem'}, dimensions={0} | all-to-all | bytes 131072 | tf_op jit(solution)/shard_map/all_to_all | solution.py:860
  75.2 1.3 %shard_map.82 = f32[36,32,128]{2,1,0:T(8,128)} custom-call(f32[16,8,128]{2,1,0:T(8,128)S(1)} %all_to_all.15.red, f32[36,32,128]{2,1,0:T(8,128)S(1)} %bitcast.15, f32[36,32,128]{2,1,0:T(8,128)S(1)} %get-tuple-element.51.t0, f32[36,32,128]{2,1,0:T(8,128)S(1)} %get-tuple-element.55.t1, f32[36,32,128]{2,1,0:T(8,128)S(1)} %get-tuple-element.56.t2, ...), custom_call_target="tpu_custom_call" | custom-call | flops 4000000 | bytes 3604480 | tf_op jit(solution)/shard_map/pallas_call | solution.py:109
  (18 shorter events, 0.1 us)
Async XLA Ops:
  0.0 7.3 %copy-start.3 = (s32[2,8,128]{2,1,0:T(8,128)S(1)}, s32[2,8,128]{2,1,0:T(8,128)}, u32[]{:S(2)}) copy-start(s32[2,8,128]{2,1,0:T(8,128)} %sides.1) | copy-start | bytes 24580
  0.0 7.3 %copy-start.4 = (s32[8,128]{1,0:T(8,128)S(1)}, s32[8,128]{1,0:T(8,128)}, u32[]{:S(2)}) copy-start(s32[8,128]{1,0:T(8,128)} %links.1) | copy-start | bytes 12292
  0.0 7.3 %copy-start.5 = (f32[128]{0:T(128)S(1)}, f32[128]{0:T(128)}, u32[]{:S(2)}) copy-start(f32[128]{0:T(128)} %param.9) | copy-start | bytes 1540
  0.0 7.3 %copy-start.6 = (s32[128]{0:T(128)S(1)}, s32[128]{0:T(128)}, u32[]{:S(2)}) copy-start(s32[128]{0:T(128)} %param.12) | copy-start | bytes 1540
  2.6 15.6 %copy-start.1 = (f32[2,256,6,6,16]{1,4,3,2,0:T(8,128)S(1)}, f32[2,256,6,6,16]{1,4,3,2,0:T(8,128)}, u32[]{:S(2)}) copy-start(f32[2,256,6,6,16]{1,4,3,2,0:T(8,128)} %param.8) | copy-start | bytes 3538948
  2.6 15.6 %copy-start.2 = (bf16[2,256,256]{2,1,0:T(8,128)(2,1)S(1)}, bf16[2,256,256]{2,1,0:T(8,128)(2,1)}, u32[]{:S(2)}) copy-start(bf16[2,256,256]{2,1,0:T(8,128)(2,1)} %constant.11.clone.synth) | copy-start | bytes 786436
  2.7 15.6 %all-to-all-start = ((f32[8,144,128]{2,1,0:T(8,128)}), f32[8,144,128]{2,1,0:T(8,128)S(1)}, u32[]{:S(2)}, u32[]{:S(2)}) async-start(f32[8,144,128]{2,1,0:T(8,128)} %shard_map.74), calls=%async_computation | async-start | bytes 1179648 | tf_op jit(solution)/shard_map/all_to_all | solution.py:783
  23.6 17.4 %all-to-all-start.1 = ((f32[8,144,128]{2,1,0:T(8,128)}), f32[8,144,128]{2,1,0:T(8,128)S(1)}, u32[]{:S(2)}, u32[]{:S(2)}) async-start(f32[8,144,128]{2,1,0:T(8,128)} %shard_map.76), calls=%async_computation.1 | async-start | bytes 1179648 | tf_op jit(solution)/shard_map/all_to_all | solution.py:834
  27.2 8.1 %collective-permute-start.1 = (f32[48,128]{1,0:T(8,128)S(1)}, f32[48,128]{1,0:T(8,128)S(1)}, u32[]{:S(2)}, u32[]{:S(2)}) collective-permute-start(f32[48,128]{1,0:T(8,128)S(1)} %get-tuple-element.49.to_w), channel_id=1, source_target_pairs={{0,15},{1,0},{2,1},{3,2},{4,3},{5,4},{6,5},{7,6},{8,7},{9,8},{10,9... | collective-permute-start | bytes 73736 | tf_op jit(solution)/shard_map/ppermute | solution.py:763
  33.8 7.1 %collective-permute-start = (f32[48,128]{1,0:T(8,128)S(1)}, f32[48,128]{1,0:T(8,128)S(1)}, u32[]{:S(2)}, u32[]{:S(2)}) collective-permute-start(f32[48,128]{1,0:T(8,128)S(1)} %get-tuple-element.50.to_e), channel_id=1, source_target_pairs={{0,1},{1,2},{2,3},{3,4},{4,5},{5,6},{6,7},{7,8},{8,9},{9,10},{10,1... | collective-permute-start | bytes 73736 | tf_op jit(solution)/shard_map/ppermute | solution.py:763
  42.8 5.2 %collective-permute-start.3 = (f32[48,128]{1,0:T(8,128)S(1)}, f32[48,128]{1,0:T(8,128)S(1)}, u32[]{:S(2)}, u32[]{:S(2)}) collective-permute-start(f32[48,128]{1,0:T(8,128)S(1)} %get-tuple-element.53.to_w), channel_id=1, source_target_pairs={{0,15},{1,0},{2,1},{3,2},{4,3},{5,4},{6,5},{7,6},{8,7},{9,8},{10,9... | collective-permute-start | bytes 73736 | tf_op jit(solution)/shard_map/ppermute | solution.py:763
  46.4 7.1 %collective-permute-start.2 = (f32[48,128]{1,0:T(8,128)S(1)}, f32[48,128]{1,0:T(8,128)S(1)}, u32[]{:S(2)}, u32[]{:S(2)}) collective-permute-start(f32[48,128]{1,0:T(8,128)S(1)} %get-tuple-element.54.to_e), channel_id=1, source_target_pairs={{0,1},{1,2},{2,3},{3,4},{4,5},{5,6},{6,7},{7,8},{8,9},{9,10},{10,1... | collective-permute-start | bytes 73736 | tf_op jit(solution)/shard_map/ppermute | solution.py:763
  55.8 3.9 %collective-permute-start.5 = (f32[48,128]{1,0:T(8,128)S(1)}, f32[48,128]{1,0:T(8,128)S(1)}, u32[]{:S(2)}, u32[]{:S(2)}) collective-permute-start(f32[48,128]{1,0:T(8,128)S(1)} %get-tuple-element.58.to_w), channel_id=1, source_target_pairs={{0,15},{1,0},{2,1},{3,2},{4,3},{5,4},{6,5},{7,6},{8,7},{9,8},{10,9... | collective-permute-start | bytes 73736 | tf_op jit(solution)/shard_map/ppermute | solution.py:763
  55.9 7.2 %collective-permute-start.4 = (f32[48,128]{1,0:T(8,128)S(1)}, f32[48,128]{1,0:T(8,128)S(1)}, u32[]{:S(2)}, u32[]{:S(2)}) collective-permute-start(f32[48,128]{1,0:T(8,128)S(1)} %get-tuple-element.59.to_e), channel_id=1, source_target_pairs={{0,1},{1,2},{2,3},{3,4},{4,5},{5,6},{6,7},{7,8},{8,9},{9,10},{10,1... | collective-permute-start | bytes 73736 | tf_op jit(solution)/shard_map/ppermute | solution.py:763
  63.1 12.1 %copy-start = (f32[32,6,6,128]{3,0,2,1:T(8,128)S(1)}, f32[32,6,6,128]{3,0,2,1:T(8,128)}, u32[]{:S(2)}) copy-start(f32[32,6,6,128]{3,0,2,1:T(8,128)} %param.7) | copy-start | bytes 1769476

commit v7 on v5

--- a/solution.py
+++ b/solution.py
@@ -16,7 +16,8 @@
 VMEM = pltpu.VMEM
 SMEM = pltpu.SMEM
 HBM = pltpu.HBM
-SELF, ANY, LOCAL = 2, 4, 10
+MIXED = 7
+SELF, ANY, FIRST, LAYOUT, LOCAL = 2, 4, 6, 7, 10
 
 
 def lagrange_at(points, targets):
@@ -135,7 +136,7 @@
 
 
 def prep_kernel(
-    place, links, sides, visc, layout, meta, idx, edge_idx, tab, own_c, far_c, edge_own, edge_far
+    place, links, sides, visc, layout, idx, edge_idx, tab, own_c, far_c, edge_own, edge_far
 ):
     me = place[1]
     dev = lax.shift_right_logical(links[...], 7)
@@ -147,10 +148,8 @@
     whole = (inside == 0) & (other == 0)
     second = jnp.bitwise_and(lax.broadcasted_iota(jnp.int32, (8, 128), 0), 1) == 1
     odd_one = jnp.where(inside == 3, 0.0, jnp.where(whole & ~second, 0.0, 1.0))
-    meta[0] = place[0]
-    meta[1] = place[1]
-    meta[2] = jnp.max(odd_one).astype(jnp.int32)
-    meta[3] = jnp.max(layout[...].astype(F32)).astype(jnp.int32)
+    idx[FIRST : FIRST + 1, :] = jnp.full((1, 128), 32 * place[0], jnp.int32)
+    idx[LAYOUT : LAYOUT + 1, :] = layout[...]
     row = lax.broadcasted_iota(jnp.int32, (128, 128), 0)
     col = lane_ids((128, 128))
     lane = lane_ids((1, 128))
@@ -177,7 +176,7 @@
         for t in range(2):
             rank = jnp.sum(jnp.where(row < far[t], named, 0.0), axis=0, keepdims=True)
             ranks.append(jnp.where(rem[t] > 0, rank.astype(jnp.int32), 0))
-    idx[6:10, :] = jnp.zeros((4, 128), jnp.int32)
+    idx[8:10, :] = jnp.zeros((2, 128), jnp.int32)
     idx[18:24, :] = jnp.zeros((6, 128), jnp.int32)
 
     west = lane < 64
@@ -227,7 +226,7 @@
     tab[2:3, :] = nu
     for face in range(4):
         tab[3 + face : 4 + face, :] = whole[2 * face : 2 * face + 1].astype(F32)
-    tab[7:8, :] = jnp.zeros((1, 128), F32)
+    tab[MIXED : MIXED + 1, :] = jnp.max(odd_one, axis=0, keepdims=True)
     mine_m = [PENALTY * HALVES[o].T @ np.diag(W) @ HALVES[o] for o in range(3)]
     far_m = [
         [-PENALTY * HALVES[o].T @ np.diag(W) @ HALVES[c] for c in range(3)] for o in range(3)
@@ -266,12 +265,15 @@
     ]
 
 
-def either(meta, loop):
+def either(tab, loop):
+    mixed = jnp.max(tab[MIXED : MIXED + 1, :]) > 0.5
     for plain in (True, False):
 
-        @pl.when((meta[2] == 0) == plain)
+        @pl.when(mixed != plain)
         def _(plain=plain):
-            lax.fori_loop(0, 4, lambda group, carry: loop(group, plain) or carry, 0)
+            lax.fori_loop(
+                0, 4, lambda group, carry: loop(group, plain) or carry, 0, unroll=2 if plain else 1
+            )
 
 
 def weighted(factors, values):
@@ -282,7 +284,7 @@
 
 
 def plain_terms(env, v):
-    _, idx, tab, _, _ = env
+    idx, tab, _, _ = env
 
     def of_face(face):
         active = row_of(tab, 3 + face)
@@ -298,7 +300,7 @@
 
 
 def general_terms(env, v):
-    _, idx, _, own_c, far_c = env
+    idx, _, own_c, far_c = env
     found = []
     for face in range(4):
         mine = [v(n) for n in face_nodes(face)]
@@ -320,14 +322,14 @@
 
 
 def inner(group, env, v_ref, plain, emit):
-    meta, _, tab, _, _ = env
+    idx, tab, _, _ = env
     rows = group_rows(group)
 
     def v(n):
         return v_ref[n, rows, :]
 
     terms = (plain_terms if plain else general_terms)(env, v)
-    q = meta[0] * 32 + group * 8 + lax.broadcasted_iota(jnp.int32, (8, 128), 0)
+    q = row_of(idx, FIRST) + group * 8 + lax.broadcasted_iota(jnp.int32, (8, 128), 0)
     harmonic = lax.shift_right_logical(q + 1, 1).astype(F32) * SPANWISE
     cx, cy = row_of(tab, 0), row_of(tab, 1)
     shift = 1.0 + 0.5 * tab[2:3, :] * (harmonic * harmonic)
@@ -350,17 +352,18 @@
                 emit(n, value)
 
 
-def compact(group, idx, v_ref, h_ref, send_w, send_e):
-    rows = group_rows(group)
+def compact(idx, v_ref, h_ref, send_w, send_e):
     part = lax.shift_right_logical(lane_ids((8, 128)), 4)
     for face, ref in ((0, send_w), (1, send_e)):
         index = row_of(idx, face)
         for b in range(6):
             n = face_nodes(face)[b]
-            low, high = take(v_ref[n, rows, :], index), take(h_ref[n, rows, :], index)
-            old = ref[8 * b : 8 * b + 8, :]
-            new = jnp.where(part == group, low, jnp.where(part == group + 4, high, old))
-            ref[8 * b : 8 * b + 8, :] = new
+            value = take(v_ref[n, 0:8, :], index)
+            for k in range(1, 8):
+                source = v_ref if k < 4 else h_ref
+                other = take(source[n, 8 * (k % 4) : 8 * (k % 4) + 8, :], index)
+                value = jnp.where(part == k, other, value)
+            ref[8 * b : 8 * b + 8, :] = value
 
 
 def outer(group, idx, edge, first):
@@ -425,8 +428,8 @@
     return emit
 
 
-def guess_kernel(meta, idx, tab, own_c, far_c, u_far, out, send_w, send_e, u, sem):
-    env = (meta, idx, tab, own_c, far_c)
+def guess_kernel(idx, tab, own_c, far_c, u_far, out, send_w, send_e, u, sem):
+    env = (idx, tab, own_c, far_c)
     copy = pltpu.make_async_copy(u_far, u, sem)
     copy.start()
     copy.wait()
@@ -438,9 +441,9 @@
             out[n, rows, :] = float(W[n // 6] * W[n % 6]) * u[n, rows, :] - value
 
         inner(group, env, u, plain, emit)
-        compact(group, idx, u, u, send_w, send_e)
-
-    either(meta, loop)
+
+    either(tab, loop)
+    compact(idx, u, u, send_w, send_e)
 
 
 def guess_edge_kernel(edge_idx, edge_own, edge_far, to_w, to_e, from_w, from_e, edge):
@@ -451,23 +454,27 @@
 
 
 def residual_kernel(
-    meta, idx, tab, own_c, far_c, back, base, edge, out, h_out, send_w, send_e
+    idx, tab, own_c, far_c, back, base, edge, out, h_out, send_w, send_e
 ):
-    env = (meta, idx, tab, own_c, far_c)
-    for g in range(9):
-        turned = back[:, 16 * g : 16 * g + 16, :].reshape(128, 128).T
+    env = (idx, tab, own_c, far_c)
+
+    def turn(g, carry):
+        part = pl.ds(pl.multiple_of(16 * g, 16), 16)
+        turned = back[:, part, :].reshape(128, 128).T
         for m in range(4):
-            n = 4 * g + m
-            out[n] = base[n] + turned[32 * m : 32 * m + 32]
+            out[4 * g + m] = base[4 * g + m] + turned[32 * m : 32 * m + 32]
+        return carry
+
+    lax.fori_loop(0, 9, turn, 0, unroll=3)
 
     def loop(group, plain):
         rows = group_rows(group)
         for n, extra in outer(group, idx, edge, 0).items():
             out[n, rows, :] -= extra
         inner(group, env, out, plain, store(h_out, rows))
-        compact(group, idx, out, h_out, send_w, send_e)
-
-    either(meta, loop)
+
+    either(tab, loop)
+    compact(idx, out, h_out, send_w, send_e)
 
 
 def edge_steps(tables, to_w, to_e, from_w, from_e, before, edge, keep):
@@ -496,55 +503,59 @@
 
 
 def two_steps_kernel(
-    meta, idx, tab, own_c, far_c, edge_idx, edge_own, edge_far,
+    idx, tab, own_c, far_c, edge_idx, edge_own, edge_far,
     t0, h0, to_w, to_e, from_w, from_e,
-    t1, t2, h2, send_w, send_e, keep, part, edge, acc, pad,
+    t1, t2, h2, send_w, send_e, keep, edge,
 ):
-    env = (meta, idx, tab, own_c, far_c)
+    env = (idx, tab, own_c, far_c)
     tables = (edge_idx, edge_own, edge_far)
     edge_steps(tables, to_w, to_e, from_w, from_e, None, edge, keep)
 
     def loop(group, plain):
         rows = group_rows(group)
         extra = outer(group, idx, edge, 0)
-        sums = [jnp.zeros((8, 128), F32)] * 5
         for n in range(36):
             image = h0[n, rows, :]
             if n in extra:
                 image = image + extra[n]
-            a = t0[n, rows, :]
-            b = (1.0 / HALF) * image - a
-            t1[n, rows, :] = b
-            for k, term in enumerate((a * a, a * b, b * b)):
-                sums[k] = sums[k] + term
+            t1[n, rows, :] = (1.0 / HALF) * image - t0[n, rows, :]
         extra_next = outer(group, idx, edge, 48)
 
         def emit(n, image):
             if n in extra_next:
                 image = image + extra_next[n]
-            b = t1[n, rows, :]
-            c = (2.0 / HALF) * image - 2.0 * b - t0[n, rows, :]
-            t2[n, rows, :] = c
-            sums[3] = sums[3] + b * c
-            sums[4] = sums[4] + c * c
+            t2[n, rows, :] = (2.0 / HALF) * image - 2.0 * t1[n, rows, :] - t0[n, rows, :]
 
         inner(group, env, t1, plain, emit)
+        inner(group, env, t2, plain, store(h2, rows))
+
+    either(tab, loop)
+    compact(idx, t2, h2, send_w, send_e)
+
+
+def sums_kernel(t0, t1, t2, part, acc, pad):
+    def body(group, carry):
+        rows = group_rows(group)
+        sums = [jnp.zeros((8, 128), F32)] * 5
+        for n in range(36):
+            a, b, c = t0[n, rows, :], t1[n, rows, :], t2[n, rows, :]
+            for k, term in enumerate((a * a, a * b, b * b, b * c, c * c)):
+                sums[k] = sums[k] + term
         for k in range(5):
             acc[rows, 128 * k : 128 * k + 128] = sums[k]
-        inner(group, env, t2, plain, store(h2, rows))
-        compact(group, idx, t2, h2, send_w, send_e)
-
-    either(meta, loop)
+        return carry
+
+    lax.fori_loop(0, 4, body, 0)
     store_sums(acc, pad, 0, 5)
     part[...] = pad[...]
 
 
 def last_steps_kernel(
-    meta, idx, tab, own_c, far_c, edge_idx, edge_own, edge_far,
+    idx, tab, own_c, far_c, edge_idx, edge_own, edge_far,
     t1, t2, h2, to_w, to_e, from_w, from_e, keep, part,
     t3, red, edge, acc, pad,
 ):
-    env = (meta, idx, tab, own_c, far_c)
+    env = (idx, tab, own_c, far_c)
     tables = (edge_idx, edge_own, edge_far)
     edge_steps(tables, to_w, to_e, from_w, from_e, keep, edge, None)
 
@@ -573,7 +584,7 @@
         for k in range(3):
             acc[rows, 128 * k : 128 * k + 128] = sums[k]
 
-    either(meta, loop)
+    either(tab, loop)
     store_sums(acc, pad, 5, 3)
     row = lax.broadcasted_iota(jnp.int32, (8, 128), 0)
     mixed = jnp.where(row < 5, part[...], pad[...])
@@ -624,8 +635,12 @@
         coef[k] = jnp.broadcast_to(turned[0:32, k : k + 1], (32, 128))
     copies = []
     for c in range(3):
-        for n in range(12 * c, 12 * c + 12):
-            held[n] = x0[n] + coef[0] * t0[n] + coef[1] * t1[n] + coef[2] * t2[n] + coef[3] * t3[n]
+        def add(n, carry):
+            terms = coef[0] * t0[n] + coef[1] * t1[n] + coef[2] * t2[n] + coef[3] * t3[n]
+            held[n] = x0[n] + terms
+            return carry
+
+        lax.fori_loop(12 * c, 12 * c + 12, add, 0, unroll=3)
         part = pl.ds(12 * c, 12)
         copies.append(pltpu.make_async_copy(held.at[part], out.at[part], sems.at[c]))
         copies[c].start()
@@ -670,7 +685,7 @@
     return dot(high, table[0]) + dot(high, table[1]) + dot(low, table[0])
 
 
-def advect_kernel(meta, came, speed, synth, out, high, low, phys, ready, sem):
+def advect_kernel(idx, came, speed, synth, out, high, low, phys, ready, sem):
     for g in range(9):
         for h in range(2):
             pieces = block_turn([came[4 * h + s, 16 * g : 16 * g + 16, :] for s in range(4)])
@@ -682,7 +697,7 @@
     for i in range(2):
         part = slice(288 * i, 288 * i + 288)
         phys[part, :] = product3(high[part, :], low[part, :], synth, 1)
-    wide = meta[3] == 0
+    wide = jnp.broadcast_to(idx[LAYOUT : LAYOUT + 1, :], (16, 128)) == 0
     sx = jnp.where(wide, 2.0, 1.0)
     sy = jnp.where(wide, 1.0, 2.0)
     for h in range(2):
@@ -744,10 +759,9 @@
     came = lax.all_to_all(packed, "plane", 0, 0, tiled=True)
 
     table = shape(36, 8, 128)
-    meta, idx, edge_idx, tab, own_c, far_c, edge_own, edge_far = call(
+    idx, edge_idx, tab, own_c, far_c, edge_own, edge_far = call(
         prep_kernel,
         [
-            shape(4, dtype=jnp.int32),
             shape(24, 128, dtype=jnp.int32),
             shape(8, 128, dtype=jnp.int32),
             shape(8, 128),
@@ -756,13 +770,12 @@
         [],
         [place, mortar_links, mortar_sides, viscosity[None], layout[None]],
         [SMEM] + [VMEM] * 4,
-        [SMEM] + [VMEM] * 7,
     )
-    head = [meta, idx, tab, own_c, far_c]
+    head = [idx, tab, own_c, far_c]
     edges = [edge_idx, edge_own, edge_far]
 
     def run(kernel, outs, scratch, args):
-        return call(kernel, outs, scratch, args, [SMEM if a is meta else VMEM for a in args])
+        return call(kernel, outs, scratch, args, [VMEM] * len(args))
 
     def trade(send_w, send_e):
         return shift_by(send_e, 1), shift_by(send_w, -1)
@@ -772,7 +785,7 @@
         [vol, edge, edge],
         [VMEM((36, 32, 128), F32), pltpu.SemaphoreType.DMA],
         head + [u],
-        [SMEM] + [VMEM] * 4 + [HBM],
+        [VMEM] * 4 + [HBM],
     )
     came, *sent = lax.optimization_barrier((came, *sent))
     back = call(
@@ -785,8 +798,8 @@
             VMEM((8, 144, 128), F32),
             pltpu.SemaphoreType.DMA,
         ],
-        [meta, came, speed, synth],
-        [SMEM, VMEM, VMEM, VMEM],
+        [idx, came, speed, synth],
+        [VMEM] * 4,
         [HBM],
         grant=8,
     )[0]
@@ -803,13 +816,14 @@
 
     t0, h0, *sent = run(residual_kernel, [vol, vol, edge, edge], [], head + [back, base, guess_edge])
     got = trade(*sent)
-    t1, t2, h2, to_w, to_e, keep, part = run(
+    t1, t2, h2, to_w, to_e, keep = run(
         two_steps_kernel,
-        [vol, vol, vol, edge, edge, both, shape(8, 128)],
-        work(5),
+        [vol, vol, vol, edge, edge, both],
+        [VMEM((96, 128), F32)],
         head + edges + [t0, h0, *sent, *got],
     )
     got = trade(to_w, to_e)
+    part = run(sums_kernel, [shape(8, 128)], work(5)[1:], [t0, t1, t2])[0]
     t3, red = run(
         last_steps_kernel,
         [vol, shape(16, 8, 128)],

time: 74.6 us -> 71.9 us (0.964)
  Pallas kernels: 17 us -> 13.8 us
    pallas_call x9 -> x10, Pallas kernels: 17 us -> 13.8 us  [call(): pl.pallas_call(kernel, out_shape=outs, in_specs=[pl.BlockSpec(memory_spac...]
    all_to_all x1, waiting for transfers between devices: 7.02 us -> 7.94 us  [shards(): came = lax.all_to_all(packed, 'plane', 0, 0, tiled=True)]
  transfers between devices with their start and end apart: 8 -> 8, of which waited for: 7 -> 7; matrix products, arithmetic and copies ran while one was open for 0% -> 0% of each run, Pallas kernels for 6% -> 5%
where the time goes in v7:
time: 71.9 us; the launch traced here: 71.5 us
  waiting for transfers between devices  26.9 us (37%)
  starting transfers between devices  20.4 us (28%)
  Pallas kernels  13.8 us (19%)
  blocking collectives  10.2 us (14%)
    ppermute x6, waiting for transfers between devices, shift_by(): lax.ppermute(array, 'elem', [(i, (i + by) % count) for i in range(count)])  19 us
    pallas_call x10, Pallas kernels, call(): pl.pallas_call(kernel, out_shape=outs, in_specs=[pl.BlockSpec(memory_spac...  13.8 us
    ppermute x6, starting transfers between devices, shift_by(): lax.ppermute(array, 'elem', [(i, (i + by) % count) for i in range(count)])  12.3 us
    all_to_all x1, blocking collectives, shards(): red = lax.all_to_all(red, 'elem', 0, 0, tiled=True)  10.2 us
    all_to_all x1, waiting for transfers between devices, shards(): came = lax.all_to_all(packed, 'plane', 0, 0, tiled=True)  7.94 us
    all_to_all x1, starting transfers between devices, shards(): came = lax.all_to_all(packed, 'plane', 0, 0, tiled=True)  4.53 us
    all_to_all x1, starting transfers between devices, shards(): back = lax.all_to_all(back, 'plane', 0, 0, tiled=True)  3.55 us
  transfers between devices with their start and end apart: 8, of which 7 were waited for; matrix products, arithmetic and copies ran while one was open for 0% of the time, Pallas kernels for 5%

profile of v7, /device:TPU:0, one launch (start us, length us, event | category | flops | bytes accessed | tf_op | source)
XLA Modules:
  0.0 71.5 jit_solution(16020927659819199735)
XLA Ops:
  0.0 2.1 %shard_map.74 = f32[8,144,128]{2,1,0:T(8,128)} custom-call(f32[36,32,128]{2,1,0:T(8,128)} %bitcast.13), custom_call_target="tpu_custom_call" | custom-call | flops 4000000 | bytes 1179648 | tf_op jit(solution)/shard_map/pallas_call | solution.py:110
  2.2 4.5 %all-to-all-start = ((f32[8,144,128]{2,1,0:T(8,128)}), f32[8,144,128]{2,1,0:T(8,128)S(1)}, u32[]{:S(2)}, u32[]{:S(2)}) async-start(f32[8,144,128]{2,1,0:T(8,128)} %shard_map.74), calls=%async_computation | async-start | bytes 1179648 | tf_op jit(solution)/shard_map/all_to_all | solution.py:759
  6.7 0.1 pad_add_fusion.place
  6.8 1.2 %shard_map.73 = (s32[24,128]{1,0:T(8,128)S(1)}, s32[8,128]{1,0:T(8,128)S(1)}, f32[8,128]{1,0:T(8,128)S(1)}, f32[36,8,128]{2,1,0:T(8,128)S(1)}, f32[36,8,128]{2,1...) custom-call(s32[2]{0:T(128)S(1)} %pad_add_fusion.place, s32[8,128]{1,0:T(8,128)S(1)} %copy-done.4, ...), custom_call_target="tpu_custom_call" | custom-call | flops 4000000 | bytes 623624 | tf_op jit(solution)/shard_map/pallas_call | solution.py:110
  7.9 1.8 %shard_map.75 = (f32[36,32,128]{2,1,0:T(8,128)S(1)}, f32[48,128]{1,0:T(8,128)S(1)}, f32[48,128]{1,0:T(8,128)S(1)}) custom-call(s32[24,128]{1,0:T(8,128)S(1)} %get-tuple-element.33.idx, f32[8,128]{1,0:T(8,128)S(1)} %get-tuple-element.34.tab, f32[36,8,128]{2,1,0:T(8,128)S(1)} %get-tuple-element.35.own_c, f32[36,8,128]{2,1,0:T(8,128)S(1)} %get-tuple-element.36.far_c, ...), custom_call_target="tpu_custom_call" | custom-call | flops 4000000 | bytes 1540096 | tf_op jit(solution)/shard_map/pallas_call | solution.py:110
  9.8 7.9 %all-to-all-done.came = f32[8,144,128]{2,1,0:T(8,128)S(1)} async-done(((f32[8,144,128]{2,1,0:T(8,128)}), f32[8,144,128]{2,1,0:T(8,128)S(1)}, u32[]{:S(2)}, u32[]{:S(2)}) %all-to-all-start) | async-done | bytes 589856 | tf_op jit(solution)/shard_map/all_to_all | solution.py:759
  17.7 2.5 %shard_map.76 = f32[8,144,128]{2,1,0:T(8,128)} custom-call(s32[24,128]{1,0:T(8,128)S(1)} %get-tuple-element.33.idx, f32[8,144,128]{2,1,0:T(8,128)S(1)} %all-to-all-done.came, f32[2,36,16,256]{3,2,1,0:T(8,128)S(1)} %bitcast.16, bf16[2,256,256]{2,1,0:T(8,128)(2,1)S(1)} %copy-done.2), custom_call_target="tpu_custom_call" | custom-call | flops 4000000 | bytes 2895872 | tf_op jit(solution)/shard_map/pallas_call | solution.py:110
  20.3 3.6 %all-to-all-start.1 = ((f32[8,144,128]{2,1,0:T(8,128)}), f32[8,144,128]{2,1,0:T(8,128)S(1)}, u32[]{:S(2)}, u32[]{:S(2)}) async-start(f32[8,144,128]{2,1,0:T(8,128)} %shard_map.76), calls=%async_computation.1 | async-start | bytes 1179648 | tf_op jit(solution)/shard_map/all_to_all | solution.py:807
  23.8 6.6 %collective-permute-start.1 = (f32[48,128]{1,0:T(8,128)S(1)}, f32[48,128]{1,0:T(8,128)S(1)}, u32[]{:S(2)}, u32[]{:S(2)}) collective-permute-start(f32[48,128]{1,0:T(8,128)S(1)} %get-tuple-element.47.to_w), channel_id=1, source_target_pairs={{0,15},{1,0},{2,1},{3,2},{4,3},{5,4},{6,5},{7,6},{8,7},{9,8},{10,9... | collective-permute-start | bytes 73736 | tf_op jit(solution)/shard_map/ppermute | solution.py:739
  30.4 1.5 %collective-permute-done.1.from_e = f32[48,128]{1,0:T(8,128)S(1)} collective-permute-done((f32[48,128]{1,0:T(8,128)S(1)}, f32[48,128]{1,0:T(8,128)S(1)}, u32[]{:S(2)}, u32[]{:S(2)}) %collective-permute-start.1) | collective-permute-done | bytes 24608 | tf_op jit(solution)/shard_map/ppermute | solution.py:739
  31.9 5.6 %collective-permute-done.from_w = f32[48,128]{1,0:T(8,128)S(1)} collective-permute-done((f32[48,128]{1,0:T(8,128)S(1)}, f32[48,128]{1,0:T(8,128)S(1)}, u32[]{:S(2)}, u32[]{:S(2)}) %collective-permute-start) | collective-permute-done | bytes 24608 | tf_op jit(solution)/shard_map/ppermute | solution.py:739
  37.5 0.2 shard_map.77.edge
  37.7 1.2 %shard_map.78 = (f32[36,32,128]{2,1,0:T(8,128)S(1)}, f32[36,32,128]{2,1,0:T(8,128)S(1)}, f32[48,128]{1,0:T(8,128)S(1)}, f32[48,128]{1,0:T(8,128)S(1)}) custom-call(s32[24,128]{1,0:T(8,128)S(1)} %get-tuple-element.33.idx, f32[8,128]{1,0:T(8,128)S(1)} %get-tuple-element.34.tab, f32[36,8,128]{2,1,0:T(8,128)S(1)} %get-tuple-element.35.own_c, ...), custom_call_target="tpu_custom_call" | custom-call | flops 4000000 | bytes 2744320 | tf_op jit(solution)/shard_map/pallas_call | solution.py:110
  38.9 3.6 %collective-permute-start.3 = (f32[48,128]{1,0:T(8,128)S(1)}, f32[48,128]{1,0:T(8,128)S(1)}, u32[]{:S(2)}, u32[]{:S(2)}) collective-permute-start(f32[48,128]{1,0:T(8,128)S(1)} %get-tuple-element.51.to_w), channel_id=1, source_target_pairs={{0,15},{1,0},{2,1},{3,2},{4,3},{5,4},{6,5},{7,6},{8,7},{9,8},{10,9... | collective-permute-start | bytes 73736 | tf_op jit(solution)/shard_map/ppermute | solution.py:739
  42.6 1.5 %collective-permute-done.3.from_e = f32[48,128]{1,0:T(8,128)S(1)} collective-permute-done((f32[48,128]{1,0:T(8,128)S(1)}, f32[48,128]{1,0:T(8,128)S(1)}, u32[]{:S(2)}, u32[]{:S(2)}) %collective-permute-start.3) | collective-permute-done | bytes 24608 | tf_op jit(solution)/shard_map/ppermute | solution.py:739
  44.1 5.6 %collective-permute-done.2.from_w = f32[48,128]{1,0:T(8,128)S(1)} collective-permute-done((f32[48,128]{1,0:T(8,128)S(1)}, f32[48,128]{1,0:T(8,128)S(1)}, u32[]{:S(2)}, u32[]{:S(2)}) %collective-permute-start.2) | collective-permute-done | bytes 24608 | tf_op jit(solution)/shard_map/ppermute | solution.py:739
  49.7 1.6 %shard_map.79 = (f32[36,32,128]{2,1,0:T(8,128)S(1)}, f32[36,32,128]{2,1,0:T(8,128)S(1)}, f32[36,32,128]{2,1,0:T(8,128)S(1)}, f32[48,128]{1,0:T(8,128)S(1)}, f32[...) custom-call(s32[24,128]{1,0:T(8,128)S(1)} %get-tuple-element.33.idx, f32[8,128]{1,0:T(8,128)S(1)} %get-tuple-element.34.tab, ...), custom_call_target="tpu_custom_call" | custom-call | flops 4000000 | bytes 3756032 | tf_op jit(solution)/shard_map/pallas_call | solution.py:110
  51.5 2.0 %collective-permute-start.4 = (f32[48,128]{1,0:T(8,128)S(1)}, f32[48,128]{1,0:T(8,128)S(1)}, u32[]{:S(2)}, u32[]{:S(2)}) collective-permute-start(f32[48,128]{1,0:T(8,128)S(1)} %get-tuple-element.57.to_e), channel_id=1, source_target_pairs={{0,1},{1,2},{2,3},{3,4},{4,5},{5,6},{6,7},{7,8},{8,9},{9,10},{10,1... | collective-permute-start | bytes 73736 | tf_op jit(solution)/shard_map/ppermute | solution.py:739
  53.5 0.5 shard_map.80.part
  54.0 1.3 %collective-permute-done.5.from_e = f32[48,128]{1,0:T(8,128)S(1)} collective-permute-done((f32[48,128]{1,0:T(8,128)S(1)}, f32[48,128]{1,0:T(8,128)S(1)}, u32[]{:S(2)}, u32[]{:S(2)}) %collective-permute-start.5) | collective-permute-done | bytes 24608 | tf_op jit(solution)/shard_map/ppermute | solution.py:739
  55.3 3.4 %collective-permute-done.4.from_w = f32[48,128]{1,0:T(8,128)S(1)} collective-permute-done((f32[48,128]{1,0:T(8,128)S(1)}, f32[48,128]{1,0:T(8,128)S(1)}, u32[]{:S(2)}, u32[]{:S(2)}) %collective-permute-start.4) | collective-permute-done | bytes 24608 | tf_op jit(solution)/shard_map/ppermute | solution.py:739
  58.7 1.4 %shard_map.81 = (f32[36,32,128]{2,1,0:T(8,128)S(1)}, f32[16,8,128]{2,1,0:T(8,128)S(1)}) custom-call(s32[24,128]{1,0:T(8,128)S(1)} %get-tuple-element.33.idx, f32[8,128]{1,0:T(8,128)S(1)} %get-tuple-element.34.tab, f32[36,8,128]{2,1,0:T(8,128)S(1)} %get-tuple-element.35.own_c, f32[36,8,128]{2,1,0:T(8,128)S(1)} %get-tuple-element.36.far_c, ...), custom_call_target="tpu_custom_call" | custom-call | flops 4000000 | bytes 3186688 | tf_op jit(solution)/shard_map/pallas_call | solution.py:110
  60.0 10.2 %all_to_all.15.red = f32[16,8,128]{2,1,0:T(8,128)S(1)} all-to-all(f32[16,8,128]{2,1,0:T(8,128)S(1)} %get-tuple-element.59), channel_id=1, replica_groups=mesh['plane'=8,'elem'=16] {'elem'}, dimensions={0} | all-to-all | bytes 131072 | tf_op jit(solution)/shard_map/all_to_all | solution.py:833
  70.3 1.2 %shard_map.82 = f32[36,32,128]{2,1,0:T(8,128)} custom-call(f32[16,8,128]{2,1,0:T(8,128)S(1)} %all_to_all.15.red, f32[36,32,128]{2,1,0:T(8,128)S(1)} %bitcast.15, f32[36,32,128]{2,1,0:T(8,128)S(1)} %get-tuple-element.49.t0, f32[36,32,128]{2,1,0:T(8,128)S(1)} %get-tuple-element.53.t1, f32[36,32,128]{2,1,0:T(8,128)S(1)} %get-tuple-element.54.t2, ...), custom_call_target="tpu_custom_call" | custom-call | flops 4000000 | bytes 3604480 | tf_op jit(solution)/shard_map/pallas_call | solution.py:110
  (18 shorter events, 0.1 us)
Async XLA Ops:
  0.0 6.8 %copy-start.3 = (s32[2,8,128]{2,1,0:T(8,128)S(1)}, s32[2,8,128]{2,1,0:T(8,128)}, u32[]{:S(2)}) copy-start(s32[2,8,128]{2,1,0:T(8,128)} %sides.1) | copy-start | bytes 24580
  0.0 6.8 %copy-start.4 = (s32[8,128]{1,0:T(8,128)S(1)}, s32[8,128]{1,0:T(8,128)}, u32[]{:S(2)}) copy-start(s32[8,128]{1,0:T(8,128)} %links.1) | copy-start | bytes 12292
  0.0 6.8 %copy-start.5 = (f32[128]{0:T(128)S(1)}, f32[128]{0:T(128)}, u32[]{:S(2)}) copy-start(f32[128]{0:T(128)} %param.9) | copy-start | bytes 1540
  0.0 6.8 %copy-start.6 = (s32[128]{0:T(128)S(1)}, s32[128]{0:T(128)}, u32[]{:S(2)}) copy-start(s32[128]{0:T(128)} %param.12) | copy-start | bytes 1540
  2.1 15.6 %copy-start.1 = (f32[2,256,6,6,16]{1,4,3,2,0:T(8,128)S(1)}, f32[2,256,6,6,16]{1,4,3,2,0:T(8,128)}, u32[]{:S(2)}) copy-start(f32[2,256,6,6,16]{1,4,3,2,0:T(8,128)} %param.8) | copy-start | bytes 3538948
  2.1 15.6 %copy-start.2 = (bf16[2,256,256]{2,1,0:T(8,128)(2,1)S(1)}, bf16[2,256,256]{2,1,0:T(8,128)(2,1)}, u32[]{:S(2)}) copy-start(bf16[2,256,256]{2,1,0:T(8,128)(2,1)} %constant.11.clone.synth) | copy-start | bytes 786436
  2.2 15.6 %all-to-all-start = ((f32[8,144,128]{2,1,0:T(8,128)}), f32[8,144,128]{2,1,0:T(8,128)S(1)}, u32[]{:S(2)}, u32[]{:S(2)}) async-start(f32[8,144,128]{2,1,0:T(8,128)} %shard_map.74), calls=%async_computation | async-start | bytes 1179648 | tf_op jit(solution)/shard_map/all_to_all | solution.py:759
  20.3 17.4 %all-to-all-start.1 = ((f32[8,144,128]{2,1,0:T(8,128)}), f32[8,144,128]{2,1,0:T(8,128)S(1)}, u32[]{:S(2)}, u32[]{:S(2)}) async-start(f32[8,144,128]{2,1,0:T(8,128)} %shard_map.76), calls=%async_computation.1 | async-start | bytes 1179648 | tf_op jit(solution)/shard_map/all_to_all | solution.py:807
  23.8 8.1 %collective-permute-start.1 = (f32[48,128]{1,0:T(8,128)S(1)}, f32[48,128]{1,0:T(8,128)S(1)}, u32[]{:S(2)}, u32[]{:S(2)}) collective-permute-start(f32[48,128]{1,0:T(8,128)S(1)} %get-tuple-element.47.to_w), channel_id=1, source_target_pairs={{0,15},{1,0},{2,1},{3,2},{4,3},{5,4},{6,5},{7,6},{8,7},{9,8},{10,9... | collective-permute-start | bytes 73736 | tf_op jit(solution)/shard_map/ppermute | solution.py:739
  30.4 7.1 %collective-permute-start = (f32[48,128]{1,0:T(8,128)S(1)}, f32[48,128]{1,0:T(8,128)S(1)}, u32[]{:S(2)}, u32[]{:S(2)}) collective-permute-start(f32[48,128]{1,0:T(8,128)S(1)} %get-tuple-element.48.to_e), channel_id=1, source_target_pairs={{0,1},{1,2},{2,3},{3,4},{4,5},{5,6},{6,7},{7,8},{8,9},{9,10},{10,1... | collective-permute-start | bytes 73736 | tf_op jit(solution)/shard_map/ppermute | solution.py:739
  38.9 5.2 %collective-permute-start.3 = (f32[48,128]{1,0:T(8,128)S(1)}, f32[48,128]{1,0:T(8,128)S(1)}, u32[]{:S(2)}, u32[]{:S(2)}) collective-permute-start(f32[48,128]{1,0:T(8,128)S(1)} %get-tuple-element.51.to_w), channel_id=1, source_target_pairs={{0,15},{1,0},{2,1},{3,2},{4,3},{5,4},{6,5},{7,6},{8,7},{9,8},{10,9... | collective-permute-start | bytes 73736 | tf_op jit(solution)/shard_map/ppermute | solution.py:739
  42.6 7.1 %collective-permute-start.2 = (f32[48,128]{1,0:T(8,128)S(1)}, f32[48,128]{1,0:T(8,128)S(1)}, u32[]{:S(2)}, u32[]{:S(2)}) collective-permute-start(f32[48,128]{1,0:T(8,128)S(1)} %get-tuple-element.52.to_e), channel_id=1, source_target_pairs={{0,1},{1,2},{2,3},{3,4},{4,5},{5,6},{6,7},{7,8},{8,9},{9,10},{10,1... | collective-permute-start | bytes 73736 | tf_op jit(solution)/shard_map/ppermute | solution.py:739
  51.4 3.9 %collective-permute-start.5 = (f32[48,128]{1,0:T(8,128)S(1)}, f32[48,128]{1,0:T(8,128)S(1)}, u32[]{:S(2)}, u32[]{:S(2)}) collective-permute-start(f32[48,128]{1,0:T(8,128)S(1)} %get-tuple-element.56.to_w), channel_id=1, source_target_pairs={{0,15},{1,0},{2,1},{3,2},{4,3},{5,4},{6,5},{7,6},{8,7},{9,8},{10,9... | collective-permute-start | bytes 73736 | tf_op jit(solution)/shard_map/ppermute | solution.py:739
  51.5 7.2 %collective-permute-start.4 = (f32[48,128]{1,0:T(8,128)S(1)}, f32[48,128]{1,0:T(8,128)S(1)}, u32[]{:S(2)}, u32[]{:S(2)}) collective-permute-start(f32[48,128]{1,0:T(8,128)S(1)} %get-tuple-element.57.to_e), channel_id=1, source_target_pairs={{0,1},{1,2},{2,3},{3,4},{4,5},{5,6},{6,7},{7,8},{8,9},{9,10},{10,1... | collective-permute-start | bytes 73736 | tf_op jit(solution)/shard_map/ppermute | solution.py:739
  58.7 11.6 %copy-start = (f32[32,6,6,128]{3,0,2,1:T(8,128)S(1)}, f32[32,6,6,128]{3,0,2,1:T(8,128)}, u32[]{:S(2)}) copy-start(f32[32,6,6,128]{3,0,2,1:T(8,128)} %param.7) | copy-start | bytes 1769476

commit v8 on v7

--- a/solution.py
+++ b/solution.py
@@ -135,10 +135,10 @@
     return take(*wide)[0:1]
 
 
-def prep_kernel(
-    place, links, sides, visc, layout, idx, edge_idx, tab, own_c, far_c, edge_own, edge_far
+def build_tables(
+    links, sides, visc, layout, idx, edge_idx, tab, own_c, far_c, edge_own, edge_far
 ):
-    me = place[1]
+    me = lax.axis_index("elem")
     dev = lax.shift_right_logical(links[...], 7)
     loc = jnp.bitwise_and(links[...], 127)
     remote = (dev != me).astype(jnp.int32)
@@ -148,7 +148,7 @@
     whole = (inside == 0) & (other == 0)
     second = jnp.bitwise_and(lax.broadcasted_iota(jnp.int32, (8, 128), 0), 1) == 1
     odd_one = jnp.where(inside == 3, 0.0, jnp.where(whole & ~second, 0.0, 1.0))
-    idx[FIRST : FIRST + 1, :] = jnp.full((1, 128), 32 * place[0], jnp.int32)
+    idx[FIRST : FIRST + 1, :] = jnp.full((1, 128), 32 * lax.axis_index("plane"), jnp.int32)
     idx[LAYOUT : LAYOUT + 1, :] = layout[...]
     row = lax.broadcasted_iota(jnp.int32, (128, 128), 0)
     col = lane_ids((128, 128))
@@ -428,11 +428,17 @@
     return emit
 
 
-def guess_kernel(idx, tab, own_c, far_c, u_far, out, send_w, send_e, u, sem):
-    env = (idx, tab, own_c, far_c)
+def guess_kernel(
+    links, sides, visc, layout, u_far,
+    idx, edge_idx, tab, own_c, far_c, edge_own, edge_far, out, send_w, send_e, u, sem,
+):
     copy = pltpu.make_async_copy(u_far, u, sem)
     copy.start()
+    build_tables(
+        links, sides, visc, layout, idx, edge_idx, tab, own_c, far_c, edge_own, edge_far
+    )
     copy.wait()
+    env = (idx, tab, own_c, far_c)
 
     def loop(group, plain):
         rows = group_rows(group)
@@ -685,7 +691,7 @@
     return dot(high, table[0]) + dot(high, table[1]) + dot(low, table[0])
 
 
-def advect_kernel(idx, came, speed, synth, out, high, low, phys, ready, sem):
+def advect_kernel(idx, came, speed, synth, out, high, low, phys):
     for g in range(9):
         for h in range(2):
             pieces = block_turn([came[4 * h + s, 16 * g : 16 * g + 16, :] for s in range(4)])
@@ -728,10 +734,7 @@
                 [norm * phys[16 * (4 * g + m) : 16 * (4 * g + m) + 16, cols] for m in range(4)]
             )
             for s in range(4):
-                ready[4 * h + s, 16 * g : 16 * g + 16, :] = pieces[s]
-    copy = pltpu.make_async_copy(ready, out, sem)
-    copy.start()
-    copy.wait()
+                out[4 * h + s, 16 * g : 16 * g + 16, :] = pieces[s]
 
 
 def shift_by(array, by):
@@ -743,8 +746,6 @@
     u = jnp.transpose(scalar_modes, (1, 2, 0, 3)).reshape(36, 32, 128)
     speed = jnp.transpose(velocity, (0, 2, 3, 4, 1)).reshape(2, 36, 16, 256)
     synth = jnp.asarray(split_table(plane_tables(256)))
-    place = jnp.stack([lax.axis_index("plane"), lax.axis_index("elem")]).astype(jnp.int32)
-
     vol, edge = shape(36, 32, 128), shape(48, 128)
     both = shape(96, 128)
     blocks = shape(8, 144, 128)
@@ -759,17 +760,18 @@
     came = lax.all_to_all(packed, "plane", 0, 0, tiled=True)
 
     table = shape(36, 8, 128)
-    idx, edge_idx, tab, own_c, far_c, edge_own, edge_far = call(
-        prep_kernel,
+    idx, edge_idx, tab, own_c, far_c, edge_own, edge_far, base, *sent = call(
+        guess_kernel,
         [
             shape(24, 128, dtype=jnp.int32),
             shape(8, 128, dtype=jnp.int32),
             shape(8, 128),
         ]
-        + [table] * 4,
-        [],
-        [place, mortar_links, mortar_sides, viscosity[None], layout[None]],
-        [SMEM] + [VMEM] * 4,
+        + [table] * 4
+        + [vol, edge, edge],
+        [VMEM((36, 32, 128), F32), pltpu.SemaphoreType.DMA],
+        [mortar_links, mortar_sides, viscosity[None], layout[None], u],
+        [VMEM] * 4 + [HBM],
     )
     head = [idx, tab, own_c, far_c]
     edges = [edge_idx, edge_own, edge_far]
@@ -780,14 +782,8 @@
     def trade(send_w, send_e):
         return shift_by(send_e, 1), shift_by(send_w, -1)
 
-    base, *sent = call(
-        guess_kernel,
-        [vol, edge, edge],
-        [VMEM((36, 32, 128), F32), pltpu.SemaphoreType.DMA],
-        head + [u],
-        [VMEM] * 4 + [HBM],
-    )
-    came, *sent = lax.optimization_barrier((came, *sent))
+    guess_edge = run(guess_edge_kernel, [shape(48, 128)], [], [*edges, *sent, *trade(*sent)])[0]
+    came, guess_edge = lax.optimization_barrier((came, guess_edge))
     back = call(
         advect_kernel,
         [blocks],
@@ -795,17 +791,12 @@
             VMEM((576, 256), BF16),
             VMEM((576, 256), BF16),
             VMEM((576, 256), F32),
-            VMEM((8, 144, 128), F32),
-            pltpu.SemaphoreType.DMA,
         ],
         [idx, came, speed, synth],
         [VMEM] * 4,
-        [HBM],
         grant=8,
     )[0]
-    back, *sent = lax.optimization_barrier((back, *sent))
     back = lax.all_to_all(back, "plane", 0, 0, tiled=True)
-    guess_edge = run(guess_edge_kernel, [shape(48, 128)], [], [*edges, *sent, *trade(*sent)])[0]
 
     def work(count):
         return [

time: 71.9 us -> 71 us (0.987)
  blocking collectives: 10.2 us -> 25.9 us
  waiting for transfers between devices: 26.9 us -> 17 us
  starting transfers between devices: 20.4 us -> 15.3 us
  Pallas kernels: 13.8 us -> 12.4 us
    all_to_all x0 -> x1, blocking collectives: none -> 15.7 us  [shards(): back = lax.all_to_all(back, 'plane', 0, 0, tiled=True)]
    all_to_all x1, waiting for transfers between devices: 7.94 us -> 0.01 us  [shards(): came = lax.all_to_all(packed, 'plane', 0, 0, tiled=True)]
    all_to_all x1 -> x0, starting transfers between devices: 3.55 us -> none  [shards(): back = lax.all_to_all(back, 'plane', 0, 0, tiled=True)]
    ppermute x6, waiting for transfers between devices: 19 us -> 17 us  [shift_by(): lax.ppermute(array, 'elem', [(i, (i + by) % count) for i in range(count)])]
    ppermute x6, starting transfers between devices: 12.3 us -> 10.7 us  [shift_by(): lax.ppermute(array, 'elem', [(i, (i + by) % count) for i in range(count)])]
    pallas_call x10 -> x9, Pallas kernels: 13.8 us -> 12.4 us  [call(): pl.pallas_call(kernel, out_shape=outs, in_specs=[pl.BlockSpec(memory_spac...]
  transfers between devices with their start and end apart: 8 -> 7, of which waited for: 7 -> 6; matrix products, arithmetic and copies ran while one was open for 0% -> 0% of each run, Pallas kernels for 5% -> 4%
where the time goes in v8:
time: 71 us; the launch traced here: 70.7 us
  blocking collectives  25.9 us (36%)
  waiting for transfers between devices  17 us (24%)
  starting transfers between devices  15.3 us (22%)
  Pallas kernels  12.4 us (17%)
    ppermute x6, waiting for transfers between devices, shift_by(): lax.ppermute(array, 'elem', [(i, (i + by) % count) for i in range(count)])  17 us
    all_to_all x1, blocking collectives, shards(): back = lax.all_to_all(back, 'plane', 0, 0, tiled=True)  15.7 us
    pallas_call x9, Pallas kernels, call(): pl.pallas_call(kernel, out_shape=outs, in_specs=[pl.BlockSpec(memory_spac...  12.4 us
    ppermute x6, starting transfers between devices, shift_by(): lax.ppermute(array, 'elem', [(i, (i + by) % count) for i in range(count)])  10.7 us
    all_to_all x1, blocking collectives, shards(): red = lax.all_to_all(red, 'elem', 0, 0, tiled=True)  10.2 us
    all_to_all x1, starting transfers between devices, shards(): came = lax.all_to_all(packed, 'plane', 0, 0, tiled=True)  4.53 us
  transfers between devices with their start and end apart: 7, of which 6 were waited for; matrix products, arithmetic and copies ran while one was open for 0% of the time, Pallas kernels for 4%

profile of v8, /device:TPU:0, one launch (start us, length us, event | category | flops | bytes accessed | tf_op | source)
XLA Modules:
  0.0 70.7 jit_solution(17138357170521391357)
XLA Ops:
  0.0 2.1 %shard_map.74 = f32[8,144,128]{2,1,0:T(8,128)} custom-call(f32[36,32,128]{2,1,0:T(8,128)} %bitcast.11), custom_call_target="tpu_custom_call" | custom-call | flops 4000000 | bytes 1179648 | tf_op jit(solution)/shard_map/pallas_call | solution.py:110
  2.1 0.0 copy-start.2
  2.2 4.5 %all-to-all-start = ((f32[8,144,128]{2,1,0:T(8,128)}), f32[8,144,128]{2,1,0:T(8,128)S(1)}, u32[]{:S(2)}, u32[]{:S(2)}) async-start(f32[8,144,128]{2,1,0:T(8,128)} %shard_map.74), calls=%async_computation | async-start | bytes 1179648 | tf_op jit(solution)/shard_map/all_to_all | solution.py:760
  6.7 2.4 %shard_map.73 = (s32[24,128]{1,0:T(8,128)S(1)}, s32[8,128]{1,0:T(8,128)S(1)}, f32[8,128]{1,0:T(8,128)S(1)}, f32[36,8,128]{2,1,0:T(8,128)S(1)}, f32[36,8,128]{2,1...) custom-call(s32[8,128]{1,0:T(8,128)S(1)} %copy-done.4, ...), custom_call_target="tpu_custom_call" | custom-call | flops 4000000 | bytes 1852416 | tf_op jit(solution)/shard_map/pallas_call | solution.py:110
  9.1 6.6 %collective-permute-start.1 = (f32[48,128]{1,0:T(8,128)S(1)}, f32[48,128]{1,0:T(8,128)S(1)}, u32[]{:S(2)}, u32[]{:S(2)}) collective-permute-start(f32[48,128]{1,0:T(8,128)S(1)} %get-tuple-element.36.to_w), channel_id=1, source_target_pairs={{0,15},{1,0},{2,1},{3,2},{4,3},{5,4},{6,5},{7,6},{8,7},{9,8},{10,9... | collective-permute-start | bytes 73736 | tf_op jit(solution)/shard_map/ppermute | solution.py:742
  15.7 1.5 %collective-permute-done.1.from_e = f32[48,128]{1,0:T(8,128)S(1)} collective-permute-done((f32[48,128]{1,0:T(8,128)S(1)}, f32[48,128]{1,0:T(8,128)S(1)}, u32[]{:S(2)}, u32[]{:S(2)}) %collective-permute-start.1) | collective-permute-done | bytes 24608 | tf_op jit(solution)/shard_map/ppermute | solution.py:742
  17.2 5.6 %collective-permute-done.from_w = f32[48,128]{1,0:T(8,128)S(1)} collective-permute-done((f32[48,128]{1,0:T(8,128)S(1)}, f32[48,128]{1,0:T(8,128)S(1)}, u32[]{:S(2)}, u32[]{:S(2)}) %collective-permute-start) | collective-permute-done | bytes 24608 | tf_op jit(solution)/shard_map/ppermute | solution.py:742
  22.8 0.2 shard_map.75.edge
  23.0 1.7 %shard_map.76 = f32[8,144,128]{2,1,0:T(8,128)S(1)} custom-call(s32[24,128]{1,0:T(8,128)S(1)} %get-tuple-element.29.idx, f32[8,144,128]{2,1,0:T(8,128)S(1)} %all-to-all-done.came, f32[2,36,16,256]{3,2,1,0:T(8,128)S(1)} %bitcast.14, bf16[2,256,256]{2,1,0:T(8,128)(2,1)S(1)} %copy-done.2), custom_call_target="tpu_custom_call" | custom-call | flops 4000000 | bytes 2895872 | tf_op jit(solution)/shard_map/pallas_call | solution.py:110
  24.7 15.7 %all_to_all.15.back = f32[8,144,128]{2,1,0:T(8,128)S(1)} all-to-all(f32[8,144,128]{2,1,0:T(8,128)S(1)} %shard_map.76), channel_id=1, replica_groups=mesh['plane'=8,'elem'=16] {'plane'}, dimensions={0} | all-to-all | bytes 1179648 | tf_op jit(solution)/shard_map/all_to_all | solution.py:799
  40.4 1.2 %shard_map.77 = (f32[36,32,128]{2,1,0:T(8,128)S(1)}, f32[36,32,128]{2,1,0:T(8,128)S(1)}, f32[48,128]{1,0:T(8,128)S(1)}, f32[48,128]{1,0:T(8,128)S(1)}) custom-call(s32[24,128]{1,0:T(8,128)S(1)} %get-tuple-element.29.idx, f32[8,128]{1,0:T(8,128)S(1)} %get-tuple-element.30.tab, f32[36,8,128]{2,1,0:T(8,128)S(1)} %get-tuple-element.31.own_c, ...), custom_call_target="tpu_custom_call" | custom-call | flops 4000000 | bytes 2744320 | tf_op jit(solution)/shard_map/pallas_call | solution.py:110
  41.6 0.1 collective-permute-start.3
  41.7 2.0 %collective-permute-start.2 = (f32[48,128]{1,0:T(8,128)S(1)}, f32[48,128]{1,0:T(8,128)S(1)}, u32[]{:S(2)}, u32[]{:S(2)}) collective-permute-start(f32[48,128]{1,0:T(8,128)S(1)} %get-tuple-element.44.to_e), channel_id=1, source_target_pairs={{0,1},{1,2},{2,3},{3,4},{4,5},{5,6},{6,7},{7,8},{8,9},{9,10},{10,1... | collective-permute-start | bytes 73736 | tf_op jit(solution)/shard_map/ppermute | solution.py:742
  43.7 1.8 %collective-permute-done.3.from_e = f32[48,128]{1,0:T(8,128)S(1)} collective-permute-done((f32[48,128]{1,0:T(8,128)S(1)}, f32[48,128]{1,0:T(8,128)S(1)}, u32[]{:S(2)}, u32[]{:S(2)}) %collective-permute-start.3) | collective-permute-done | bytes 24608 | tf_op jit(solution)/shard_map/ppermute | solution.py:742
  45.5 3.4 %collective-permute-done.2.from_w = f32[48,128]{1,0:T(8,128)S(1)} collective-permute-done((f32[48,128]{1,0:T(8,128)S(1)}, f32[48,128]{1,0:T(8,128)S(1)}, u32[]{:S(2)}, u32[]{:S(2)}) %collective-permute-start.2) | collective-permute-done | bytes 24608 | tf_op jit(solution)/shard_map/ppermute | solution.py:742
  48.9 1.6 %shard_map.78 = (f32[36,32,128]{2,1,0:T(8,128)S(1)}, f32[36,32,128]{2,1,0:T(8,128)S(1)}, f32[36,32,128]{2,1,0:T(8,128)S(1)}, f32[48,128]{1,0:T(8,128)S(1)}, f32[...) custom-call(s32[24,128]{1,0:T(8,128)S(1)} %get-tuple-element.29.idx, f32[8,128]{1,0:T(8,128)S(1)} %get-tuple-element.30.tab, ...), custom_call_target="tpu_custom_call" | custom-call | flops 4000000 | bytes 3756032 | tf_op jit(solution)/shard_map/pallas_call | solution.py:110
  50.6 0.1 collective-permute-start.5
  50.7 2.0 %collective-permute-start.4 = (f32[48,128]{1,0:T(8,128)S(1)}, f32[48,128]{1,0:T(8,128)S(1)}, u32[]{:S(2)}, u32[]{:S(2)}) collective-permute-start(f32[48,128]{1,0:T(8,128)S(1)} %get-tuple-element.49.to_e), channel_id=1, source_target_pairs={{0,1},{1,2},{2,3},{3,4},{4,5},{5,6},{6,7},{7,8},{8,9},{9,10},{10,1... | collective-permute-start | bytes 73736 | tf_op jit(solution)/shard_map/ppermute | solution.py:742
  52.7 0.5 shard_map.79.part
  53.2 1.3 %collective-permute-done.5.from_e = f32[48,128]{1,0:T(8,128)S(1)} collective-permute-done((f32[48,128]{1,0:T(8,128)S(1)}, f32[48,128]{1,0:T(8,128)S(1)}, u32[]{:S(2)}, u32[]{:S(2)}) %collective-permute-start.5) | collective-permute-done | bytes 24608 | tf_op jit(solution)/shard_map/ppermute | solution.py:742
  54.5 3.4 %collective-permute-done.4.from_w = f32[48,128]{1,0:T(8,128)S(1)} collective-permute-done((f32[48,128]{1,0:T(8,128)S(1)}, f32[48,128]{1,0:T(8,128)S(1)}, u32[]{:S(2)}, u32[]{:S(2)}) %collective-permute-start.4) | collective-permute-done | bytes 24608 | tf_op jit(solution)/shard_map/ppermute | solution.py:742
  57.9 1.4 %shard_map.80 = (f32[36,32,128]{2,1,0:T(8,128)S(1)}, f32[16,8,128]{2,1,0:T(8,128)S(1)}) custom-call(s32[24,128]{1,0:T(8,128)S(1)} %get-tuple-element.29.idx, f32[8,128]{1,0:T(8,128)S(1)} %get-tuple-element.30.tab, f32[36,8,128]{2,1,0:T(8,128)S(1)} %get-tuple-element.31.own_c, f32[36,8,128]{2,1,0:T(8,128)S(1)} %get-tuple-element.32.far_c, ...), custom_call_target="tpu_custom_call" | custom-call | flops 4000000 | bytes 3186688 | tf_op jit(solution)/shard_map/pallas_call | solution.py:110
  59.3 10.2 %all_to_all.16.red = f32[16,8,128]{2,1,0:T(8,128)S(1)} all-to-all(f32[16,8,128]{2,1,0:T(8,128)S(1)} %get-tuple-element.51), channel_id=1, replica_groups=mesh['plane'=8,'elem'=16] {'elem'}, dimensions={0} | all-to-all | bytes 131072 | tf_op jit(solution)/shard_map/all_to_all | solution.py:824
  69.5 1.2 %shard_map.81 = f32[36,32,128]{2,1,0:T(8,128)} custom-call(f32[16,8,128]{2,1,0:T(8,128)S(1)} %all_to_all.16.red, f32[36,32,128]{2,1,0:T(8,128)S(1)} %bitcast.13, f32[36,32,128]{2,1,0:T(8,128)S(1)} %get-tuple-element.41.t0, f32[36,32,128]{2,1,0:T(8,128)S(1)} %get-tuple-element.45.t1, f32[36,32,128]{2,1,0:T(8,128)S(1)} %get-tuple-element.46.t2, ...), custom_call_target="tpu_custom_call" | custom-call | flops 4000000 | bytes 3604480 | tf_op jit(solution)/shard_map/pallas_call | solution.py:110
  (15 shorter events, 0.0 us)
Async XLA Ops:
  0.0 6.7 %copy-start.3 = (s32[2,8,128]{2,1,0:T(8,128)S(1)}, s32[2,8,128]{2,1,0:T(8,128)}, u32[]{:S(2)}) copy-start(s32[2,8,128]{2,1,0:T(8,128)} %sides.1) | copy-start | bytes 24580
  0.0 6.7 %copy-start.4 = (s32[8,128]{1,0:T(8,128)S(1)}, s32[8,128]{1,0:T(8,128)}, u32[]{:S(2)}) copy-start(s32[8,128]{1,0:T(8,128)} %links.1) | copy-start | bytes 12292
  0.0 6.7 %copy-start.5 = (f32[128]{0:T(128)S(1)}, f32[128]{0:T(128)}, u32[]{:S(2)}) copy-start(f32[128]{0:T(128)} %param.9) | copy-start | bytes 1540
  0.0 6.7 %copy-start.6 = (s32[128]{0:T(128)S(1)}, s32[128]{0:T(128)}, u32[]{:S(2)}) copy-start(s32[128]{0:T(128)} %param.12) | copy-start | bytes 1540
  2.1 20.9 %copy-start.1 = (f32[2,256,6,6,16]{1,4,3,2,0:T(8,128)S(1)}, f32[2,256,6,6,16]{1,4,3,2,0:T(8,128)}, u32[]{:S(2)}) copy-start(f32[2,256,6,6,16]{1,4,3,2,0:T(8,128)} %param.8) | copy-start | bytes 3538948
  2.1 20.9 %copy-start.2 = (bf16[2,256,256]{2,1,0:T(8,128)(2,1)S(1)}, bf16[2,256,256]{2,1,0:T(8,128)(2,1)}, u32[]{:S(2)}) copy-start(bf16[2,256,256]{2,1,0:T(8,128)(2,1)} %constant.2.clone.synth) | copy-start | bytes 786436
  2.2 20.9 %all-to-all-start = ((f32[8,144,128]{2,1,0:T(8,128)}), f32[8,144,128]{2,1,0:T(8,128)S(1)}, u32[]{:S(2)}, u32[]{:S(2)}) async-start(f32[8,144,128]{2,1,0:T(8,128)} %shard_map.74), calls=%async_computation | async-start | bytes 1179648 | tf_op jit(solution)/shard_map/all_to_all | solution.py:760
  9.1 8.1 %collective-permute-start.1 = (f32[48,128]{1,0:T(8,128)S(1)}, f32[48,128]{1,0:T(8,128)S(1)}, u32[]{:S(2)}, u32[]{:S(2)}) collective-permute-start(f32[48,128]{1,0:T(8,128)S(1)} %get-tuple-element.36.to_w), channel_id=1, source_target_pairs={{0,15},{1,0},{2,1},{3,2},{4,3},{5,4},{6,5},{7,6},{8,7},{9,8},{10,9... | collective-permute-start | bytes 73736 | tf_op jit(solution)/shard_map/ppermute | solution.py:742
  15.7 7.1 %collective-permute-start = (f32[48,128]{1,0:T(8,128)S(1)}, f32[48,128]{1,0:T(8,128)S(1)}, u32[]{:S(2)}, u32[]{:S(2)}) collective-permute-start(f32[48,128]{1,0:T(8,128)S(1)} %get-tuple-element.37.to_e), channel_id=1, source_target_pairs={{0,1},{1,2},{2,3},{3,4},{4,5},{5,6},{6,7},{7,8},{8,9},{9,10},{10,1... | collective-permute-start | bytes 73736 | tf_op jit(solution)/shard_map/ppermute | solution.py:742
  41.6 3.9 %collective-permute-start.3 = (f32[48,128]{1,0:T(8,128)S(1)}, f32[48,128]{1,0:T(8,128)S(1)}, u32[]{:S(2)}, u32[]{:S(2)}) collective-permute-start(f32[48,128]{1,0:T(8,128)S(1)} %get-tuple-element.43.to_w), channel_id=1, source_target_pairs={{0,15},{1,0},{2,1},{3,2},{4,3},{5,4},{6,5},{7,6},{8,7},{9,8},{10,9... | collective-permute-start | bytes 73736 | tf_op jit(solution)/shard_map/ppermute | solution.py:742
  41.7 7.2 %collective-permute-start.2 = (f32[48,128]{1,0:T(8,128)S(1)}, f32[48,128]{1,0:T(8,128)S(1)}, u32[]{:S(2)}, u32[]{:S(2)}) collective-permute-start(f32[48,128]{1,0:T(8,128)S(1)} %get-tuple-element.44.to_e), channel_id=1, source_target_pairs={{0,1},{1,2},{2,3},{3,4},{4,5},{5,6},{6,7},{7,8},{8,9},{9,10},{10,1... | collective-permute-start | bytes 73736 | tf_op jit(solution)/shard_map/ppermute | solution.py:742
  50.6 3.9 %collective-permute-start.5 = (f32[48,128]{1,0:T(8,128)S(1)}, f32[48,128]{1,0:T(8,128)S(1)}, u32[]{:S(2)}, u32[]{:S(2)}) collective-permute-start(f32[48,128]{1,0:T(8,128)S(1)} %get-tuple-element.48.to_w), channel_id=1, source_target_pairs={{0,15},{1,0},{2,1},{3,2},{4,3},{5,4},{6,5},{7,6},{8,7},{9,8},{10,9... | collective-permute-start | bytes 73736 | tf_op jit(solution)/shard_map/ppermute | solution.py:742
  50.7 7.2 %collective-permute-start.4 = (f32[48,128]{1,0:T(8,128)S(1)}, f32[48,128]{1,0:T(8,128)S(1)}, u32[]{:S(2)}, u32[]{:S(2)}) collective-permute-start(f32[48,128]{1,0:T(8,128)S(1)} %get-tuple-element.49.to_e), channel_id=1, source_target_pairs={{0,1},{1,2},{2,3},{3,4},{4,5},{5,6},{6,7},{7,8},{8,9},{9,10},{10,1... | collective-permute-start | bytes 73736 | tf_op jit(solution)/shard_map/ppermute | solution.py:742
  57.9 11.6 %copy-start = (f32[32,6,6,128]{3,0,2,1:T(8,128)S(1)}, f32[32,6,6,128]{3,0,2,1:T(8,128)}, u32[]{:S(2)}) copy-start(f32[32,6,6,128]{3,0,2,1:T(8,128)} %param.7) | copy-start | bytes 1769476

commit v9 on v8

--- a/solution.py
+++ b/solution.py
@@ -133,6 +133,18 @@
 def take_row(value, index):
     wide = jnp.broadcast_to(value, (8, 128)), jnp.broadcast_to(index, (8, 128))
     return take(*wide)[0:1]
+
+
+def boundary(remote, side):
+    row = lax.broadcasted_iota(jnp.int32, (128, 128), 0)
+    col = lane_ids((128, 128))
+    any_rem = jnp.maximum(remote[2 * side : 2 * side + 1], remote[2 * side + 1 : 2 * side + 2])
+    before = jnp.sum(jnp.where(col < row, any_rem, 0).astype(F32), axis=1, keepdims=True)
+    mine = jnp.sum(jnp.where(col == row, any_rem, 0).astype(F32), axis=1, keepdims=True)
+    slot = jnp.bitwise_and(lane_ids((1, 128)), 15).astype(F32)
+    chosen = jnp.where((before == slot) & (mine > 0.0), 1.0, 0.0)
+    listed = jnp.sum(chosen * row.astype(F32), axis=0, keepdims=True)
+    return listed, jnp.sum(chosen, axis=0, keepdims=True), before
 
 
 def build_tables(
@@ -159,11 +171,9 @@
         rem = [remote[2 * side + t : 2 * side + t + 1] for t in range(2)]
         far = [loc[2 * side + t : 2 * side + t + 1] for t in range(2)]
         any_rem = jnp.maximum(rem[0], rem[1])
-        before = jnp.sum(jnp.where(col < row, any_rem, 0).astype(F32), axis=1, keepdims=True)
-        mine = jnp.sum(jnp.where(col == row, any_rem, 0).astype(F32), axis=1, keepdims=True)
-        chosen = jnp.where((before == slot.astype(F32)) & (mine > 0.0), 1.0, 0.0)
-        listed.append(jnp.sum(chosen * row.astype(F32), axis=0, keepdims=True).astype(jnp.int32))
-        present.append(jnp.sum(chosen, axis=0, keepdims=True).astype(jnp.int32))
+        places, filled, before = boundary(remote, side)
+        listed.append(places.astype(jnp.int32))
+        present.append(filled.astype(jnp.int32))
         idx[side : side + 1, :] = listed[side]
         mine_at = jnp.sum(jnp.where(row == col, before, 0.0), axis=0, keepdims=True)
         mine_at = jnp.where(any_rem > 0, mine_at.astype(jnp.int32), 0)
@@ -430,7 +440,7 @@
 
 def guess_kernel(
     links, sides, visc, layout, u_far,
-    idx, edge_idx, tab, own_c, far_c, edge_own, edge_far, out, send_w, send_e, u, sem,
+    idx, edge_idx, tab, own_c, far_c, edge_own, edge_far, out, u, sem,
 ):
     copy = pltpu.make_async_copy(u_far, u, sem)
     copy.start()
@@ -449,7 +459,6 @@
         inner(group, env, u, plain, emit)
 
     either(tab, loop)
-    compact(idx, u, u, send_w, send_e)
 
 
 def guess_edge_kernel(edge_idx, edge_own, edge_far, to_w, to_e, from_w, from_e, edge):
@@ -654,12 +663,19 @@
         copy.wait()
 
 
-def pack_kernel(u, out, held, ready, sems):
+def pack_kernel(u, links, out, send_w, send_e, held, ready, near_links, lists, sems):
     loads, stores = [], []
+    first = pltpu.make_async_copy(links, near_links, sems.at[6])
+    first.start()
     for c in range(3):
         part = pl.ds(12 * c, 12)
         loads.append(pltpu.make_async_copy(u.at[part], held.at[part], sems.at[c]))
         loads[c].start()
+    first.wait()
+    dev = lax.shift_right_logical(near_links[...], 7)
+    remote = (dev != lax.axis_index("elem")).astype(jnp.int32)
+    for side in range(2):
+        lists[side : side + 1, :] = boundary(remote, side)[0].astype(jnp.int32)
     for c in range(3):
         loads[c].wait()
         for g in range(3 * c, 3 * c + 3):
@@ -668,6 +684,7 @@
         part = pl.ds(48 * c, 48)
         stores.append(pltpu.make_async_copy(ready.at[:, part], out.at[:, part], sems.at[3 + c]))
         stores[c].start()
+    compact(lists, held, held, send_w, send_e)
     for copy in stores:
         copy.wait()
 
@@ -749,18 +766,24 @@
     vol, edge = shape(36, 32, 128), shape(48, 128)
     both = shape(96, 128)
     blocks = shape(8, 144, 128)
-    packed = call(
+    packed, *sent = call(
         pack_kernel,
-        [blocks],
-        [VMEM((36, 32, 128), F32), VMEM((8, 144, 128), F32), pltpu.SemaphoreType.DMA((6,))],
-        [u],
-        [HBM],
-        [HBM],
-    )[0]
+        [blocks, edge, edge],
+        [
+            VMEM((36, 32, 128), F32),
+            VMEM((8, 144, 128), F32),
+            VMEM((8, 128), jnp.int32),
+            VMEM((8, 128), jnp.int32),
+            pltpu.SemaphoreType.DMA((7,)),
+        ],
+        [u, mortar_links],
+        [HBM, HBM],
+        [HBM, VMEM, VMEM],
+    )
     came = lax.all_to_all(packed, "plane", 0, 0, tiled=True)
 
     table = shape(36, 8, 128)
-    idx, edge_idx, tab, own_c, far_c, edge_own, edge_far, base, *sent = call(
+    idx, edge_idx, tab, own_c, far_c, edge_own, edge_far, base = call(
         guess_kernel,
         [
             shape(24, 128, dtype=jnp.int32),
@@ -768,7 +791,7 @@
             shape(8, 128),
         ]
         + [table] * 4
-        + [vol, edge, edge],
+        + [vol],
         [VMEM((36, 32, 128), F32), pltpu.SemaphoreType.DMA],
         [mortar_links, mortar_sides, viscosity[None], layout[None], u],
         [VMEM] * 4 + [HBM],
@@ -783,7 +806,7 @@
         return shift_by(send_e, 1), shift_by(send_w, -1)
 
     guess_edge = run(guess_edge_kernel, [shape(48, 128)], [], [*edges, *sent, *trade(*sent)])[0]
-    came, guess_edge = lax.optimization_barrier((came, guess_edge))
+    came, guess_edge, base = lax.optimization_barrier((came, guess_edge, base))
     back = call(
         advect_kernel,
         [blocks],

time: 71 us -> 70 us (0.986)
  waiting for transfers between devices: 17 us -> 16.1 us
    ppermute x6, waiting for transfers between devices: 17 us -> 16.1 us  [shift_by(): lax.ppermute(array, 'elem', [(i, (i + by) % count) for i in range(count)])]
  transfers between devices with their start and end apart: 7 -> 7, of which waited for: 6 -> 5; matrix products, arithmetic and copies ran while one was open for 0% -> 0% of each run, Pallas kernels for 4% -> 4%
where the time goes in v9:
time: 70 us; the launch traced here: 69.6 us
  blocking collectives  25.9 us (37%)
  waiting for transfers between devices  16.1 us (23%)
  starting transfers between devices  15.2 us (22%)
  Pallas kernels  12.2 us (17%)
    ppermute x6, waiting for transfers between devices, shift_by(): lax.ppermute(array, 'elem', [(i, (i + by) % count) for i in range(count)])  16.1 us
    all_to_all x1, blocking collectives, shards(): back = lax.all_to_all(back, 'plane', 0, 0, tiled=True)  15.7 us
    pallas_call x9, Pallas kernels, call(): pl.pallas_call(kernel, out_shape=outs, in_specs=[pl.BlockSpec(memory_spac...  12.2 us
    ppermute x6, starting transfers between devices, shift_by(): lax.ppermute(array, 'elem', [(i, (i + by) % count) for i in range(count)])  10.7 us
    all_to_all x1, blocking collectives, shards(): red = lax.all_to_all(red, 'elem', 0, 0, tiled=True)  10.2 us
    all_to_all x1, starting transfers between devices, shards(): came = lax.all_to_all(packed, 'plane', 0, 0, tiled=True)  4.53 us
  transfers between devices with their start and end apart: 7, of which 5 were waited for; matrix products, arithmetic and copies ran while one was open for 0% of the time, Pallas kernels for 4%

profile of v9, /device:TPU:0, one launch (start us, length us, event | category | flops | bytes accessed | tf_op | source)
XLA Modules:
  0.0 69.6 jit_solution(7677428233025017702)
XLA Ops:
  0.0 2.1 %shard_map.74 = (f32[8,144,128]{2,1,0:T(8,128)}, f32[48,128]{1,0:T(8,128)S(1)}, f32[48,128]{1,0:T(8,128)S(1)}) custom-call(f32[36,32,128]{2,1,0:T(8,128)} %bitcast.11, s32[8,128]{1,0:T(8,128)} %links.3), custom_call_target="tpu_custom_call" | custom-call | flops 4000000 | bytes 1232896 | tf_op jit(solution)/shard_map/pallas_call | solution.py:110
  2.2 0.0 copy-start.1
  2.2 0.0 copy-start.2
  2.2 4.5 %all-to-all-start = ((f32[8,144,128]{2,1,0:T(8,128)}), f32[8,144,128]{2,1,0:T(8,128)S(1)}, u32[]{:S(2)}, u32[]{:S(2)}) async-start(f32[8,144,128]{2,1,0:T(8,128)} %get-tuple-element.38), calls=%async_computation | async-start | bytes 1179648 | tf_op jit(solution)/shard_map/all_to_all | solution.py:783
  6.7 6.5 %collective-permute-start.1 = (f32[48,128]{1,0:T(8,128)S(1)}, f32[48,128]{1,0:T(8,128)S(1)}, u32[]{:S(2)}, u32[]{:S(2)}) collective-permute-start(f32[48,128]{1,0:T(8,128)S(1)} %get-tuple-element.39.to_w), channel_id=1, source_target_pairs={{0,15},{1,0},{2,1},{3,2},{4,3},{5,4},{6,5},{7,6},{8,7},{9,8},{10,9... | collective-permute-start | bytes 73736 | tf_op jit(solution)/shard_map/ppermute | solution.py:759
  13.2 2.3 %shard_map.73 = (s32[24,128]{1,0:T(8,128)S(1)}, s32[8,128]{1,0:T(8,128)S(1)}, f32[8,128]{1,0:T(8,128)S(1)}, f32[36,8,128]{2,1,0:T(8,128)S(1)}, f32[36,8,128]{2,1...) custom-call(s32[8,128]{1,0:T(8,128)S(1)} %copy-done.3, ...), custom_call_target="tpu_custom_call" | custom-call | flops 4000000 | bytes 1803264 | tf_op jit(solution)/shard_map/pallas_call | solution.py:110
  15.5 4.8 %collective-permute-done.from_w = f32[48,128]{1,0:T(8,128)S(1)} collective-permute-done((f32[48,128]{1,0:T(8,128)S(1)}, f32[48,128]{1,0:T(8,128)S(1)}, u32[]{:S(2)}, u32[]{:S(2)}) %collective-permute-start) | collective-permute-done | bytes 24608 | tf_op jit(solution)/shard_map/ppermute | solution.py:759
  20.3 0.2 shard_map.75.edge
  20.5 1.7 %shard_map.76 = f32[8,144,128]{2,1,0:T(8,128)S(1)} custom-call(s32[24,128]{1,0:T(8,128)S(1)} %get-tuple-element.31.idx, f32[8,144,128]{2,1,0:T(8,128)S(1)} %all-to-all-done.came, f32[2,36,16,256]{3,2,1,0:T(8,128)S(1)} %bitcast.14, bf16[2,256,256]{2,1,0:T(8,128)(2,1)S(1)} %copy-done.2), custom_call_target="tpu_custom_call" | custom-call | flops 4000000 | bytes 2895872 | tf_op jit(solution)/shard_map/pallas_call | solution.py:110
  22.2 15.7 %all_to_all.15.back = f32[8,144,128]{2,1,0:T(8,128)S(1)} all-to-all(f32[8,144,128]{2,1,0:T(8,128)S(1)} %shard_map.76), channel_id=1, replica_groups=mesh['plane'=8,'elem'=16] {'plane'}, dimensions={0} | all-to-all | bytes 1179648 | tf_op jit(solution)/shard_map/all_to_all | solution.py:822
  37.9 1.2 %shard_map.77 = (f32[36,32,128]{2,1,0:T(8,128)S(1)}, f32[36,32,128]{2,1,0:T(8,128)S(1)}, f32[48,128]{1,0:T(8,128)S(1)}, f32[48,128]{1,0:T(8,128)S(1)}) custom-call(s32[24,128]{1,0:T(8,128)S(1)} %get-tuple-element.31.idx, f32[8,128]{1,0:T(8,128)S(1)} %get-tuple-element.32.tab, f32[36,8,128]{2,1,0:T(8,128)S(1)} %get-tuple-element.33.own_c, ...), custom_call_target="tpu_custom_call" | custom-call | flops 4000000 | bytes 2744320 | tf_op jit(solution)/shard_map/pallas_call | solution.py:110
  39.2 1.5 %collective-permute-start.3 = (f32[48,128]{1,0:T(8,128)S(1)}, f32[48,128]{1,0:T(8,128)S(1)}, u32[]{:S(2)}, u32[]{:S(2)}) collective-permute-start(f32[48,128]{1,0:T(8,128)S(1)} %get-tuple-element.47.to_w), channel_id=1, source_target_pairs={{0,15},{1,0},{2,1},{3,2},{4,3},{5,4},{6,5},{7,6},{8,7},{9,8},{10,9... | collective-permute-start | bytes 73736 | tf_op jit(solution)/shard_map/ppermute | solution.py:759
  40.7 0.6 collective-permute-start.2
  41.3 1.8 %collective-permute-done.3.from_e = f32[48,128]{1,0:T(8,128)S(1)} collective-permute-done((f32[48,128]{1,0:T(8,128)S(1)}, f32[48,128]{1,0:T(8,128)S(1)}, u32[]{:S(2)}, u32[]{:S(2)}) %collective-permute-start.3) | collective-permute-done | bytes 24608 | tf_op jit(solution)/shard_map/ppermute | solution.py:759
  43.1 4.8 %collective-permute-done.2.from_w = f32[48,128]{1,0:T(8,128)S(1)} collective-permute-done((f32[48,128]{1,0:T(8,128)S(1)}, f32[48,128]{1,0:T(8,128)S(1)}, u32[]{:S(2)}, u32[]{:S(2)}) %collective-permute-start.2) | collective-permute-done | bytes 24608 | tf_op jit(solution)/shard_map/ppermute | solution.py:759
  47.9 1.6 %shard_map.78 = (f32[36,32,128]{2,1,0:T(8,128)S(1)}, f32[36,32,128]{2,1,0:T(8,128)S(1)}, f32[36,32,128]{2,1,0:T(8,128)S(1)}, f32[48,128]{1,0:T(8,128)S(1)}, f32[...) custom-call(s32[24,128]{1,0:T(8,128)S(1)} %get-tuple-element.31.idx, f32[8,128]{1,0:T(8,128)S(1)} %get-tuple-element.32.tab, ...), custom_call_target="tpu_custom_call" | custom-call | flops 4000000 | bytes 3756032 | tf_op jit(solution)/shard_map/pallas_call | solution.py:110
  49.5 0.1 collective-permute-start.5
  49.6 2.0 %collective-permute-start.4 = (f32[48,128]{1,0:T(8,128)S(1)}, f32[48,128]{1,0:T(8,128)S(1)}, u32[]{:S(2)}, u32[]{:S(2)}) collective-permute-start(f32[48,128]{1,0:T(8,128)S(1)} %get-tuple-element.53.to_e), channel_id=1, source_target_pairs={{0,1},{1,2},{2,3},{3,4},{4,5},{5,6},{6,7},{7,8},{8,9},{9,10},{10,1... | collective-permute-start | bytes 73736 | tf_op jit(solution)/shard_map/ppermute | solution.py:759
  51.6 0.5 shard_map.79.part
  52.1 1.3 %collective-permute-done.5.from_e = f32[48,128]{1,0:T(8,128)S(1)} collective-permute-done((f32[48,128]{1,0:T(8,128)S(1)}, f32[48,128]{1,0:T(8,128)S(1)}, u32[]{:S(2)}, u32[]{:S(2)}) %collective-permute-start.5) | collective-permute-done | bytes 24608 | tf_op jit(solution)/shard_map/ppermute | solution.py:759
  53.4 3.4 %collective-permute-done.4.from_w = f32[48,128]{1,0:T(8,128)S(1)} collective-permute-done((f32[48,128]{1,0:T(8,128)S(1)}, f32[48,128]{1,0:T(8,128)S(1)}, u32[]{:S(2)}, u32[]{:S(2)}) %collective-permute-start.4) | collective-permute-done | bytes 24608 | tf_op jit(solution)/shard_map/ppermute | solution.py:759
  56.8 1.4 %shard_map.80 = (f32[36,32,128]{2,1,0:T(8,128)S(1)}, f32[16,8,128]{2,1,0:T(8,128)S(1)}) custom-call(s32[24,128]{1,0:T(8,128)S(1)} %get-tuple-element.31.idx, f32[8,128]{1,0:T(8,128)S(1)} %get-tuple-element.32.tab, f32[36,8,128]{2,1,0:T(8,128)S(1)} %get-tuple-element.33.own_c, f32[36,8,128]{2,1,0:T(8,128)S(1)} %get-tuple-element.34.far_c, ...), custom_call_target="tpu_custom_call" | custom-call | flops 4000000 | bytes 3186688 | tf_op jit(solution)/shard_map/pallas_call | solution.py:110
  58.2 10.2 %all_to_all.16.red = f32[16,8,128]{2,1,0:T(8,128)S(1)} all-to-all(f32[16,8,128]{2,1,0:T(8,128)S(1)} %get-tuple-element.55), channel_id=1, replica_groups=mesh['plane'=8,'elem'=16] {'elem'}, dimensions={0} | all-to-all | bytes 131072 | tf_op jit(solution)/shard_map/all_to_all | solution.py:847
  68.4 1.2 %shard_map.81 = f32[36,32,128]{2,1,0:T(8,128)} custom-call(f32[16,8,128]{2,1,0:T(8,128)S(1)} %all_to_all.16.red, f32[36,32,128]{2,1,0:T(8,128)S(1)} %bitcast.13, f32[36,32,128]{2,1,0:T(8,128)S(1)} %get-tuple-element.45.t0, f32[36,32,128]{2,1,0:T(8,128)S(1)} %get-tuple-element.49.t1, f32[36,32,128]{2,1,0:T(8,128)S(1)} %get-tuple-element.50.t2, ...), custom_call_target="tpu_custom_call" | custom-call | flops 4000000 | bytes 3604480 | tf_op jit(solution)/shard_map/pallas_call | solution.py:110
  (15 shorter events, 0.0 us)
Async XLA Ops:
  0.0 13.2 %copy-start.3 = (s32[8,128]{1,0:T(8,128)S(1)}, s32[8,128]{1,0:T(8,128)}, u32[]{:S(2)}) copy-start(s32[8,128]{1,0:T(8,128)} %links.3) | copy-start | bytes 12292
  0.0 13.2 %copy-start.6 = (s32[128]{0:T(128)S(1)}, s32[128]{0:T(128)}, u32[]{:S(2)}) copy-start(s32[128]{0:T(128)} %param.12) | copy-start | bytes 1540
  0.0 13.2 %copy-start.4 = (s32[2,8,128]{2,1,0:T(8,128)S(1)}, s32[2,8,128]{2,1,0:T(8,128)}, u32[]{:S(2)}) copy-start(s32[2,8,128]{2,1,0:T(8,128)} %sides.1) | copy-start | bytes 24580
  0.0 13.2 %copy-start.5 = (f32[128]{0:T(128)S(1)}, f32[128]{0:T(128)}, u32[]{:S(2)}) copy-start(f32[128]{0:T(128)} %param.9) | copy-start | bytes 1540
  2.2 18.4 %copy-start.1 = (f32[2,256,6,6,16]{1,4,3,2,0:T(8,128)S(1)}, f32[2,256,6,6,16]{1,4,3,2,0:T(8,128)}, u32[]{:S(2)}) copy-start(f32[2,256,6,6,16]{1,4,3,2,0:T(8,128)} %param.8) | copy-start | bytes 3538948
  2.2 18.4 %copy-start.2 = (bf16[2,256,256]{2,1,0:T(8,128)(2,1)S(1)}, bf16[2,256,256]{2,1,0:T(8,128)(2,1)}, u32[]{:S(2)}) copy-start(bf16[2,256,256]{2,1,0:T(8,128)(2,1)} %constant.2.clone.synth) | copy-start | bytes 786436
  2.2 18.3 %all-to-all-start = ((f32[8,144,128]{2,1,0:T(8,128)}), f32[8,144,128]{2,1,0:T(8,128)S(1)}, u32[]{:S(2)}, u32[]{:S(2)}) async-start(f32[8,144,128]{2,1,0:T(8,128)} %get-tuple-element.38), calls=%async_computation | async-start | bytes 1179648 | tf_op jit(solution)/shard_map/all_to_all | solution.py:783
  6.7 8.8 %collective-permute-start.1 = (f32[48,128]{1,0:T(8,128)S(1)}, f32[48,128]{1,0:T(8,128)S(1)}, u32[]{:S(2)}, u32[]{:S(2)}) collective-permute-start(f32[48,128]{1,0:T(8,128)S(1)} %get-tuple-element.39.to_w), channel_id=1, source_target_pairs={{0,15},{1,0},{2,1},{3,2},{4,3},{5,4},{6,5},{7,6},{8,7},{9,8},{10,9... | collective-permute-start | bytes 73736 | tf_op jit(solution)/shard_map/ppermute | solution.py:759
  13.2 7.1 %collective-permute-start = (f32[48,128]{1,0:T(8,128)S(1)}, f32[48,128]{1,0:T(8,128)S(1)}, u32[]{:S(2)}, u32[]{:S(2)}) collective-permute-start(f32[48,128]{1,0:T(8,128)S(1)} %get-tuple-element.40.to_e), channel_id=1, source_target_pairs={{0,1},{1,2},{2,3},{3,4},{4,5},{5,6},{6,7},{7,8},{8,9},{9,10},{10,1... | collective-permute-start | bytes 73736 | tf_op jit(solution)/shard_map/ppermute | solution.py:759
  39.2 3.9 %collective-permute-start.3 = (f32[48,128]{1,0:T(8,128)S(1)}, f32[48,128]{1,0:T(8,128)S(1)}, u32[]{:S(2)}, u32[]{:S(2)}) collective-permute-start(f32[48,128]{1,0:T(8,128)S(1)} %get-tuple-element.47.to_w), channel_id=1, source_target_pairs={{0,15},{1,0},{2,1},{3,2},{4,3},{5,4},{6,5},{7,6},{8,7},{9,8},{10,9... | collective-permute-start | bytes 73736 | tf_op jit(solution)/shard_map/ppermute | solution.py:759
  40.7 7.1 %collective-permute-start.2 = (f32[48,128]{1,0:T(8,128)S(1)}, f32[48,128]{1,0:T(8,128)S(1)}, u32[]{:S(2)}, u32[]{:S(2)}) collective-permute-start(f32[48,128]{1,0:T(8,128)S(1)} %get-tuple-element.48.to_e), channel_id=1, source_target_pairs={{0,1},{1,2},{2,3},{3,4},{4,5},{5,6},{6,7},{7,8},{8,9},{9,10},{10,1... | collective-permute-start | bytes 73736 | tf_op jit(solution)/shard_map/ppermute | solution.py:759
  49.5 3.9 %collective-permute-start.5 = (f32[48,128]{1,0:T(8,128)S(1)}, f32[48,128]{1,0:T(8,128)S(1)}, u32[]{:S(2)}, u32[]{:S(2)}) collective-permute-start(f32[48,128]{1,0:T(8,128)S(1)} %get-tuple-element.52.to_w), channel_id=1, source_target_pairs={{0,15},{1,0},{2,1},{3,2},{4,3},{5,4},{6,5},{7,6},{8,7},{9,8},{10,9... | collective-permute-start | bytes 73736 | tf_op jit(solution)/shard_map/ppermute | solution.py:759
  49.6 7.2 %collective-permute-start.4 = (f32[48,128]{1,0:T(8,128)S(1)}, f32[48,128]{1,0:T(8,128)S(1)}, u32[]{:S(2)}, u32[]{:S(2)}) collective-permute-start(f32[48,128]{1,0:T(8,128)S(1)} %get-tuple-element.53.to_e), channel_id=1, source_target_pairs={{0,1},{1,2},{2,3},{3,4},{4,5},{5,6},{6,7},{7,8},{8,9},{9,10},{10,1... | collective-permute-start | bytes 73736 | tf_op jit(solution)/shard_map/ppermute | solution.py:759
  56.8 11.6 %copy-start = (f32[32,6,6,128]{3,0,2,1:T(8,128)S(1)}, f32[32,6,6,128]{3,0,2,1:T(8,128)}, u32[]{:S(2)}) copy-start(f32[32,6,6,128]{3,0,2,1:T(8,128)} %param.7) | copy-start | bytes 1769476

commit v10 on v9

--- a/solution.py
+++ b/solution.py
@@ -331,7 +331,10 @@
     return found
 
 
-def inner(group, env, v_ref, plain, emit):
+FACE_LINES, INSIDE_LINES, ALL_LINES = (0,), (1, 2), (0, 1, 2)
+
+
+def inner(group, env, v_ref, plain, emit, pairs=ALL_LINES):
     idx, tab, _, _ = env
     rows = group_rows(group)
 
@@ -346,7 +349,7 @@
     plus, minus = STIFF_FOLD
     even = [[v(6 * a + j) + v(30 - 6 * a + j) for a in range(3)] for j in range(6)]
     odd = [[v(6 * a + j) - v(30 - 6 * a + j) for a in range(3)] for j in range(6)]
-    for i in range(3):
+    for i in pairs:
         e = [weighted(plus[i], even[j]) for j in range(6)]
         o = [weighted(minus[i], odd[j]) for j in range(6)]
         for line in (i, 5 - i):
@@ -362,7 +365,11 @@
                 emit(n, value)
 
 
-def compact(idx, v_ref, h_ref, send_w, send_e):
+def line_at(n):
+    return n if n < 6 else n - 24
+
+
+def compact(idx, v_ref, h_ref, send_w, send_e, at=line_at):
     part = lax.shift_right_logical(lane_ids((8, 128)), 4)
     for face, ref in ((0, send_w), (1, send_e)):
         index = row_of(idx, face)
@@ -370,8 +377,9 @@
             n = face_nodes(face)[b]
             value = take(v_ref[n, 0:8, :], index)
             for k in range(1, 8):
-                source = v_ref if k < 4 else h_ref
-                other = take(source[n, 8 * (k % 4) : 8 * (k % 4) + 8, :], index)
+                part_rows = slice(8 * (k % 4), 8 * (k % 4) + 8)
+                source = v_ref[n, part_rows, :] if k < 4 else h_ref[at(n), part_rows, :]
+                other = take(source, index)
                 value = jnp.where(part == k, other, value)
             ref[8 * b : 8 * b + 8, :] = value
 
@@ -431,11 +439,29 @@
 HALF = 10.0
 
 
-def store(ref, rows):
+def store_lines(ref, rows):
     def emit(n, value):
-        ref[n, rows, :] = value
+        ref[line_at(n), rows, :] = value
 
     return emit
+
+
+def inside_kernel(idx, tab, own_c, far_c, v, out):
+    env = (idx, tab, own_c, far_c)
+
+    def loop(group, plain):
+        rows = group_rows(group)
+
+        def emit(n, value):
+            out[n - 6, rows, :] = value
+
+        inner(group, env, v, plain, emit, INSIDE_LINES)
+
+    either(tab, loop)
+
+
+def line_image(lines, inside, n, rows):
+    return inside[n - 6, rows, :] if 6 <= n < 30 else lines[line_at(n), rows, :]
 
 
 def guess_kernel(
@@ -486,7 +512,7 @@
         rows = group_rows(group)
         for n, extra in outer(group, idx, edge, 0).items():
             out[n, rows, :] -= extra
-        inner(group, env, out, plain, store(h_out, rows))
+        inner(group, env, out, plain, store_lines(h_out, rows), FACE_LINES)
 
     either(tab, loop)
     compact(idx, out, h_out, send_w, send_e)
@@ -519,7 +545,7 @@
 
 def two_steps_kernel(
     idx, tab, own_c, far_c, edge_idx, edge_own, edge_far,
-    t0, h0, to_w, to_e, from_w, from_e,
+    t0, h0, h0_in, to_w, to_e, from_w, from_e,
     t1, t2, h2, send_w, send_e, keep, edge,
 ):
     env = (idx, tab, own_c, far_c)
@@ -530,7 +556,7 @@
         rows = group_rows(group)
         extra = outer(group, idx, edge, 0)
         for n in range(36):
-            image = h0[n, rows, :]
+            image = line_image(h0, h0_in, n, rows)
             if n in extra:
                 image = image + extra[n]
             t1[n, rows, :] = (1.0 / HALF) * image - t0[n, rows, :]
@@ -542,7 +568,7 @@
             t2[n, rows, :] = (2.0 / HALF) * image - 2.0 * t1[n, rows, :] - t0[n, rows, :]
 
         inner(group, env, t1, plain, emit)
-        inner(group, env, t2, plain, store(h2, rows))
+        inner(group, env, t2, plain, store_lines(h2, rows), FACE_LINES)
 
     either(tab, loop)
     compact(idx, t2, h2, send_w, send_e)
@@ -567,7 +593,7 @@
 
 def last_steps_kernel(
     idx, tab, own_c, far_c, edge_idx, edge_own, edge_far,
-    t1, t2, h2, to_w, to_e, from_w, from_e, keep, part,
+    t1, t2, h2, h2_in, to_w, to_e, from_w, from_e, keep, part,
     t3, red, edge, acc, pad,
 ):
     env = (idx, tab, own_c, far_c)
@@ -579,7 +605,7 @@
         extra = outer(group, idx, edge, 0)
         sums = [jnp.zeros((8, 128), F32)] * 3
         for n in range(36):
-            image = h2[n, rows, :]
+            image = line_image(h2, h2_in, n, rows)
             if n in extra:
                 image = image + extra[n]
             c = t2[n, rows, :]
@@ -684,7 +710,7 @@
         part = pl.ds(48 * c, 48)
         stores.append(pltpu.make_async_copy(ready.at[:, part], out.at[:, part], sems.at[3 + c]))
         stores[c].start()
-    compact(lists, held, held, send_w, send_e)
+    compact(lists, held, held, send_w, send_e, lambda n: n)
     for copy in stores:
         copy.wait()
 
@@ -828,21 +854,26 @@
             VMEM((8, 128), F32),
         ]
 
-    t0, h0, *sent = run(residual_kernel, [vol, vol, edge, edge], [], head + [back, base, guess_edge])
+    lines, insides = shape(12, 32, 128), shape(24, 32, 128)
+    t0, h0, *sent = run(
+        residual_kernel, [vol, lines, edge, edge], [], head + [back, base, guess_edge]
+    )
     got = trade(*sent)
+    h0_in = run(inside_kernel, [insides], [], head + [t0])[0]
     t1, t2, h2, to_w, to_e, keep = run(
         two_steps_kernel,
-        [vol, vol, vol, edge, edge, both],
+        [vol, vol, lines, edge, edge, both],
         [VMEM((96, 128), F32)],
-        head + edges + [t0, h0, *sent, *got],
+        head + edges + [t0, h0, h0_in, *sent, *got],
     )
     got = trade(to_w, to_e)
+    h2_in = run(inside_kernel, [insides], [], head + [t2])[0]
     part = run(sums_kernel, [shape(8, 128)], work(5)[1:], [t0, t1, t2])[0]
     t3, red = run(
         last_steps_kernel,
         [vol, shape(16, 8, 128)],
         work(3),
-        head + edges + [t1, t2, h2, to_w, to_e, *got, keep, part],
+        head + edges + [t1, t2, h2, h2_in, to_w, to_e, *got, keep, part],
     )
     red = lax.all_to_all(red, "elem", 0, 0, tiled=True)
     out = call(

time: 70 us -> 69.6 us (level)
  waiting for transfers between devices: 16.1 us -> 15.2 us
    ppermute x6, waiting for transfers between devices: 16.1 us -> 15.2 us  [shift_by(): lax.ppermute(array, 'elem', [(i, (i + by) % count) for i in range(count)])]
    pallas_call x9 -> x11, Pallas kernels: 12.2 us -> 12.8 us  [call(): pl.pallas_call(kernel, out_shape=outs, in_specs=[pl.BlockSpec(memory_spac...]
  transfers between devices with their start and end apart: 7 -> 7, of which waited for: 5 -> 5; matrix products, arithmetic and copies ran while one was open for 0% -> 0% of each run, Pallas kernels for 4% -> 6%
where the time goes in v10:
time: 69.6 us; the launch traced here: 69.3 us
  blocking collectives  25.9 us (37%)
  starting transfers between devices  15.2 us (22%)
  waiting for transfers between devices  15.2 us (22%)
  Pallas kernels  12.8 us (18%)
    all_to_all x1, blocking collectives, shards(): back = lax.all_to_all(back, 'plane', 0, 0, tiled=True)  15.7 us
    ppermute x6, waiting for transfers between devices, shift_by(): lax.ppermute(array, 'elem', [(i, (i + by) % count) for i in range(count)])  15.2 us
    pallas_call x11, Pallas kernels, call(): pl.pallas_call(kernel, out_shape=outs, in_specs=[pl.BlockSpec(memory_spac...  12.8 us
    ppermute x6, starting transfers between devices, shift_by(): lax.ppermute(array, 'elem', [(i, (i + by) % count) for i in range(count)])  10.7 us
    all_to_all x1, blocking collectives, shards(): red = lax.all_to_all(red, 'elem', 0, 0, tiled=True)  10.2 us
    all_to_all x1, starting transfers between devices, shards(): came = lax.all_to_all(packed, 'plane', 0, 0, tiled=True)  4.53 us
  transfers between devices with their start and end apart: 7, of which 5 were waited for; matrix products, arithmetic and copies ran while one was open for 0% of the time, Pallas kernels for 6%

profile of v10, /device:TPU:0, one launch (start us, length us, event | category | flops | bytes accessed | tf_op | source)
XLA Modules:
  0.0 69.3 jit_solution(18207179169962133343)
XLA Ops:
  0.0 2.1 %shard_map.74 = (f32[8,144,128]{2,1,0:T(8,128)}, f32[48,128]{1,0:T(8,128)S(1)}, f32[48,128]{1,0:T(8,128)S(1)}) custom-call(f32[36,32,128]{2,1,0:T(8,128)} %bitcast.11, s32[8,128]{1,0:T(8,128)} %links.3), custom_call_target="tpu_custom_call" | custom-call | flops 4000000 | bytes 1232896 | tf_op jit(solution)/shard_map/pallas_call | solution.py:110
  2.2 4.5 %all-to-all-start = ((f32[8,144,128]{2,1,0:T(8,128)}), f32[8,144,128]{2,1,0:T(8,128)S(1)}, u32[]{:S(2)}, u32[]{:S(2)}) async-start(f32[8,144,128]{2,1,0:T(8,128)} %get-tuple-element.38), calls=%async_computation | async-start | bytes 1179648 | tf_op jit(solution)/shard_map/all_to_all | solution.py:809
  6.7 6.5 %collective-permute-start.1 = (f32[48,128]{1,0:T(8,128)S(1)}, f32[48,128]{1,0:T(8,128)S(1)}, u32[]{:S(2)}, u32[]{:S(2)}) collective-permute-start(f32[48,128]{1,0:T(8,128)S(1)} %get-tuple-element.39.to_w), channel_id=1, source_target_pairs={{0,15},{1,0},{2,1},{3,2},{4,3},{5,4},{6,5},{7,6},{8,7},{9,8},{10,9... | collective-permute-start | bytes 73736 | tf_op jit(solution)/shard_map/ppermute | solution.py:785
  13.2 2.3 %shard_map.73 = (s32[24,128]{1,0:T(8,128)S(1)}, s32[8,128]{1,0:T(8,128)S(1)}, f32[8,128]{1,0:T(8,128)S(1)}, f32[36,8,128]{2,1,0:T(8,128)S(1)}, f32[36,8,128]{2,1...) custom-call(s32[8,128]{1,0:T(8,128)S(1)} %copy-done.3, ...), custom_call_target="tpu_custom_call" | custom-call | flops 4000000 | bytes 1803264 | tf_op jit(solution)/shard_map/pallas_call | solution.py:110
  15.5 4.8 %collective-permute-done.from_w = f32[48,128]{1,0:T(8,128)S(1)} collective-permute-done((f32[48,128]{1,0:T(8,128)S(1)}, f32[48,128]{1,0:T(8,128)S(1)}, u32[]{:S(2)}, u32[]{:S(2)}) %collective-permute-start) | collective-permute-done | bytes 24608 | tf_op jit(solution)/shard_map/ppermute | solution.py:785
  20.3 0.2 shard_map.75.edge
  20.5 1.7 %shard_map.76 = f32[8,144,128]{2,1,0:T(8,128)S(1)} custom-call(s32[24,128]{1,0:T(8,128)S(1)} %get-tuple-element.31.idx, f32[8,144,128]{2,1,0:T(8,128)S(1)} %all-to-all-done.came, f32[2,36,16,256]{3,2,1,0:T(8,128)S(1)} %bitcast.14, bf16[2,256,256]{2,1,0:T(8,128)(2,1)S(1)} %copy-done.2), custom_call_target="tpu_custom_call" | custom-call | flops 4000000 | bytes 2895872 | tf_op jit(solution)/shard_map/pallas_call | solution.py:110
  22.2 15.7 %all_to_all.15.back = f32[8,144,128]{2,1,0:T(8,128)S(1)} all-to-all(f32[8,144,128]{2,1,0:T(8,128)S(1)} %shard_map.76), channel_id=1, replica_groups=mesh['plane'=8,'elem'=16] {'plane'}, dimensions={0} | all-to-all | bytes 1179648 | tf_op jit(solution)/shard_map/all_to_all | solution.py:848
  37.9 1.1 %shard_map.77 = (f32[36,32,128]{2,1,0:T(8,128)S(1)}, f32[12,32,128]{2,1,0:T(8,128)S(1)}, f32[48,128]{1,0:T(8,128)S(1)}, f32[48,128]{1,0:T(8,128)S(1)}) custom-call(s32[24,128]{1,0:T(8,128)S(1)} %get-tuple-element.31.idx, f32[8,128]{1,0:T(8,128)S(1)} %get-tuple-element.32.tab, f32[36,8,128]{2,1,0:T(8,128)S(1)} %get-tuple-element.33.own_c, ...), custom_call_target="tpu_custom_call" | custom-call | flops 4000000 | bytes 2351104 | tf_op jit(solution)/shard_map/pallas_call | solution.py:110
  39.0 1.6 %collective-permute-start.3 = (f32[48,128]{1,0:T(8,128)S(1)}, f32[48,128]{1,0:T(8,128)S(1)}, u32[]{:S(2)}, u32[]{:S(2)}) collective-permute-start(f32[48,128]{1,0:T(8,128)S(1)} %get-tuple-element.47.to_w), channel_id=1, source_target_pairs={{0,15},{1,0},{2,1},{3,2},{4,3},{5,4},{6,5},{7,6},{8,7},{9,8},{10,9... | collective-permute-start | bytes 73736 | tf_op jit(solution)/shard_map/ppermute | solution.py:785
  40.6 0.5 collective-permute-start.2
  41.1 0.5 shard_map.78.h0_in
  41.6 1.3 %collective-permute-done.3.from_e = f32[48,128]{1,0:T(8,128)S(1)} collective-permute-done((f32[48,128]{1,0:T(8,128)S(1)}, f32[48,128]{1,0:T(8,128)S(1)}, u32[]{:S(2)}, u32[]{:S(2)}) %collective-permute-start.3) | collective-permute-done | bytes 24608 | tf_op jit(solution)/shard_map/ppermute | solution.py:785
  42.9 4.8 %collective-permute-done.2.from_w = f32[48,128]{1,0:T(8,128)S(1)} collective-permute-done((f32[48,128]{1,0:T(8,128)S(1)}, f32[48,128]{1,0:T(8,128)S(1)}, u32[]{:S(2)}, u32[]{:S(2)}) %collective-permute-start.2) | collective-permute-done | bytes 24608 | tf_op jit(solution)/shard_map/ppermute | solution.py:785
  47.7 1.4 %shard_map.79 = (f32[36,32,128]{2,1,0:T(8,128)S(1)}, f32[36,32,128]{2,1,0:T(8,128)S(1)}, f32[12,32,128]{2,1,0:T(8,128)S(1)}, f32[48,128]{1,0:T(8,128)S(1)}, f32[...) custom-call(s32[24,128]{1,0:T(8,128)S(1)} %get-tuple-element.31.idx, f32[8,128]{1,0:T(8,128)S(1)} %get-tuple-element.32.tab, ...), custom_call_target="tpu_custom_call" | custom-call | flops 4000000 | bytes 3362816 | tf_op jit(solution)/shard_map/pallas_call | solution.py:110
  49.1 0.1 collective-permute-start.5
  49.2 2.0 %collective-permute-start.4 = (f32[48,128]{1,0:T(8,128)S(1)}, f32[48,128]{1,0:T(8,128)S(1)}, u32[]{:S(2)}, u32[]{:S(2)}) collective-permute-start(f32[48,128]{1,0:T(8,128)S(1)} %get-tuple-element.53.to_e), channel_id=1, source_target_pairs={{0,1},{1,2},{2,3},{3,4},{4,5},{5,6},{6,7},{7,8},{8,9},{9,10},{10,1... | collective-permute-start | bytes 73736 | tf_op jit(solution)/shard_map/ppermute | solution.py:785
  51.2 0.5 shard_map.80.h2_in
  51.7 0.5 shard_map.81.part
  52.2 0.8 %collective-permute-done.5.from_e = f32[48,128]{1,0:T(8,128)S(1)} collective-permute-done((f32[48,128]{1,0:T(8,128)S(1)}, f32[48,128]{1,0:T(8,128)S(1)}, u32[]{:S(2)}, u32[]{:S(2)}) %collective-permute-start.5) | collective-permute-done | bytes 24608 | tf_op jit(solution)/shard_map/ppermute | solution.py:785
  53.0 3.4 %collective-permute-done.4.from_w = f32[48,128]{1,0:T(8,128)S(1)} collective-permute-done((f32[48,128]{1,0:T(8,128)S(1)}, f32[48,128]{1,0:T(8,128)S(1)}, u32[]{:S(2)}, u32[]{:S(2)}) %collective-permute-start.4) | collective-permute-done | bytes 24608 | tf_op jit(solution)/shard_map/ppermute | solution.py:785
  56.4 1.4 %shard_map.82 = (f32[36,32,128]{2,1,0:T(8,128)S(1)}, f32[16,8,128]{2,1,0:T(8,128)S(1)}) custom-call(s32[24,128]{1,0:T(8,128)S(1)} %get-tuple-element.31.idx, f32[8,128]{1,0:T(8,128)S(1)} %get-tuple-element.32.tab, f32[36,8,128]{2,1,0:T(8,128)S(1)} %get-tuple-element.33.own_c, f32[36,8,128]{2,1,0:T(8,128)S(1)} %get-tuple-element.34.far_c, ...), custom_call_target="tpu_custom_call" | custom-call | flops 4000000 | bytes 3186688 | tf_op jit(solution)/shard_map/pallas_call | solution.py:110
  57.8 10.2 %all_to_all.16.red = f32[16,8,128]{2,1,0:T(8,128)S(1)} all-to-all(f32[16,8,128]{2,1,0:T(8,128)S(1)} %get-tuple-element.55), channel_id=1, replica_groups=mesh['plane'=8,'elem'=16] {'elem'}, dimensions={0} | all-to-all | bytes 131072 | tf_op jit(solution)/shard_map/all_to_all | solution.py:878
  68.0 1.2 %shard_map.83 = f32[36,32,128]{2,1,0:T(8,128)} custom-call(f32[16,8,128]{2,1,0:T(8,128)S(1)} %all_to_all.16.red, f32[36,32,128]{2,1,0:T(8,128)S(1)} %bitcast.13, f32[36,32,128]{2,1,0:T(8,128)S(1)} %get-tuple-element.45.v.t0, f32[36,32,128]{2,1,0:T(8,128)S(1)} %get-tuple-element.49.t1, f32[36,32,128]{2,1,0:T(8,128)S(1)} %get-tuple-element.50.v.t2, ...), custom_call_target="tpu_custom_call" | custom-call | flops 4000000 | bytes 3604480 | tf_op jit(solution)/shard_map/pallas_call | solution.py:110
  (17 shorter events, 0.0 us)
Async XLA Ops:
  0.0 13.2 %copy-start.3 = (s32[8,128]{1,0:T(8,128)S(1)}, s32[8,128]{1,0:T(8,128)}, u32[]{:S(2)}) copy-start(s32[8,128]{1,0:T(8,128)} %links.3) | copy-start | bytes 12292
  0.0 13.2 %copy-start.6 = (s32[128]{0:T(128)S(1)}, s32[128]{0:T(128)}, u32[]{:S(2)}) copy-start(s32[128]{0:T(128)} %param.12) | copy-start | bytes 1540
  0.0 13.2 %copy-start.4 = (s32[2,8,128]{2,1,0:T(8,128)S(1)}, s32[2,8,128]{2,1,0:T(8,128)}, u32[]{:S(2)}) copy-start(s32[2,8,128]{2,1,0:T(8,128)} %sides.1) | copy-start | bytes 24580
  0.0 13.2 %copy-start.5 = (f32[128]{0:T(128)S(1)}, f32[128]{0:T(128)}, u32[]{:S(2)}) copy-start(f32[128]{0:T(128)} %param.9) | copy-start | bytes 1540
  2.2 18.4 %copy-start.1 = (f32[2,256,6,6,16]{1,4,3,2,0:T(8,128)S(1)}, f32[2,256,6,6,16]{1,4,3,2,0:T(8,128)}, u32[]{:S(2)}) copy-start(f32[2,256,6,6,16]{1,4,3,2,0:T(8,128)} %param.8) | copy-start | bytes 3538948
  2.2 18.4 %copy-start.2 = (bf16[2,256,256]{2,1,0:T(8,128)(2,1)S(1)}, bf16[2,256,256]{2,1,0:T(8,128)(2,1)}, u32[]{:S(2)}) copy-start(bf16[2,256,256]{2,1,0:T(8,128)(2,1)} %constant.2.clone.synth) | copy-start | bytes 786436
  2.2 18.3 %all-to-all-start = ((f32[8,144,128]{2,1,0:T(8,128)}), f32[8,144,128]{2,1,0:T(8,128)S(1)}, u32[]{:S(2)}, u32[]{:S(2)}) async-start(f32[8,144,128]{2,1,0:T(8,128)} %get-tuple-element.38), calls=%async_computation | async-start | bytes 1179648 | tf_op jit(solution)/shard_map/all_to_all | solution.py:809
  6.7 8.8 %collective-permute-start.1 = (f32[48,128]{1,0:T(8,128)S(1)}, f32[48,128]{1,0:T(8,128)S(1)}, u32[]{:S(2)}, u32[]{:S(2)}) collective-permute-start(f32[48,128]{1,0:T(8,128)S(1)} %get-tuple-element.39.to_w), channel_id=1, source_target_pairs={{0,15},{1,0},{2,1},{3,2},{4,3},{5,4},{6,5},{7,6},{8,7},{9,8},{10,9... | collective-permute-start | bytes 73736 | tf_op jit(solution)/shard_map/ppermute | solution.py:785
  13.2 7.1 %collective-permute-start = (f32[48,128]{1,0:T(8,128)S(1)}, f32[48,128]{1,0:T(8,128)S(1)}, u32[]{:S(2)}, u32[]{:S(2)}) collective-permute-start(f32[48,128]{1,0:T(8,128)S(1)} %get-tuple-element.40.to_e), channel_id=1, source_target_pairs={{0,1},{1,2},{2,3},{3,4},{4,5},{5,6},{6,7},{7,8},{8,9},{9,10},{10,1... | collective-permute-start | bytes 73736 | tf_op jit(solution)/shard_map/ppermute | solution.py:785
  39.0 3.9 %collective-permute-start.3 = (f32[48,128]{1,0:T(8,128)S(1)}, f32[48,128]{1,0:T(8,128)S(1)}, u32[]{:S(2)}, u32[]{:S(2)}) collective-permute-start(f32[48,128]{1,0:T(8,128)S(1)} %get-tuple-element.47.to_w), channel_id=1, source_target_pairs={{0,15},{1,0},{2,1},{3,2},{4,3},{5,4},{6,5},{7,6},{8,7},{9,8},{10,9... | collective-permute-start | bytes 73736 | tf_op jit(solution)/shard_map/ppermute | solution.py:785
  40.6 7.1 %collective-permute-start.2 = (f32[48,128]{1,0:T(8,128)S(1)}, f32[48,128]{1,0:T(8,128)S(1)}, u32[]{:S(2)}, u32[]{:S(2)}) collective-permute-start(f32[48,128]{1,0:T(8,128)S(1)} %get-tuple-element.48.to_e), channel_id=1, source_target_pairs={{0,1},{1,2},{2,3},{3,4},{4,5},{5,6},{6,7},{7,8},{8,9},{9,10},{10,1... | collective-permute-start | bytes 73736 | tf_op jit(solution)/shard_map/ppermute | solution.py:785
  49.1 3.9 %collective-permute-start.5 = (f32[48,128]{1,0:T(8,128)S(1)}, f32[48,128]{1,0:T(8,128)S(1)}, u32[]{:S(2)}, u32[]{:S(2)}) collective-permute-start(f32[48,128]{1,0:T(8,128)S(1)} %get-tuple-element.52.to_w), channel_id=1, source_target_pairs={{0,15},{1,0},{2,1},{3,2},{4,3},{5,4},{6,5},{7,6},{8,7},{9,8},{10,9... | collective-permute-start | bytes 73736 | tf_op jit(solution)/shard_map/ppermute | solution.py:785
  49.2 7.2 %collective-permute-start.4 = (f32[48,128]{1,0:T(8,128)S(1)}, f32[48,128]{1,0:T(8,128)S(1)}, u32[]{:S(2)}, u32[]{:S(2)}) collective-permute-start(f32[48,128]{1,0:T(8,128)S(1)} %get-tuple-element.53.to_e), channel_id=1, source_target_pairs={{0,1},{1,2},{2,3},{3,4},{4,5},{5,6},{6,7},{7,8},{8,9},{9,10},{10,1... | collective-permute-start | bytes 73736 | tf_op jit(solution)/shard_map/ppermute | solution.py:785
  56.4 11.6 %copy-start = (f32[32,6,6,128]{3,0,2,1:T(8,128)S(1)}, f32[32,6,6,128]{3,0,2,1:T(8,128)}, u32[]{:S(2)}) copy-start(f32[32,6,6,128]{3,0,2,1:T(8,128)} %param.7) | copy-start | bytes 1769476

commit v11 on v10

--- a/solution.py
+++ b/solution.py
@@ -369,7 +369,7 @@
     return n if n < 6 else n - 24
 
 
-def compact(idx, v_ref, h_ref, send_w, send_e, at=line_at):
+def compact(idx, v_ref, h_ref, send_e, send_w, at=line_at):
     part = lax.shift_right_logical(lane_ids((8, 128)), 4)
     for face, ref in ((0, send_w), (1, send_e)):
         index = row_of(idx, face)
@@ -399,7 +399,7 @@
     return [ref[8 * b : 8 * b + 8, :] for b in range(6)]
 
 
-def merge(to_w, to_e):
+def merge(to_e, to_w):
     west = lane_ids((8, 128)) < 64
     plain, inner_h = [], []
     for w, e in zip(edge_blocks(to_w), edge_blocks(to_e)):
@@ -487,15 +487,15 @@
     either(tab, loop)
 
 
-def guess_edge_kernel(edge_idx, edge_own, edge_far, to_w, to_e, from_w, from_e, edge):
-    mine, _ = merge(to_w, to_e)
-    theirs, _ = merge(from_w, from_e)
+def guess_edge_kernel(edge_idx, edge_own, edge_far, to_e, to_w, from_e, from_w, edge):
+    mine, _ = merge(to_e, to_w)
+    theirs, _ = merge(from_e, from_w)
     for b, value in enumerate(edge_term(edge_idx, edge_own, edge_far, mine, theirs, 0)):
         edge[8 * b : 8 * b + 8, :] = value
 
 
 def residual_kernel(
-    idx, tab, own_c, far_c, back, base, edge, out, h_out, send_w, send_e
+    idx, tab, own_c, far_c, back, base, edge, out, h_out, send_e, send_w
 ):
     env = (idx, tab, own_c, far_c)
 
@@ -515,13 +515,13 @@
         inner(group, env, out, plain, store_lines(h_out, rows), FACE_LINES)
 
     either(tab, loop)
-    compact(idx, out, h_out, send_w, send_e)
-
-
-def edge_steps(tables, to_w, to_e, from_w, from_e, before, edge, keep):
+    compact(idx, out, h_out, send_e, send_w)
+
+
+def edge_steps(tables, to_e, to_w, from_e, from_w, before, edge, keep):
     edge_idx, edge_own, edge_far = tables
-    mine, mine_h = merge(to_w, to_e)
-    theirs, theirs_h = merge(from_w, from_e)
+    mine, mine_h = merge(to_e, to_w)
+    theirs, theirs_h = merge(from_e, from_w)
     scale = (1.0 if before is None else 2.0) / HALF
     first = edge_term(edge_idx, edge_own, edge_far, mine, theirs, 0)
     facing = edge_term(edge_idx, edge_own, edge_far, theirs, mine, 2)
@@ -545,12 +545,12 @@
 
 def two_steps_kernel(
     idx, tab, own_c, far_c, edge_idx, edge_own, edge_far,
-    t0, h0, h0_in, to_w, to_e, from_w, from_e,
-    t1, t2, h2, send_w, send_e, keep, edge,
+    t0, h0, h0_in, to_e, to_w, from_e, from_w,
+    t1, t2, h2, send_e, send_w, keep, edge,
 ):
     env = (idx, tab, own_c, far_c)
     tables = (edge_idx, edge_own, edge_far)
-    edge_steps(tables, to_w, to_e, from_w, from_e, None, edge, keep)
+    edge_steps(tables, to_e, to_w, from_e, from_w, None, edge, keep)
 
     def loop(group, plain):
         rows = group_rows(group)
@@ -571,7 +571,7 @@
         inner(group, env, t2, plain, store_lines(h2, rows), FACE_LINES)
 
     either(tab, loop)
-    compact(idx, t2, h2, send_w, send_e)
+    compact(idx, t2, h2, send_e, send_w)
 
 
 def sums_kernel(t0, t1, t2, part, acc, pad):
@@ -593,12 +593,12 @@
 
 def last_steps_kernel(
     idx, tab, own_c, far_c, edge_idx, edge_own, edge_far,
-    t1, t2, h2, h2_in, to_w, to_e, from_w, from_e, keep, part,
+    t1, t2, h2, h2_in, to_e, to_w, from_e, from_w, keep, part,
     t3, red, edge, acc, pad,
 ):
     env = (idx, tab, own_c, far_c)
     tables = (edge_idx, edge_own, edge_far)
-    edge_steps(tables, to_w, to_e, from_w, from_e, keep, edge, None)
+    edge_steps(tables, to_e, to_w, from_e, from_w, keep, edge, None)
 
     def loop(group, plain):
         rows = group_rows(group)
@@ -634,9 +634,10 @@
 
 
 def finish_kernel(red, x0, t0, t1, t2, t3, out, coef, held, sems):
-    total = red[0]
-    for k in range(1, 16):
-        total = total + red[k]
+    parts = [red[k] for k in range(16)]
+    while len(parts) > 1:
+        parts = [a + b for a, b in zip(parts[::2], parts[1::2])]
+    total = parts[0]
     even = [total[2 * k : 2 * k + 1] for k in range(4)]
     odd = [total[2 * k + 1 : 2 * k + 2] for k in range(4)]
     moment = []
@@ -674,6 +675,7 @@
     turned = jnp.concatenate(weight + [jnp.zeros((4, 128), F32)], axis=0).T
     for k in range(4):
         coef[k] = jnp.broadcast_to(turned[0:32, k : k + 1], (32, 128))
+    cuts = (0, 15, 30, 36)
     copies = []
     for c in range(3):
         def add(n, carry):
@@ -681,20 +683,21 @@
             held[n] = x0[n] + terms
             return carry
 
-        lax.fori_loop(12 * c, 12 * c + 12, add, 0, unroll=3)
-        part = pl.ds(12 * c, 12)
+        lax.fori_loop(cuts[c], cuts[c + 1], add, 0, unroll=3)
+        part = pl.ds(cuts[c], cuts[c + 1] - cuts[c])
         copies.append(pltpu.make_async_copy(held.at[part], out.at[part], sems.at[c]))
         copies[c].start()
     for copy in copies:
         copy.wait()
 
 
-def pack_kernel(u, links, out, send_w, send_e, held, ready, near_links, lists, sems):
+def pack_kernel(u, links, out, send_e, send_w, held, ready, near_links, lists, sems):
     loads, stores = [], []
     first = pltpu.make_async_copy(links, near_links, sems.at[6])
     first.start()
+    cuts = (0, 4, 8, 9)
     for c in range(3):
-        part = pl.ds(12 * c, 12)
+        part = pl.ds(4 * cuts[c], 4 * (cuts[c + 1] - cuts[c]))
         loads.append(pltpu.make_async_copy(u.at[part], held.at[part], sems.at[c]))
         loads[c].start()
     first.wait()
@@ -704,13 +707,13 @@
         lists[side : side + 1, :] = boundary(remote, side)[0].astype(jnp.int32)
     for c in range(3):
         loads[c].wait()
-        for g in range(3 * c, 3 * c + 3):
+        for g in range(cuts[c], cuts[c + 1]):
             turned = held[4 * g : 4 * g + 4].reshape(128, 128).T
             ready[:, 16 * g : 16 * g + 16, :] = turned.reshape(8, 16, 128)
-        part = pl.ds(48 * c, 48)
+        part = pl.ds(16 * cuts[c], 16 * (cuts[c + 1] - cuts[c]))
         stores.append(pltpu.make_async_copy(ready.at[:, part], out.at[:, part], sems.at[3 + c]))
         stores[c].start()
-    compact(lists, held, held, send_w, send_e, lambda n: n)
+    compact(lists, held, held, send_e, send_w, lambda n: n)
     for copy in stores:
         copy.wait()
 
@@ -828,8 +831,9 @@
     def run(kernel, outs, scratch, args):
         return call(kernel, outs, scratch, args, [VMEM] * len(args))
 
-    def trade(send_w, send_e):
-        return shift_by(send_e, 1), shift_by(send_w, -1)
+    def trade(send_e, send_w):
+        from_w = shift_by(send_e, 1)
+        return shift_by(send_w, -1), from_w
 
     guess_edge = run(guess_edge_kernel, [shape(48, 128)], [], [*edges, *sent, *trade(*sent)])[0]
     came, guess_edge, base = lax.optimization_barrier((came, guess_edge, base))
@@ -860,20 +864,20 @@
     )
     got = trade(*sent)
     h0_in = run(inside_kernel, [insides], [], head + [t0])[0]
-    t1, t2, h2, to_w, to_e, keep = run(
+    t1, t2, h2, to_e, to_w, keep = run(
         two_steps_kernel,
         [vol, vol, lines, edge, edge, both],
         [VMEM((96, 128), F32)],
         head + edges + [t0, h0, h0_in, *sent, *got],
     )
-    got = trade(to_w, to_e)
+    got = trade(to_e, to_w)
     h2_in = run(inside_kernel, [insides], [], head + [t2])[0]
     part = run(sums_kernel, [shape(8, 128)], work(5)[1:], [t0, t1, t2])[0]
     t3, red = run(
         last_steps_kernel,
         [vol, shape(16, 8, 128)],
         work(3),
-        head + edges + [t1, t2, h2, h2_in, to_w, to_e, *got, keep, part],
+        head + edges + [t1, t2, h2, h2_in, to_e, to_w, *got, keep, part],
     )
     red = lax.all_to_all(red, "elem", 0, 0, tiled=True)
     out = call(

time: 69.6 us -> 68.2 us (0.980)
  waiting for transfers between devices: 15.2 us -> 3.99 us
  starting transfers between devices: 15.2 us -> 23.1 us
  blocking collectives: 25.9 us -> 27.9 us
    ppermute x6, waiting for transfers between devices: 15.2 us -> 2 us  [shift_by(): lax.ppermute(array, 'elem', [(i, (i + by) % count) for i in range(count)])]
    ppermute x6, starting transfers between devices: 10.7 us -> 18.6 us  [shift_by(): lax.ppermute(array, 'elem', [(i, (i + by) % count) for i in range(count)])]
    all_to_all x1, blocking collectives: 10.2 us -> 14.3 us  [shards(): red = lax.all_to_all(red, 'elem', 0, 0, tiled=True)]
    all_to_all x1, blocking collectives: 15.7 us -> 13.7 us  [shards(): back = lax.all_to_all(back, 'plane', 0, 0, tiled=True)]
    all_to_all x1, waiting for transfers between devices: 0.01 us -> 1.98 us  [shards(): came = lax.all_to_all(packed, 'plane', 0, 0, tiled=True)]
  transfers between devices with their start and end apart: 7 -> 7, of which waited for: 5 -> 3; matrix products, arithmetic and copies ran while one was open for 0% -> 0% of each run, Pallas kernels for 6% -> 6%
where the time goes in v11:
time: 68.2 us; the launch traced here: 67.9 us
  blocking collectives  27.9 us (41%)
  starting transfers between devices  23.1 us (34%)
  Pallas kernels  12.7 us (19%)
  waiting for transfers between devices  3.99 us (6%)
    ppermute x6, starting transfers between devices, shift_by(): lax.ppermute(array, 'elem', [(i, (i + by) % count) for i in range(count)])  18.6 us
    all_to_all x1, blocking collectives, shards(): red = lax.all_to_all(red, 'elem', 0, 0, tiled=True)  14.3 us
    all_to_all x1, blocking collectives, shards(): back = lax.all_to_all(back, 'plane', 0, 0, tiled=True)  13.7 us
    pallas_call x11, Pallas kernels, call(): pl.pallas_call(kernel, out_shape=outs, in_specs=[pl.BlockSpec(memory_spac...  12.7 us
    all_to_all x1, starting transfers between devices, shards(): came = lax.all_to_all(packed, 'plane', 0, 0, tiled=True)  4.53 us
    ppermute x6, waiting for transfers between devices, shift_by(): lax.ppermute(array, 'elem', [(i, (i + by) % count) for i in range(count)])  2 us
    all_to_all x1, waiting for transfers between devices, shards(): came = lax.all_to_all(packed, 'plane', 0, 0, tiled=True)  1.98 us
  transfers between devices with their start and end apart: 7, of which 3 were waited for; matrix products, arithmetic and copies ran while one was open for 0% of the time, Pallas kernels for 6%

profile of v11, /device:TPU:0, one launch (start us, length us, event | category | flops | bytes accessed | tf_op | source)
XLA Modules:
  0.0 67.9 jit_solution(7221614912019014537)
XLA Ops:
  0.0 2.1 %shard_map.74 = (f32[8,144,128]{2,1,0:T(8,128)}, f32[48,128]{1,0:T(8,128)S(1)}, f32[48,128]{1,0:T(8,128)S(1)}) custom-call(f32[36,32,128]{2,1,0:T(8,128)} %bitcast.11, s32[8,128]{1,0:T(8,128)} %links.3), custom_call_target="tpu_custom_call" | custom-call | flops 4000000 | bytes 1232896 | tf_op jit(solution)/shard_map/pallas_call | solution.py:110
  2.1 0.0 copy-start.2
  2.1 4.5 %all-to-all-start = ((f32[8,144,128]{2,1,0:T(8,128)}), f32[8,144,128]{2,1,0:T(8,128)S(1)}, u32[]{:S(2)}, u32[]{:S(2)}) async-start(f32[8,144,128]{2,1,0:T(8,128)} %get-tuple-element.38), calls=%async_computation | async-start | bytes 1179648 | tf_op jit(solution)/shard_map/all_to_all | solution.py:812
  6.7 1.6 %collective-permute-start.1 = (f32[48,128]{1,0:T(8,128)S(1)}, f32[48,128]{1,0:T(8,128)S(1)}, u32[]{:S(2)}, u32[]{:S(2)}) collective-permute-start(f32[48,128]{1,0:T(8,128)S(1)} %get-tuple-element.39.to_e), channel_id=1, source_target_pairs={{0,1},{1,2},{2,3},{3,4},{4,5},{5,6},{6,7},{7,8},{8,9},{9,10},{10,1... | collective-permute-start | bytes 73736 | tf_op jit(solution)/shard_map/ppermute | solution.py:788
  8.2 5.0 %collective-permute-start = (f32[48,128]{1,0:T(8,128)S(1)}, f32[48,128]{1,0:T(8,128)S(1)}, u32[]{:S(2)}, u32[]{:S(2)}) collective-permute-start(f32[48,128]{1,0:T(8,128)S(1)} %get-tuple-element.40.to_w), channel_id=1, source_target_pairs={{0,15},{1,0},{2,1},{3,2},{4,3},{5,4},{6,5},{7,6},{8,7},{9,8},{10,9... | collective-permute-start | bytes 73736 | tf_op jit(solution)/shard_map/ppermute | solution.py:788
  13.2 2.3 %shard_map.73 = (s32[24,128]{1,0:T(8,128)S(1)}, s32[8,128]{1,0:T(8,128)S(1)}, f32[8,128]{1,0:T(8,128)S(1)}, f32[36,8,128]{2,1,0:T(8,128)S(1)}, f32[36,8,128]{2,1...) custom-call(s32[8,128]{1,0:T(8,128)S(1)} %copy-done.3, ...), custom_call_target="tpu_custom_call" | custom-call | flops 4000000 | bytes 1803264 | tf_op jit(solution)/shard_map/pallas_call | solution.py:110
  15.5 0.2 shard_map.75.edge
  15.7 2.0 %all-to-all-done.came = f32[8,144,128]{2,1,0:T(8,128)S(1)} async-done(((f32[8,144,128]{2,1,0:T(8,128)}), f32[8,144,128]{2,1,0:T(8,128)S(1)}, u32[]{:S(2)}, u32[]{:S(2)}) %all-to-all-start) | async-done | bytes 589856 | tf_op jit(solution)/shard_map/all_to_all | solution.py:812
  17.7 1.7 %shard_map.76 = f32[8,144,128]{2,1,0:T(8,128)S(1)} custom-call(s32[24,128]{1,0:T(8,128)S(1)} %get-tuple-element.31.idx, f32[8,144,128]{2,1,0:T(8,128)S(1)} %all-to-all-done.came, f32[2,36,16,256]{3,2,1,0:T(8,128)S(1)} %bitcast.14, bf16[2,256,256]{2,1,0:T(8,128)(2,1)S(1)} %copy-done.2), custom_call_target="tpu_custom_call" | custom-call | flops 4000000 | bytes 2895872 | tf_op jit(solution)/shard_map/pallas_call | solution.py:110
  19.4 13.7 %all_to_all.15.back = f32[8,144,128]{2,1,0:T(8,128)S(1)} all-to-all(f32[8,144,128]{2,1,0:T(8,128)S(1)} %shard_map.76), channel_id=1, replica_groups=mesh['plane'=8,'elem'=16] {'plane'}, dimensions={0} | all-to-all | bytes 1179648 | tf_op jit(solution)/shard_map/all_to_all | solution.py:852
  33.1 1.1 %shard_map.77 = (f32[36,32,128]{2,1,0:T(8,128)S(1)}, f32[12,32,128]{2,1,0:T(8,128)S(1)}, f32[48,128]{1,0:T(8,128)S(1)}, f32[48,128]{1,0:T(8,128)S(1)}) custom-call(s32[24,128]{1,0:T(8,128)S(1)} %get-tuple-element.31.idx, f32[8,128]{1,0:T(8,128)S(1)} %get-tuple-element.32.tab, f32[36,8,128]{2,1,0:T(8,128)S(1)} %get-tuple-element.33.own_c, ...), custom_call_target="tpu_custom_call" | custom-call | flops 4000000 | bytes 2351104 | tf_op jit(solution)/shard_map/pallas_call | solution.py:110
  34.1 1.5 %collective-permute-start.3 = (f32[48,128]{1,0:T(8,128)S(1)}, f32[48,128]{1,0:T(8,128)S(1)}, u32[]{:S(2)}, u32[]{:S(2)}) collective-permute-start(f32[48,128]{1,0:T(8,128)S(1)} %get-tuple-element.47.to_e), channel_id=1, source_target_pairs={{0,1},{1,2},{2,3},{3,4},{4,5},{5,6},{6,7},{7,8},{8,9},{9,10},{10,1... | collective-permute-start | bytes 73736 | tf_op jit(solution)/shard_map/ppermute | solution.py:788
  35.6 5.0 %collective-permute-start.2 = (f32[48,128]{1,0:T(8,128)S(1)}, f32[48,128]{1,0:T(8,128)S(1)}, u32[]{:S(2)}, u32[]{:S(2)}) collective-permute-start(f32[48,128]{1,0:T(8,128)S(1)} %get-tuple-element.48.to_w), channel_id=1, source_target_pairs={{0,15},{1,0},{2,1},{3,2},{4,3},{5,4},{6,5},{7,6},{8,7},{9,8},{10,9... | collective-permute-start | bytes 73736 | tf_op jit(solution)/shard_map/ppermute | solution.py:788
  40.6 0.5 shard_map.78.h0_in
  41.1 1.3 %collective-permute-done.3.from_w = f32[48,128]{1,0:T(8,128)S(1)} collective-permute-done((f32[48,128]{1,0:T(8,128)S(1)}, f32[48,128]{1,0:T(8,128)S(1)}, u32[]{:S(2)}, u32[]{:S(2)}) %collective-permute-start.3) | collective-permute-done | bytes 24608 | tf_op jit(solution)/shard_map/ppermute | solution.py:788
  42.3 1.4 %shard_map.79 = (f32[36,32,128]{2,1,0:T(8,128)S(1)}, f32[36,32,128]{2,1,0:T(8,128)S(1)}, f32[12,32,128]{2,1,0:T(8,128)S(1)}, f32[48,128]{1,0:T(8,128)S(1)}, f32[...) custom-call(s32[24,128]{1,0:T(8,128)S(1)} %get-tuple-element.31.idx, f32[8,128]{1,0:T(8,128)S(1)} %get-tuple-element.32.tab, ...), custom_call_target="tpu_custom_call" | custom-call | flops 4000000 | bytes 3362816 | tf_op jit(solution)/shard_map/pallas_call | solution.py:110
  43.8 0.1 collective-permute-start.5
  43.8 5.5 %collective-permute-start.4 = (f32[48,128]{1,0:T(8,128)S(1)}, f32[48,128]{1,0:T(8,128)S(1)}, u32[]{:S(2)}, u32[]{:S(2)}) collective-permute-start(f32[48,128]{1,0:T(8,128)S(1)} %get-tuple-element.53.to_w), channel_id=1, source_target_pairs={{0,15},{1,0},{2,1},{3,2},{4,3},{5,4},{6,5},{7,6},{8,7},{9,8},{10,9... | collective-permute-start | bytes 73736 | tf_op jit(solution)/shard_map/ppermute | solution.py:788
  49.3 0.5 shard_map.80.h2_in
  49.8 0.5 shard_map.81.part
  50.3 0.7 %collective-permute-done.5.from_w = f32[48,128]{1,0:T(8,128)S(1)} collective-permute-done((f32[48,128]{1,0:T(8,128)S(1)}, f32[48,128]{1,0:T(8,128)S(1)}, u32[]{:S(2)}, u32[]{:S(2)}) %collective-permute-start.5) | collective-permute-done | bytes 24608 | tf_op jit(solution)/shard_map/ppermute | solution.py:788
  51.0 1.4 %shard_map.82 = (f32[36,32,128]{2,1,0:T(8,128)S(1)}, f32[16,8,128]{2,1,0:T(8,128)S(1)}) custom-call(s32[24,128]{1,0:T(8,128)S(1)} %get-tuple-element.31.idx, f32[8,128]{1,0:T(8,128)S(1)} %get-tuple-element.32.tab, f32[36,8,128]{2,1,0:T(8,128)S(1)} %get-tuple-element.33.own_c, f32[36,8,128]{2,1,0:T(8,128)S(1)} %get-tuple-element.34.far_c, ...), custom_call_target="tpu_custom_call" | custom-call | flops 4000000 | bytes 3186688 | tf_op jit(solution)/shard_map/pallas_call | solution.py:110
  52.4 14.3 %all_to_all.16.red = f32[16,8,128]{2,1,0:T(8,128)S(1)} all-to-all(f32[16,8,128]{2,1,0:T(8,128)S(1)} %get-tuple-element.55), channel_id=1, replica_groups=mesh['plane'=8,'elem'=16] {'elem'}, dimensions={0} | all-to-all | bytes 131072 | tf_op jit(solution)/shard_map/all_to_all | solution.py:882
  66.7 1.2 %shard_map.83 = f32[36,32,128]{2,1,0:T(8,128)} custom-call(f32[16,8,128]{2,1,0:T(8,128)S(1)} %all_to_all.16.red, f32[36,32,128]{2,1,0:T(8,128)S(1)} %bitcast.13, f32[36,32,128]{2,1,0:T(8,128)S(1)} %get-tuple-element.45.v.t0, f32[36,32,128]{2,1,0:T(8,128)S(1)} %get-tuple-element.49.t1, f32[36,32,128]{2,1,0:T(8,128)S(1)} %get-tuple-element.50.v.t2, ...), custom_call_target="tpu_custom_call" | custom-call | flops 4000000 | bytes 3604480 | tf_op jit(solution)/shard_map/pallas_call | solution.py:110
  (17 shorter events, 0.0 us)
Async XLA Ops:
  0.0 13.2 %copy-start.3 = (s32[8,128]{1,0:T(8,128)S(1)}, s32[8,128]{1,0:T(8,128)}, u32[]{:S(2)}) copy-start(s32[8,128]{1,0:T(8,128)} %links.3) | copy-start | bytes 12292
  0.0 13.2 %copy-start.6 = (s32[128]{0:T(128)S(1)}, s32[128]{0:T(128)}, u32[]{:S(2)}) copy-start(s32[128]{0:T(128)} %param.12) | copy-start | bytes 1540
  0.0 13.2 %copy-start.4 = (s32[2,8,128]{2,1,0:T(8,128)S(1)}, s32[2,8,128]{2,1,0:T(8,128)}, u32[]{:S(2)}) copy-start(s32[2,8,128]{2,1,0:T(8,128)} %sides.1) | copy-start | bytes 24580
  0.0 13.2 %copy-start.5 = (f32[128]{0:T(128)S(1)}, f32[128]{0:T(128)}, u32[]{:S(2)}) copy-start(f32[128]{0:T(128)} %param.9) | copy-start | bytes 1540
  2.1 15.6 %copy-start.1 = (f32[2,256,6,6,16]{1,4,3,2,0:T(8,128)S(1)}, f32[2,256,6,6,16]{1,4,3,2,0:T(8,128)}, u32[]{:S(2)}) copy-start(f32[2,256,6,6,16]{1,4,3,2,0:T(8,128)} %param.8) | copy-start | bytes 3538948
  2.1 15.6 %copy-start.2 = (bf16[2,256,256]{2,1,0:T(8,128)(2,1)S(1)}, bf16[2,256,256]{2,1,0:T(8,128)(2,1)}, u32[]{:S(2)}) copy-start(bf16[2,256,256]{2,1,0:T(8,128)(2,1)} %constant.2.clone.synth) | copy-start | bytes 786436
  2.1 15.6 %all-to-all-start = ((f32[8,144,128]{2,1,0:T(8,128)}), f32[8,144,128]{2,1,0:T(8,128)S(1)}, u32[]{:S(2)}, u32[]{:S(2)}) async-start(f32[8,144,128]{2,1,0:T(8,128)} %get-tuple-element.38), calls=%async_computation | async-start | bytes 1179648 | tf_op jit(solution)/shard_map/all_to_all | solution.py:812
  6.7 8.9 %collective-permute-start.1 = (f32[48,128]{1,0:T(8,128)S(1)}, f32[48,128]{1,0:T(8,128)S(1)}, u32[]{:S(2)}, u32[]{:S(2)}) collective-permute-start(f32[48,128]{1,0:T(8,128)S(1)} %get-tuple-element.39.to_e), channel_id=1, source_target_pairs={{0,1},{1,2},{2,3},{3,4},{4,5},{5,6},{6,7},{7,8},{8,9},{9,10},{10,1... | collective-permute-start | bytes 73736 | tf_op jit(solution)/shard_map/ppermute | solution.py:788
  8.2 7.3 %collective-permute-start = (f32[48,128]{1,0:T(8,128)S(1)}, f32[48,128]{1,0:T(8,128)S(1)}, u32[]{:S(2)}, u32[]{:S(2)}) collective-permute-start(f32[48,128]{1,0:T(8,128)S(1)} %get-tuple-element.40.to_w), channel_id=1, source_target_pairs={{0,15},{1,0},{2,1},{3,2},{4,3},{5,4},{6,5},{7,6},{8,7},{9,8},{10,9... | collective-permute-start | bytes 73736 | tf_op jit(solution)/shard_map/ppermute | solution.py:788
  34.1 8.2 %collective-permute-start.3 = (f32[48,128]{1,0:T(8,128)S(1)}, f32[48,128]{1,0:T(8,128)S(1)}, u32[]{:S(2)}, u32[]{:S(2)}) collective-permute-start(f32[48,128]{1,0:T(8,128)S(1)} %get-tuple-element.47.to_e), channel_id=1, source_target_pairs={{0,1},{1,2},{2,3},{3,4},{4,5},{5,6},{6,7},{7,8},{8,9},{9,10},{10,1... | collective-permute-start | bytes 73736 | tf_op jit(solution)/shard_map/ppermute | solution.py:788
  35.6 6.7 %collective-permute-start.2 = (f32[48,128]{1,0:T(8,128)S(1)}, f32[48,128]{1,0:T(8,128)S(1)}, u32[]{:S(2)}, u32[]{:S(2)}) collective-permute-start(f32[48,128]{1,0:T(8,128)S(1)} %get-tuple-element.48.to_w), channel_id=1, source_target_pairs={{0,15},{1,0},{2,1},{3,2},{4,3},{5,4},{6,5},{7,6},{8,7},{9,8},{10,9... | collective-permute-start | bytes 73736 | tf_op jit(solution)/shard_map/ppermute | solution.py:788
  43.8 7.3 %collective-permute-start.5 = (f32[48,128]{1,0:T(8,128)S(1)}, f32[48,128]{1,0:T(8,128)S(1)}, u32[]{:S(2)}, u32[]{:S(2)}) collective-permute-start(f32[48,128]{1,0:T(8,128)S(1)} %get-tuple-element.52.to_e), channel_id=1, source_target_pairs={{0,1},{1,2},{2,3},{3,4},{4,5},{5,6},{6,7},{7,8},{8,9},{9,10},{10,1... | collective-permute-start | bytes 73736 | tf_op jit(solution)/shard_map/ppermute | solution.py:788
  43.8 7.2 %collective-permute-start.4 = (f32[48,128]{1,0:T(8,128)S(1)}, f32[48,128]{1,0:T(8,128)S(1)}, u32[]{:S(2)}, u32[]{:S(2)}) collective-permute-start(f32[48,128]{1,0:T(8,128)S(1)} %get-tuple-element.53.to_w), channel_id=1, source_target_pairs={{0,15},{1,0},{2,1},{3,2},{4,3},{5,4},{6,5},{7,6},{8,7},{9,8},{10,9... | collective-permute-start | bytes 73736 | tf_op jit(solution)/shard_map/ppermute | solution.py:788
  51.0 15.6 %copy-start = (f32[32,6,6,128]{3,0,2,1:T(8,128)S(1)}, f32[32,6,6,128]{3,0,2,1:T(8,128)}, u32[]{:S(2)}) copy-start(f32[32,6,6,128]{3,0,2,1:T(8,128)} %param.7) | copy-start | bytes 1769476

commit v12 on v11

--- a/solution.py
+++ b/solution.py
@@ -495,7 +495,7 @@
 
 
 def residual_kernel(
-    idx, tab, own_c, far_c, back, base, edge, out, h_out, send_e, send_w
+    idx, tab, own_c, far_c, back, base, edge, out, h_out, send_w, send_e
 ):
     env = (idx, tab, own_c, far_c)
 
@@ -545,8 +545,8 @@
 
 def two_steps_kernel(
     idx, tab, own_c, far_c, edge_idx, edge_own, edge_far,
-    t0, h0, h0_in, to_e, to_w, from_e, from_w,
-    t1, t2, h2, send_e, send_w, keep, edge,
+    t0, h0, h0_in, to_w, to_e, from_w, from_e,
+    t1, t2, h2, send_w, send_e, keep, edge,
 ):
     env = (idx, tab, own_c, far_c)
     tables = (edge_idx, edge_own, edge_far)
@@ -593,7 +593,7 @@
 
 def last_steps_kernel(
     idx, tab, own_c, far_c, edge_idx, edge_own, edge_far,
-    t1, t2, h2, h2_in, to_e, to_w, from_e, from_w, keep, part,
+    t1, t2, h2, h2_in, to_w, to_e, from_w, from_e, keep, part,
     t3, red, edge, acc, pad,
 ):
     env = (idx, tab, own_c, far_c)
@@ -831,6 +831,9 @@
     def run(kernel, outs, scratch, args):
         return call(kernel, outs, scratch, args, [VMEM] * len(args))
 
+    def trade_back(send_w, send_e):
+        return shift_by(send_e, 1), shift_by(send_w, -1)
+
     def trade(send_e, send_w):
         from_w = shift_by(send_e, 1)
         return shift_by(send_w, -1), from_w
@@ -859,25 +862,25 @@
         ]
 
     lines, insides = shape(12, 32, 128), shape(24, 32, 128)
-    t0, h0, *sent = run(
+    t0, h0, to_w, to_e = run(
         residual_kernel, [vol, lines, edge, edge], [], head + [back, base, guess_edge]
     )
-    got = trade(*sent)
+    got = trade_back(to_w, to_e)
     h0_in = run(inside_kernel, [insides], [], head + [t0])[0]
-    t1, t2, h2, to_e, to_w, keep = run(
+    t1, t2, h2, to_w, to_e, keep = run(
         two_steps_kernel,
         [vol, vol, lines, edge, edge, both],
         [VMEM((96, 128), F32)],
-        head + edges + [t0, h0, h0_in, *sent, *got],
+        head + edges + [t0, h0, h0_in, to_w, to_e, *got],
     )
-    got = trade(to_e, to_w)
+    got = trade_back(to_w, to_e)
     h2_in = run(inside_kernel, [insides], [], head + [t2])[0]
     part = run(sums_kernel, [shape(8, 128)], work(5)[1:], [t0, t1, t2])[0]
     t3, red = run(
         last_steps_kernel,
         [vol, shape(16, 8, 128)],
         work(3),
-        head + edges + [t1, t2, h2, h2_in, to_e, to_w, *got, keep, part],
+        head + edges + [t1, t2, h2, h2_in, to_w, to_e, *got, keep, part],
     )
     red = lax.all_to_all(red, "elem", 0, 0, tiled=True)
     out = call(

time: 68.2 us -> 69.5 us (1.019)
  waiting for transfers between devices: 3.99 us -> 12.9 us
  blocking collectives: 27.9 us -> 23.9 us
  starting transfers between devices: 23.1 us -> 19.5 us
    ppermute x6, waiting for transfers between devices: 2 us -> 10.9 us  [shift_by(): lax.ppermute(array, 'elem', [(i, (i + by) % count) for i in range(count)])]
    all_to_all x1, blocking collectives: 14.3 us -> 10.2 us  [shards(): red = lax.all_to_all(red, 'elem', 0, 0, tiled=True)]
    ppermute x6, starting transfers between devices: 18.6 us -> 15 us  [shift_by(): lax.ppermute(array, 'elem', [(i, (i + by) % count) for i in range(count)])]
  transfers between devices with their start and end apart: 7 -> 7, of which waited for: 3 -> 5; matrix products, arithmetic and copies ran while one was open for 0% -> 0% of each run, Pallas kernels for 6% -> 6%
where the time goes in v12:
time: 69.5 us; the launch traced here: 69.2 us
  blocking collectives  23.9 us (34%)
  starting transfers between devices  19.5 us (28%)
  waiting for transfers between devices  12.9 us (19%)
  Pallas kernels  12.7 us (18%)
    ppermute x6, starting transfers between devices, shift_by(): lax.ppermute(array, 'elem', [(i, (i + by) % count) for i in range(count)])  15 us
    all_to_all x1, blocking collectives, shards(): back = lax.all_to_all(back, 'plane', 0, 0, tiled=True)  13.7 us
    pallas_call x11, Pallas kernels, call(): pl.pallas_call(kernel, out_shape=outs, in_specs=[pl.BlockSpec(memory_spac...  12.7 us
    ppermute x6, waiting for transfers between devices, shift_by(): lax.ppermute(array, 'elem', [(i, (i + by) % count) for i in range(count)])  10.9 us
    all_to_all x1, blocking collectives, shards(): red = lax.all_to_all(red, 'elem', 0, 0, tiled=True)  10.2 us
    all_to_all x1, starting transfers between devices, shards(): came = lax.all_to_all(packed, 'plane', 0, 0, tiled=True)  4.53 us
    all_to_all x1, waiting for transfers between devices, shards(): came = lax.all_to_all(packed, 'plane', 0, 0, tiled=True)  1.98 us
  transfers between devices with their start and end apart: 7, of which 5 were waited for; matrix products, arithmetic and copies ran while one was open for 0% of the time, Pallas kernels for 6%

profile of v12, /device:TPU:0, one launch (start us, length us, event | category | flops | bytes accessed | tf_op | source)
XLA Modules:
  0.0 69.2 jit_solution(1210360433942263589)
XLA Ops:
  0.0 2.1 %shard_map.74 = (f32[8,144,128]{2,1,0:T(8,128)}, f32[48,128]{1,0:T(8,128)S(1)}, f32[48,128]{1,0:T(8,128)S(1)}) custom-call(f32[36,32,128]{2,1,0:T(8,128)} %bitcast.11, s32[8,128]{1,0:T(8,128)} %links.3), custom_call_target="tpu_custom_call" | custom-call | flops 4000000 | bytes 1232896 | tf_op jit(solution)/shard_map/pallas_call | solution.py:110
  2.1 4.5 %all-to-all-start = ((f32[8,144,128]{2,1,0:T(8,128)}), f32[8,144,128]{2,1,0:T(8,128)S(1)}, u32[]{:S(2)}, u32[]{:S(2)}) async-start(f32[8,144,128]{2,1,0:T(8,128)} %get-tuple-element.38), calls=%async_computation | async-start | bytes 1179648 | tf_op jit(solution)/shard_map/all_to_all | solution.py:812
  6.7 1.6 %collective-permute-start.1 = (f32[48,128]{1,0:T(8,128)S(1)}, f32[48,128]{1,0:T(8,128)S(1)}, u32[]{:S(2)}, u32[]{:S(2)}) collective-permute-start(f32[48,128]{1,0:T(8,128)S(1)} %get-tuple-element.39.to_e), channel_id=1, source_target_pairs={{0,1},{1,2},{2,3},{3,4},{4,5},{5,6},{6,7},{7,8},{8,9},{9,10},{10,1... | collective-permute-start | bytes 73736 | tf_op jit(solution)/shard_map/ppermute | solution.py:788
  8.2 5.0 %collective-permute-start = (f32[48,128]{1,0:T(8,128)S(1)}, f32[48,128]{1,0:T(8,128)S(1)}, u32[]{:S(2)}, u32[]{:S(2)}) collective-permute-start(f32[48,128]{1,0:T(8,128)S(1)} %get-tuple-element.40.to_w), channel_id=1, source_target_pairs={{0,15},{1,0},{2,1},{3,2},{4,3},{5,4},{6,5},{7,6},{8,7},{9,8},{10,9... | collective-permute-start | bytes 73736 | tf_op jit(solution)/shard_map/ppermute | solution.py:788
  13.2 2.3 %shard_map.73 = (s32[24,128]{1,0:T(8,128)S(1)}, s32[8,128]{1,0:T(8,128)S(1)}, f32[8,128]{1,0:T(8,128)S(1)}, f32[36,8,128]{2,1,0:T(8,128)S(1)}, f32[36,8,128]{2,1...) custom-call(s32[8,128]{1,0:T(8,128)S(1)} %copy-done.3, ...), custom_call_target="tpu_custom_call" | custom-call | flops 4000000 | bytes 1803264 | tf_op jit(solution)/shard_map/pallas_call | solution.py:110
  15.5 0.2 shard_map.75.edge
  15.7 2.0 %all-to-all-done.came = f32[8,144,128]{2,1,0:T(8,128)S(1)} async-done(((f32[8,144,128]{2,1,0:T(8,128)}), f32[8,144,128]{2,1,0:T(8,128)S(1)}, u32[]{:S(2)}, u32[]{:S(2)}) %all-to-all-start) | async-done | bytes 589856 | tf_op jit(solution)/shard_map/all_to_all | solution.py:812
  17.7 1.7 %shard_map.76 = f32[8,144,128]{2,1,0:T(8,128)S(1)} custom-call(s32[24,128]{1,0:T(8,128)S(1)} %get-tuple-element.31.idx, f32[8,144,128]{2,1,0:T(8,128)S(1)} %all-to-all-done.came, f32[2,36,16,256]{3,2,1,0:T(8,128)S(1)} %bitcast.14, bf16[2,256,256]{2,1,0:T(8,128)(2,1)S(1)} %copy-done.2), custom_call_target="tpu_custom_call" | custom-call | flops 4000000 | bytes 2895872 | tf_op jit(solution)/shard_map/pallas_call | solution.py:110
  19.4 13.7 %all_to_all.15.back = f32[8,144,128]{2,1,0:T(8,128)S(1)} all-to-all(f32[8,144,128]{2,1,0:T(8,128)S(1)} %shard_map.76), channel_id=1, replica_groups=mesh['plane'=8,'elem'=16] {'plane'}, dimensions={0} | all-to-all | bytes 1179648 | tf_op jit(solution)/shard_map/all_to_all | solution.py:855
  33.1 1.1 %shard_map.77 = (f32[36,32,128]{2,1,0:T(8,128)S(1)}, f32[12,32,128]{2,1,0:T(8,128)S(1)}, f32[48,128]{1,0:T(8,128)S(1)}, f32[48,128]{1,0:T(8,128)S(1)}) custom-call(s32[24,128]{1,0:T(8,128)S(1)} %get-tuple-element.31.idx, f32[8,128]{1,0:T(8,128)S(1)} %get-tuple-element.32.tab, f32[36,8,128]{2,1,0:T(8,128)S(1)} %get-tuple-element.33.own_c, ...), custom_call_target="tpu_custom_call" | custom-call | flops 4000000 | bytes 2351104 | tf_op jit(solution)/shard_map/pallas_call | solution.py:110
  34.1 6.4 %collective-permute-start.3 = (f32[48,128]{1,0:T(8,128)S(1)}, f32[48,128]{1,0:T(8,128)S(1)}, u32[]{:S(2)}, u32[]{:S(2)}) collective-permute-start(f32[48,128]{1,0:T(8,128)S(1)} %get-tuple-element.47.to_w), channel_id=1, source_target_pairs={{0,15},{1,0},{2,1},{3,2},{4,3},{5,4},{6,5},{7,6},{8,7},{9,8},{10,9... | collective-permute-start | bytes 73736 | tf_op jit(solution)/shard_map/ppermute | solution.py:788
  40.5 0.5 shard_map.78.h0_in
  41.0 1.1 %collective-permute-done.3.from_e = f32[48,128]{1,0:T(8,128)S(1)} collective-permute-done((f32[48,128]{1,0:T(8,128)S(1)}, f32[48,128]{1,0:T(8,128)S(1)}, u32[]{:S(2)}, u32[]{:S(2)}) %collective-permute-start.3) | collective-permute-done | bytes 24608 | tf_op jit(solution)/shard_map/ppermute | solution.py:788
  42.0 5.6 %collective-permute-done.2.from_w = f32[48,128]{1,0:T(8,128)S(1)} collective-permute-done((f32[48,128]{1,0:T(8,128)S(1)}, f32[48,128]{1,0:T(8,128)S(1)}, u32[]{:S(2)}, u32[]{:S(2)}) %collective-permute-start.2) | collective-permute-done | bytes 24608 | tf_op jit(solution)/shard_map/ppermute | solution.py:788
  47.7 1.4 %shard_map.79 = (f32[36,32,128]{2,1,0:T(8,128)S(1)}, f32[36,32,128]{2,1,0:T(8,128)S(1)}, f32[12,32,128]{2,1,0:T(8,128)S(1)}, f32[48,128]{1,0:T(8,128)S(1)}, f32[...) custom-call(s32[24,128]{1,0:T(8,128)S(1)} %get-tuple-element.31.idx, f32[8,128]{1,0:T(8,128)S(1)} %get-tuple-element.32.tab, ...), custom_call_target="tpu_custom_call" | custom-call | flops 4000000 | bytes 3362816 | tf_op jit(solution)/shard_map/pallas_call | solution.py:110
  49.1 0.1 collective-permute-start.5
  49.2 2.0 %collective-permute-start.4 = (f32[48,128]{1,0:T(8,128)S(1)}, f32[48,128]{1,0:T(8,128)S(1)}, u32[]{:S(2)}, u32[]{:S(2)}) collective-permute-start(f32[48,128]{1,0:T(8,128)S(1)} %get-tuple-element.53.to_e), channel_id=1, source_target_pairs={{0,1},{1,2},{2,3},{3,4},{4,5},{5,6},{6,7},{7,8},{8,9},{9,10},{10,1... | collective-permute-start | bytes 73736 | tf_op jit(solution)/shard_map/ppermute | solution.py:788
  51.2 0.5 shard_map.80.h2_in
  51.6 0.5 shard_map.81.part
  52.2 0.8 %collective-permute-done.5.from_e = f32[48,128]{1,0:T(8,128)S(1)} collective-permute-done((f32[48,128]{1,0:T(8,128)S(1)}, f32[48,128]{1,0:T(8,128)S(1)}, u32[]{:S(2)}, u32[]{:S(2)}) %collective-permute-start.5) | collective-permute-done | bytes 24608 | tf_op jit(solution)/shard_map/ppermute | solution.py:788
  53.0 3.4 %collective-permute-done.4.from_w = f32[48,128]{1,0:T(8,128)S(1)} collective-permute-done((f32[48,128]{1,0:T(8,128)S(1)}, f32[48,128]{1,0:T(8,128)S(1)}, u32[]{:S(2)}, u32[]{:S(2)}) %collective-permute-start.4) | collective-permute-done | bytes 24608 | tf_op jit(solution)/shard_map/ppermute | solution.py:788
  56.4 1.4 %shard_map.82 = (f32[36,32,128]{2,1,0:T(8,128)S(1)}, f32[16,8,128]{2,1,0:T(8,128)S(1)}) custom-call(s32[24,128]{1,0:T(8,128)S(1)} %get-tuple-element.31.idx, f32[8,128]{1,0:T(8,128)S(1)} %get-tuple-element.32.tab, f32[36,8,128]{2,1,0:T(8,128)S(1)} %get-tuple-element.33.own_c, f32[36,8,128]{2,1,0:T(8,128)S(1)} %get-tuple-element.34.far_c, ...), custom_call_target="tpu_custom_call" | custom-call | flops 4000000 | bytes 3186688 | tf_op jit(solution)/shard_map/pallas_call | solution.py:110
  57.7 10.2 %all_to_all.16.red = f32[16,8,128]{2,1,0:T(8,128)S(1)} all-to-all(f32[16,8,128]{2,1,0:T(8,128)S(1)} %get-tuple-element.55), channel_id=1, replica_groups=mesh['plane'=8,'elem'=16] {'elem'}, dimensions={0} | all-to-all | bytes 131072 | tf_op jit(solution)/shard_map/all_to_all | solution.py:885
  68.0 1.2 %shard_map.83 = f32[36,32,128]{2,1,0:T(8,128)} custom-call(f32[16,8,128]{2,1,0:T(8,128)S(1)} %all_to_all.16.red, f32[36,32,128]{2,1,0:T(8,128)S(1)} %bitcast.13, f32[36,32,128]{2,1,0:T(8,128)S(1)} %get-tuple-element.45.v.t0, f32[36,32,128]{2,1,0:T(8,128)S(1)} %get-tuple-element.49.t1, f32[36,32,128]{2,1,0:T(8,128)S(1)} %get-tuple-element.50.v.t2, ...), custom_call_target="tpu_custom_call" | custom-call | flops 4000000 | bytes 3604480 | tf_op jit(solution)/shard_map/pallas_call | solution.py:110
  (17 shorter events, 0.0 us)
Async XLA Ops:
  0.0 13.2 %copy-start.3 = (s32[8,128]{1,0:T(8,128)S(1)}, s32[8,128]{1,0:T(8,128)}, u32[]{:S(2)}) copy-start(s32[8,128]{1,0:T(8,128)} %links.3) | copy-start | bytes 12292
  0.0 13.2 %copy-start.6 = (s32[128]{0:T(128)S(1)}, s32[128]{0:T(128)}, u32[]{:S(2)}) copy-start(s32[128]{0:T(128)} %param.12) | copy-start | bytes 1540
  0.0 13.2 %copy-start.4 = (s32[2,8,128]{2,1,0:T(8,128)S(1)}, s32[2,8,128]{2,1,0:T(8,128)}, u32[]{:S(2)}) copy-start(s32[2,8,128]{2,1,0:T(8,128)} %sides.1) | copy-start | bytes 24580
  0.0 13.2 %copy-start.5 = (f32[128]{0:T(128)S(1)}, f32[128]{0:T(128)}, u32[]{:S(2)}) copy-start(f32[128]{0:T(128)} %param.9) | copy-start | bytes 1540
  2.1 15.6 %copy-start.1 = (f32[2,256,6,6,16]{1,4,3,2,0:T(8,128)S(1)}, f32[2,256,6,6,16]{1,4,3,2,0:T(8,128)}, u32[]{:S(2)}) copy-start(f32[2,256,6,6,16]{1,4,3,2,0:T(8,128)} %param.8) | copy-start | bytes 3538948
  2.1 15.6 %copy-start.2 = (bf16[2,256,256]{2,1,0:T(8,128)(2,1)S(1)}, bf16[2,256,256]{2,1,0:T(8,128)(2,1)}, u32[]{:S(2)}) copy-start(bf16[2,256,256]{2,1,0:T(8,128)(2,1)} %constant.2.clone.synth) | copy-start | bytes 786436
  2.1 15.6 %all-to-all-start = ((f32[8,144,128]{2,1,0:T(8,128)}), f32[8,144,128]{2,1,0:T(8,128)S(1)}, u32[]{:S(2)}, u32[]{:S(2)}) async-start(f32[8,144,128]{2,1,0:T(8,128)} %get-tuple-element.38), calls=%async_computation | async-start | bytes 1179648 | tf_op jit(solution)/shard_map/all_to_all | solution.py:812
  6.7 8.9 %collective-permute-start.1 = (f32[48,128]{1,0:T(8,128)S(1)}, f32[48,128]{1,0:T(8,128)S(1)}, u32[]{:S(2)}, u32[]{:S(2)}) collective-permute-start(f32[48,128]{1,0:T(8,128)S(1)} %get-tuple-element.39.to_e), channel_id=1, source_target_pairs={{0,1},{1,2},{2,3},{3,4},{4,5},{5,6},{6,7},{7,8},{8,9},{9,10},{10,1... | collective-permute-start | bytes 73736 | tf_op jit(solution)/shard_map/ppermute | solution.py:788
  8.2 7.3 %collective-permute-start = (f32[48,128]{1,0:T(8,128)S(1)}, f32[48,128]{1,0:T(8,128)S(1)}, u32[]{:S(2)}, u32[]{:S(2)}) collective-permute-start(f32[48,128]{1,0:T(8,128)S(1)} %get-tuple-element.40.to_w), channel_id=1, source_target_pairs={{0,15},{1,0},{2,1},{3,2},{4,3},{5,4},{6,5},{7,6},{8,7},{9,8},{10,9... | collective-permute-start | bytes 73736 | tf_op jit(solution)/shard_map/ppermute | solution.py:788
  34.1 7.9 %collective-permute-start.3 = (f32[48,128]{1,0:T(8,128)S(1)}, f32[48,128]{1,0:T(8,128)S(1)}, u32[]{:S(2)}, u32[]{:S(2)}) collective-permute-start(f32[48,128]{1,0:T(8,128)S(1)} %get-tuple-element.47.to_w), channel_id=1, source_target_pairs={{0,15},{1,0},{2,1},{3,2},{4,3},{5,4},{6,5},{7,6},{8,7},{9,8},{10,9... | collective-permute-start | bytes 73736 | tf_op jit(solution)/shard_map/ppermute | solution.py:788
  40.5 7.1 %collective-permute-start.2 = (f32[48,128]{1,0:T(8,128)S(1)}, f32[48,128]{1,0:T(8,128)S(1)}, u32[]{:S(2)}, u32[]{:S(2)}) collective-permute-start(f32[48,128]{1,0:T(8,128)S(1)} %get-tuple-element.48.to_e), channel_id=1, source_target_pairs={{0,1},{1,2},{2,3},{3,4},{4,5},{5,6},{6,7},{7,8},{8,9},{9,10},{10,1... | collective-permute-start | bytes 73736 | tf_op jit(solution)/shard_map/ppermute | solution.py:788
  49.1 3.9 %collective-permute-start.5 = (f32[48,128]{1,0:T(8,128)S(1)}, f32[48,128]{1,0:T(8,128)S(1)}, u32[]{:S(2)}, u32[]{:S(2)}) collective-permute-start(f32[48,128]{1,0:T(8,128)S(1)} %get-tuple-element.52.to_w), channel_id=1, source_target_pairs={{0,15},{1,0},{2,1},{3,2},{4,3},{5,4},{6,5},{7,6},{8,7},{9,8},{10,9... | collective-permute-start | bytes 73736 | tf_op jit(solution)/shard_map/ppermute | solution.py:788
  49.2 7.2 %collective-permute-start.4 = (f32[48,128]{1,0:T(8,128)S(1)}, f32[48,128]{1,0:T(8,128)S(1)}, u32[]{:S(2)}, u32[]{:S(2)}) collective-permute-start(f32[48,128]{1,0:T(8,128)S(1)} %get-tuple-element.53.to_e), channel_id=1, source_target_pairs={{0,1},{1,2},{2,3},{3,4},{4,5},{5,6},{6,7},{7,8},{8,9},{9,10},{10,1... | collective-permute-start | bytes 73736 | tf_op jit(solution)/shard_map/ppermute | solution.py:788
  56.4 11.6 %copy-start = (f32[32,6,6,128]{3,0,2,1:T(8,128)S(1)}, f32[32,6,6,128]{3,0,2,1:T(8,128)}, u32[]{:S(2)}) copy-start(f32[32,6,6,128]{3,0,2,1:T(8,128)} %param.7) | copy-start | bytes 1769476

commit v13 on v11

--- a/solution.py
+++ b/solution.py
@@ -282,7 +282,7 @@
         @pl.when(mixed != plain)
         def _(plain=plain):
             lax.fori_loop(
-                0, 4, lambda group, carry: loop(group, plain) or carry, 0, unroll=2 if plain else 1
+                0, 4, lambda group, carry: loop(group, plain) or carry, 0, unroll=4 if plain else 1
             )
 
 

time: 68.2 us -> 68.2 us (level)
  no operation moved by 1% of the time
where the time goes in v13:
time: 68.2 us; the launch traced here: 67.9 us
  blocking collectives  27.9 us (41%)
  starting transfers between devices  23.1 us (34%)
  Pallas kernels  12.7 us (19%)
  waiting for transfers between devices  4.03 us (6%)
    ppermute x6, starting transfers between devices, shift_by(): lax.ppermute(array, 'elem', [(i, (i + by) % count) for i in range(count)])  18.6 us
    all_to_all x1, blocking collectives, shards(): red = lax.all_to_all(red, 'elem', 0, 0, tiled=True)  14.3 us
    all_to_all x1, blocking collectives, shards(): back = lax.all_to_all(back, 'plane', 0, 0, tiled=True)  13.7 us
    pallas_call x11, Pallas kernels, call(): pl.pallas_call(kernel, out_shape=outs, in_specs=[pl.BlockSpec(memory_spac...  12.7 us
    all_to_all x1, starting transfers between devices, shards(): came = lax.all_to_all(packed, 'plane', 0, 0, tiled=True)  4.53 us
    ppermute x6, waiting for transfers between devices, shift_by(): lax.ppermute(array, 'elem', [(i, (i + by) % count) for i in range(count)])  2.03 us
    all_to_all x1, waiting for transfers between devices, shards(): came = lax.all_to_all(packed, 'plane', 0, 0, tiled=True)  2 us
  transfers between devices with their start and end apart: 7, of which 3 were waited for; matrix products, arithmetic and copies ran while one was open for 0% of the time, Pallas kernels for 6%

profile of v13, /device:TPU:0, one launch (start us, length us, event | category | flops | bytes accessed | tf_op | source)
XLA Modules:
  0.0 67.9 jit_solution(10933497862606733791)
XLA Ops:
  0.0 2.1 %shard_map.74 = (f32[8,144,128]{2,1,0:T(8,128)}, f32[48,128]{1,0:T(8,128)S(1)}, f32[48,128]{1,0:T(8,128)S(1)}) custom-call(f32[36,32,128]{2,1,0:T(8,128)} %bitcast.11, s32[8,128]{1,0:T(8,128)} %links.3), custom_call_target="tpu_custom_call" | custom-call | flops 4000000 | bytes 1232896 | tf_op jit(solution)/shard_map/pallas_call | solution.py:110
  2.1 0.0 copy-start.2
  2.1 4.5 %all-to-all-start = ((f32[8,144,128]{2,1,0:T(8,128)}), f32[8,144,128]{2,1,0:T(8,128)S(1)}, u32[]{:S(2)}, u32[]{:S(2)}) async-start(f32[8,144,128]{2,1,0:T(8,128)} %get-tuple-element.38), calls=%async_computation | async-start | bytes 1179648 | tf_op jit(solution)/shard_map/all_to_all | solution.py:812
  6.7 1.6 %collective-permute-start.1 = (f32[48,128]{1,0:T(8,128)S(1)}, f32[48,128]{1,0:T(8,128)S(1)}, u32[]{:S(2)}, u32[]{:S(2)}) collective-permute-start(f32[48,128]{1,0:T(8,128)S(1)} %get-tuple-element.39.to_e), channel_id=1, source_target_pairs={{0,1},{1,2},{2,3},{3,4},{4,5},{5,6},{6,7},{7,8},{8,9},{9,10},{10,1... | collective-permute-start | bytes 73736 | tf_op jit(solution)/shard_map/ppermute | solution.py:788
  8.2 5.0 %collective-permute-start = (f32[48,128]{1,0:T(8,128)S(1)}, f32[48,128]{1,0:T(8,128)S(1)}, u32[]{:S(2)}, u32[]{:S(2)}) collective-permute-start(f32[48,128]{1,0:T(8,128)S(1)} %get-tuple-element.40.to_w), channel_id=1, source_target_pairs={{0,15},{1,0},{2,1},{3,2},{4,3},{5,4},{6,5},{7,6},{8,7},{9,8},{10,9... | collective-permute-start | bytes 73736 | tf_op jit(solution)/shard_map/ppermute | solution.py:788
  13.2 2.3 %shard_map.73 = (s32[24,128]{1,0:T(8,128)S(1)}, s32[8,128]{1,0:T(8,128)S(1)}, f32[8,128]{1,0:T(8,128)S(1)}, f32[36,8,128]{2,1,0:T(8,128)S(1)}, f32[36,8,128]{2,1...) custom-call(s32[8,128]{1,0:T(8,128)S(1)} %copy-done.3, ...), custom_call_target="tpu_custom_call" | custom-call | flops 4000000 | bytes 1803264 | tf_op jit(solution)/shard_map/pallas_call | solution.py:110
  15.5 0.2 shard_map.75.edge
  15.7 2.0 %all-to-all-done.came = f32[8,144,128]{2,1,0:T(8,128)S(1)} async-done(((f32[8,144,128]{2,1,0:T(8,128)}), f32[8,144,128]{2,1,0:T(8,128)S(1)}, u32[]{:S(2)}, u32[]{:S(2)}) %all-to-all-start) | async-done | bytes 589856 | tf_op jit(solution)/shard_map/all_to_all | solution.py:812
  17.7 1.7 %shard_map.76 = f32[8,144,128]{2,1,0:T(8,128)S(1)} custom-call(s32[24,128]{1,0:T(8,128)S(1)} %get-tuple-element.31.idx, f32[8,144,128]{2,1,0:T(8,128)S(1)} %all-to-all-done.came, f32[2,36,16,256]{3,2,1,0:T(8,128)S(1)} %bitcast.14, bf16[2,256,256]{2,1,0:T(8,128)(2,1)S(1)} %copy-done.2), custom_call_target="tpu_custom_call" | custom-call | flops 4000000 | bytes 2895872 | tf_op jit(solution)/shard_map/pallas_call | solution.py:110
  19.4 13.7 %all_to_all.15.back = f32[8,144,128]{2,1,0:T(8,128)S(1)} all-to-all(f32[8,144,128]{2,1,0:T(8,128)S(1)} %shard_map.76), channel_id=1, replica_groups=mesh['plane'=8,'elem'=16] {'plane'}, dimensions={0} | all-to-all | bytes 1179648 | tf_op jit(solution)/shard_map/all_to_all | solution.py:852
  33.0 1.1 %shard_map.77 = (f32[36,32,128]{2,1,0:T(8,128)S(1)}, f32[12,32,128]{2,1,0:T(8,128)S(1)}, f32[48,128]{1,0:T(8,128)S(1)}, f32[48,128]{1,0:T(8,128)S(1)}) custom-call(s32[24,128]{1,0:T(8,128)S(1)} %get-tuple-element.31.idx, f32[8,128]{1,0:T(8,128)S(1)} %get-tuple-element.32.tab, f32[36,8,128]{2,1,0:T(8,128)S(1)} %get-tuple-element.33.own_c, ...), custom_call_target="tpu_custom_call" | custom-call | flops 4000000 | bytes 2351104 | tf_op jit(solution)/shard_map/pallas_call | solution.py:110
  34.1 1.5 %collective-permute-start.3 = (f32[48,128]{1,0:T(8,128)S(1)}, f32[48,128]{1,0:T(8,128)S(1)}, u32[]{:S(2)}, u32[]{:S(2)}) collective-permute-start(f32[48,128]{1,0:T(8,128)S(1)} %get-tuple-element.47.to_e), channel_id=1, source_target_pairs={{0,1},{1,2},{2,3},{3,4},{4,5},{5,6},{6,7},{7,8},{8,9},{9,10},{10,1... | collective-permute-start | bytes 73736 | tf_op jit(solution)/shard_map/ppermute | solution.py:788
  35.6 5.0 %collective-permute-start.2 = (f32[48,128]{1,0:T(8,128)S(1)}, f32[48,128]{1,0:T(8,128)S(1)}, u32[]{:S(2)}, u32[]{:S(2)}) collective-permute-start(f32[48,128]{1,0:T(8,128)S(1)} %get-tuple-element.48.to_w), channel_id=1, source_target_pairs={{0,15},{1,0},{2,1},{3,2},{4,3},{5,4},{6,5},{7,6},{8,7},{9,8},{10,9... | collective-permute-start | bytes 73736 | tf_op jit(solution)/shard_map/ppermute | solution.py:788
  40.6 0.4 shard_map.78.h0_in
  41.0 1.3 %collective-permute-done.3.from_w = f32[48,128]{1,0:T(8,128)S(1)} collective-permute-done((f32[48,128]{1,0:T(8,128)S(1)}, f32[48,128]{1,0:T(8,128)S(1)}, u32[]{:S(2)}, u32[]{:S(2)}) %collective-permute-start.3) | collective-permute-done | bytes 24608 | tf_op jit(solution)/shard_map/ppermute | solution.py:788
  42.3 1.4 %shard_map.79 = (f32[36,32,128]{2,1,0:T(8,128)S(1)}, f32[36,32,128]{2,1,0:T(8,128)S(1)}, f32[12,32,128]{2,1,0:T(8,128)S(1)}, f32[48,128]{1,0:T(8,128)S(1)}, f32[...) custom-call(s32[24,128]{1,0:T(8,128)S(1)} %get-tuple-element.31.idx, f32[8,128]{1,0:T(8,128)S(1)} %get-tuple-element.32.tab, ...), custom_call_target="tpu_custom_call" | custom-call | flops 4000000 | bytes 3362816 | tf_op jit(solution)/shard_map/pallas_call | solution.py:110
  43.7 0.1 collective-permute-start.5
  43.8 5.5 %collective-permute-start.4 = (f32[48,128]{1,0:T(8,128)S(1)}, f32[48,128]{1,0:T(8,128)S(1)}, u32[]{:S(2)}, u32[]{:S(2)}) collective-permute-start(f32[48,128]{1,0:T(8,128)S(1)} %get-tuple-element.53.to_w), channel_id=1, source_target_pairs={{0,15},{1,0},{2,1},{3,2},{4,3},{5,4},{6,5},{7,6},{8,7},{9,8},{10,9... | collective-permute-start | bytes 73736 | tf_op jit(solution)/shard_map/ppermute | solution.py:788
  49.3 0.4 shard_map.80.h2_in
  49.7 0.5 shard_map.81.part
  50.3 0.7 %collective-permute-done.5.from_w = f32[48,128]{1,0:T(8,128)S(1)} collective-permute-done((f32[48,128]{1,0:T(8,128)S(1)}, f32[48,128]{1,0:T(8,128)S(1)}, u32[]{:S(2)}, u32[]{:S(2)}) %collective-permute-start.5) | collective-permute-done | bytes 24608 | tf_op jit(solution)/shard_map/ppermute | solution.py:788
  51.0 1.3 %shard_map.82 = (f32[36,32,128]{2,1,0:T(8,128)S(1)}, f32[16,8,128]{2,1,0:T(8,128)S(1)}) custom-call(s32[24,128]{1,0:T(8,128)S(1)} %get-tuple-element.31.idx, f32[8,128]{1,0:T(8,128)S(1)} %get-tuple-element.32.tab, f32[36,8,128]{2,1,0:T(8,128)S(1)} %get-tuple-element.33.own_c, f32[36,8,128]{2,1,0:T(8,128)S(1)} %get-tuple-element.34.far_c, ...), custom_call_target="tpu_custom_call" | custom-call | flops 4000000 | bytes 3186688 | tf_op jit(solution)/shard_map/pallas_call | solution.py:110
  52.4 14.3 %all_to_all.16.red = f32[16,8,128]{2,1,0:T(8,128)S(1)} all-to-all(f32[16,8,128]{2,1,0:T(8,128)S(1)} %get-tuple-element.55), channel_id=1, replica_groups=mesh['plane'=8,'elem'=16] {'elem'}, dimensions={0} | all-to-all | bytes 131072 | tf_op jit(solution)/shard_map/all_to_all | solution.py:882
  66.6 1.2 %shard_map.83 = f32[36,32,128]{2,1,0:T(8,128)} custom-call(f32[16,8,128]{2,1,0:T(8,128)S(1)} %all_to_all.16.red, f32[36,32,128]{2,1,0:T(8,128)S(1)} %bitcast.13, f32[36,32,128]{2,1,0:T(8,128)S(1)} %get-tuple-element.45.v.t0, f32[36,32,128]{2,1,0:T(8,128)S(1)} %get-tuple-element.49.t1, f32[36,32,128]{2,1,0:T(8,128)S(1)} %get-tuple-element.50.v.t2, ...), custom_call_target="tpu_custom_call" | custom-call | flops 4000000 | bytes 3604480 | tf_op jit(solution)/shard_map/pallas_call | solution.py:110
  (17 shorter events, 0.0 us)
Async XLA Ops:
  0.0 13.2 %copy-start.3 = (s32[8,128]{1,0:T(8,128)S(1)}, s32[8,128]{1,0:T(8,128)}, u32[]{:S(2)}) copy-start(s32[8,128]{1,0:T(8,128)} %links.3) | copy-start | bytes 12292
  0.0 13.2 %copy-start.6 = (s32[128]{0:T(128)S(1)}, s32[128]{0:T(128)}, u32[]{:S(2)}) copy-start(s32[128]{0:T(128)} %param.12) | copy-start | bytes 1540
  0.0 13.2 %copy-start.4 = (s32[2,8,128]{2,1,0:T(8,128)S(1)}, s32[2,8,128]{2,1,0:T(8,128)}, u32[]{:S(2)}) copy-start(s32[2,8,128]{2,1,0:T(8,128)} %sides.1) | copy-start | bytes 24580
  0.0 13.2 %copy-start.5 = (f32[128]{0:T(128)S(1)}, f32[128]{0:T(128)}, u32[]{:S(2)}) copy-start(f32[128]{0:T(128)} %param.9) | copy-start | bytes 1540
  2.1 15.6 %copy-start.1 = (f32[2,256,6,6,16]{1,4,3,2,0:T(8,128)S(1)}, f32[2,256,6,6,16]{1,4,3,2,0:T(8,128)}, u32[]{:S(2)}) copy-start(f32[2,256,6,6,16]{1,4,3,2,0:T(8,128)} %param.8) | copy-start | bytes 3538948
  2.1 15.6 %copy-start.2 = (bf16[2,256,256]{2,1,0:T(8,128)(2,1)S(1)}, bf16[2,256,256]{2,1,0:T(8,128)(2,1)}, u32[]{:S(2)}) copy-start(bf16[2,256,256]{2,1,0:T(8,128)(2,1)} %constant.2.clone.synth) | copy-start | bytes 786436
  2.1 15.6 %all-to-all-start = ((f32[8,144,128]{2,1,0:T(8,128)}), f32[8,144,128]{2,1,0:T(8,128)S(1)}, u32[]{:S(2)}, u32[]{:S(2)}) async-start(f32[8,144,128]{2,1,0:T(8,128)} %get-tuple-element.38), calls=%async_computation | async-start | bytes 1179648 | tf_op jit(solution)/shard_map/all_to_all | solution.py:812
  6.7 8.9 %collective-permute-start.1 = (f32[48,128]{1,0:T(8,128)S(1)}, f32[48,128]{1,0:T(8,128)S(1)}, u32[]{:S(2)}, u32[]{:S(2)}) collective-permute-start(f32[48,128]{1,0:T(8,128)S(1)} %get-tuple-element.39.to_e), channel_id=1, source_target_pairs={{0,1},{1,2},{2,3},{3,4},{4,5},{5,6},{6,7},{7,8},{8,9},{9,10},{10,1... | collective-permute-start | bytes 73736 | tf_op jit(solution)/shard_map/ppermute | solution.py:788
  8.2 7.3 %collective-permute-start = (f32[48,128]{1,0:T(8,128)S(1)}, f32[48,128]{1,0:T(8,128)S(1)}, u32[]{:S(2)}, u32[]{:S(2)}) collective-permute-start(f32[48,128]{1,0:T(8,128)S(1)} %get-tuple-element.40.to_w), channel_id=1, source_target_pairs={{0,15},{1,0},{2,1},{3,2},{4,3},{5,4},{6,5},{7,6},{8,7},{9,8},{10,9... | collective-permute-start | bytes 73736 | tf_op jit(solution)/shard_map/ppermute | solution.py:788
  34.1 8.2 %collective-permute-start.3 = (f32[48,128]{1,0:T(8,128)S(1)}, f32[48,128]{1,0:T(8,128)S(1)}, u32[]{:S(2)}, u32[]{:S(2)}) collective-permute-start(f32[48,128]{1,0:T(8,128)S(1)} %get-tuple-element.47.to_e), channel_id=1, source_target_pairs={{0,1},{1,2},{2,3},{3,4},{4,5},{5,6},{6,7},{7,8},{8,9},{9,10},{10,1... | collective-permute-start | bytes 73736 | tf_op jit(solution)/shard_map/ppermute | solution.py:788
  35.6 6.7 %collective-permute-start.2 = (f32[48,128]{1,0:T(8,128)S(1)}, f32[48,128]{1,0:T(8,128)S(1)}, u32[]{:S(2)}, u32[]{:S(2)}) collective-permute-start(f32[48,128]{1,0:T(8,128)S(1)} %get-tuple-element.48.to_w), channel_id=1, source_target_pairs={{0,15},{1,0},{2,1},{3,2},{4,3},{5,4},{6,5},{7,6},{8,7},{9,8},{10,9... | collective-permute-start | bytes 73736 | tf_op jit(solution)/shard_map/ppermute | solution.py:788
  43.7 7.3 %collective-permute-start.5 = (f32[48,128]{1,0:T(8,128)S(1)}, f32[48,128]{1,0:T(8,128)S(1)}, u32[]{:S(2)}, u32[]{:S(2)}) collective-permute-start(f32[48,128]{1,0:T(8,128)S(1)} %get-tuple-element.52.to_e), channel_id=1, source_target_pairs={{0,1},{1,2},{2,3},{3,4},{4,5},{5,6},{6,7},{7,8},{8,9},{9,10},{10,1... | collective-permute-start | bytes 73736 | tf_op jit(solution)/shard_map/ppermute | solution.py:788
  43.8 7.2 %collective-permute-start.4 = (f32[48,128]{1,0:T(8,128)S(1)}, f32[48,128]{1,0:T(8,128)S(1)}, u32[]{:S(2)}, u32[]{:S(2)}) collective-permute-start(f32[48,128]{1,0:T(8,128)S(1)} %get-tuple-element.53.to_w), channel_id=1, source_target_pairs={{0,15},{1,0},{2,1},{3,2},{4,3},{5,4},{6,5},{7,6},{8,7},{9,8},{10,9... | collective-permute-start | bytes 73736 | tf_op jit(solution)/shard_map/ppermute | solution.py:788
  51.0 15.6 %copy-start = (f32[32,6,6,128]{3,0,2,1:T(8,128)S(1)}, f32[32,6,6,128]{3,0,2,1:T(8,128)}, u32[]{:S(2)}) copy-start(f32[32,6,6,128]{3,0,2,1:T(8,128)} %param.7) | copy-start | bytes 1769476
